TPU v7x, 32 devices: a whole 2x2x4 slice. The times are simulated.
32 devices in a mesh: dp: 8 (over y, x, core), tensor: 4 (over z).
Axes of the slice: x: 2, y: 2, z: 4, core: 2. Of those that a mesh axis runs over, the one named last changes fastest.
Arguments:
- tokens: bfloat16 [16384, 2048], P(('dp', 'tensor')), may hold values from -6 to 6
- upstream: bfloat16 [16384, 2048], P(('dp', 'tensor')), may hold values from -6 to 6
- lengths: int32 [8, 4], P('dp'), may hold values from 1 to 1024, as said below
- positions: int32 [8, 2048], P('dp'), may hold values from 0 to 9214, as said below
- pages: int32 [256], replicated, may hold values from 0 to 255, as said below
- attn_gain: bfloat16 [2048], P('dp'), may hold values from 0.099609375 to 1.8984375
- w_query: bfloat16 [2048, 2048], P('dp', 'tensor'), may hold values from -0.125 to 0.125
- w_key: bfloat16 [2048, 512], P('dp', 'tensor'), may hold values from -0.125 to 0.125
- w_value: bfloat16 [2048, 512], P('dp', 'tensor'), may hold values from -0.125 to 0.125
- w_out: bfloat16 [2048, 2048], P('tensor', 'dp'), may hold values from -1 to 1
- mlp_gain: bfloat16 [2048], P('dp'), may hold values from 0.099609375 to 1.8984375
- w_gate: bfloat16 [2048, 8192], P('dp', 'tensor'), may hold values from -0.125 to 0.125
- w_up: bfloat16 [2048, 8192], P('dp', 'tensor'), may hold values from -0.125 to 0.125
- w_down: bfloat16 [8192, 2048], P('tensor', 'dp'), may hold values from -0.0625 to 0.0625
Outputs:
- output: bfloat16 [16384, 2048], P(('dp', 'tensor'))
- grad_tokens: bfloat16 [16384, 2048], P(('dp', 'tensor'))
- grad_attn_gain: float32 [2048], P('dp')
- grad_w_query: float32 [2048, 2048], P('dp', 'tensor')
- grad_w_key: float32 [2048, 512], P('dp', 'tensor')
- grad_w_value: float32 [2048, 512], P('dp', 'tensor')
- grad_w_out: float32 [2048, 2048], P('tensor', 'dp')
- grad_mlp_gain: float32 [2048], P('dp')
- grad_w_gate: float32 [2048, 8192], P('dp', 'tensor')
- grad_w_up: float32 [2048, 8192], P('dp', 'tensor')
- grad_w_down: float32 [8192, 2048], P('tensor', 'dp')
Inputs may be any that keep to these rules, and one draw needn't show every extreme that they name: `lengths`: each row sums to 1920; the rows of a group past that sum are padding; the largest length in every row is exactly 1024. The rows of one sequence hold consecutive positions rising by one from its first position, which is below 8192; the longest sequence of each group starts at 8191; padding rows hold 0. A permutation; dealt page j and given page pages[j] lie on devices with the same tensor index, and the 8 dealt pages of one device come one from each dp index.
All inputs are finite; a program needn't handle non-finite values.
Results may differ from a plain program's by a relative error of at most 0.025.
Values may be sent and summed in bfloat16 or wider, within the bound.
A program may use at most 320 MiB of HBM per device.

v0:
```python
import jax
import jax.numpy as jnp
from jax import lax
from jax.sharding import PartitionSpec as P

HD = 64


epsilon = 1e-05
theta_base = 500000.0
masked_score = -1e30
block_rows = 512


def rope_tables(positions, head_dim):
    half_dim = head_dim // 2
    inverse_freq = theta_base ** (-(jnp.arange(half_dim, dtype=jnp.float32) * 2.0) / head_dim)
    angles = positions.astype(jnp.float32)[:, None] * inverse_freq[None, :]
    cos_table = jnp.concatenate([jnp.cos(angles), jnp.cos(angles)], axis=1)
    sine_table = jnp.concatenate([jnp.sin(angles), jnp.sin(angles)], axis=1)
    return (cos_table, sine_table)


def rotate(values, cos_table, sine_table):
    half_dim = values.shape[-1] // 2
    turned = jnp.concatenate([-values[..., half_dim:], values[..., :half_dim]], axis=-1)
    return values * cos_table[:, None, :] + turned * sine_table[:, None, :]


def unrotate(grads, cos_table, sine_table):
    half_dim = grads.shape[-1] // 2
    scaled = grads * sine_table[:, None, :]
    return grads * cos_table[:, None, :] + jnp.concatenate(
        [scaled[..., half_dim:], -scaled[..., :half_dim]], axis=-1
    )


def rms_scale(hidden):
    return lax.rsqrt(jnp.mean(hidden * hidden, axis=1, keepdims=True) + epsilon)


def norm_back(grad_norm, hidden, scale_rows, gain):
    normed = hidden * scale_rows
    gain_part = jnp.sum(grad_norm * normed, axis=0)
    inner = grad_norm * gain
    grad_hidden = scale_rows * (inner - normed * jnp.mean(inner * normed, axis=1, keepdims=True))
    return (grad_hidden, gain_part)


def contract_rows(left, right):
    return lax.dot_general(
        left, right, (((0,), (0,)), ((), ())), preferred_element_type=jnp.float32
    )


def contract_cols(left, right):
    return lax.dot_general(
        left, right, (((1,), (1,)), ((), ())), preferred_element_type=jnp.float32
    )


def masked_scores(q_block, keys_rot, segment, row_ids, row_start, block_len, score_scale):
    raw_scores = (
        jnp.einsum("qkgd,rkd->kgqr", q_block, keys_rot, preferred_element_type=jnp.float32)
        * score_scale
    )
    seg_rows = lax.dynamic_slice_in_dim(segment, row_start, block_len, 0)
    query_ids = row_start + jnp.arange(block_len, dtype=jnp.int32)
    allowed = (seg_rows[:, None] == segment[None, :]) & (row_ids[None, :] <= query_ids[:, None])
    return jnp.where(allowed[None, None], raw_scores, masked_score)


def attend_forward(queries, keys_rot, values, segment, score_scale):
    total_rows, q_heads, head_dim = queries.shape
    kv_heads = keys_rot.shape[1]
    groups = q_heads // kv_heads
    block_len = min(block_rows, total_rows)
    row_ids = jnp.arange(total_rows, dtype=jnp.int32)

    def one_block(row_start):
        q_block = lax.dynamic_slice_in_dim(queries, row_start, block_len, 0).reshape(
            block_len, kv_heads, groups, head_dim
        )
        scores = masked_scores(
            q_block, keys_rot, segment, row_ids, row_start, block_len, score_scale
        )
        row_max = jnp.max(scores, axis=-1, keepdims=True)
        exp_scores = jnp.exp(scores - row_max)
        row_sum = jnp.sum(exp_scores, axis=-1, keepdims=True)
        probs_low = (exp_scores / row_sum).astype(jnp.bfloat16)
        mixed = jnp.einsum("kgqr,rkd->qkgd", probs_low, values, preferred_element_type=jnp.float32)
        return (
            mixed.reshape(block_len, q_heads * head_dim).astype(jnp.bfloat16),
            (row_max + jnp.log(row_sum))[..., 0],
        )

    block_starts = jnp.arange(total_rows // block_len, dtype=jnp.int32) * block_len
    mixed_rows, log_sums = lax.map(one_block, block_starts)
    return (mixed_rows.reshape(total_rows, q_heads * head_dim), log_sums)


def attend_backward(queries, keys_rot, values, segment, log_sums, grad_mixed, score_scale):
    total_rows, q_heads, head_dim = queries.shape
    kv_heads = keys_rot.shape[1]
    groups = q_heads // kv_heads
    block_len = min(block_rows, total_rows)
    row_ids = jnp.arange(total_rows, dtype=jnp.int32)

    def one_block(carry, block_item):
        grad_keys, grad_vals = carry
        row_start, block_lse = block_item
        q_block = lax.dynamic_slice_in_dim(queries, row_start, block_len, 0).reshape(
            block_len, kv_heads, groups, head_dim
        )
        scores = masked_scores(
            q_block, keys_rot, segment, row_ids, row_start, block_len, score_scale
        )
        probs = jnp.exp(scores - block_lse[..., None])
        probs_low = probs.astype(jnp.bfloat16)
        grad_block = lax.dynamic_slice_in_dim(grad_mixed, row_start, block_len, 0).reshape(
            block_len, kv_heads, groups, head_dim
        )
        grad_probs = jnp.einsum(
            "qkgd,rkd->kgqr", grad_block, values, preferred_element_type=jnp.float32
        )
        inner = jnp.sum(probs * grad_probs, axis=-1, keepdims=True)
        grad_scores = (probs * (grad_probs - inner)).astype(jnp.bfloat16)
        grad_query = (
            jnp.einsum("kgqr,rkd->qkgd", grad_scores, keys_rot, preferred_element_type=jnp.float32)
            * score_scale
        )
        grad_keys = (
            grad_keys
            + jnp.einsum("kgqr,qkgd->rkd", grad_scores, q_block, preferred_element_type=jnp.float32)
            * score_scale
        )
        grad_vals = grad_vals + jnp.einsum(
            "kgqr,qkgd->rkd", probs_low, grad_block, preferred_element_type=jnp.float32
        )
        return ((grad_keys, grad_vals), grad_query.reshape(block_len, q_heads, head_dim))

    block_starts = jnp.arange(total_rows // block_len, dtype=jnp.int32) * block_len
    zero_kv = jnp.zeros((total_rows, kv_heads, head_dim), jnp.float32)
    (grad_keys, grad_vals), grad_queries = lax.scan(
        one_block, (zero_kv, zero_kv), (block_starts, log_sums)
    )
    return (grad_queries.reshape(total_rows, q_heads, head_dim), grad_keys, grad_vals)


def local(
    tokens,
    upstream,
    lengths,
    positions,
    pages,
    attn_gain,
    w_query,
    w_key,
    w_value,
    w_out,
    mlp_gain,
    w_gate,
    w_up,
    w_down,
):
    dp_count = lax.axis_size("dp")
    tp_count = lax.axis_size("tensor")
    dp_index = lax.axis_index("dp")
    tp_index = lax.axis_index("tensor")
    tok_dev = tokens.shape[0]
    tok_group = tok_dev * tp_count
    page_rows = tok_dev // dp_count
    head_dim = HD
    device = dp_index * tp_count + tp_index
    group_pages = tp_count * dp_count
    page_count = pages.shape[0]
    local_ids = jnp.arange(dp_count, dtype=jnp.int32)
    inverse = (
        jnp.zeros((page_count,), jnp.int32).at[pages].set(jnp.arange(page_count, dtype=jnp.int32))
    )
    dest_group = inverse[device * dp_count + local_ids] // group_pages
    send_order = jnp.zeros((dp_count,), jnp.int32).at[dest_group].set(local_ids)
    source_group = lax.dynamic_slice_in_dim(pages, device * dp_count, dp_count) // group_pages
    back_order = jnp.zeros((dp_count,), jnp.int32).at[source_group].set(local_ids)

    def reorder(rows, block_order):
        blocks = rows.reshape(dp_count, page_rows, rows.shape[1])
        return jnp.take(blocks, block_order, axis=0).reshape(rows.shape)

    got_tokens, got_upstream = (
        lax.all_to_all(reorder(tokens, send_order), "dp", split_axis=0, concat_axis=0, tiled=True),
        lax.all_to_all(
            reorder(upstream, send_order), "dp", split_axis=0, concat_axis=0, tiled=True
        ),
    )
    hidden_in = reorder(got_tokens, source_group).astype(jnp.float32)
    grad_top = reorder(got_upstream, source_group).astype(jnp.float32)
    seq_lens = lengths[0]
    seq_ends = jnp.cumsum(seq_lens)
    row_ids = jnp.arange(tok_group, dtype=jnp.int32)
    segment = jnp.sum((row_ids[:, None] >= seq_ends[None, :]).astype(jnp.int32), axis=1)
    valid_all = (segment < seq_lens.shape[0]).astype(jnp.float32)
    valid_rows = lax.dynamic_slice_in_dim(valid_all, tp_index * tok_dev, tok_dev, 0)
    cos_table, sine_table = rope_tables(positions[0], head_dim)
    weights = (
        lax.all_gather(attn_gain, "dp", axis=0, tiled=True),
        lax.all_gather(mlp_gain, "dp", axis=0, tiled=True),
        lax.all_gather(w_query, "dp", axis=0, tiled=True),
        lax.all_gather(w_key, "dp", axis=0, tiled=True),
        lax.all_gather(w_value, "dp", axis=0, tiled=True),
        lax.all_gather(w_gate, "dp", axis=0, tiled=True),
        lax.all_gather(w_up, "dp", axis=0, tiled=True),
        lax.all_gather(w_out, "dp", axis=1, tiled=True),
        lax.all_gather(w_down, "dp", axis=1, tiled=True),
    )
    (
        gain_one,
        gain_two,
        full_query,
        full_key,
        full_value,
        full_gate,
        full_up,
        full_out,
        full_down,
    ) = weights
    q_heads = full_query.shape[1] // head_dim
    kv_heads = full_key.shape[1] // head_dim
    score_scale = head_dim ** (-0.5)
    scale_one = rms_scale(hidden_in)
    normed_one = (hidden_in * scale_one * gain_one.astype(jnp.float32)).astype(jnp.bfloat16)
    attn_rows = lax.all_gather(normed_one, "tensor", axis=0, tiled=True)
    query_pre = jnp.dot(attn_rows, full_query, preferred_element_type=jnp.float32).reshape(
        tok_group, q_heads, head_dim
    )
    key_pre = jnp.dot(attn_rows, full_key, preferred_element_type=jnp.float32).reshape(
        tok_group, kv_heads, head_dim
    )
    queries = rotate(query_pre, cos_table, sine_table).astype(jnp.bfloat16)
    keys_rot = rotate(key_pre, cos_table, sine_table).astype(jnp.bfloat16)
    values = (
        jnp.dot(attn_rows, full_value, preferred_element_type=jnp.float32)
        .reshape(tok_group, kv_heads, head_dim)
        .astype(jnp.bfloat16)
    )
    attended, log_sums = attend_forward(queries, keys_rot, values, segment, score_scale)
    branch_one = lax.psum_scatter(
        jnp.dot(attended, full_out, preferred_element_type=jnp.float32).astype(jnp.bfloat16),
        "tensor",
        scatter_dimension=0,
        tiled=True,
    ).astype(jnp.float32)
    hidden_mid = hidden_in + branch_one
    scale_two = rms_scale(hidden_mid)
    normed_two = (hidden_mid * scale_two * gain_two.astype(jnp.float32)).astype(jnp.bfloat16)
    mlp_rows = lax.all_gather(normed_two, "tensor", axis=0, tiled=True)
    gate_pre = jnp.dot(mlp_rows, full_gate, preferred_element_type=jnp.float32)
    up_pre = jnp.dot(mlp_rows, full_up, preferred_element_type=jnp.float32)
    sigmoid_gate = jax.nn.sigmoid(gate_pre)
    activated = gate_pre * sigmoid_gate
    inner_act = (activated * up_pre).astype(jnp.bfloat16)
    branch_two = lax.psum_scatter(
        jnp.dot(inner_act, full_down, preferred_element_type=jnp.float32).astype(jnp.bfloat16),
        "tensor",
        scatter_dimension=0,
        tiled=True,
    ).astype(jnp.float32)
    hidden_out = hidden_mid + branch_two
    result = (hidden_out * valid_rows[:, None]).astype(jnp.bfloat16)
    grad_out = grad_top * valid_rows[:, None]
    grad_mlp = lax.all_gather(grad_out.astype(jnp.bfloat16), "tensor", axis=0, tiled=True)
    grad_down = contract_rows(inner_act, grad_mlp)
    grad_inner = contract_cols(grad_mlp, full_down)
    grad_upre = (grad_inner * activated).astype(jnp.bfloat16)
    grad_gpre = (
        grad_inner * up_pre * sigmoid_gate * (1.0 + gate_pre * (1.0 - sigmoid_gate))
    ).astype(jnp.bfloat16)
    grad_gate = contract_rows(mlp_rows, grad_gpre)
    grad_up = contract_rows(mlp_rows, grad_upre)
    grad_normed_two = lax.psum_scatter(
        (contract_cols(grad_gpre, full_gate) + contract_cols(grad_upre, full_up)).astype(
            jnp.bfloat16
        ),
        "tensor",
        scatter_dimension=0,
        tiled=True,
    ).astype(jnp.float32)
    grad_mid_norm, gain_two_part = norm_back(
        grad_normed_two, hidden_mid, scale_two, gain_two.astype(jnp.float32)
    )
    grad_mid = grad_out + grad_mid_norm
    grad_attn = lax.all_gather(grad_mid.astype(jnp.bfloat16), "tensor", axis=0, tiled=True)
    grad_wout = contract_rows(attended, grad_attn)
    grad_attended = contract_cols(grad_attn, full_out).astype(jnp.bfloat16)
    grad_queries, grad_keys, grad_vals = attend_backward(
        queries, keys_rot, values, segment, log_sums, grad_attended, score_scale
    )
    grad_qpre = (
        unrotate(grad_queries, cos_table, sine_table)
        .reshape(tok_group, q_heads * head_dim)
        .astype(jnp.bfloat16)
    )
    grad_kpre = (
        unrotate(grad_keys, cos_table, sine_table)
        .reshape(tok_group, kv_heads * head_dim)
        .astype(jnp.bfloat16)
    )
    grad_vpre = grad_vals.reshape(tok_group, kv_heads * head_dim).astype(jnp.bfloat16)
    grad_wquery = contract_rows(attn_rows, grad_qpre)
    grad_wkey = contract_rows(attn_rows, grad_kpre)
    grad_wvalue = contract_rows(attn_rows, grad_vpre)
    grad_normed_one = lax.psum_scatter(
        (
            contract_cols(grad_qpre, full_query)
            + contract_cols(grad_kpre, full_key)
            + contract_cols(grad_vpre, full_value)
        ).astype(jnp.bfloat16),
        "tensor",
        scatter_dimension=0,
        tiled=True,
    ).astype(jnp.float32)
    grad_in_norm, gain_one_part = norm_back(
        grad_normed_one, hidden_in, scale_one, gain_one.astype(jnp.float32)
    )
    grad_in = grad_mid + grad_in_norm
    grad_sums = (
        lax.psum_scatter(
            gain_one_part.astype(jnp.bfloat16), "dp", scatter_dimension=0, tiled=True
        ).astype(jnp.float32),
        lax.psum_scatter(
            gain_two_part.astype(jnp.bfloat16), "dp", scatter_dimension=0, tiled=True
        ).astype(jnp.float32),
        lax.psum_scatter(
            grad_wquery.astype(jnp.bfloat16), "dp", scatter_dimension=0, tiled=True
        ).astype(jnp.float32),
        lax.psum_scatter(
            grad_wkey.astype(jnp.bfloat16), "dp", scatter_dimension=0, tiled=True
        ).astype(jnp.float32),
        lax.psum_scatter(
            grad_wvalue.astype(jnp.bfloat16), "dp", scatter_dimension=0, tiled=True
        ).astype(jnp.float32),
        lax.psum_scatter(
            grad_gate.astype(jnp.bfloat16), "dp", scatter_dimension=0, tiled=True
        ).astype(jnp.float32),
        lax.psum_scatter(
            grad_up.astype(jnp.bfloat16), "dp", scatter_dimension=0, tiled=True
        ).astype(jnp.float32),
        lax.psum_scatter(
            grad_wout.astype(jnp.bfloat16), "dp", scatter_dimension=1, tiled=True
        ).astype(jnp.float32),
        lax.psum_scatter(
            grad_down.astype(jnp.bfloat16), "dp", scatter_dimension=1, tiled=True
        ).astype(jnp.float32),
    )
    (
        gain_one_sum,
        gain_two_sum,
        sum_query,
        sum_key,
        sum_value,
        sum_gate,
        sum_up,
        sum_out,
        sum_down,
    ) = grad_sums
    gain_totals = lax.psum((gain_one_sum, gain_two_sum), "tensor")
    back_result, back_grad = (
        lax.all_to_all(reorder(result, back_order), "dp", split_axis=0, concat_axis=0, tiled=True),
        lax.all_to_all(
            reorder(grad_in.astype(jnp.bfloat16), back_order),
            "dp",
            split_axis=0,
            concat_axis=0,
            tiled=True,
        ),
    )
    return (
        reorder(back_result, dest_group),
        reorder(back_grad, dest_group),
        gain_totals[0],
        sum_query,
        sum_key,
        sum_value,
        sum_out,
        gain_totals[1],
        sum_gate,
        sum_up,
        sum_down,
    )


def solution(mesh):
    return jax.shard_map(
        local,
        mesh=mesh,
        in_specs=(
            P(("dp", "tensor"), None),
            P(("dp", "tensor"), None),
            P("dp", None),
            P("dp", None),
            P(),
            P("dp"),
            P("dp", "tensor"),
            P("dp", "tensor"),
            P("dp", "tensor"),
            P("tensor", "dp"),
            P("dp"),
            P("dp", "tensor"),
            P("dp", "tensor"),
            P("tensor", "dp"),
        ),
        out_specs=(
            P(("dp", "tensor"), None),
            P(("dp", "tensor"), None),
            P("dp"),
            P("dp", "tensor"),
            P("dp", "tensor"),
            P("dp", "tensor"),
            P("tensor", "dp"),
            P("dp"),
            P("dp", "tensor"),
            P("dp", "tensor"),
            P("tensor", "dp"),
        ),
        check_vma=False,
    )
```

profile of v0, /device:TPU:0, one launch (start us, length us, event | category | flops | bytes accessed | tf_op | source)
XLA Modules:
  0.0 2822.6 jit_solution(15391028750762285061)
XLA Ops:
  25.9 29.6 %all-gather = bf16[8,1,256]{2,1,0:T(2,128)(2,1)S(1)} all-gather(bf16[1,1,256]{2,1,0:T(2,128)(2,1)S(1)} %reshape.538), channel_id=1, replica_groups=mesh['dp'=8,'tensor'=4] {'dp'}, dimensions={0}, use_global_device_ids=true | all-gather | bytes 4608 | tf_op jit(solution)/shard_map/all_gather | solution.py:206
  83.2 127.5 %all-gather.12.cloned.1.call-done = bf16[2048,2048]{1,0:T(8,128)(2,1)} async-done(((bf16[512,2048]{1,0:T(8,128)(2,1)}), bf16[2048,2048]{1,0:T(8,128)(2,1)}) %all-gather.12.cloned.1.call-update) | async-done | bytes 8388624 | tf_op jit(solution)/shard_map/all_gather | solution.py:232
  218.0 20.7 all-gather.14.cloned.1.call-done
  254.9 201.4 %while.28 = (s32[]{:T(128)}, bf16[4,512,512]{2,1,0:T(8,128)(2,1)}, f32[4,2,4,512]{3,2,1,0:T(4,128)}, s32[4]{0:T(128)S(1)}, s32[2048]{0:T(1024)S(1)}, /*index=5*/...) while((s32[]{:T(128)}, bf16[4,512,512]{2,1,0:T(8,128)(2,1)}, ...), condition=%wide.region_8.10_spmd.clone, body=%wide.region_5.9_spmd.clone.sunk | while | flops 2251551232 | bytes 110250160 | solution.py:98
  476.3 135.1 %reduce-scatter.12.cloned.1.call-done = bf16[512,2048]{1,0:T(8,128)(2,1)} async-done(((bf16[2048,2048]{1,0:T(8,128)(2,1)}), bf16[512,2048]{1,0:T(8,128)(2,1)}) %reduce-scatter.12.cloned.1.call-update) | async-done | bytes 2097168 | tf_op jit(solution)/shard_map/reduce_scatter | solution.py:247
  621.3 37.7 %all-to-all-done.2 = bf16[8,64,2048]{2,1,0:T(8,128)(2,1)S(1)} async-done(((bf16[8,64,2048]{2,1,0:T(8,128)(2,1)}), bf16[8,64,2048]{2,1,0:T(8,128)(2,1)S(1)}, u32[]{:S(2)}, u32[]{:S(2)}) %all-to-all-start.2) | async-done | bytes 2097184 | tf_op jit(solution)/shard_map/all_to_all | solution.py:192
  665.8 24.1 all-gather.22.cloned.1.call-done
  689.9 151.7 %all-gather.18.cloned.1.call-done = bf16[2048,2048]{1,0:T(8,128)(2,1)} async-done(((bf16[512,2048]{1,0:T(8,128)(2,1)}), bf16[2048,2048]{1,0:T(8,128)(2,1)}) %all-gather.18.cloned.1.call-update) | async-done | bytes 8388624 | tf_op jit(solution)/shard_map/all_gather | solution.py:256
  841.6 24.5 fusion.80
  866.0 30.1 %all-gather.20.cloned.1.call-done = bf16[2048,2048]{1,0:T(8,128)(2,1)} async-done(((bf16[256,2048]{1,0:T(8,128)(2,1)}), bf16[2048,2048]{1,0:T(8,128)(2,1)}) %all-gather.20.cloned.1.call-update) | async-done | bytes 8388624 | tf_op jit(solution)/shard_map/all_gather | solution.py:211
  896.1 24.2 fusion.79
  920.3 127.6 %all-gather.26.cloned.1.call-done = bf16[2048,2048]{1,0:T(8,128)(2,1)} async-done(((bf16[512,2048]{1,0:T(8,128)(2,1)}), bf16[2048,2048]{1,0:T(8,128)(2,1)}) %all-gather.26.cloned.1.call-update) | async-done | bytes 8388624 | tf_op jit(solution)/shard_map/all_gather | solution.py:271
  1047.9 56.1 %all-gather.24.cloned.1.call-done = bf16[2048,2048]{1,0:T(8,128)(2,1)} async-done(((bf16[2048,256]{1,0:T(8,128)(2,1)}), bf16[2048,2048]{1,0:T(8,128)(2,1)}) %all-gather.24.cloned.1.call-update) | async-done | bytes 8388624 | tf_op jit(solution)/shard_map/all_gather | solution.py:214
  1104.0 37.0 %multiply_convert_fusion = (bf16[2048,2048]{1,0:T(8,128)(2,1)}, bf16[2048,2048]{1,0:T(8,128)(2,1)}, bf16[2048,2048]{1,0:T(8,128)(2,1)}) fusion(f32[2048,2048]{1,0:T(8,128)} %fusion.79, f32[2048,2048]{1,0:T(8,128)} %fusion.80, bf16[2048,2048]{1,0:T(8,128)(2,1)} %all-gather.26.cloned.1.call-done, bf16[2048,2048]{1,0:T(8,128)(2,1)} %all-gather.24.cloned.1.call-done), kind=kOutput, calls=%fused_computation.65 | convolution fusion | flops 17242783744 | bytes 75497472 | tf_op jit(solution)/shard_map/dot_general | solution.py:57
  1141.0 24.4 fusion.81
  1165.4 25.7 add_convert_fusion.1
  1191.2 144.6 %reduce-scatter.16.cloned.1.call-done = bf16[512,2048]{1,0:T(8,128)(2,1)} async-done(((bf16[2048,2048]{1,0:T(8,128)(2,1)}), bf16[512,2048]{1,0:T(8,128)(2,1)}) %reduce-scatter.16.cloned.1.call-update) | async-done | bytes 2097168 | tf_op jit(solution)/shard_map/reduce_scatter | solution.py:280
  1344.7 150.4 %all-gather.28.cloned.1.call-done = bf16[2048,2048]{1,0:T(8,128)(2,1)} async-done(((bf16[512,2048]{1,0:T(8,128)(2,1)}), bf16[2048,2048]{1,0:T(8,128)(2,1)}) %all-gather.28.cloned.1.call-update) | async-done | bytes 8388624 | tf_op jit(solution)/shard_map/all_gather | solution.py:292
  1505.0 509.5 %while.29 = (s32[]{:T(128)}, f32[2048,2,64]{0,2,1:T(8,128)S(1)}, f32[2048,2,64]{0,2,1:T(8,128)}, f32[4,512,8,64]{1,0,3,2:T(4,128)}, s32[4]{0:T(128)S(1)}, /*inde...) while((s32[]{:T(128)}, f32[2048,2,64]{0,2,1:T(8,128)S(1)}, ...), condition=%wide.region_17.19_spmd.clone, body=%wide.region_15.18_spmd.clone.sunk | while | flops 5499253248 | bytes 351930752 | solution.py:144
  1527.7 15.0 fusion.172
  1542.7 24.3 fusion.169
  1567.0 27.7 fusion.170
  1611.6 21.0 dynamic_update_slice.22
  1654.9 15.0 fusion.172
  1670.0 24.3 fusion.169
  1694.3 27.7 fusion.170
  1738.9 21.0 dynamic_update_slice.22
  1797.2 24.3 fusion.169
  1821.5 27.7 fusion.170
  1866.1 21.0 dynamic_update_slice.22
  1924.4 24.3 fusion.169
  1948.7 27.7 fusion.170
  1993.3 21.0 dynamic_update_slice.22
  2048.8 15.4 add_convert_fusion
  2064.3 23.8 convolution_convert_fusion.3
  2088.2 23.9 convolution_convert_fusion
  2112.1 24.2 convolution_convert_fusion.1
  2136.4 24.1 convolution_convert_fusion.2
  2185.0 22.1 reduce-scatter.18.cloned.1.call-done
  2210.3 144.4 %reduce-scatter.14.cloned.1.call-done = bf16[512,2048]{1,0:T(8,128)(2,1)} async-done(((bf16[2048,2048]{1,0:T(8,128)(2,1)}), bf16[512,2048]{1,0:T(8,128)(2,1)}) %reduce-scatter.14.cloned.1.call-update) | async-done | bytes 2097168 | tf_op jit(solution)/shard_map/reduce_scatter | solution.py:262
  2386.6 33.0 %all-to-all-done.3 = bf16[8,64,2048]{2,1,0:T(8,128)(2,1)S(1)} async-done(((bf16[8,64,2048]{2,1,0:T(8,128)(2,1)}), bf16[8,64,2048]{2,1,0:T(8,128)(2,1)S(1)}, u32[]{:S(2)}, u32[]{:S(2)}) %all-to-all-start.3) | async-done | bytes 2097184 | tf_op jit(solution)/shard_map/all_to_all | solution.py:369
  2425.2 32.0 %reduce-scatter.32.cloned.1.call-done = bf16[2048,256]{1,0:T(8,128)(2,1)} async-done(((bf16[2048,2048]{1,0:T(8,128)(2,1)}), bf16[2048,256]{1,0:T(8,128)(2,1)}) %reduce-scatter.32.cloned.1.call-update) | async-done | bytes 1048592 | tf_op jit(solution)/shard_map/reduce_scatter | solution.py:351
  2460.0 77.9 %reduce-scatter.30.cloned.1.call-done = bf16[256,2048]{1,0:T(8,128)(2,1)} async-done(((bf16[2048,2048]{1,0:T(8,128)(2,1)}), bf16[256,2048]{1,0:T(8,128)(2,1)}) %reduce-scatter.30.cloned.1.call-update) | async-done | bytes 1048592 | tf_op jit(solution)/shard_map/reduce_scatter | solution.py:345
  2540.6 71.8 %reduce-scatter.28.cloned.1.call-done = bf16[256,2048]{1,0:T(8,128)(2,1)} async-done(((bf16[2048,2048]{1,0:T(8,128)(2,1)}), bf16[256,2048]{1,0:T(8,128)(2,1)}) %reduce-scatter.28.cloned.1.call-update) | async-done | bytes 1048592 | tf_op jit(solution)/shard_map/reduce_scatter | solution.py:342
  2615.2 35.1 %reduce-scatter.24.cloned.1.call-done = bf16[256,128]{1,0:T(8,128)(2,1)} async-done(((bf16[2048,128]{1,0:T(8,128)(2,1)}), bf16[256,128]{1,0:T(8,128)(2,1)}) %reduce-scatter.24.cloned.1.call-update) | async-done | bytes 65552 | tf_op jit(solution)/shard_map/reduce_scatter | solution.py:339
  2651.9 36.2 %reduce-scatter.22.cloned.1.call-done = bf16[256,128]{1,0:T(8,128)(2,1)} async-done(((bf16[2048,128]{1,0:T(8,128)(2,1)}), bf16[256,128]{1,0:T(8,128)(2,1)}) %reduce-scatter.22.cloned.1.call-update) | async-done | bytes 65552 | tf_op jit(solution)/shard_map/reduce_scatter | solution.py:336
  2689.6 43.4 %reduce-scatter.26.cloned.1.call-done = bf16[512,256]{1,0:T(8,128)(2,1)} async-done(((bf16[512,2048]{1,0:T(8,128)(2,1)}), bf16[512,256]{1,0:T(8,128)(2,1)}) %reduce-scatter.26.cloned.1.call-update) | async-done | bytes 262160 | tf_op jit(solution)/shard_map/reduce_scatter | solution.py:348
  2734.8 43.2 %reduce-scatter.20.cloned.1.call-done = bf16[256,512]{1,0:T(8,128)(2,1)} async-done(((bf16[2048,512]{1,0:T(8,128)(2,1)}), bf16[256,512]{1,0:T(8,128)(2,1)}) %reduce-scatter.20.cloned.1.call-update) | async-done | bytes 262160 | tf_op jit(solution)/shard_map/reduce_scatter | solution.py:333
  (420 shorter events, 645.8 us)
Async XLA Ops:
  20.6 35.2 %all-to-all-start = ((bf16[8,64,2048]{2,1,0:T(8,128)(2,1)}), bf16[8,64,2048]{2,1,0:T(8,128)(2,1)}, u32[]{:S(2)}, u32[]{:S(2)}) async-start(bf16[8,64,2048]{2,1,0:T(8,128)(2,1)} %get-tuple-element.303), calls=%async_computation | async-start | bytes 4194304 | tf_op jit(solution)/shard_map/all_to_all | solution.py:191
  25.9 184.8 %all-gather.12.cloned.1.call-start = ((), (), s32[]{:S(2)}) async-start(), calls=%async_computation.15 | async-start | bytes 10485760 | tf_op jit(solution)/shard_map/all_gather | solution.py:232
  60.9 177.8 %all-gather.14.cloned.1.call-start = ((), (), s32[]{:S(2)}) async-start(), calls=%async_computation.16 | async-start | bytes 2359296 | tf_op jit(solution)/shard_map/all_gather | solution.py:208
  61.7 394.7 %all-gather.16.cloned.1.call-start = ((), (), s32[]{:S(2)}) async-start(), calls=%async_computation.17 | async-start | bytes 2359296 | tf_op jit(solution)/shard_map/all_gather | solution.py:213
  62.4 549.0 %reduce-scatter.12.cloned.1.call-start = ((), (), s32[]{:S(2)}) async-start(), calls=%async_computation.18 | async-start | bytes 10485760 | tf_op jit(solution)/shard_map/reduce_scatter | solution.py:247
  71.8 145.2 %copy-start.24 = (bf16[2048,128]{1,0:T(8,128)(2,1)}, bf16[2048,128]{1,0:T(8,128)(2,1)S(1)}, u32[]{:S(2)}) copy-start(bf16[2048,128]{1,0:T(8,128)(2,1)S(1)} %all_gather.42) | copy-start | bytes 1572868
  82.1 168.3 %copy-start.22 = (bf16[2048,128]{1,0:T(8,128)(2,1)}, bf16[2048,128]{1,0:T(8,128)(2,1)S(1)}, u32[]{:S(2)}) copy-start(bf16[2048,128]{1,0:T(8,128)(2,1)S(1)} %all_gather.43) | copy-start | bytes 1572868
  83.2 164.7 %copy-start.17 = (f32[2048,64]{0,1:T(8,128)}, f32[2048,64]{0,1:T(8,128)S(1)}, u32[]{:S(2)}) copy-start(f32[2048,64]{0,1:T(8,128)S(1)} %get-tuple-element.305) | copy-start | bytes 1572868
  83.2 164.7 %copy-start.19 = (f32[2048,64]{0,1:T(8,128)}, f32[2048,64]{0,1:T(8,128)S(1)}, u32[]{:S(2)}) copy-start(f32[2048,64]{0,1:T(8,128)S(1)} %get-tuple-element.304) | copy-start | bytes 1572868
  456.3 164.9 %copy-start.31 = (s32[2048]{0:T(1024)}, s32[2048]{0:T(1024)S(1)}, u32[]{:S(2)}) copy-start(s32[2048]{0:T(1024)S(1)} %get-tuple-element.567) | copy-start | bytes 24580
  466.8 144.6 %copy-start.4 = (bf16[8,64,2048]{2,1,0:T(8,128)(2,1)S(1)}, bf16[8,64,2048]{2,1,0:T(8,128)(2,1)}, u32[]{:S(2)}) copy-start(bf16[8,64,2048]{2,1,0:T(8,128)(2,1)} %copy-done.3) | copy-start | bytes 6291460
  466.8 144.6 %copy-start.46 = (pred[8]{0:T(512)(128)(4,1)S(1)}, pred[8]{0:T(512)(128)(4,1)}, u32[]{:S(2)}) copy-start(pred[8]{0:T(512)(128)(4,1)} %copy-done.45) | copy-start | bytes 28
  466.9 223.0 %all-gather.22.cloned.1.call-start = ((), (), s32[]{:S(2)}) async-start(), calls=%async_computation.21 | async-start | bytes 9437184 | tf_op jit(solution)/shard_map/all_gather | solution.py:212
  467.5 374.1 %all-gather.18.cloned.1.call-start = ((), (), s32[]{:S(2)}) async-start(), calls=%async_computation.19 | async-start | bytes 10485760 | tf_op jit(solution)/shard_map/all_gather | solution.py:256
  476.3 140.4 %copy-start.35 = (f32[8,1,256]{2,1,0:T(1,128)}, f32[8,1,256]{2,1,0:T(1,128)S(1)}, u32[]{:S(2)}) copy-start(f32[8,1,256]{2,1,0:T(1,128)S(1)} %convert_element_type.258) | copy-start | bytes 24580
  616.7 279.4 %all-gather.20.cloned.1.call-start = ((), (), s32[]{:S(2)}) async-start(), calls=%async_computation.20 | async-start | bytes 9437184 | tf_op jit(solution)/shard_map/all_gather | solution.py:211
  617.5 41.5 %all-to-all-start.2 = ((bf16[8,64,2048]{2,1,0:T(8,128)(2,1)}), bf16[8,64,2048]{2,1,0:T(8,128)(2,1)S(1)}, u32[]{:S(2)}, u32[]{:S(2)}) async-start(bf16[8,64,2048]{2,1,0:T(8,128)(2,1)} %get-tuple-element.302), calls=%async_computation.4 | async-start | bytes 4194304 | tf_op jit(solution)/shard_map/all_to_all | solution.py:192
  621.2 426.8 %all-gather.26.cloned.1.call-start = ((), (), s32[]{:S(2)}) async-start(), calls=%async_computation.24 | async-start | bytes 10485760 | tf_op jit(solution)/shard_map/all_gather | solution.py:271
  621.3 41.7 %copy-start.51 = (f32[512]{0:T(512)}, f32[512]{0:T(512)S(1)}, u32[]{:S(2)}) copy-start(f32[512]{0:T(512)S(1)} %fusion.65) | copy-start | bytes 6148
  662.9 203.1 %copy-start.11 = (bf16[8,64,2048]{2,1,0:T(8,128)(2,1)}, bf16[8,64,2048]{2,1,0:T(8,128)(2,1)S(1)}, u32[]{:S(2)}) copy-start(bf16[8,64,2048]{2,1,0:T(8,128)(2,1)S(1)} %broadcast_select_fusion.4) | copy-start | bytes 6291460
  665.0 439.0 %all-gather.24.cloned.1.call-start = ((), (), s32[]{:S(2)}) async-start(), calls=%async_computation.22 | async-start | bytes 9437184 | tf_op jit(solution)/shard_map/all_gather | solution.py:214
  665.7 670.0 %reduce-scatter.16.cloned.1.call-start = ((), (), s32[]{:S(2)}) async-start(), calls=%async_computation.25 | async-start | bytes 10485760 | tf_op jit(solution)/shard_map/reduce_scatter | solution.py:280
  1191.1 144.7 %copy-start.5 = (bf16[8,64,2048]{2,1,0:T(8,128)(2,1)S(1)}, bf16[8,64,2048]{2,1,0:T(8,128)(2,1)}, u32[]{:S(2)}) copy-start(bf16[8,64,2048]{2,1,0:T(8,128)(2,1)} %copy-done.3) | copy-start | bytes 6291460
  1191.1 144.7 %copy-start.36 = (f32[8,1,256]{2,1,0:T(1,128)S(1)}, f32[8,1,256]{2,1,0:T(1,128)}, u32[]{:S(2)}) copy-start(f32[8,1,256]{2,1,0:T(1,128)} %copy-done.35) | copy-start | bytes 24580
  1191.1 144.7 %copy-start.43 = (f32[512]{0:T(512)S(1)}, f32[512]{0:T(512)}, u32[]{:S(2)}) copy-start(f32[512]{0:T(512)} %copy-done.42) | copy-start | bytes 6148
  1191.1 144.7 %copy-start.47 = (pred[8]{0:T(512)(128)(4,1)S(1)}, pred[8]{0:T(512)(128)(4,1)}, u32[]{:S(2)}) copy-start(pred[8]{0:T(512)(128)(4,1)} %copy-done.45) | copy-start | bytes 28
  1191.1 150.0 %copy-start.52 = (f32[512]{0:T(512)S(1)}, f32[512]{0:T(512)}, u32[]{:S(2)}) copy-start(f32[512]{0:T(512)} %copy-done.51) | copy-start | bytes 6148
  1191.1 304.0 %all-gather.28.cloned.1.call-start = ((), (), s32[]{:S(2)}) async-start(), calls=%async_computation.26 | async-start | bytes 10485760 | tf_op jit(solution)/shard_map/all_gather | solution.py:292
  1344.6 862.5 %reduce-scatter.18.cloned.1.call-start = ((), (), s32[]{:S(2)}) async-start(), calls=%async_computation.27 | async-start | bytes 10485760 | tf_op jit(solution)/shard_map/reduce_scatter | solution.py:312
  1344.7 160.3 %copy-start.32 = (s32[2048]{0:T(1024)S(1)}, s32[2048]{0:T(1024)}, u32[]{:S(2)}) copy-start(s32[2048]{0:T(1024)} %copy-done.31) | copy-start | bytes 24580
  1344.7 160.3 %copy-start.69 = (s32[4]{0:T(128)S(1)}, s32[4]{0:T(128)}, u32[]{:S(2)}) copy-start(s32[4]{0:T(128)} %copy-done.68) | copy-start | bytes 52
  2064.2 290.4 %reduce-scatter.14.cloned.1.call-start = ((), (), s32[]{:S(2)}) async-start(), calls=%async_computation.23 | async-start | bytes 10485760 | tf_op jit(solution)/shard_map/reduce_scatter | solution.py:262
  2088.1 369.2 %reduce-scatter.32.cloned.1.call-start = ((), (), s32[]{:S(2)}) async-start(), calls=%async_computation.34 | async-start | bytes 9437184 | tf_op jit(solution)/shard_map/reduce_scatter | solution.py:351
  2112.1 425.8 %reduce-scatter.30.cloned.1.call-start = ((), (), s32[]{:S(2)}) async-start(), calls=%async_computation.33 | async-start | bytes 9437184 | tf_op jit(solution)/shard_map/reduce_scatter | solution.py:345
  2136.3 476.1 %reduce-scatter.28.cloned.1.call-start = ((), (), s32[]{:S(2)}) async-start(), calls=%async_computation.32 | async-start | bytes 9437184 | tf_op jit(solution)/shard_map/reduce_scatter | solution.py:342
  2160.5 489.9 %reduce-scatter.24.cloned.1.call-start = ((), (), s32[]{:S(2)}) async-start(), calls=%async_computation.30 | async-start | bytes 589824 | tf_op jit(solution)/shard_map/reduce_scatter | solution.py:339
  2167.1 520.9 %reduce-scatter.22.cloned.1.call-start = ((), (), s32[]{:S(2)}) async-start(), calls=%async_computation.29 | async-start | bytes 589824 | tf_op jit(solution)/shard_map/reduce_scatter | solution.py:336
  2174.0 559.0 %reduce-scatter.26.cloned.1.call-start = ((), (), s32[]{:S(2)}) async-start(), calls=%async_computation.31 | async-start | bytes 2359296 | tf_op jit(solution)/shard_map/reduce_scatter | solution.py:348
  2184.1 170.5 %copy-start.37 = (f32[8,1,256]{2,1,0:T(1,128)S(1)}, f32[8,1,256]{2,1,0:T(1,128)}, u32[]{:S(2)}) copy-start(f32[8,1,256]{2,1,0:T(1,128)} %copy-done.35) | copy-start | bytes 24580
  2184.1 170.5 %copy-start.44 = (f32[512]{0:T(512)S(1)}, f32[512]{0:T(512)}, u32[]{:S(2)}) copy-start(f32[512]{0:T(512)} %copy-done.42) | copy-start | bytes 6148
  2184.1 170.5 %copy-start.53 = (f32[512]{0:T(512)S(1)}, f32[512]{0:T(512)}, u32[]{:S(2)}) copy-start(f32[512]{0:T(512)} %copy-done.51) | copy-start | bytes 6148
  2184.2 170.5 %copy-start.55 = (f32[512]{0:T(512)S(1)}, f32[512]{0:T(512)}, u32[]{:S(2)}) copy-start(f32[512]{0:T(512)} %copy-done.54) | copy-start | bytes 6148
  2372.8 46.8 %all-to-all-start.3 = ((bf16[8,64,2048]{2,1,0:T(8,128)(2,1)}), bf16[8,64,2048]{2,1,0:T(8,128)(2,1)S(1)}, u32[]{:S(2)}, u32[]{:S(2)}) async-start(bf16[8,64,2048]{2,1,0:T(8,128)(2,1)} %get-tuple-element.300), calls=%async_computation.7 | async-start | bytes 4194304 | tf_op jit(solution)/shard_map/all_to_all | solution.py:369
  2376.4 401.5 %reduce-scatter.20.cloned.1.call-start = ((), (), s32[]{:S(2)}) async-start(), calls=%async_computation.28 | async-start | bytes 2359296 | tf_op jit(solution)/shard_map/reduce_scatter | solution.py:333
  2386.6 37.4 %copy-start.67 = (u32[32]{0:T(128)S(1)}, u32[32]{0:T(128)}, u32[]{:S(2)}) copy-start(u32[32]{0:T(128)} %constant.131) | copy-start | bytes 388
  2386.6 38.6 %copy-start.62 = (s32[8]{0:T(128)S(1)}, s32[8]{0:T(128)}, u32[]{:S(2)}) copy-start(s32[8]{0:T(128)} %copy-done.61) | copy-start | bytes 100
  2419.6 387.6 %all-to-all-start.1 = ((bf16[8,64,2048]{2,1,0:T(8,128)(2,1)}), bf16[8,64,2048]{2,1,0:T(8,128)(2,1)}, u32[]{:S(2)}, u32[]{:S(2)}) async-start(bf16[8,64,2048]{2,1,0:T(8,128)(2,1)} %get-tuple-element.301), calls=%async_computation.3 | async-start | bytes 4194304 | tf_op jit(solution)/shard_map/all_to_all | solution.py:368
  2460.0 319.8 %copy-start.56 = (bf16[2048]{0:T(1024)(128)(2,1)S(1)}, bf16[2048]{0:T(1024)(128)(2,1)}, u32[]{:S(2)}) copy-start(bf16[2048]{0:T(1024)(128)(2,1)} %get-tuple-element.229) | copy-start | bytes 12292
  (63 other events, 655.0 us)
Sparse Core Ops, SparseCore 0:
  61.0 149.6 all-gather.11
  212.6 26.1 all-gather.13
  240.6 28.1 all-gather.15
  467.0 144.3 reduce-scatter.11
  613.1 76.7 all-gather.21
  691.9 149.6 all-gather.17
  843.4 52.6 all-gather.19
  898.2 149.6 all-gather.25
  1049.8 54.1 all-gather.23
  1191.2 144.4 reduce-scatter.15
  1344.7 150.3 all-gather.27
  2064.4 142.6 reduce-scatter.17
  2209.4 145.1 reduce-scatter.13
  2358.0 99.2 reduce-scatter.31
  2461.0 76.8 reduce-scatter.29
  2541.2 71.2 reduce-scatter.27
  2616.3 34.0 reduce-scatter.23
  2653.9 34.1 reduce-scatter.21
  2691.7 41.2 reduce-scatter.25
  2736.7 41.1 reduce-scatter.19
where the time goes:
time: 2830 us; the launch traced here: 2820 us
  waiting for transfers between devices  1550 us (55%)
  matrix products  716 us (25%)
  other arithmetic  260 us (9%)
  local copies, waits for them, and re-layouts  164 us (6%)
  blocking collectives  82.8 us (3%)
    all_gather x1, waiting for transfers between devices, local(): mlp_rows = lax.all_gather(normed_two, 'tensor', axis=0, tiled=True)  152 us
    all_gather x1, waiting for transfers between devices, local(): lax.all_gather(grad_mid.astype(jnp.bfloat16), 'tensor', axis=0, tiled=True)  150 us
    reduce_scatter x1, waiting for transfers between devices, local(): lax.psum_scatter((contract_cols(grad_gpre, full_gate) + contract_cols(gra...  145 us
    reduce_scatter x1, waiting for transfers between devices, local(): lax.psum_scatter(jnp.dot(inner_act, full_down, preferred_element_type=jnp...  144 us
    reduce_scatter x1, waiting for transfers between devices, local(): lax.psum_scatter(jnp.dot(attended, full_out, preferred_element_type=jnp.f...  135 us
    dot_general x7, matrix products, contract_cols(): lax.dot_general(left, right, (((1,), (1,)), ((), ())), preferred_element_...  129 us
    all_gather x1, waiting for transfers between devices, local(): lax.all_gather(grad_out.astype(jnp.bfloat16), 'tensor', axis=0, tiled=True)  128 us
    all_gather x1, waiting for transfers between devices, local(): attn_rows = lax.all_gather(normed_one, 'tensor', axis=0, tiled=True)  127 us
  transfers between devices with their start and end apart: 24, of which 21 were waited for; matrix products, arithmetic and copies ran while one was open for 16% of the time, Pallas kernels for 0%

commit v1 on v0

v1 whole, which is shorter than its diff:
```python
import functools

import jax
import jax.numpy as jnp
from jax import lax
from jax.experimental import pallas as pl
from jax.experimental.pallas import tpu as pltpu
from jax.sharding import PartitionSpec as P

HD = 64
HALF = HD // 2

epsilon = 1e-05
theta_base = 500000.0
masked_score = -1e30
score_scale = HD**-0.5
block_rows = 256
MESH = pl.DeviceIdType.MESH
f32 = jnp.float32
bf16 = jnp.bfloat16


def dot_nn(left, right):
    return lax.dot_general(left, right, (((1,), (0,)), ((), ())), preferred_element_type=f32)


def dot_nt(left, right):
    return lax.dot_general(left, right, (((1,), (1,)), ((), ())), preferred_element_type=f32)


def dot_tn(left, right):
    return lax.dot_general(left, right, (((0,), (0,)), ((), ())), preferred_element_type=f32)


def exchange_kernel(dp_count, tp_count, page_rows, to_heads, src, dst, send_sem, recv_sem, own_sem):
    count = dp_count * tp_count
    my_dp = lax.axis_index("dp")
    my_tp = lax.axis_index("tensor")
    me = my_dp * tp_count + my_tp

    def split(peer):
        return lax.div(peer, tp_count), lax.rem(peer, tp_count)

    barrier = pltpu.get_barrier_semaphore()

    def greet(j, carry):
        p_dp, p_tp = split(lax.rem(me + j, count))
        pl.semaphore_signal(
            barrier, inc=1, device_id={"dp": p_dp, "tensor": p_tp}, device_id_type=MESH
        )
        return carry

    lax.fori_loop(1, count, greet, 0)
    pl.semaphore_wait(barrier, count - 1)

    def ends(p_dp, p_tp, peer):
        if to_heads:
            return src.at[p_tp, pl.ds(p_dp * page_rows, page_rows), :], dst.at[me]
        return src.at[peer], dst.at[my_tp, pl.ds(my_dp * page_rows, page_rows), :]

    own_src, own_dst = ends(my_dp, my_tp, me)
    own = pltpu.make_async_copy(own_src, own_dst, own_sem)
    own.start()

    def copy_to(j):
        peer = lax.rem(me + j, count)
        p_dp, p_tp = split(peer)
        block_src, block_dst = ends(p_dp, p_tp, peer)
        return pltpu.make_async_remote_copy(
            src_ref=block_src,
            dst_ref=block_dst,
            send_sem=send_sem.at[j],
            recv_sem=recv_sem.at[j],
            device_id={"dp": p_dp, "tensor": p_tp},
            device_id_type=MESH,
        )

    def start(j, carry):
        copy_to(j).start()
        return carry

    def finish(j, carry):
        copy_to(j).wait()
        return carry

    lax.fori_loop(1, count, start, 0)
    own.wait()
    lax.fori_loop(1, count, finish, 0)


def exchange(array, dp_count, tp_count, page_rows, to_heads, collective_id):
    cols = array.shape[-1]
    count = dp_count * tp_count
    if to_heads:
        out_shape = (count, page_rows, cols)
    else:
        out_shape = (tp_count, dp_count * page_rows, cols)
    nbytes = array.size * 2
    return pl.pallas_call(
        functools.partial(exchange_kernel, dp_count, tp_count, page_rows, to_heads),
        out_shape=jax.ShapeDtypeStruct(out_shape, array.dtype),
        in_specs=[pl.BlockSpec(memory_space=pl.ANY)],
        out_specs=pl.BlockSpec(memory_space=pl.ANY),
        scratch_shapes=[
            pltpu.SemaphoreType.DMA((count,)),
            pltpu.SemaphoreType.DMA((count,)),
            pltpu.SemaphoreType.DMA,
        ],
        compiler_params=pltpu.CompilerParams(collective_id=collective_id, has_side_effects=True),
        cost_estimate=pl.CostEstimate(flops=0, bytes_accessed=40 * nbytes, transcendentals=0),
        name="exchange",
    )(array)


def prep_kernel(pages_per, q_heads, kv_heads, perm, *refs):
    page_refs = refs[:pages_per]
    cos_ref, sin_ref, q_t, k_t, k_rows, v_t, v_rows = refs[pages_per:]
    rows = jnp.concatenate([r[0].astype(f32) for r in page_refs], axis=0)
    turned = rows.T
    cos, sin = cos_ref[...], sin_ref[...]

    def rope(base):
        first, second = turned[base : base + HALF], turned[base + HALF : base + HD]
        return jnp.concatenate([first * cos - second * sin, second * cos + first * sin], axis=0)

    for h in range(q_heads):
        roped = rope(h * HD).astype(bf16)
        q_t[h * HD : (h + 1) * HD, :] = (roped.astype(f32) * score_scale).astype(bf16)
    k_base = q_heads * HD
    v_base = k_base + kv_heads * HD
    for g in range(kv_heads):
        roped = rope(k_base + g * HD)
        k_t[g * HD : (g + 1) * HD, :] = roped.astype(bf16)
        k_rows[g] = roped.T.astype(bf16)
        v_t[g * HD : (g + 1) * HD, :] = turned[v_base + g * HD : v_base + (g + 1) * HD].astype(bf16)
        v_rows[g] = rows[:, v_base + g * HD : v_base + (g + 1) * HD].astype(bf16)


def prepare(slots, perm, cos_t, sin_t, q_heads, kv_heads):
    page_rows, cols = slots.shape[1:]
    total_rows = slots.shape[0] * page_rows
    lanes = 128
    pages_per = lanes // page_rows

    def page_spec(a):
        return pl.BlockSpec(
            (1, page_rows, cols), lambda i, perm_ref, a=a: (perm_ref[i * pages_per + a], 0, 0)
        )

    table = pl.BlockSpec((HALF, lanes), lambda i, perm_ref: (0, i))
    return pl.pallas_call(
        functools.partial(prep_kernel, pages_per, q_heads, kv_heads),
        grid_spec=pltpu.PrefetchScalarGridSpec(
            num_scalar_prefetch=1,
            grid=(total_rows // lanes,),
            in_specs=[page_spec(a) for a in range(pages_per)] + [table, table],
            out_specs=[
                pl.BlockSpec((q_heads * HD, lanes), lambda i, perm_ref: (0, i)),
                pl.BlockSpec((kv_heads * HD, lanes), lambda i, perm_ref: (0, i)),
                pl.BlockSpec((kv_heads, lanes, HD), lambda i, perm_ref: (0, i, 0)),
                pl.BlockSpec((kv_heads * HD, lanes), lambda i, perm_ref: (0, i)),
                pl.BlockSpec((kv_heads, lanes, HD), lambda i, perm_ref: (0, i, 0)),
            ],
        ),
        out_shape=[
            jax.ShapeDtypeStruct((q_heads * HD, total_rows), bf16),
            jax.ShapeDtypeStruct((kv_heads * HD, total_rows), bf16),
            jax.ShapeDtypeStruct((kv_heads, total_rows, HD), bf16),
            jax.ShapeDtypeStruct((kv_heads * HD, total_rows), bf16),
            jax.ShapeDtypeStruct((kv_heads, total_rows, HD), bf16),
        ],
        cost_estimate=pl.CostEstimate(
            flops=8 * slots.size, bytes_accessed=6 * slots.size, transcendentals=0
        ),
        name="prepare",
    )(perm, *([slots] * pages_per), cos_t, sin_t)


def block_bias(i, j, begin_row, block_len):
    keys = j * block_len + lax.broadcasted_iota(jnp.int32, (block_len, block_len), 0)
    queries = i * block_len + lax.broadcasted_iota(jnp.int32, (block_len, block_len), 1)
    allowed = (keys >= begin_row) & (keys <= queries)
    return jnp.where(allowed, 0.0, masked_score)


def forward_kernel(
    q_heads, kv_heads, page_rows, first_block, perm,
    q_t, k_rows, v_t, begin, o_t, lse, o_slots, acc, top, total, stage, sems,
):
    i = pl.program_id(0)
    block_len = q_t.shape[1]
    per_group = q_heads // kv_heads
    acc[...] = jnp.zeros_like(acc)
    top[...] = jnp.full_like(top, masked_score)
    total[...] = jnp.zeros_like(total)
    begin_row = begin[...]

    def visit(j, carry):
        bias = block_bias(i, j, begin_row, block_len)
        at = pl.ds(pl.multiple_of(j * block_len, block_len), block_len)
        for h in range(q_heads):
            g = h // per_group
            span = slice(h * HD, (h + 1) * HD)
            scores = dot_nn(k_rows[g, at, :], q_t[span, :]) + bias
            old = top[h : h + 1, :]
            new = jnp.maximum(old, jnp.max(scores, axis=0, keepdims=True))
            weights = jnp.exp(scores - new)
            fade = jnp.exp(old - new)
            total[h : h + 1, :] = total[h : h + 1, :] * fade + jnp.sum(
                weights, axis=0, keepdims=True
            )
            top[h : h + 1, :] = new
            acc[span, :] = acc[span, :] * fade + dot_nn(
                v_t[g * HD : (g + 1) * HD, at], weights.astype(bf16)
            )
        return carry

    lax.fori_loop(first_block[i], i + 1, visit, 0)
    lse[...] = top[...] + jnp.log(total[...])
    scaled = [
        acc[h * HD : (h + 1) * HD, :] / total[h : h + 1, :] for h in range(q_heads)
    ]
    mixed = jnp.concatenate(scaled, axis=0)
    o_t[...] = mixed.astype(bf16)
    pages = block_len // page_rows
    stage[...] = mixed.T.astype(bf16).reshape(pages, page_rows, q_heads * HD)
    copies = [
        pltpu.make_async_copy(stage.at[a], o_slots.at[perm[i * pages + a]], sems.at[a])
        for a in range(pages)
    ]
    for copy in copies:
        copy.start()
    for copy in copies:
        copy.wait()


def attend_forward(q_t, k_rows, v_t, begin, first_block, perm, page_rows, block_len):
    total_rows = q_t.shape[1]
    kv_heads = k_rows.shape[0]
    q_heads = q_t.shape[0] // HD
    pages = block_len // page_rows
    return pl.pallas_call(
        functools.partial(forward_kernel, q_heads, kv_heads, page_rows),
        grid_spec=pltpu.PrefetchScalarGridSpec(
            num_scalar_prefetch=2,
            grid=(total_rows // block_len,),
            in_specs=[
                pl.BlockSpec((q_heads * HD, block_len), lambda i, *_: (0, i)),
                pl.BlockSpec((kv_heads, total_rows, HD), lambda i, *_: (0, 0, 0)),
                pl.BlockSpec((kv_heads * HD, total_rows), lambda i, *_: (0, 0)),
                pl.BlockSpec((1, block_len), lambda i, *_: (0, i)),
            ],
            out_specs=[
                pl.BlockSpec((q_heads * HD, block_len), lambda i, *_: (0, i)),
                pl.BlockSpec((q_heads, block_len), lambda i, *_: (0, i)),
                pl.BlockSpec(memory_space=pl.ANY),
            ],
            scratch_shapes=[
                pltpu.VMEM((q_heads * HD, block_len), f32),
                pltpu.VMEM((q_heads, block_len), f32),
                pltpu.VMEM((q_heads, block_len), f32),
                pltpu.VMEM((pages, page_rows, q_heads * HD), bf16),
                pltpu.SemaphoreType.DMA((pages,)),
            ],
        ),
        out_shape=[
            jax.ShapeDtypeStruct((q_heads * HD, total_rows), bf16),
            jax.ShapeDtypeStruct((q_heads, total_rows), f32),
            jax.ShapeDtypeStruct((total_rows // page_rows, page_rows, q_heads * HD), bf16),
        ],
        cost_estimate=pl.CostEstimate(
            flops=q_heads * total_rows * total_rows * HD,
            bytes_accessed=8 * q_t.size,
            transcendentals=q_heads * total_rows * total_rows // 4,
        ),
        name="attend_forward",
    )(first_block, perm, q_t, k_rows, v_t, begin)


def backward_kernel(
    q_heads, kv_heads, page_rows, pages, first_block, perm, *refs
):
    grad_pages = refs[:pages]
    (
        q_t, k_rows, k_t, v_rows, o_t, lse, begin, cos_ref, sin_ref, cos_all, sin_all,
        out, grad_q, grad_k, grad_v, stage, kv_stage, sems, kv_sems,
    ) = refs[pages:]
    i = pl.program_id(0)
    steps = pl.num_programs(0)
    block_len = q_t.shape[1]
    per_group = q_heads // kv_heads
    q_cols = q_heads * HD
    kv_cols = kv_heads * HD

    @pl.when(i == 0)
    def _():
        grad_k[...] = jnp.zeros_like(grad_k)
        grad_v[...] = jnp.zeros_like(grad_v)

    grad_rows = jnp.concatenate([r[0].astype(f32) for r in grad_pages], axis=0)
    grad_t = grad_rows.T
    grad_low = grad_t.astype(bf16)
    inner = [
        jnp.sum(
            grad_t[h * HD : (h + 1) * HD] * o_t[h * HD : (h + 1) * HD, :].astype(f32),
            axis=0,
            keepdims=True,
        )
        for h in range(q_heads)
    ]
    grad_q[...] = jnp.zeros_like(grad_q)
    begin_row = begin[...]

    def visit(j, carry):
        bias = block_bias(i, j, begin_row, block_len)
        at = pl.ds(pl.multiple_of(j * block_len, block_len), block_len)
        for g in range(kv_heads):
            kv_span = slice(g * HD, (g + 1) * HD)
            keys, vals, keys_t = k_rows[g, at, :], v_rows[g, at, :], k_t[kv_span, at]
            add_k = jnp.zeros((HD, block_len), f32)
            add_v = jnp.zeros((HD, block_len), f32)
            for h in range(g * per_group, (g + 1) * per_group):
                span = slice(h * HD, (h + 1) * HD)
                queries = q_t[span, :]
                probs = jnp.exp(dot_nn(keys, queries) + bias - lse[h : h + 1, :])
                grad_h = grad_low[span]
                grad_probs = dot_nn(vals, grad_h)
                grad_scores = (probs * (grad_probs - inner[h])).astype(bf16)
                add_v = add_v + dot_nt(grad_h, probs.astype(bf16))
                add_k = add_k + dot_nt(queries, grad_scores)
                grad_q[span, :] = grad_q[span, :] + dot_nn(keys_t, grad_scores)
            grad_k[kv_span, at] = grad_k[kv_span, at] + add_k
            grad_v[kv_span, at] = grad_v[kv_span, at] + add_v
        return carry

    lax.fori_loop(first_block[i], i + 1, visit, 0)

    def unrope(value, cos, sin):
        first, second = value[:HALF], value[HALF:]
        return jnp.concatenate([first * cos + second * sin, second * cos - first * sin], axis=0)

    cos, sin = cos_ref[...], sin_ref[...]
    parts = [
        unrope(grad_q[h * HD : (h + 1) * HD, :] * score_scale, cos, sin) for h in range(q_heads)
    ]
    stage[...] = jnp.concatenate(parts, axis=0).T.astype(bf16).reshape(pages, page_rows, q_cols)
    copies = [
        pltpu.make_async_copy(
            stage.at[a], out.at[perm[i * pages + a], :, pl.ds(0, q_cols)], sems.at[a]
        )
        for a in range(pages)
    ]
    for copy in copies:
        copy.start()
    for copy in copies:
        copy.wait()

    @pl.when(i == steps - 1)
    def _():
        all_pages = kv_stage.shape[0]
        cos, sin = cos_all[...], sin_all[...]
        parts = [unrope(grad_k[g * HD : (g + 1) * HD, :], cos, sin) for g in range(kv_heads)]
        both = jnp.concatenate(parts + [grad_v[...]], axis=0)
        kv_stage[...] = both.T.astype(bf16).reshape(all_pages, page_rows, 2 * kv_cols)
        copies = [
            pltpu.make_async_copy(
                kv_stage.at[a], out.at[perm[a], :, pl.ds(q_cols, 2 * kv_cols)], kv_sems.at[a]
            )
            for a in range(all_pages)
        ]
        for copy in copies:
            copy.start()
        for copy in copies:
            copy.wait()


def attend_backward(
    grad_slots, q_t, k_rows, k_t, v_rows, o_t, lse, begin, cos_t, sin_t, first_block, perm,
    page_rows, block_len,
):
    total_rows = q_t.shape[1]
    kv_heads = k_rows.shape[0]
    q_heads = q_t.shape[0] // HD
    pages = block_len // page_rows
    all_pages = total_rows // page_rows
    q_cols = q_heads * HD
    kv_cols = kv_heads * HD

    def page_spec(a):
        return pl.BlockSpec(
            (1, page_rows, q_cols),
            lambda i, first_ref, perm_ref, a=a: (perm_ref[i * pages + a], 0, 0),
        )

    def whole(shape):
        return pl.BlockSpec(shape, lambda i, *_: (0,) * len(shape))

    def column(rows):
        return pl.BlockSpec((rows, block_len), lambda i, *_: (0, i))

    return pl.pallas_call(
        functools.partial(backward_kernel, q_heads, kv_heads, page_rows, pages),
        grid_spec=pltpu.PrefetchScalarGridSpec(
            num_scalar_prefetch=2,
            grid=(total_rows // block_len,),
            in_specs=[page_spec(a) for a in range(pages)]
            + [
                column(q_cols),
                whole((kv_heads, total_rows, HD)),
                whole((kv_cols, total_rows)),
                whole((kv_heads, total_rows, HD)),
                column(q_cols),
                column(q_heads),
                column(1),
                column(HALF),
                column(HALF),
                whole((HALF, total_rows)),
                whole((HALF, total_rows)),
            ],
            out_specs=pl.BlockSpec(memory_space=pl.ANY),
            scratch_shapes=[
                pltpu.VMEM((q_cols, block_len), f32),
                pltpu.VMEM((kv_cols, total_rows), f32),
                pltpu.VMEM((kv_cols, total_rows), f32),
                pltpu.VMEM((pages, page_rows, q_cols), bf16),
                pltpu.VMEM((all_pages, page_rows, 2 * kv_cols), bf16),
                pltpu.SemaphoreType.DMA((pages,)),
                pltpu.SemaphoreType.DMA((all_pages,)),
            ],
        ),
        out_shape=jax.ShapeDtypeStruct((all_pages, page_rows, q_cols + 2 * kv_cols), bf16),
        cost_estimate=pl.CostEstimate(
            flops=3 * q_heads * total_rows * total_rows * HD,
            bytes_accessed=12 * q_t.size,
            transcendentals=q_heads * total_rows * total_rows // 4,
        ),
        name="attend_backward",
    )(
        first_block, perm, *([grad_slots] * pages), q_t, k_rows, k_t, v_rows, o_t, lse, begin,
        cos_t, sin_t, cos_t, sin_t,
    )


def rms_scale(hidden):
    return lax.rsqrt(jnp.mean(hidden * hidden, axis=1, keepdims=True) + epsilon)


def norm_back(grad_norm, hidden, scale_rows, gain):
    normed = hidden * scale_rows
    gain_part = jnp.sum(grad_norm * normed, axis=0)
    inner = grad_norm * gain
    grad_hidden = scale_rows * (inner - normed * jnp.mean(inner * normed, axis=1, keepdims=True))
    return (grad_hidden, gain_part)


def local(
    tokens,
    upstream,
    lengths,
    positions,
    pages,
    attn_gain,
    w_query,
    w_key,
    w_value,
    w_out,
    mlp_gain,
    w_gate,
    w_up,
    w_down,
):
    dp_count = lax.axis_size("dp")
    tp_count = lax.axis_size("tensor")
    dp_index = lax.axis_index("dp")
    tp_index = lax.axis_index("tensor")
    tok_dev, width = tokens.shape
    tok_group = tok_dev * tp_count
    page_rows = tok_dev // dp_count
    group_pages = tp_count * dp_count
    page_count = pages.shape[0]
    device = dp_index * tp_count + tp_index
    everyone = ("tensor", "dp")

    local_ids = jnp.arange(dp_count, dtype=jnp.int32)
    inverse = (
        jnp.zeros((page_count,), jnp.int32).at[pages].set(jnp.arange(page_count, dtype=jnp.int32))
    )
    dealt = lax.dynamic_slice_in_dim(inverse, device * dp_count, dp_count)
    dest_group = dealt // group_pages
    send_order = jnp.zeros((dp_count,), jnp.int32).at[dest_group].set(local_ids)
    group_sources = lax.dynamic_slice_in_dim(pages, dp_index * group_pages, group_pages)
    perm = (
        (group_sources // group_pages) * tp_count
        + jnp.arange(group_pages, dtype=jnp.int32) // dp_count
    ).astype(jnp.int32)

    def reorder(rows, order):
        blocks = rows.reshape(dp_count, page_rows, rows.shape[1])
        return jnp.take(blocks, order, axis=0).reshape(rows.shape)

    hidden_in = reorder(tokens, send_order).astype(f32)
    grad_top = reorder(upstream, send_order).astype(f32)
    seq_lens = lengths[0]
    seq_ends = jnp.cumsum(seq_lens)
    place = (jnp.take(dealt, send_order) % group_pages) * page_rows
    place_rows = (place[:, None] + jnp.arange(page_rows, dtype=jnp.int32)[None, :]).reshape(-1)
    valid_rows = (place_rows < seq_ends[-1]).astype(f32)[:, None]

    row_ids = jnp.arange(tok_group, dtype=jnp.int32)
    begin = jnp.max(
        jnp.where(row_ids[:, None] >= seq_ends[None, :], seq_ends[None, :], 0), axis=1
    ).astype(jnp.int32)
    block_len = min(block_rows, tok_group)
    first_block = begin[::block_len] // block_len
    begin = begin[None, :]
    inverse_freq = theta_base ** (-(jnp.arange(HALF, dtype=f32) * 2.0) / HD)
    angles = inverse_freq[:, None] * positions.astype(f32)
    cos_t, sin_t = jnp.cos(angles), jnp.sin(angles)

    q_cols, kv_cols = w_query.shape[1], w_key.shape[1]
    q_heads, kv_heads = q_cols // HD, kv_cols // HD
    qkv_shard = jnp.concatenate([w_query, w_key, w_value], axis=1)
    row_shard = qkv_shard.shape[0]

    def gather_all(shard):
        full = lax.all_gather(shard, everyone, axis=0, tiled=False)
        return full.reshape(tp_count, dp_count * shard.shape[0], shard.shape[1])

    def scatter_all(full):
        blocks = full.reshape(tp_count * dp_count, row_shard, full.shape[2])
        return lax.psum_scatter(blocks, everyone, scatter_dimension=0, tiled=False)

    w_qkv = gather_all(qkv_shard)
    w_out_t = gather_all(w_out.T)
    gains = lax.all_gather(jnp.stack([attn_gain, mlp_gain]), "dp", axis=1, tiled=True)
    gain_one, gain_two = gains[0].astype(f32), gains[1].astype(f32)
    full_gate = lax.all_gather(w_gate, "dp", axis=0, tiled=True)
    full_up = lax.all_gather(w_up, "dp", axis=0, tiled=True)
    full_down = lax.all_gather(w_down, "dp", axis=1, tiled=True)

    scale_one = rms_scale(hidden_in)
    normed_one = (hidden_in * scale_one * gain_one).astype(bf16)
    qkv = jnp.einsum("rk,tkc->trc", normed_one, w_qkv, preferred_element_type=f32).astype(bf16)
    trade = functools.partial(
        exchange, dp_count=dp_count, tp_count=tp_count, page_rows=page_rows
    )
    qkv_slots = trade(qkv, to_heads=True, collective_id=0)
    q_t, k_t, k_rows, v_t, v_rows = prepare(qkv_slots, perm, cos_t, sin_t, q_heads, kv_heads)
    o_t, lse, o_slots = attend_forward(
        q_t, k_rows, v_t, begin, first_block, perm, page_rows, block_len
    )
    mixed = trade(o_slots, to_heads=False, collective_id=1)
    branch_one = jnp.einsum("trc,tkc->rk", mixed, w_out_t, preferred_element_type=f32)
    hidden_mid = hidden_in + branch_one

    scale_two = rms_scale(hidden_mid)
    normed_two = (hidden_mid * scale_two * gain_two).astype(bf16)
    mlp_rows = lax.all_gather(normed_two, "tensor", axis=0, tiled=True)
    grad_out = grad_top * valid_rows
    grad_mlp = lax.all_gather(grad_out.astype(bf16), "tensor", axis=0, tiled=True)
    gate_pre = dot_nn(mlp_rows, full_gate)
    up_pre = dot_nn(mlp_rows, full_up)
    sigmoid_gate = jax.nn.sigmoid(gate_pre)
    activated = gate_pre * sigmoid_gate
    inner_act = (activated * up_pre).astype(bf16)
    branch_two = lax.psum_scatter(
        dot_nn(inner_act, full_down).astype(bf16), "tensor", scatter_dimension=0, tiled=True
    ).astype(f32)
    result = ((hidden_mid + branch_two) * valid_rows).astype(bf16)

    grad_down = dot_tn(inner_act, grad_mlp)
    grad_inner = dot_nt(grad_mlp, full_down)
    grad_upre = (grad_inner * activated).astype(bf16)
    grad_gpre = (
        grad_inner * up_pre * sigmoid_gate * (1.0 + gate_pre * (1.0 - sigmoid_gate))
    ).astype(bf16)
    grad_gate = dot_tn(mlp_rows, grad_gpre)
    grad_up = dot_tn(mlp_rows, grad_upre)
    grad_normed_two = lax.psum_scatter(
        (dot_nt(grad_gpre, full_gate) + dot_nt(grad_upre, full_up)).astype(bf16),
        "tensor",
        scatter_dimension=0,
        tiled=True,
    ).astype(f32)
    grad_mid_norm, gain_two_part = norm_back(grad_normed_two, hidden_mid, scale_two, gain_two)
    grad_mid = grad_out + grad_mid_norm

    grad_z = grad_mid.astype(bf16)
    grad_mixed = jnp.einsum("rk,tkc->trc", grad_z, w_out_t, preferred_element_type=f32).astype(
        bf16
    )
    grad_slots = trade(grad_mixed, to_heads=True, collective_id=2)
    grad_wout_t = jnp.einsum("rk,trc->tkc", grad_z, mixed, preferred_element_type=f32)
    grad_qkv_slots = attend_backward(
        grad_slots, q_t, k_rows, k_t, v_rows, o_t, lse, begin, cos_t, sin_t, first_block, perm,
        page_rows, block_len,
    )
    grad_qkv = trade(grad_qkv_slots, to_heads=False, collective_id=3)
    grad_wqkv = jnp.einsum("rk,trc->tkc", normed_one, grad_qkv, preferred_element_type=f32)
    grad_normed_one = jnp.einsum("trc,tkc->rk", grad_qkv, w_qkv, preferred_element_type=f32)
    grad_in_norm, gain_one_part = norm_back(grad_normed_one, hidden_in, scale_one, gain_one)
    grad_in = (grad_mid + grad_in_norm).astype(bf16)

    def reduce_dp(grad, axis):
        return lax.psum_scatter(
            grad.astype(bf16), "dp", scatter_dimension=axis, tiled=True
        ).astype(f32)

    sum_down = reduce_dp(grad_down, 1)
    sum_gate = reduce_dp(grad_gate, 0)
    sum_up = reduce_dp(grad_up, 0)
    sum_out = scatter_all(grad_wout_t.astype(bf16)).astype(f32).T
    sum_qkv = scatter_all(grad_wqkv.astype(bf16)).astype(f32)
    gain_sums = lax.psum(jnp.stack([gain_one_part, gain_two_part]), everyone)
    gain_shard = attn_gain.shape[0]
    gain_sums = lax.dynamic_slice_in_dim(gain_sums, dp_index * gain_shard, gain_shard, 1)
    return (
        reorder(result, dest_group),
        reorder(grad_in, dest_group),
        gain_sums[0],
        sum_qkv[:, :q_cols],
        sum_qkv[:, q_cols : q_cols + kv_cols],
        sum_qkv[:, q_cols + kv_cols :],
        sum_out,
        gain_sums[1],
        sum_gate,
        sum_up,
        sum_down,
    )


def solution(mesh):
    rows = P(("dp", "tensor"), None)
    weight = P("dp", "tensor")
    weight_t = P("tensor", "dp")
    return jax.shard_map(
        local,
        mesh=mesh,
        in_specs=(
            rows,
            rows,
            P("dp", None),
            P("dp", None),
            P(),
            P("dp"),
            weight,
            weight,
            weight,
            weight_t,
            P("dp"),
            weight,
            weight,
            weight_t,
        ),
        out_specs=(
            rows,
            rows,
            P("dp"),
            weight,
            weight,
            weight,
            weight_t,
            P("dp"),
            weight,
            weight,
            weight_t,
        ),
        check_vma=False,
    )
```

time: 2830 us -> 1820 us (0.64)
  waiting for transfers between devices: 1550 us -> 962 us
  matrix products: 716 us -> 296 us
  Pallas kernels: 0 us -> 378 us
  other arithmetic: 260 us -> 47.6 us
  local copies, waits for them, and re-layouts: 164 us -> 62.2 us
  blocking collectives: 82.8 us -> 49.8 us
    dot_general x49 -> x15, matrix products: 716 us -> 296 us  [the longest x3 86.9 us: dot_nt(): lax.dot_general(left, right, (((1,), (1,)), ((), ())), preferred_element_...]
    pallas_call x0 -> x7, Pallas kernels: none -> 378 us  [the longest x4 252 us: exchange(): pl.pallas_call(functools.partial(exchange_kernel, dp_count, tp_count, pag...]
    reduce_scatter x11 -> x7, waiting for transfers between devices: 786 us -> 449 us  [the longest x2 251 us: scatter_all(): return lax.psum_scatter(blocks, everyone, scatter_dimension=0, tiled=False)]
    all_gather x8 -> x6, waiting for transfers between devices: 537 us -> 369 us  [the longest x2 155 us: gather_all(): full = lax.all_gather(shard, everyone, axis=0, tiled=False)]
    convert_element_type x27 -> x10, other arithmetic: 149 us -> 21.6 us  [the longest x3 8.33 us: reduce_dp(): return lax.psum_scatter(grad.astype(bf16), 'dp', scatter_dimension=axis,...]
    dynamic_update_slice x16 -> x0, local copies, waits for them, and re-layouts: 92.5 us -> none  [the longest x8 88.4 us: attend_backward(): lax.scan(one_block, (zero_kv, zero_kv), (block_starts, log_sums))]
    all_to_all x4 -> x0, waiting for transfers between devices: 70.7 us -> none  [the longest x1 37.7 us: local(): lax.all_to_all(reorder(upstream, send_order), 'dp', split_axis=0, concat_...]
    reduce_sum x5 -> x0, other arithmetic: 60 us -> none  [the longest x4 59.9 us: one_block(): row_sum = jnp.sum(exp_scores, axis=-1, keepdims=True)]
  transfers between devices with their start and end apart: 24 -> 14, of which waited for: 21 -> 11; matrix products, arithmetic and copies ran while one was open for 16% -> 17% of each run, Pallas kernels for 0% -> 21%
where the time goes in v1:
time: 1820 us; the launch traced here: 1810 us
  waiting for transfers between devices  962 us (53%)
  Pallas kernels  378 us (21%)
  matrix products  296 us (16%)
  local copies, waits for them, and re-layouts  62.2 us (3%)
  blocking collectives  49.8 us (3%)
  other arithmetic  47.6 us (3%)
    pallas_call x4, Pallas kernels, exchange(): pl.pallas_call(functools.partial(exchange_kernel, dp_count, tp_count, pag...  252 us
    reduce_scatter x2, waiting for transfers between devices, scatter_all(): return lax.psum_scatter(blocks, everyone, scatter_dimension=0, tiled=False)  251 us
    all_gather x2, waiting for transfers between devices, gather_all(): full = lax.all_gather(shard, everyone, axis=0, tiled=False)  155 us
    reduce_scatter x1, waiting for transfers between devices, local(): lax.psum_scatter(dot_nn(inner_act, full_down).astype(bf16), 'tensor', sca...  144 us
    all_gather x1, waiting for transfers between devices, local(): mlp_rows = lax.all_gather(normed_two, 'tensor', axis=0, tiled=True)  141 us
    all_gather x1, waiting for transfers between devices, local(): lax.all_gather(grad_out.astype(bf16), 'tensor', axis=0, tiled=True)  128 us
    dot_general x3, matrix products, dot_nt(): lax.dot_general(left, right, (((1,), (1,)), ((), ())), preferred_element_...  86.9 us
    dot_general x3, matrix products, dot_nn(): lax.dot_general(left, right, (((1,), (0,)), ((), ())), preferred_element_...  71.9 us
  transfers between devices with their start and end apart: 14, of which 11 were waited for; matrix products, arithmetic and copies ran while one was open for 17% of the time, Pallas kernels for 21%

profile of v1, /device:TPU:0, one launch (start us, length us, event | category | flops | bytes accessed | tf_op | source)
XLA Modules:
  0.0 1811.7 jit_solution(2178709679440389609)
XLA Ops:
  17.1 10.3 all_gather.32
  28.6 2.3 fusion.18
  34.7 69.1 %all-gather.22.cloned.1.call-done = bf16[8192,512]{0,1:T(8,128)(2,1)} async-done(((bf16[256,512]{0,1:T(8,128)(2,1)}), bf16[8192,512]{0,1:T(8,128)(2,1)}) %all-gather.22.cloned.1.call-update) | async-done | bytes 8388624 | tf_op jit(solution)/shard_map/all_gather | solution.py:526
  103.8 12.0 copy.40
  115.8 85.6 %all-gather.20.cloned.1.call-done = bf16[8192,768]{1,0:T(8,128)(2,1)} async-done(((bf16[256,768]{1,0:T(8,128)(2,1)}), bf16[8192,768]{1,0:T(8,128)(2,1)}) %all-gather.20.cloned.1.call-update) | async-done | bytes 12582928 | tf_op jit(solution)/shard_map/all_gather | solution.py:526
  201.5 12.9 convert_bitcast_fusion.2.src
  214.4 71.9 %exchange.4.refs_0_.refs_1_ = bf16[32,64,768]{2,1,0:T(8,128)(2,1)} custom-call(bf16[4,512,768]{2,1,0:T(8,128)(2,1)} %convert_bitcast_fusion.2.src), custom_call_target="tpu_custom_call" | custom-call | bytes 125829120 | tf_op jit(solution)/shard_map/exchange/pallas_call | solution.py:99
  286.3 12.2 prepare.1
  298.4 56.2 %attend_forward.1 = (bf16[512,2048]{1,0:T(8,128)(2,1)}, f32[8,2048]{1,0:T(8,128)}, bf16[32,64,512]{2,1,0:T(8,128)(2,1)}) custom-call(s32[8]{0:T(128)} %and_select_fusion.3.first_block, s32[32]{0:T(128)} %fusion.30.perm, bf16[512,2048]{1,0:T(8,128)(2,1)} %get-tuple-element.20.q_t.refs_4_, bf16[2,2048,64]{2,1,0:T(8,128)(2,1)} %get-tuple-element.21.k_rows.refs_5_, ...), custom_call_target="tpu_custom_call" | custom-call | flops 2147483648 | bytes 8388608 | tf_op jit(solution)/shard_map/attend_forward/pallas_call | solution.py:242
  354.6 53.3 %exchange.5 = bf16[4,512,512]{2,1,0:T(8,128)(2,1)} custom-call(bf16[32,64,512]{2,1,0:T(8,128)(2,1)} %get-tuple-element.23.src), custom_call_target="tpu_custom_call" | custom-call | bytes 83886080 | tf_op jit(solution)/shard_map/exchange/pallas_call | solution.py:99
  407.9 7.8 multiply_reduce_fusion
  415.8 2.0 copy-done.2
  428.3 141.4 %all-gather.10.cloned.1.call-done = bf16[2048,2048]{1,0:T(8,128)(2,1)} async-done(((bf16[512,2048]{1,0:T(8,128)(2,1)}), bf16[2048,2048]{1,0:T(8,128)(2,1)}) %all-gather.10.cloned.1.call-update) | async-done | bytes 8388624 | tf_op jit(solution)/shard_map/all_gather | solution.py:558
  569.7 24.2 %fusion.39 = f32[2048,2048]{1,0:T(8,128)} fusion(bf16[2048,2048]{1,0:T(8,128)(2,1)} %all-gather.10.cloned.1.call-done, bf16[2048,2048]{1,0:T(8,128)(2,1)} %all-gather.12.cloned.1.call-done), kind=kOutput, calls=%fused_computation.117 | convolution fusion | flops 17179869184 | bytes 33554432 | tf_op jit(solution)/shard_map/dot_general | solution.py:24
  593.9 30.2 %all-gather.14.cloned.1.call-done = bf16[2048,2048]{1,0:T(8,128)(2,1)} async-done(((bf16[256,2048]{1,0:T(8,128)(2,1)}), bf16[2048,2048]{1,0:T(8,128)(2,1)}) %all-gather.14.cloned.1.call-update) | async-done | bytes 8388624 | tf_op jit(solution)/shard_map/all_gather | solution.py:538
  624.1 24.2 %fusion.40 = f32[2048,2048]{1,0:T(8,128)} fusion(bf16[2048,2048]{1,0:T(8,128)(2,1)} %all-gather.10.cloned.1.call-done, bf16[2048,2048]{1,0:T(8,128)(2,1)} %all-gather.14.cloned.1.call-done), kind=kOutput, calls=%fused_computation.118 | convolution fusion | flops 17179869184 | bytes 33554432 | tf_op jit(solution)/shard_map/dot_general | solution.py:24
  648.3 127.5 %all-gather.18.cloned.1.call-done = bf16[2048,2048]{1,0:T(8,128)(2,1)} async-done(((bf16[512,2048]{1,0:T(8,128)(2,1)}), bf16[2048,2048]{1,0:T(8,128)(2,1)}) %all-gather.18.cloned.1.call-update) | async-done | bytes 8388624 | tf_op jit(solution)/shard_map/all_gather | solution.py:560
  775.8 56.1 %all-gather.16.cloned.1.call-done = bf16[2048,2048]{1,0:T(8,128)(2,1)} async-done(((bf16[2048,256]{1,0:T(8,128)(2,1)}), bf16[2048,2048]{1,0:T(8,128)(2,1)}) %all-gather.16.cloned.1.call-update) | async-done | bytes 8388624 | tf_op jit(solution)/shard_map/all_gather | solution.py:539
  831.9 36.7 %multiply_convert_fusion = (bf16[2048,2048]{1,0:T(8,128)(2,1)}, bf16[2048,2048]{1,0:T(8,128)(2,1)}, bf16[2048,2048]{1,0:T(8,128)(2,1)}) fusion(f32[2048,2048]{1,0:T(8,128)} %fusion.39, f32[2048,2048]{1,0:T(8,128)} %fusion.40, bf16[2048,2048]{1,0:T(8,128)(2,1)} %all-gather.18.cloned.1.call-done, bf16[2048,2048]{1,0:T(8,128)(2,1)} %all-gather.16.cloned.1.call-done), kind=kOutput, calls=%fused_computation.8 | convolution fusion | flops 17242783744 | bytes 75497472 | tf_op jit(solution)/shard_map/dot_general | solution.py:28
  868.6 24.3 %fusion.41 = f32[2048,2048]{1,0:T(8,128)} fusion(bf16[2048,2048]{1,0:T(8,128)(2,1)} %get-tuple-element.62, bf16[2048,2048]{1,0:T(8,128)(2,1)} %all-gather.12.cloned.1.call-done), kind=kOutput, calls=%fused_computation.119 | convolution fusion | flops 17179869184 | bytes 33554432 | tf_op jit(solution)/shard_map/dot_general | solution.py:28
  892.9 25.9 %add_convert_fusion = bf16[2048,2048]{1,0:T(8,128)(2,1)} fusion(f32[2048,2048]{1,0:T(8,128)} %fusion.41, bf16[2048,2048]{1,0:T(8,128)(2,1)} %get-tuple-element.61, bf16[2048,2048]{1,0:T(8,128)(2,1)} %all-gather.14.cloned.1.call-done), kind=kOutput, calls=%fused_computation.7 | convolution fusion | flops 17188257792 | bytes 41943040 | tf_op jit(solution)/shard_map/dot_general | solution.py:28
  918.9 23.6 %convolution_convert_fusion.3 = bf16[2048,2048]{1,0:T(8,128)(2,1)} fusion(bf16[2048,2048]{1,0:T(8,128)(2,1)} %get-tuple-element.63, bf16[2048,2048]{1,0:T(8,128)(2,1)} %all-gather.16.cloned.1.call-done), kind=kOutput, calls=%fused_computation.18 | convolution fusion | flops 17184063488 | bytes 25165824 | tf_op jit(solution)/shard_map/dot_general | solution.py:24
  942.5 24.1 %convolution_convert_fusion.2 = bf16[2048,2048]{1,0:T(8,128)(2,1)} fusion(bf16[2048,2048]{1,0:T(8,128)(2,1)} %all-gather.10.cloned.1.call-done, bf16[2048,2048]{1,0:T(8,128)(2,1)} %get-tuple-element.62), kind=kOutput, calls=%fused_computation.17 | convolution fusion | flops 17184063488 | bytes 25165824 | tf_op jit(solution)/shard_map/dot_general | solution.py:32
  966.6 23.7 %convolution_convert_fusion.1 = bf16[2048,2048]{1,0:T(8,128)(2,1)} fusion(bf16[2048,2048]{1,0:T(8,128)(2,1)} %all-gather.10.cloned.1.call-done, bf16[2048,2048]{1,0:T(8,128)(2,1)} %get-tuple-element.61), kind=kOutput, calls=%fused_computation.16 | convolution fusion | flops 17184063488 | bytes 25165824 | tf_op jit(solution)/shard_map/dot_general | solution.py:32
  990.4 23.8 %convolution_convert_fusion = bf16[2048,2048]{1,0:T(8,128)(2,1)} fusion(bf16[2048,2048]{1,0:T(8,128)(2,1)} %get-tuple-element.63, bf16[2048,2048]{1,0:T(8,128)(2,1)} %all-gather.18.cloned.1.call-done), kind=kOutput, calls=%fused_computation.15 | convolution fusion | flops 17184063488 | bytes 25165824 | tf_op jit(solution)/shard_map/dot_general | solution.py:32
  1015.0 48.5 %reduce-scatter.10.cloned.1.call-done = bf16[512,2048]{1,0:T(8,128)(2,1)} async-done(((bf16[2048,2048]{1,0:T(8,128)(2,1)}), bf16[512,2048]{1,0:T(8,128)(2,1)}) %reduce-scatter.10.cloned.1.call-update) | async-done | bytes 2097168 | tf_op jit(solution)/shard_map/reduce_scatter | solution.py:579
  1063.5 4.0 fusion.6
  1067.5 143.6 %reduce-scatter.8.cloned.1.call-done = bf16[512,2048]{1,0:T(8,128)(2,1)} async-done(((bf16[2048,2048]{1,0:T(8,128)(2,1)}), bf16[512,2048]{1,0:T(8,128)(2,1)}) %reduce-scatter.8.cloned.1.call-update) | async-done | bytes 2097168 | tf_op jit(solution)/shard_map/reduce_scatter | solution.py:566
  1211.1 5.6 fusion.5
  1218.6 9.7 convert_bitcast_fusion.3.src
  1228.3 51.6 %exchange.6.refs_0_.refs_1_.refs_2_.refs_3_ = bf16[32,64,512]{2,1,0:T(8,128)(2,1)} custom-call(bf16[4,512,512]{2,1,0:T(8,128)(2,1)} %convert_bitcast_fusion.3.src), custom_call_target="tpu_custom_call" | custom-call | bytes 83886080 | tf_op jit(solution)/shard_map/exchange/pallas_call | solution.py:99
  1279.9 58.4 %attend_backward.1.src = bf16[32,64,768]{2,1,0:T(8,128)(2,1)} custom-call(s32[8]{0:T(128)} %and_select_fusion.3.first_block, s32[32]{0:T(128)} %fusion.30.perm, bf16[32,64,512]{2,1,0:T(8,128)(2,1)} %exchange.6.refs_0_.refs_1_.refs_2_.refs_3_, bf16[32,64,512]{2,1,0:T(8,128)(2,1)} %exchange.6.refs_0_.refs_1_.refs_2_.refs_3_, ...), custom_call_target="tpu_custom_call" | custom-call | flops 6442450944 | bytes 12582912 | tf_op jit(solution)/shard_map/attend_backward/pallas_call | solution.py:401
  1338.3 74.9 %exchange.7 = bf16[4,512,768]{2,1,0:T(8,128)(2,1)} custom-call(bf16[32,64,768]{2,1,0:T(8,128)(2,1)} %attend_backward.1.src), custom_call_target="tpu_custom_call" | custom-call | bytes 125829120 | tf_op jit(solution)/shard_map/exchange/pallas_call | solution.py:99
  1413.2 12.9 fusion.8
  1426.2 11.8 convert_bitcast_fusion
  1437.9 16.9 copy.42
  1455.1 10.9 convert_bitcast_fusion.1
  1466.0 11.5 copy.44
  1478.2 2.8 convert_element_type.162
  1481.0 2.8 convert_element_type.164
  1483.9 6.1 reduce-scatter.20.cloned.1.call-done
  1490.0 2.7 convert_element_type.166
  1492.7 5.9 fusion.16
  1498.6 3.8 gather_fusion.4
  1504.4 39.5 %psum.7 = f32[2,2048]{1,0:T(2,128)S(1)} all-reduce(f32[2,2048]{1,0:T(2,128)S(1)} %pad_maximum_fusion.1), channel_id=1, replica_groups=mesh['dp'=8,'tensor'=4] {'tensor','dp'}, use_global_device_ids=true, to_apply=%region_12.14 | all-reduce | flops 4096 | bytes 32768 | tf_op jit(solution)/shard_map/psum | solution.py:614
  1544.5 4.8 broadcast_select_fusion
  1549.3 103.1 %reduce-scatter.12.cloned.1.call-done = bf16[1,256,768]{2,1,0:T(8,128)(2,1)} async-done(((bf16[32,256,768]{2,1,0:T(8,128)(2,1)}), bf16[1,256,768]{2,1,0:T(8,128)(2,1)}) %reduce-scatter.12.cloned.1.call-update) | async-done | bytes 393232 | tf_op jit(solution)/shard_map/reduce_scatter | solution.py:531
  1655.1 147.6 %reduce-scatter.14.cloned.1.call-done = bf16[1,256,512]{2,1,0:T(8,128)(2,1)} async-done(((bf16[32,256,512]{2,1,0:T(8,128)(2,1)}), bf16[1,256,512]{2,1,0:T(8,128)(2,1)}) %reduce-scatter.14.cloned.1.call-update) | async-done | bytes 262160 | tf_op jit(solution)/shard_map/reduce_scatter | solution.py:531
  (136 shorter events, 36.2 us)
Async XLA Ops:
  7.2 7.5 copy-start
  7.2 20.3 %copy-start.26 = (s32[256]{0:T(256)S(1)}, s32[256]{0:T(256)}, u32[]{:S(2)}) copy-start(s32[256]{0:T(256)} %param.20) | copy-start | bytes 3076
  7.2 9.4 copy-start.27
  7.2 9.4 copy-start.28
  7.2 9.4 copy-start.21
  7.2 9.4 copy-start.29
  7.2 96.5 %all-gather.22.cloned.1.call-start = ((), (), s32[]{:S(2)}) async-start(), calls=%async_computation.20 | async-start | bytes 8650752 | tf_op jit(solution)/shard_map/all_gather | solution.py:526
  8.0 193.5 %all-gather.20.cloned.1.call-start = ((), (), s32[]{:S(2)}) async-start(), calls=%async_computation.19 | async-start | bytes 12976128 | tf_op jit(solution)/shard_map/all_gather | solution.py:526
  9.9 418.4 %all-gather.12.cloned.1.call-start = ((), (), s32[]{:S(2)}) async-start(), calls=%async_computation.8 | async-start | bytes 9437184 | tf_op jit(solution)/shard_map/all_gather | solution.py:537
  10.6 559.1 %all-gather.10.cloned.1.call-start = ((), (), s32[]{:S(2)}) async-start(), calls=%async_computation.7 | async-start | bytes 10485760 | tf_op jit(solution)/shard_map/all_gather | solution.py:558
  13.4 17.6 copy-start.24
  17.0 17.7 copy-start.22
  30.9 377.0 %copy-start.3 = (bf16[8,64,2048]{2,1,0:T(8,128)(2,1)}, bf16[8,64,2048]{2,1,0:T(8,128)(2,1)S(1)}, u32[]{:S(2)}) copy-start(bf16[8,64,2048]{2,1,0:T(8,128)(2,1)S(1)} %get-tuple-element.60) | copy-start | bytes 6291460
  30.9 1.9 copy-start.15
  31.0 1.8 copy-start.13
  31.0 384.8 %copy-start.11 = (f32[1,2048]{1,0:T(1,128)}, f32[1,2048]{1,0:T(1,128)S(1)}, u32[]{:S(2)}) copy-start(f32[1,2048]{1,0:T(1,128)S(1)} %get-tuple-element.73) | copy-start | bytes 24580
  415.7 2.1 copy-start.2
  415.8 2.0 copy-start.17
  417.8 3.0 copy-start.10
  419.6 204.6 %all-gather.14.cloned.1.call-start = ((), (), s32[]{:S(2)}) async-start(), calls=%async_computation.9 | async-start | bytes 9437184 | tf_op jit(solution)/shard_map/all_gather | solution.py:538
  420.2 355.6 %all-gather.18.cloned.1.call-start = ((), (), s32[]{:S(2)}) async-start(), calls=%async_computation.12 | async-start | bytes 10485760 | tf_op jit(solution)/shard_map/all_gather | solution.py:560
  423.6 3.9 copy-start.19
  425.4 168.4 %copy-start.5 = (bf16[8,64,2048]{2,1,0:T(8,128)(2,1)}, bf16[8,64,2048]{2,1,0:T(8,128)(2,1)S(1)}, u32[]{:S(2)}) copy-start(bf16[8,64,2048]{2,1,0:T(8,128)(2,1)S(1)} %broadcast_select_fusion.2) | copy-start | bytes 6291460
  427.5 404.4 %all-gather.16.cloned.1.call-start = ((), (), s32[]{:S(2)}) async-start(), calls=%async_computation.10 | async-start | bytes 9437184 | tf_op jit(solution)/shard_map/all_gather | solution.py:539
  428.2 635.2 %reduce-scatter.10.cloned.1.call-start = ((), (), s32[]{:S(2)}) async-start(), calls=%async_computation.13 | async-start | bytes 10485760 | tf_op jit(solution)/shard_map/reduce_scatter | solution.py:579
  918.8 292.2 %reduce-scatter.8.cloned.1.call-start = ((), (), s32[]{:S(2)}) async-start(), calls=%async_computation.11 | async-start | bytes 10485760 | tf_op jit(solution)/shard_map/reduce_scatter | solution.py:566
  942.5 535.8 %reduce-scatter.16.cloned.1.call-start = ((), (), s32[]{:S(2)}) async-start(), calls=%async_computation.16 | async-start | bytes 9437184 | tf_op jit(solution)/shard_map/reduce_scatter | solution.py:605
  966.6 514.4 %reduce-scatter.18.cloned.1.call-start = ((), (), s32[]{:S(2)}) async-start(), calls=%async_computation.17 | async-start | bytes 9437184 | tf_op jit(solution)/shard_map/reduce_scatter | solution.py:605
  990.3 499.7 %reduce-scatter.20.cloned.1.call-start = ((), (), s32[]{:S(2)}) async-start(), calls=%async_computation.18 | async-start | bytes 9437184 | tf_op jit(solution)/shard_map/reduce_scatter | solution.py:605
  1014.2 0.7 copy-start.16
  1014.2 49.2 %copy-start.12 = (f32[1,2048]{1,0:T(1,128)S(1)}, f32[1,2048]{1,0:T(1,128)}, u32[]{:S(2)}) copy-start(f32[1,2048]{1,0:T(1,128)} %copy-done.11) | copy-start | bytes 24580
  1014.2 49.2 %copy-start.18 = (f32[512]{0:T(512)S(1)}, f32[512]{0:T(512)}, u32[]{:S(2)}) copy-start(f32[512]{0:T(512)} %copy-done.17) | copy-start | bytes 6148
  1014.2 196.8 %copy-start.6 = (bf16[8,64,2048]{2,1,0:T(8,128)(2,1)S(1)}, bf16[8,64,2048]{2,1,0:T(8,128)(2,1)}, u32[]{:S(2)}) copy-start(bf16[8,64,2048]{2,1,0:T(8,128)(2,1)} %copy-done.5) | copy-start | bytes 6291460
  1014.3 196.8 %copy-start.20 = (f32[512]{0:T(512)S(1)}, f32[512]{0:T(512)}, u32[]{:S(2)}) copy-start(f32[512]{0:T(512)} %copy-done.19) | copy-start | bytes 6148
  1014.3 638.2 %reduce-scatter.12.cloned.1.call-start = ((), (), s32[]{:S(2)}) async-start(), calls=%async_computation.14 | async-start | bytes 12976128 | tf_op jit(solution)/shard_map/reduce_scatter | solution.py:531
  1216.6 2.0 copy-start.7
  1338.3 74.9 %copy-start.4 = (bf16[8,64,2048]{2,1,0:T(8,128)(2,1)S(1)}, bf16[8,64,2048]{2,1,0:T(8,128)(2,1)}, u32[]{:S(2)}) copy-start(bf16[8,64,2048]{2,1,0:T(8,128)(2,1)} %copy-done.3) | copy-start | bytes 6291460
  1338.3 74.9 %copy-start.14 = (f32[1,2048]{1,0:T(1,128)S(1)}, f32[1,2048]{1,0:T(1,128)}, u32[]{:S(2)}) copy-start(f32[1,2048]{1,0:T(1,128)} %copy-done.13) | copy-start | bytes 24580
  1413.2 12.9 copy-start.9
  1454.8 347.9 %reduce-scatter.14.cloned.1.call-start = ((), (), s32[]{:S(2)}) async-start(), calls=%async_computation.15 | async-start | bytes 8650752 | tf_op jit(solution)/shard_map/reduce_scatter | solution.py:531
  1477.5 0.7 copy-start.25
  1498.6 3.8 copy-start.8
  1498.6 45.9 %copy-start.23 = (pred[8]{0:T(512)(128)(4,1)S(1)}, pred[8]{0:T(512)(128)(4,1)}, u32[]{:S(2)}) copy-start(pred[8]{0:T(512)(128)(4,1)} %get-tuple-element.54) | copy-start | bytes 28
  1544.5 260.2 %copy-start.1 = (bf16[512,2048]{1,0:T(8,128)(2,1)S(1)}, bf16[512,2048]{1,0:T(8,128)(2,1)}, u32[]{:S(2)}) copy-start(bf16[512,2048]{1,0:T(8,128)(2,1)} %param.16) | copy-start | bytes 6291460
Sparse Core Ops, SparseCore 0:
  11.0 92.7 all-gather.21
  107.2 94.1 all-gather.19
  203.3 84.1 all-gather.11
  419.7 149.9 all-gather.9
  571.5 52.6 all-gather.13
  626.1 149.6 all-gather.17
  777.7 54.1 all-gather.15
  918.9 144.4 reduce-scatter.9
  1065.8 145.1 reduce-scatter.7
  1214.4 88.7 reduce-scatter.15
  1307.0 104.0 reduce-scatter.17
  1414.5 75.4 reduce-scatter.19
  1497.1 155.3 reduce-scatter.11
  1654.6 148.0 reduce-scatter.13

commit v2 on v1

--- a/solution.py
+++ b/solution.py
@@ -4,6 +4,7 @@
 import jax.numpy as jnp
 from jax import lax
 from jax.experimental import pallas as pl
+from jax.experimental.layout import Layout, with_layout_constraint
 from jax.experimental.pallas import tpu as pltpu
 from jax.sharding import PartitionSpec as P
 
@@ -30,86 +31,6 @@
 
 def dot_tn(left, right):
     return lax.dot_general(left, right, (((0,), (0,)), ((), ())), preferred_element_type=f32)
-
-
-def exchange_kernel(dp_count, tp_count, page_rows, to_heads, src, dst, send_sem, recv_sem, own_sem):
-    count = dp_count * tp_count
-    my_dp = lax.axis_index("dp")
-    my_tp = lax.axis_index("tensor")
-    me = my_dp * tp_count + my_tp
-
-    def split(peer):
-        return lax.div(peer, tp_count), lax.rem(peer, tp_count)
-
-    barrier = pltpu.get_barrier_semaphore()
-
-    def greet(j, carry):
-        p_dp, p_tp = split(lax.rem(me + j, count))
-        pl.semaphore_signal(
-            barrier, inc=1, device_id={"dp": p_dp, "tensor": p_tp}, device_id_type=MESH
-        )
-        return carry
-
-    lax.fori_loop(1, count, greet, 0)
-    pl.semaphore_wait(barrier, count - 1)
-
-    def ends(p_dp, p_tp, peer):
-        if to_heads:
-            return src.at[p_tp, pl.ds(p_dp * page_rows, page_rows), :], dst.at[me]
-        return src.at[peer], dst.at[my_tp, pl.ds(my_dp * page_rows, page_rows), :]
-
-    own_src, own_dst = ends(my_dp, my_tp, me)
-    own = pltpu.make_async_copy(own_src, own_dst, own_sem)
-    own.start()
-
-    def copy_to(j):
-        peer = lax.rem(me + j, count)
-        p_dp, p_tp = split(peer)
-        block_src, block_dst = ends(p_dp, p_tp, peer)
-        return pltpu.make_async_remote_copy(
-            src_ref=block_src,
-            dst_ref=block_dst,
-            send_sem=send_sem.at[j],
-            recv_sem=recv_sem.at[j],
-            device_id={"dp": p_dp, "tensor": p_tp},
-            device_id_type=MESH,
-        )
-
-    def start(j, carry):
-        copy_to(j).start()
-        return carry
-
-    def finish(j, carry):
-        copy_to(j).wait()
-        return carry
-
-    lax.fori_loop(1, count, start, 0)
-    own.wait()
-    lax.fori_loop(1, count, finish, 0)
-
-
-def exchange(array, dp_count, tp_count, page_rows, to_heads, collective_id):
-    cols = array.shape[-1]
-    count = dp_count * tp_count
-    if to_heads:
-        out_shape = (count, page_rows, cols)
-    else:
-        out_shape = (tp_count, dp_count * page_rows, cols)
-    nbytes = array.size * 2
-    return pl.pallas_call(
-        functools.partial(exchange_kernel, dp_count, tp_count, page_rows, to_heads),
-        out_shape=jax.ShapeDtypeStruct(out_shape, array.dtype),
-        in_specs=[pl.BlockSpec(memory_space=pl.ANY)],
-        out_specs=pl.BlockSpec(memory_space=pl.ANY),
-        scratch_shapes=[
-            pltpu.SemaphoreType.DMA((count,)),
-            pltpu.SemaphoreType.DMA((count,)),
-            pltpu.SemaphoreType.DMA,
-        ],
-        compiler_params=pltpu.CompilerParams(collective_id=collective_id, has_side_effects=True),
-        cost_estimate=pl.CostEstimate(flops=0, bytes_accessed=40 * nbytes, transcendentals=0),
-        name="exchange",
-    )(array)
 
 
 def prep_kernel(pages_per, q_heads, kv_heads, perm, *refs):
@@ -441,6 +362,313 @@
     )
 
 
+def feed_kernel(
+    ring, tile, own_rows, *refs
+):
+    grad_rows = refs[:ring]
+    (
+        weights, grad_all, rows_all, act_all, grads_all, mixed_all, grad_own,
+    held, grads_held, acc_n, acc_m, first_part, arrived, outgoing, mixed_stage, final_stage,
+    load_sem, keep_sem, grad_sem, mixed_sem, final_sem,
+    row_send, row_recv, sum_send, sum_recv, all_sem,
+    ) = refs[ring:]
+    me = lax.axis_index("tensor")
+    right = lax.rem(me + 1, ring)
+    left = lax.rem(me + ring - 1, ring)
+    hidden = weights.shape[1] // 3
+    tiles = hidden // tile
+
+    barrier = pltpu.get_barrier_semaphore()
+    for neighbour in (left, right):
+        pl.semaphore_signal(barrier, inc=1, device_id={"tensor": neighbour}, device_id_type=MESH)
+    pl.semaphore_wait(barrier, 2)
+
+    load = pltpu.make_async_copy(own_rows, held.at[0], load_sem)
+    load.start()
+
+    def grad_load(s):
+        return pltpu.make_async_copy(grad_rows[s], grads_held.at[s % 2], grad_sem.at[s % 2])
+
+    def grad_keep(s):
+        return pltpu.make_async_copy(
+            grads_held.at[lax.rem(s, 2)], grad_all.at[s], all_sem.at[lax.rem(s, 2)]
+        )
+
+    grad_load(0).start()
+    load.wait()
+
+    def pass_rows(s):
+        return pltpu.make_async_remote_copy(
+            src_ref=held.at[s],
+            dst_ref=held.at[s + 1],
+            send_sem=row_send.at[s],
+            recv_sem=row_recv.at[s],
+            device_id={"tensor": right},
+            device_id_type=MESH,
+        )
+
+    def pass_sum(s):
+        return pltpu.make_async_remote_copy(
+            src_ref=outgoing.at[s - 1],
+            dst_ref=arrived.at[s - 1],
+            send_sem=sum_send.at[s - 1],
+            recv_sem=sum_recv.at[s - 1],
+            device_id={"tensor": right},
+            device_id_type=MESH,
+        )
+
+    def keep(s):
+        return pltpu.make_async_copy(held.at[s], rows_all.at[s], keep_sem.at[s])
+
+    def mixed_store(s):
+        return pltpu.make_async_copy(mixed_stage, mixed_all.at[s], mixed_sem)
+
+    def chunk(s, carry):
+        @pl.when(s > 0)
+        def _():
+            pass_rows(s - 1).wait_recv()
+
+        @pl.when(s < ring - 1)
+        def _():
+            pass_rows(s).start()
+
+        keep(s).start()
+
+        @pl.when(s > 0)
+        def _():
+            grad_keep(s - 1).wait()
+
+        for k in range(ring):
+
+            @pl.when(s == k)
+            def _(k=k):
+                grad_load(k).wait()
+                if k < ring - 1:
+                    grad_load(k + 1).start()
+
+        grad_keep(s).start()
+        slot = lax.rem(s, 2)
+        acc_n[...] = jnp.zeros_like(acc_n)
+        acc_m[...] = jnp.zeros_like(acc_m)
+
+        def body(w_gate, w_up, w_down, act, grad_gate, grad_up):
+            rows = held[s]
+            gate = dot_nn(rows, w_gate[...])
+            up = dot_nn(rows, w_up[...])
+            grad_act = dot_nn(grads_held[slot], w_down[...])
+            sig = 1.0 / (1.0 + jnp.exp(-gate))
+            silu = gate * sig
+            low_act = (silu * up).astype(bf16)
+            low_up = (grad_act * silu).astype(bf16)
+            low_gate = (grad_act * up * sig * (1.0 + gate * (1.0 - sig))).astype(bf16)
+            act[...] = low_act
+            grad_gate[...] = low_gate
+            grad_up[...] = low_up
+            acc_m[...] += dot_nt(low_act, w_down[...])
+            acc_n[...] += dot_nt(low_gate, w_gate[...]) + dot_nt(low_up, w_up[...])
+
+        width, count = own_rows.shape[1], own_rows.shape[0]
+        pltpu.emit_pipeline(
+            body,
+            grid=(tiles,),
+            in_specs=[
+                pl.BlockSpec((width, tile), lambda k: (0, k)),
+                pl.BlockSpec((width, tile), lambda k: (0, k + tiles)),
+                pl.BlockSpec((width, tile), lambda k: (0, k + 2 * tiles)),
+            ],
+            out_specs=[
+                pl.BlockSpec((count, tile), lambda k: (0, k)),
+                pl.BlockSpec((count, tile), lambda k: (0, k)),
+                pl.BlockSpec((count, tile), lambda k: (0, k + tiles)),
+            ],
+        )(weights, weights, weights, act_all.at[s], grads_all.at[s], grads_all.at[s])
+
+        @pl.when(s > 0)
+        def _():
+            mixed_store(s - 1).wait()
+
+        mixed_stage[...] = acc_m[...].astype(bf16)
+        mixed_store(s).start()
+
+        @pl.when(s == 0)
+        def _():
+            first_part[...] = acc_n[...]
+
+        @pl.when(s == 1)
+        def _():
+            outgoing[0] = acc_n[...].astype(bf16)
+
+        @pl.when(s > 1)
+        def _():
+            pass_sum(s - 1).wait_recv()
+            outgoing[s - 1] = (acc_n[...] + arrived[s - 2].astype(f32)).astype(bf16)
+
+        @pl.when(s > 0)
+        def _():
+            pass_sum(s).start()
+
+        return carry
+
+    lax.fori_loop(0, ring, chunk, 0)
+    mixed_store(ring - 1).wait()
+    pass_sum(ring - 1).wait_recv()
+    final_stage[...] = (first_part[...] + arrived[ring - 2].astype(f32)).astype(bf16)
+    final = pltpu.make_async_copy(final_stage, grad_own, final_sem)
+    final.start()
+
+    def settle(s, carry):
+        keep(s).wait()
+
+        @pl.when(s < ring - 1)
+        def _():
+            pass_rows(s).wait_send()
+
+        @pl.when(s > 0)
+        def _():
+            pass_sum(s).wait_send()
+
+        return carry
+
+    lax.fori_loop(0, ring, settle, 0)
+    grad_keep(ring - 1).wait()
+    final.wait()
+
+
+def feed(own_rows, grad_rows, weights, ring, tile=256, collective_id=7):
+    count, width = own_rows.shape
+    hidden = weights.shape[1] // 3
+    any_spec = pl.BlockSpec(memory_space=pl.ANY)
+    dma = pltpu.SemaphoreType.DMA
+    return pl.pallas_call(
+        functools.partial(feed_kernel, ring, min(tile, hidden)),
+        out_shape=[
+            jax.ShapeDtypeStruct((ring, count, width), bf16),
+            jax.ShapeDtypeStruct((ring, count, width), bf16),
+            jax.ShapeDtypeStruct((ring, count, hidden), bf16),
+            jax.ShapeDtypeStruct((ring, count, 2 * hidden), bf16),
+            jax.ShapeDtypeStruct((ring, count, width), bf16),
+            jax.ShapeDtypeStruct((count, width), bf16),
+        ],
+        in_specs=[any_spec] * (2 + ring),
+        out_specs=[any_spec] * 6,
+        scratch_shapes=[
+            pltpu.VMEM((ring, count, width), bf16),
+            pltpu.VMEM((2, count, width), bf16),
+            pltpu.VMEM((count, width), f32),
+            pltpu.VMEM((count, width), f32),
+            pltpu.VMEM((count, width), f32),
+            pltpu.VMEM((ring - 1, count, width), bf16),
+            pltpu.VMEM((ring - 1, count, width), bf16),
+            pltpu.VMEM((count, width), bf16),
+            pltpu.VMEM((count, width), bf16),
+            dma,
+            dma((ring,)),
+            dma((2,)),
+            dma,
+            dma,
+            dma((ring - 1,)),
+            dma((ring - 1,)),
+            dma((ring - 1,)),
+            dma((ring - 1,)),
+            dma((2,)),
+        ],
+        compiler_params=pltpu.CompilerParams(
+            collective_id=collective_id, has_side_effects=True, vmem_limit_bytes=64 * 1024 * 1024 - 65536,
+        ),
+        cost_estimate=pl.CostEstimate(
+            flops=12 * ring * count * width * hidden,
+            bytes_accessed=8 * ring * count * width,
+            transcendentals=ring * count * hidden,
+        ),
+        name="feed_forward",
+    )(own_rows, *grad_rows, weights)
+
+
+def spread_kernel(rows, weight, out):
+    out[0] = dot_nn(rows[...], weight[0]).astype(out.dtype)
+
+
+def spread(rows, weights, part, cols):
+    shards, width, _ = weights.shape
+    count = rows.shape[0]
+    return pl.pallas_call(
+        spread_kernel,
+        grid=(shards,),
+        in_specs=[
+            pl.BlockSpec((count, width), lambda t: (0, 0)),
+            pl.BlockSpec((1, width, cols), lambda t: (t, 0, part)),
+        ],
+        out_specs=pl.BlockSpec((1, count, cols), lambda t: (t, 0, 0)),
+        out_shape=jax.ShapeDtypeStruct((shards, count, cols), bf16),
+        cost_estimate=pl.CostEstimate(
+            flops=2 * shards * count * width * cols,
+            bytes_accessed=2 * shards * width * cols,
+            transcendentals=0,
+        ),
+        name="spread",
+    )(rows, weights)
+
+
+def gather_kernel(part, weight, begin, out):
+    @pl.when(pl.program_id(0) == 0)
+    def _():
+        out[...] = begin[...]
+
+    out[...] += dot_nt(part[0], weight[0])
+
+
+def gather_sum(parts, weights, part, begin):
+    shards, count, cols = parts.shape
+    width = weights.shape[1]
+    return pl.pallas_call(
+        gather_kernel,
+        grid=(shards,),
+        in_specs=[
+            pl.BlockSpec((1, count, cols), lambda t: (t, 0, 0)),
+            pl.BlockSpec((1, width, cols), lambda t: (t, 0, part)),
+            pl.BlockSpec((count, width), lambda t: (0, 0)),
+        ],
+        out_specs=pl.BlockSpec((count, width), lambda t: (0, 0)),
+        out_shape=jax.ShapeDtypeStruct((count, width), f32),
+        cost_estimate=pl.CostEstimate(
+            flops=2 * shards * count * width * cols,
+            bytes_accessed=2 * shards * width * cols,
+            transcendentals=0,
+        ),
+        name="gather_sum",
+    )(parts, weights, begin)
+
+
+def outer_kernel(rows, part, out, turned):
+    @pl.when(pl.program_id(0) == 0)
+    def _():
+        turned[...] = rows[...].T
+
+    out[...] = dot_nn(turned[...], part[0]).astype(out.dtype)
+
+
+def outer(rows, parts):
+    shards, count, cols = parts.shape
+    width = rows.shape[1]
+    return pl.pallas_call(
+        outer_kernel,
+        grid=(shards,),
+        in_specs=[
+            pl.BlockSpec((count, width), lambda t: (0, 0)),
+            pl.BlockSpec((1, count, cols), lambda t: (t, 0, 0)),
+        ],
+        out_specs=pl.BlockSpec((width, cols), lambda t: (0, t)),
+        out_shape=jax.ShapeDtypeStruct((width, shards * cols), bf16),
+        scratch_shapes=[pltpu.VMEM((width, count), bf16)],
+        cost_estimate=pl.CostEstimate(
+            flops=2 * shards * count * width * cols,
+            bytes_accessed=2 * shards * width * cols,
+            transcendentals=0,
+        ),
+        name="outer",
+    )(rows, parts)
+
+
 def rms_scale(hidden):
     return lax.rsqrt(jnp.mean(hidden * hidden, axis=1, keepdims=True) + epsilon)
 
@@ -451,6 +679,10 @@
     inner = grad_norm * gain
     grad_hidden = scale_rows * (inner - normed * jnp.mean(inner * normed, axis=1, keepdims=True))
     return (grad_hidden, gain_part)
+
+
+def after(value, other):
+    return lax.optimization_barrier((value, other))[0]
 
 
 def local(
@@ -490,8 +722,8 @@
     send_order = jnp.zeros((dp_count,), jnp.int32).at[dest_group].set(local_ids)
     group_sources = lax.dynamic_slice_in_dim(pages, dp_index * group_pages, group_pages)
     perm = (
-        (group_sources // group_pages) * tp_count
-        + jnp.arange(group_pages, dtype=jnp.int32) // dp_count
+        (jnp.arange(group_pages, dtype=jnp.int32) // dp_count) * dp_count
+        + group_sources // group_pages
     ).astype(jnp.int32)
 
     def reorder(rows, order):
@@ -518,99 +750,141 @@
     cos_t, sin_t = jnp.cos(angles), jnp.sin(angles)
 
     q_cols, kv_cols = w_query.shape[1], w_key.shape[1]
-    q_heads, kv_heads = q_cols // HD, kv_cols // HD
-    qkv_shard = jnp.concatenate([w_query, w_key, w_value], axis=1)
-    row_shard = qkv_shard.shape[0]
+    kv_heads = kv_cols // HD
+    per_group = q_cols // kv_cols
+    group_q = per_group * HD
+    groups = range(kv_heads)
+    qkv_shards = [
+        jnp.concatenate(
+            [
+                w_query[:, g * group_q : (g + 1) * group_q],
+                w_key[:, g * HD : (g + 1) * HD],
+                w_value[:, g * HD : (g + 1) * HD],
+            ],
+            axis=1,
+        )
+        for g in groups
+    ]
 
     def gather_all(shard):
         full = lax.all_gather(shard, everyone, axis=0, tiled=False)
         return full.reshape(tp_count, dp_count * shard.shape[0], shard.shape[1])
 
-    def scatter_all(full):
-        blocks = full.reshape(tp_count * dp_count, row_shard, full.shape[2])
-        return lax.psum_scatter(blocks, everyone, scatter_dimension=0, tiled=False)
-
-    w_qkv = gather_all(qkv_shard)
-    w_out_t = gather_all(w_out.T)
+    def trade(value):
+        blocks = value.reshape(group_pages, page_rows, value.shape[-1])
+        return lax.all_to_all(blocks, everyone, split_axis=0, concat_axis=0, tiled=True)
+
+    def trade_back(value):
+        return trade(value).reshape(tp_count, tok_dev, value.shape[-1])
+
+    ring_next = [(t, (t + 1) % tp_count) for t in range(tp_count)]
+
+    def pass_on(value):
+        return lax.ppermute(value, "tensor", ring_next)
+
     gains = lax.all_gather(jnp.stack([attn_gain, mlp_gain]), "dp", axis=1, tiled=True)
     gain_one, gain_two = gains[0].astype(f32), gains[1].astype(f32)
-    full_gate = lax.all_gather(w_gate, "dp", axis=0, tiled=True)
-    full_up = lax.all_gather(w_up, "dp", axis=0, tiled=True)
-    full_down = lax.all_gather(w_down, "dp", axis=1, tiled=True)
+
+    grad_out = grad_top * valid_rows
+    grad_chunks = [grad_out.astype(bf16)]
+    for _ in range(tp_count - 1):
+        grad_chunks.append(pass_on(grad_chunks[-1]))
 
     scale_one = rms_scale(hidden_in)
     normed_one = (hidden_in * scale_one * gain_one).astype(bf16)
-    qkv = jnp.einsum("rk,tkc->trc", normed_one, w_qkv, preferred_element_type=f32).astype(bf16)
-    trade = functools.partial(
-        exchange, dp_count=dp_count, tp_count=tp_count, page_rows=page_rows
-    )
-    qkv_slots = trade(qkv, to_heads=True, collective_id=0)
-    q_t, k_t, k_rows, v_t, v_rows = prepare(qkv_slots, perm, cos_t, sin_t, q_heads, kv_heads)
-    o_t, lse, o_slots = attend_forward(
-        q_t, k_rows, v_t, begin, first_block, perm, page_rows, block_len
-    )
-    mixed = trade(o_slots, to_heads=False, collective_id=1)
-    branch_one = jnp.einsum("trc,tkc->rk", mixed, w_out_t, preferred_element_type=f32)
-    hidden_mid = hidden_in + branch_one
+    w_qkv, qkv, slots = [], [], []
+    for g in groups:
+        if g == 0:
+            w_qkv.append(gather_all(qkv_shards[g]))
+            weight = after(w_qkv[g], grad_chunks[1])
+        else:
+            w_qkv.append(gather_all(after(qkv_shards[g], qkv[-1])))
+            weight = after(w_qkv[g], slots[-1])
+        qkv.append(spread(normed_one, weight, 0, group_q + 2 * HD))
+        slots.append(trade(qkv[g]))
+    out_shard = with_layout_constraint(w_out.T, Layout(major_to_minor=(0, 1)))
+    w_out_t = gather_all(after(out_shard, qkv[-1]))
+    mlp_shard = jnp.concatenate([w_gate, w_up, w_down.T], axis=1)
+    saved, mixed = [], []
+    last = qkv[-1]
+    for g in groups:
+        q_t, k_t, k_rows, v_t, v_rows = prepare(
+            after(slots[g], last), perm, cos_t, sin_t, per_group, 1
+        )
+        if g == 0:
+            w_mlp = lax.all_gather(after(mlp_shard, q_t), "dp", axis=0, tiled=True)
+        o_t, lse, last = attend_forward(
+            q_t, k_rows, v_t, begin, first_block, perm, page_rows, block_len
+        )
+        saved.append((q_t, k_rows, k_t, v_rows, o_t, lse))
+        mixed.append(trade_back(last))
+    hidden_mid = hidden_in
+    for g in groups:
+        hidden_mid = gather_sum(mixed[g], w_out_t, g, hidden_mid)
 
     scale_two = rms_scale(hidden_mid)
     normed_two = (hidden_mid * scale_two * gain_two).astype(bf16)
-    mlp_rows = lax.all_gather(normed_two, "tensor", axis=0, tiled=True)
-    grad_out = grad_top * valid_rows
-    grad_mlp = lax.all_gather(grad_out.astype(bf16), "tensor", axis=0, tiled=True)
-    gate_pre = dot_nn(mlp_rows, full_gate)
-    up_pre = dot_nn(mlp_rows, full_up)
-    sigmoid_gate = jax.nn.sigmoid(gate_pre)
-    activated = gate_pre * sigmoid_gate
-    inner_act = (activated * up_pre).astype(bf16)
-    branch_two = lax.psum_scatter(
-        dot_nn(inner_act, full_down).astype(bf16), "tensor", scatter_dimension=0, tiled=True
-    ).astype(f32)
-    result = ((hidden_mid + branch_two) * valid_rows).astype(bf16)
-
-    grad_down = dot_tn(inner_act, grad_mlp)
-    grad_inner = dot_nt(grad_mlp, full_down)
-    grad_upre = (grad_inner * activated).astype(bf16)
-    grad_gpre = (
-        grad_inner * up_pre * sigmoid_gate * (1.0 + gate_pre * (1.0 - sigmoid_gate))
-    ).astype(bf16)
-    grad_gate = dot_tn(mlp_rows, grad_gpre)
-    grad_up = dot_tn(mlp_rows, grad_upre)
-    grad_normed_two = lax.psum_scatter(
-        (dot_nt(grad_gpre, full_gate) + dot_nt(grad_upre, full_up)).astype(bf16),
-        "tensor",
-        scatter_dimension=0,
-        tiled=True,
-    ).astype(f32)
+    grad_mlp, mlp_rows, inner_act, grad_gate_up, partial_two, grad_normed_two = feed(
+        normed_two, grad_chunks, w_mlp, tp_count
+    )
+    grad_normed_two = grad_normed_two.astype(f32)
     grad_mid_norm, gain_two_part = norm_back(grad_normed_two, hidden_mid, scale_two, gain_two)
     grad_mid = grad_out + grad_mid_norm
-
-    grad_z = grad_mid.astype(bf16)
-    grad_mixed = jnp.einsum("rk,tkc->trc", grad_z, w_out_t, preferred_element_type=f32).astype(
-        bf16
-    )
-    grad_slots = trade(grad_mixed, to_heads=True, collective_id=2)
-    grad_wout_t = jnp.einsum("rk,trc->tkc", grad_z, mixed, preferred_element_type=f32)
-    grad_qkv_slots = attend_backward(
-        grad_slots, q_t, k_rows, k_t, v_rows, o_t, lse, begin, cos_t, sin_t, first_block, perm,
-        page_rows, block_len,
-    )
-    grad_qkv = trade(grad_qkv_slots, to_heads=False, collective_id=3)
-    grad_wqkv = jnp.einsum("rk,trc->tkc", normed_one, grad_qkv, preferred_element_type=f32)
-    grad_normed_one = jnp.einsum("trc,tkc->rk", grad_qkv, w_qkv, preferred_element_type=f32)
+    branch_two = partial_two[1]
+    for s in range(2, tp_count):
+        branch_two = (pass_on(branch_two).astype(f32) + partial_two[s].astype(f32)).astype(bf16)
+    branch_two = pass_on(branch_two)
+
+    def reduce_dp(grad):
+        return lax.psum_scatter(grad.astype(bf16), "dp", scatter_dimension=0, tiled=True)
+
+    def reduce_tensor(value):
+        cols = value.shape[1] // tp_count
+        total = lax.dynamic_slice_in_dim(value, tp_index * cols, cols, 1).astype(f32)
+        for s in range(1, tp_count):
+            target = lax.rem(tp_index + s, tp_count)
+            block = lax.dynamic_slice_in_dim(value, target * cols, cols, 1)
+            pairs = [(t, (t + s) % tp_count) for t in range(tp_count)]
+            total = total + lax.ppermute(block, "tensor", pairs).astype(f32)
+        return total
+
+    def flat(value):
+        return value.reshape(tok_group, value.shape[-1])
+
+    grad_down_t = dot_tn(flat(grad_mlp), flat(inner_act)).astype(bf16)
+    sum_down = reduce_dp(grad_down_t)
+    grad_gate_up = dot_tn(flat(mlp_rows), flat(after(grad_gate_up, grad_down_t))).astype(bf16)
+    sum_gate_up = reduce_dp(grad_gate_up)
+    grad_z = after(grad_mid.astype(bf16), grad_gate_up)
+    grad_slots = [trade(spread(grad_z, w_out_t, g, group_q)) for g in groups]
+    grad_qkv = []
+    last = grad_z
+    for g in groups:
+        q_t, k_rows, k_t, v_rows, o_t, lse = saved[g]
+        back = attend_backward(
+            after(grad_slots[g], last), q_t, k_rows, k_t, v_rows, o_t, lse, begin, cos_t, sin_t,
+            first_block, perm, page_rows, block_len,
+        )
+        grad_qkv.append(trade_back(back))
+        last = (back, sum_down)
+    grad_wout = outer(after(grad_z, back), jnp.concatenate(mixed, axis=2))
+    sum_out = reduce_dp(grad_wout)
+    normed_late = after(normed_one, (sum_gate_up, grad_wout))
+    hidden = sum_gate_up.shape[1] // 2
+    grad_wqkv = outer(normed_late, jnp.concatenate(grad_qkv, axis=2))
+    sum_qkv = reduce_tensor(reduce_dp(grad_wqkv))
+    grad_normed_one = jnp.zeros((tok_dev, width), f32)
+    for g in groups:
+        grad_normed_one = gather_sum(grad_qkv[g], w_qkv[g], 0, grad_normed_one)
+    sum_out = reduce_tensor(sum_out)
+    each = group_q + 2 * HD
+    sum_qkv = [sum_qkv[:, g * each : (g + 1) * each] for g in groups]
+    result = (
+        (after(hidden_mid, back) + branch_two.astype(f32) + partial_two[0].astype(f32)) * valid_rows
+    ).astype(bf16)
     grad_in_norm, gain_one_part = norm_back(grad_normed_one, hidden_in, scale_one, gain_one)
     grad_in = (grad_mid + grad_in_norm).astype(bf16)
 
-    def reduce_dp(grad, axis):
-        return lax.psum_scatter(
-            grad.astype(bf16), "dp", scatter_dimension=axis, tiled=True
-        ).astype(f32)
-
-    sum_down = reduce_dp(grad_down, 1)
-    sum_gate = reduce_dp(grad_gate, 0)
-    sum_up = reduce_dp(grad_up, 0)
-    sum_out = scatter_all(grad_wout_t.astype(bf16)).astype(f32).T
-    sum_qkv = scatter_all(grad_wqkv.astype(bf16)).astype(f32)
     gain_sums = lax.psum(jnp.stack([gain_one_part, gain_two_part]), everyone)
     gain_shard = attn_gain.shape[0]
     gain_sums = lax.dynamic_slice_in_dim(gain_sums, dp_index * gain_shard, gain_shard, 1)
@@ -618,14 +892,14 @@
         reorder(result, dest_group),
         reorder(grad_in, dest_group),
         gain_sums[0],
-        sum_qkv[:, :q_cols],
-        sum_qkv[:, q_cols : q_cols + kv_cols],
-        sum_qkv[:, q_cols + kv_cols :],
-        sum_out,
+        jnp.concatenate([part[:, :group_q] for part in sum_qkv], axis=1),
+        jnp.concatenate([part[:, group_q : group_q + HD] for part in sum_qkv], axis=1),
+        jnp.concatenate([part[:, group_q + HD :] for part in sum_qkv], axis=1),
+        sum_out.T,
         gain_sums[1],
-        sum_gate,
-        sum_up,
-        sum_down,
+        sum_gate_up[:, :hidden].astype(f32),
+        sum_gate_up[:, hidden:].astype(f32),
+        sum_down.astype(f32).T,
     )
 
 

time: 1820 us -> 1310 us (0.72)
  waiting for transfers between devices: 962 us -> 404 us
  matrix products: 296 us -> 66 us
  Pallas kernels: 378 us -> 524 us
  blocking collectives: 49.8 us -> 138 us
  starting transfers between devices: 0.99 us -> 37.6 us
  local copies, waits for them, and re-layouts: 62.2 us -> 37.2 us
  other arithmetic: 47.6 us -> 70.3 us
    reduce_scatter x7 -> x4, waiting for transfers between devices: 449 us -> 0.03 us  [reduce_dp(): lax.psum_scatter(grad.astype(bf16), 'dp', scatter_dimension=0, tiled=True)]
    all_gather x5 -> x1, waiting for transfers between devices: 355 us -> 0.01 us  [local(): w_mlp = lax.all_gather(after(mlp_shard, q_t), 'dp', axis=0, tiled=True)]
    dot_general x12 -> x0, matrix products: 225 us -> none  [the longest x3 86.9 us: dot_nt(): lax.dot_general(left, right, (((1,), (1,)), ((), ())), preferred_element_...]
    ppermute x0 -> x12, waiting for transfers between devices: none -> 193 us  [the longest x6 168 us: pass_on(): return lax.ppermute(value, 'tensor', ring_next)]
    all_to_all x0 -> x6, waiting for transfers between devices: none -> 186 us  [trade(): lax.all_to_all(blocks, everyone, split_axis=0, concat_axis=0, tiled=True)]
    all_gather x2 -> x3, waiting for transfers between devices: 155 us -> 24.7 us  [gather_all(): full = lax.all_gather(shard, everyone, axis=0, tiled=False)]
    pallas_call x4 -> x11, Pallas kernels: 252 us -> 366 us  [the longest x1 277 us: feed(): pl.pallas_call(functools.partial(feed_kernel, ring, min(tile, hidden)), o...]
    all_to_all x0 -> x2, blocking collectives: none -> 87.1 us  [trade(): lax.all_to_all(blocks, everyone, split_axis=0, concat_axis=0, tiled=True)]
  transfers between devices with their start and end apart: 14 -> 26, of which waited for: 11 -> 12; matrix products, arithmetic and copies ran while one was open for 17% -> 11% of each run, Pallas kernels for 21% -> 18%
where the time goes in v2:
time: 1310 us; the launch traced here: 1290 us
  Pallas kernels  524 us (40%)
  waiting for transfers between devices  404 us (31%)
  blocking collectives  138 us (11%)
  other arithmetic  70.3 us (5%)
  matrix products  66 us (5%)
  starting transfers between devices  37.6 us (3%)
  local copies, waits for them, and re-layouts  37.2 us (3%)
  between operations  15.1 us (1%)
    pallas_call x1, Pallas kernels, feed(): pl.pallas_call(functools.partial(feed_kernel, ring, min(tile, hidden)), o...  277 us
    all_to_all x6, waiting for transfers between devices, trade(): lax.all_to_all(blocks, everyone, split_axis=0, concat_axis=0, tiled=True)  186 us
    ppermute x6, waiting for transfers between devices, pass_on(): return lax.ppermute(value, 'tensor', ring_next)  168 us
    all_to_all x2, blocking collectives, trade(): lax.all_to_all(blocks, everyone, split_axis=0, concat_axis=0, tiled=True)  87.1 us
    pallas_call x2, Pallas kernels, attend_backward(): pl.pallas_call(functools.partial(backward_kernel, q_heads, kv_heads, page...  69.4 us
    pallas_call x2, Pallas kernels, attend_forward(): pl.pallas_call(functools.partial(forward_kernel, q_heads, kv_heads, page_...  66.6 us
    dot_general x2, matrix products, dot_tn(): lax.dot_general(left, right, (((0,), (0,)), ((), ())), preferred_element_...  66 us
    psum x1, blocking collectives, local(): gain_sums = lax.psum(jnp.stack([gain_one_part, gain_two_part]), everyone)  41.8 us
  transfers between devices with their start and end apart: 26, of which 12 were waited for; matrix products, arithmetic and copies ran while one was open for 11% of the time, Pallas kernels for 18%

profile of v2, /device:TPU:0, one launch (start us, length us, event | category | flops | bytes accessed | tf_op | source)
XLA Modules:
  0.0 1292.1 jit_solution(2988515666713385454)
XLA Ops:
  18.5 3.6 gather_fusion.2
  22.9 4.1 broadcast_select_fusion.2
  33.9 8.9 all_gather.24
  44.1 3.9 multiply_convert_fusion.1.rows
  48.1 58.3 %collective-permute-done.refs_1_ = bf16[512,2048]{1,0:T(8,128)(2,1)} collective-permute-done((bf16[512,2048]{1,0:T(8,128)(2,1)}, bf16[512,2048]{1,0:T(8,128)(2,1)}, u32[]{:S(2)}, u32[]{:S(2)}) %collective-permute-start) | collective-permute-done | bytes 2097184 | tf_op jit(solution)/shard_map/ppermute | solution.py:783
  106.4 8.2 spread.4
  114.6 3.9 all-to-all-start
  119.5 49.6 %all-to-all-done.refs_0_.refs_1_ = bf16[32,64,384]{2,1,0:T(8,128)(2,1)S(1)} async-done(((bf16[32,64,384]{2,1,0:T(8,128)(2,1)}), bf16[32,64,384]{2,1,0:T(8,128)(2,1)S(1)}, u32[]{:S(2)}, u32[]{:S(2)}) %all-to-all-start) | async-done | bytes 1572896 | tf_op jit(solution)/shard_map/all_to_all | solution.py:775
  169.1 24.7 %all-gather.12.cloned.1.call-done = bf16[8192,384]{1,0:T(8,128)(2,1)} async-done(((bf16[256,384]{1,0:T(8,128)(2,1)}), bf16[8192,384]{1,0:T(8,128)(2,1)}) %all-gather.12.cloned.1.call-update) | async-done | bytes 6291472 | tf_op jit(solution)/shard_map/all_gather | solution.py:770
  193.8 8.3 spread.5
  208.4 10.6 prepare.2
  222.1 33.3 %attend_forward.2 = (bf16[256,2048]{1,0:T(8,128)(2,1)}, f32[4,2048]{1,0:T(4,128)}, bf16[32,64,256]{2,1,0:T(8,128)(2,1)}) custom-call(s32[8]{0:T(128)} %get-tuple-element.159.first_block, s32[32]{0:T(128)} %fusion.13.perm, bf16[256,2048]{1,0:T(8,128)(2,1)} %get-tuple-element.52.q_t.refs_4_, bf16[1,2048,64]{2,1,0:T(8,128)(2,1)} %get-tuple-element.53.k_rows.refs_5_, ...), custom_call_target="tpu_custom_call" | custom-call | flops 1073741824 | bytes 4194304 | tf_op jit(solution)/shard_map/attend_forward/pallas_call | solution.py:163
  255.4 26.0 %all-to-all-done.1.refs_0_.refs_1_ = bf16[32,64,384]{2,1,0:T(8,128)(2,1)S(1)} async-done(((bf16[32,64,384]{2,1,0:T(8,128)(2,1)}), bf16[32,64,384]{2,1,0:T(8,128)(2,1)S(1)}, u32[]{:S(2)}, u32[]{:S(2)}) %all-to-all-start.1) | async-done | bytes 1572896 | tf_op jit(solution)/shard_map/all_to_all | solution.py:775
  286.5 10.6 prepare.3
  297.1 33.3 %attend_forward.3 = (bf16[256,2048]{1,0:T(8,128)(2,1)}, f32[4,2048]{1,0:T(4,128)}, bf16[32,64,256]{2,1,0:T(8,128)(2,1)}) custom-call(s32[8]{0:T(128)} %get-tuple-element.159.first_block, s32[32]{0:T(128)} %fusion.13.perm, bf16[256,2048]{1,0:T(8,128)(2,1)} %get-tuple-element.57.q_t.refs_4_, bf16[1,2048,64]{2,1,0:T(8,128)(2,1)} %get-tuple-element.58.k_rows.refs_5_, ...), custom_call_target="tpu_custom_call" | custom-call | flops 1073741824 | bytes 4194304 | tf_op jit(solution)/shard_map/attend_forward/pallas_call | solution.py:163
  330.4 30.4 %all-to-all-done.3 = bf16[32,64,256]{2,1,0:T(8,128)(2,1)S(1)} async-done(((bf16[32,64,256]{2,1,0:T(8,128)(2,1)}), bf16[32,64,256]{2,1,0:T(8,128)(2,1)S(1)}, u32[]{:S(2)}, u32[]{:S(2)}) %all-to-all-start.3) | async-done | bytes 1048608 | tf_op jit(solution)/shard_map/all_to_all | solution.py:775
  365.9 8.6 gather_sum.4.begin
  374.5 60.2 %all-to-all-done.2 = bf16[32,64,256]{2,1,0:T(8,128)(2,1)S(1)} async-done(((bf16[32,64,256]{2,1,0:T(8,128)(2,1)}), bf16[32,64,256]{2,1,0:T(8,128)(2,1)S(1)}, u32[]{:S(2)}, u32[]{:S(2)}) %all-to-all-start.2) | async-done | bytes 1048608 | tf_op jit(solution)/shard_map/all_to_all | solution.py:775
  435.7 8.9 gather_sum.5
  449.8 277.5 %feed_forward.1 = (bf16[4,512,2048]{2,1,0:T(8,128)(2,1)}, bf16[4,512,2048]{2,1,0:T(8,128)(2,1)}, bf16[4,512,2048]{2,1,0:T(8,128)(2,1)}, bf16[4,512,4096]{2,1,0:T...) custom-call(bf16[512,2048]{1,0:T(8,128)(2,1)} %multiply_convert_fusion.own_rows, ...), custom_call_target="tpu_custom_call" | custom-call | flops 103079215104 | bytes 33554432 | tf_op jit(solution)/shard_map/feed_forward/pallas_call | solution.py:542
  727.3 24.0 %bitcast_convert_fusion.1 = bf16[2048,2048]{1,0:T(8,128)(2,1)} fusion(bf16[4,512,2048]{2,1,0:T(8,128)(2,1)} %get-tuple-element.66, bf16[4,512,2048]{2,1,0:T(8,128)(2,1)} %get-tuple-element.67), kind=kOutput, calls=%fused_computation.8 | convolution fusion | flops 17184063488 | bytes 25165824 | tf_op jit(solution)/shard_map/dot_general | solution.py:33
  751.3 42.1 %bitcast_convert_fusion = bf16[2048,4096]{1,0:T(8,128)(2,1)} fusion(bf16[4,512,2048]{2,1,0:T(8,128)(2,1)} %get-tuple-element.64, bf16[4,512,4096]{2,1,0:T(8,128)(2,1)} %get-tuple-element.68), kind=kOutput, calls=%fused_computation.7 | convolution fusion | flops 34368126976 | bytes 41943040 | tf_op jit(solution)/shard_map/dot_general | solution.py:33
  794.1 4.4 fusion.5
  798.5 3.9 fusion.20.rows
  802.4 6.2 spread.7
  808.6 5.3 all-to-all-start.5
  814.0 6.3 spread.6
  820.3 19.9 %all-to-all-done.5.refs_0_.refs_1_.refs_2_.refs_3_ = bf16[32,64,256]{2,1,0:T(8,128)(2,1)} async-done(((bf16[32,64,256]{2,1,0:T(8,128)(2,1)}), bf16[32,64,256]{2,1,0:T(8,128)(2,1)}, u32[]{:S(2)}, u32[]{:S(2)}) %all-to-all-start.5) | async-done | bytes 1048608 | tf_op jit(solution)/shard_map/all_to_all | solution.py:775
  840.1 3.8 all-to-all-start.4
  846.8 34.9 %attend_backward.2 = bf16[32,64,384]{2,1,0:T(8,128)(2,1)} custom-call(s32[8]{0:T(128)} %get-tuple-element.159.first_block, s32[32]{0:T(128)} %fusion.13.perm, bf16[32,64,256]{2,1,0:T(8,128)(2,1)} %all-to-all-done.5.refs_0_.refs_1_.refs_2_.refs_3_, bf16[32,64,256]{2,1,0:T(8,128)(2,1)} %all-to-all-done.5.refs_0_.refs_1_.refs_2_.refs_3_, ...), custom_call_target="tpu_custom_call" | custom-call | flops 3221225472 | bytes 6291456 | tf_op jit(solution)/shard_map/attend_backward/pallas_call | solution.py:322
  881.8 34.4 %attend_backward.3 = bf16[32,64,384]{2,1,0:T(8,128)(2,1)} custom-call(s32[8]{0:T(128)} %get-tuple-element.159.first_block, s32[32]{0:T(128)} %fusion.13.perm, bf16[32,64,256]{2,1,0:T(8,128)(2,1)} %all-to-all-done.4.refs_0_.refs_1_.refs_2_.refs_3_, bf16[32,64,256]{2,1,0:T(8,128)(2,1)} %all-to-all-done.4.refs_0_.refs_1_.refs_2_.refs_3_, ...), custom_call_target="tpu_custom_call" | custom-call | flops 3221225472 | bytes 6291456 | tf_op jit(solution)/shard_map/attend_backward/pallas_call | solution.py:322
  916.2 9.1 outer.2
  925.4 46.1 %all_to_all.40 = bf16[32,64,384]{2,1,0:T(8,128)(2,1)S(1)} all-to-all(bf16[32,64,384]{2,1,0:T(8,128)(2,1)} %attend_backward.2), channel_id=1, replica_groups=mesh['dp'=8,'tensor'=4] {'tensor','dp'}, dimensions={0} | all-to-all | bytes 3145728 | tf_op jit(solution)/shard_map/all_to_all | solution.py:775
  971.5 41.0 %all_to_all.41 = bf16[32,64,384]{2,1,0:T(8,128)(2,1)S(1)} all-to-all(bf16[32,64,384]{2,1,0:T(8,128)(2,1)S(1)} %copy-done.14), channel_id=1, replica_groups=mesh['dp'=8,'tensor'=4] {'tensor','dp'}, dimensions={0} | all-to-all | bytes 3145728 | tf_op jit(solution)/shard_map/all_to_all | solution.py:775
  1015.6 11.7 outer.3
  1030.5 47.8 %collective-permute-done.3 = bf16[512,2048]{1,0:T(8,128)(2,1)S(1)} collective-permute-done((bf16[512,2048]{1,0:T(8,128)(2,1)S(1)}, bf16[512,2048]{1,0:T(8,128)(2,1)S(1)}, u32[]{:S(2)}, u32[]{:S(2)}) %collective-permute-start.3) | collective-permute-done | bytes 2097184 | tf_op jit(solution)/shard_map/ppermute | solution.py:783
  1081.2 47.7 %collective-permute-done.4 = bf16[512,2048]{1,0:T(8,128)(2,1)S(1)} collective-permute-done((bf16[512,2048]{1,0:T(8,128)(2,1)S(1)}, bf16[512,2048]{1,0:T(8,128)(2,1)S(1)}, u32[]{:S(2)}, u32[]{:S(2)}) %collective-permute-start.4) | collective-permute-done | bytes 2097184 | tf_op jit(solution)/shard_map/ppermute | solution.py:783
  1128.9 3.8 fusion.8
  1135.2 11.1 gather_sum.6.begin
  1150.7 10.5 gather_sum.7
  1161.2 4.6 multiply_reduce_fusion
  1165.8 14.0 %collective-permute-done.5 = bf16[512,2048]{1,0:T(8,128)(2,1)} collective-permute-done((bf16[512,2048]{1,0:T(8,128)(2,1)}, bf16[512,2048]{1,0:T(8,128)(2,1)}, u32[]{:S(2)}, u32[]{:S(2)}) %collective-permute-start.5) | collective-permute-done | bytes 2097184 | tf_op jit(solution)/shard_map/ppermute | solution.py:783
  1179.8 7.3 add_convert_fusion
  1193.0 4.0 broadcast_select_fusion
  1199.1 41.8 %psum.7 = f32[2,2048]{1,0:T(2,128)S(1)} all-reduce(f32[2,2048]{1,0:T(2,128)S(1)} %pad_maximum_fusion.8), channel_id=1, replica_groups=mesh['dp'=8,'tensor'=4] {'tensor','dp'}, use_global_device_ids=true, to_apply=%region_11.13 | all-reduce | flops 4096 | bytes 32768 | tf_op jit(solution)/shard_map/psum | solution.py:888
  1245.9 4.4 collective-permute-start.7
  1252.8 10.8 collective-permute-done.11
  1265.9 14.9 %collective-permute-done.7 = bf16[256,768]{1,0:T(8,128)(2,1)} collective-permute-done((bf16[256,768]{1,0:T(8,128)(2,1)S(1)}, bf16[256,768]{1,0:T(8,128)(2,1)}, u32[]{:S(2)}, u32[]{:S(2)}) %collective-permute-start.7) | collective-permute-done | bytes 393248 | tf_op jit(solution)/shard_map/ppermute | solution.py:848
  (180 shorter events, 88.4 us)
Async XLA Ops:
  7.2 99.2 %all-gather.10.cloned.1.call-start = ((), (), s32[]{:S(2)}) async-start(), calls=%async_computation.17 | async-start | bytes 6488064 | tf_op jit(solution)/shard_map/all_gather | solution.py:770
  10.1 183.7 %all-gather.12.cloned.1.call-start = ((), (), s32[]{:S(2)}) async-start(), calls=%async_computation.18 | async-start | bytes 6488064 | tf_op jit(solution)/shard_map/all_gather | solution.py:770
  11.6 10.5 copy-start.29
  27.0 6.9 copy-start.34
  27.0 6.9 copy-start.35
  30.1 76.3 %collective-permute-start = (bf16[512,2048]{1,0:T(8,128)(2,1)}, bf16[512,2048]{1,0:T(8,128)(2,1)}, u32[]{:S(2)}, u32[]{:S(2)}) collective-permute-start(bf16[512,2048]{1,0:T(8,128)(2,1)} %fusion.10.refs_0_), channel_id=1, source_target_pairs={{0,1},{1,2},{2,3},{3,0},{4,5},{5,6},{6,7},{7,4},{8,9},{9,10},{10,1... | collective-permute-start | bytes 6291464 | tf_op jit(solution)/shard_map/ppermute | solution.py:783
  33.8 80.8 %copy-start.26 = (f32[512]{0:T(512)}, f32[512]{0:T(512)S(1)}, u32[]{:S(2)}) copy-start(f32[512]{0:T(512)S(1)} %rsqrt.20) | copy-start | bytes 6148
  43.6 403.7 %copy-start.18 = (f32[1,2048]{1,0:T(1,128)}, f32[1,2048]{1,0:T(1,128)S(1)}, u32[]{:S(2)}) copy-start(f32[1,2048]{1,0:T(1,128)S(1)} %get-tuple-element.150) | copy-start | bytes 24580
  106.4 12.3 copy-start.17
  114.6 54.4 %all-to-all-start = ((bf16[32,64,384]{2,1,0:T(8,128)(2,1)}), bf16[32,64,384]{2,1,0:T(8,128)(2,1)S(1)}, u32[]{:S(2)}, u32[]{:S(2)}) async-start(bf16[32,64,384]{2,1,0:T(8,128)(2,1)} %bitcast.92), calls=%async_computation | async-start | bytes 3145728 | tf_op jit(solution)/shard_map/all_to_all | solution.py:775
  118.6 247.3 %all-gather.14.cloned.1.call-start = ((), (), s32[]{:S(2)}) async-start(), calls=%async_computation.19 | async-start | bytes 8650752 | tf_op jit(solution)/shard_map/all_gather | solution.py:770
  169.1 33.0 %copy-start.6 = (bf16[32,64,384]{2,1,0:T(8,128)(2,1)}, bf16[32,64,384]{2,1,0:T(8,128)(2,1)S(1)}, u32[]{:S(2)}) copy-start(bf16[32,64,384]{2,1,0:T(8,128)(2,1)S(1)} %all-to-all-done.refs_0_.refs_1_) | copy-start | bytes 4718596
  193.8 8.4 copy-start.28
  193.8 8.4 copy-start.16
  193.8 9.1 copy-start.33
  202.1 247.7 %all-gather.8.cloned.1.call-start = ((), (), s32[]{:S(2)}) async-start(), calls=%async_computation.12 | async-start | bytes 28311552 | tf_op jit(solution)/shard_map/all_gather | solution.py:815
  219.0 62.4 %all-to-all-start.1 = ((bf16[32,64,384]{2,1,0:T(8,128)(2,1)}), bf16[32,64,384]{2,1,0:T(8,128)(2,1)S(1)}, u32[]{:S(2)}, u32[]{:S(2)}) async-start(bf16[32,64,384]{2,1,0:T(8,128)(2,1)} %bitcast.11), calls=%async_computation.1 | async-start | bytes 3145728 | tf_op jit(solution)/shard_map/all_to_all | solution.py:775
  281.4 79.4 %all-to-all-start.3 = ((bf16[32,64,256]{2,1,0:T(8,128)(2,1)}), bf16[32,64,256]{2,1,0:T(8,128)(2,1)S(1)}, u32[]{:S(2)}, u32[]{:S(2)}) async-start(bf16[32,64,256]{2,1,0:T(8,128)(2,1)} %get-tuple-element.55), calls=%async_computation.3 | async-start | bytes 2097152 | tf_op jit(solution)/shard_map/all_to_all | solution.py:775
  284.6 79.0 %collective-permute-start.1 = (bf16[512,2048]{1,0:T(8,128)(2,1)}, bf16[512,2048]{1,0:T(8,128)(2,1)}, u32[]{:S(2)}, u32[]{:S(2)}) collective-permute-start(bf16[512,2048]{1,0:T(8,128)(2,1)} %collective-permute-done.refs_1_), channel_id=1, source_target_pairs={{0,1},{1,2},{2,3},{3,0},{4,5},{5,6},{6,7},{7,4},{8,9},{9,10},{10,1... | collective-permute-start | bytes 6291464 | tf_op jit(solution)/shard_map/ppermute | solution.py:783
  360.8 5.1 copy-start.10
  360.8 73.9 %all-to-all-start.2 = ((bf16[32,64,256]{2,1,0:T(8,128)(2,1)}), bf16[32,64,256]{2,1,0:T(8,128)(2,1)S(1)}, u32[]{:S(2)}, u32[]{:S(2)}) async-start(bf16[32,64,256]{2,1,0:T(8,128)(2,1)} %get-tuple-element.60), calls=%async_computation.2 | async-start | bytes 2097152 | tf_op jit(solution)/shard_map/all_to_all | solution.py:775
  363.5 518.3 %reduce-scatter.5.cloned.1.call-start = ((), (), s32[]{:S(2)}) async-start(), calls=%async_computation.13 | async-start | bytes 9437184 | tf_op jit(solution)/shard_map/reduce_scatter | solution.py:839
  363.6 86.2 %collective-permute-start.2 = (bf16[512,2048]{1,0:T(8,128)(2,1)}, bf16[512,2048]{1,0:T(8,128)(2,1)}, u32[]{:S(2)}, u32[]{:S(2)}) collective-permute-start(bf16[512,2048]{1,0:T(8,128)(2,1)} %collective-permute-done.1.refs_2_), channel_id=1, source_target_pairs={{0,1},{1,2},{2,3},{3,0},{4,5},{5,6},{6,7},{7,4},{8,9},{9,10},{10,1... | collective-permute-start | bytes 6291464 | tf_op jit(solution)/shard_map/ppermute | solution.py:783
  751.3 264.3 %reduce-scatter.7.cloned.1.call-start = ((), (), s32[]{:S(2)}) async-start(), calls=%async_computation.14 | async-start | bytes 18874368 | tf_op jit(solution)/shard_map/reduce_scatter | solution.py:839
  808.6 31.5 %all-to-all-start.5 = ((bf16[32,64,256]{2,1,0:T(8,128)(2,1)}), bf16[32,64,256]{2,1,0:T(8,128)(2,1)}, u32[]{:S(2)}, u32[]{:S(2)}) async-start(bf16[32,64,256]{2,1,0:T(8,128)(2,1)} %bitcast.87), calls=%async_computation.5 | async-start | bytes 2097152 | tf_op jit(solution)/shard_map/all_to_all | solution.py:775
  814.0 30.0 %copy-start.11 = (bf16[32,64,256]{2,1,0:T(8,128)(2,1)S(1)}, bf16[32,64,256]{2,1,0:T(8,128)(2,1)}, u32[]{:S(2)}) copy-start(bf16[32,64,256]{2,1,0:T(8,128)(2,1)} %copy-done.10) | copy-start | bytes 3145732
  840.1 41.6 %all-to-all-start.4 = ((bf16[32,64,256]{2,1,0:T(8,128)(2,1)}), bf16[32,64,256]{2,1,0:T(8,128)(2,1)}, u32[]{:S(2)}, u32[]{:S(2)}) async-start(bf16[32,64,256]{2,1,0:T(8,128)(2,1)} %bitcast.86), calls=%async_computation.4 | async-start | bytes 2097152 | tf_op jit(solution)/shard_map/all_to_all | solution.py:775
  843.9 353.1 %reduce-scatter.11.cloned.1.call-start = ((), (), s32[]{:S(2)}) async-start(), calls=%async_computation.16 | async-start | bytes 9437184 | tf_op jit(solution)/shard_map/reduce_scatter | solution.py:839
  925.4 318.5 %reduce-scatter.9.cloned.1.call-start = ((), (), s32[]{:S(2)}) async-start(), calls=%async_computation.15 | async-start | bytes 14155776 | tf_op jit(solution)/shard_map/reduce_scatter | solution.py:839
  925.4 46.1 %copy-start.14 = (bf16[32,64,384]{2,1,0:T(8,128)(2,1)S(1)}, bf16[32,64,384]{2,1,0:T(8,128)(2,1)}, u32[]{:S(2)}) copy-start(bf16[32,64,384]{2,1,0:T(8,128)(2,1)} %attend_backward.3) | copy-start | bytes 4718596
  971.5 41.0 %copy-start.9 = (bf16[32,64,384]{2,1,0:T(8,128)(2,1)}, bf16[32,64,384]{2,1,0:T(8,128)(2,1)S(1)}, u32[]{:S(2)}) copy-start(bf16[32,64,384]{2,1,0:T(8,128)(2,1)S(1)} %all_to_all.40) | copy-start | bytes 4718596
  1029.0 49.2 %collective-permute-start.3 = (bf16[512,2048]{1,0:T(8,128)(2,1)S(1)}, bf16[512,2048]{1,0:T(8,128)(2,1)S(1)}, u32[]{:S(2)}, u32[]{:S(2)}) collective-permute-start(bf16[512,2048]{1,0:T(8,128)(2,1)S(1)} %slice_bitcast_fusion), channel_id=1, source_target_pairs={{0,1},{1,2},{2,3},{3,0},{4,5},{5,6},{6,7},{7,4},{8,9},{9,10},{10,1... | collective-permute-start | bytes 6291464 | tf_op jit(solution)/shard_map/ppermute | solution.py:783
  1081.1 51.6 %copy-start.32 = (s32[8]{0:T(128)S(1)}, s32[8]{0:T(128)}, u32[]{:S(2)}) copy-start(s32[8]{0:T(128)} %copy-done.31) | copy-start | bytes 100
  1081.1 47.8 %collective-permute-start.4 = (bf16[512,2048]{1,0:T(8,128)(2,1)S(1)}, bf16[512,2048]{1,0:T(8,128)(2,1)S(1)}, u32[]{:S(2)}, u32[]{:S(2)}) collective-permute-start(bf16[512,2048]{1,0:T(8,128)(2,1)S(1)} %fusion.9), channel_id=1, source_target_pairs={{0,1},{1,2},{2,3},{3,0},{4,5},{5,6},{6,7},{7,4},{8,9},{9,10},{10,1... | collective-permute-start | bytes 6291464 | tf_op jit(solution)/shard_map/ppermute | solution.py:783
  1132.7 47.1 %collective-permute-start.5 = (bf16[512,2048]{1,0:T(8,128)(2,1)}, bf16[512,2048]{1,0:T(8,128)(2,1)}, u32[]{:S(2)}, u32[]{:S(2)}) collective-permute-start(bf16[512,2048]{1,0:T(8,128)(2,1)} %fusion.8), channel_id=1, source_target_pairs={{0,1},{1,2},{2,3},{3,0},{4,5},{5,6},{6,7},{7,4},{8,9},{9,10},{10,1... | collective-permute-start | bytes 6291464 | tf_op jit(solution)/shard_map/ppermute | solution.py:783
  1135.2 11.1 copy-start.15
  1150.7 10.5 copy-start.21
  1150.7 10.5 copy-start.27
  1161.2 18.6 %copy-start.2 = (f32[512,2048]{1,0:T(8,128)S(1)}, f32[512,2048]{1,0:T(8,128)}, u32[]{:S(2)}) copy-start(f32[512,2048]{1,0:T(8,128)} %gather_sum.5) | copy-start | bytes 12582916
  1161.2 18.6 %copy-start.3 = (f32[8,64,2048]{2,1,0:T(8,128)S(1)}, f32[8,64,2048]{2,1,0:T(8,128)}, u32[]{:S(2)}) copy-start(f32[8,64,2048]{2,1,0:T(8,128)} %get-tuple-element.157) | copy-start | bytes 12582916
  1187.1 5.9 copy-start.30
  1197.0 53.3 %copy-start.13 = (bf16[256,4096]{1,0:T(8,128)(2,1)S(1)}, bf16[256,4096]{1,0:T(8,128)(2,1)}, u32[]{:S(2)}) copy-start(bf16[256,4096]{1,0:T(8,128)(2,1)} %reduce-scatter.7.cloned.1.call-done) | copy-start | bytes 6291460
  1199.1 51.2 %collective-permute-start.10 = (bf16[256,512]{1,0:T(8,128)(2,1)}, bf16[256,512]{1,0:T(8,128)(2,1)}, u32[]{:S(2)}, u32[]{:S(2)}) collective-permute-start(bf16[256,512]{1,0:T(8,128)(2,1)} %get-tuple-element.133), channel_id=1, source_target_pairs={{0,2},{1,3},{2,0},{3,1},{4,6},{5,7},{6,4},{7,5},{8,10},{9,11},{10,... | collective-permute-start | bytes 786440 | tf_op jit(solution)/shard_map/ppermute | solution.py:848
  1241.6 22.0 %collective-permute-start.11 = (bf16[256,512]{1,0:T(8,128)(2,1)}, bf16[256,512]{1,0:T(8,128)(2,1)}, u32[]{:S(2)}, u32[]{:S(2)}) collective-permute-start(bf16[256,512]{1,0:T(8,128)(2,1)} %get-tuple-element.132), channel_id=1, source_target_pairs={{0,3},{1,0},{2,1},{3,2},{4,7},{5,4},{6,5},{7,6},{8,11},{9,8},{10,9... | collective-permute-start | bytes 786440 | tf_op jit(solution)/shard_map/ppermute | solution.py:848
  1243.8 19.8 %collective-permute-start.9 = (bf16[256,512]{1,0:T(8,128)(2,1)S(1)}, bf16[256,512]{1,0:T(8,128)(2,1)}, u32[]{:S(2)}, u32[]{:S(2)}) collective-permute-start(bf16[256,512]{1,0:T(8,128)(2,1)S(1)} %get-tuple-element.131), channel_id=1, source_target_pairs={{0,1},{1,2},{2,3},{3,0},{4,5},{5,6},{6,7},{7,4},{8,9},{9,10},{10,1... | collective-permute-start | bytes 786440 | tf_op jit(solution)/shard_map/ppermute | solution.py:848
  1245.9 20.0 %collective-permute-start.6 = (bf16[256,768]{1,0:T(8,128)(2,1)}, bf16[256,768]{1,0:T(8,128)(2,1)S(1)}, u32[]{:S(2)}, u32[]{:S(2)}) collective-permute-start(bf16[256,768]{1,0:T(8,128)(2,1)} %get-tuple-element.128), channel_id=1, source_target_pairs={{0,1},{1,2},{2,3},{3,0},{4,5},{5,6},{6,7},{7,4},{8,9},{9,10},{10,1... | collective-permute-start | bytes 1179656 | tf_op jit(solution)/shard_map/ppermute | solution.py:848
  1245.9 34.9 %collective-permute-start.7 = (bf16[256,768]{1,0:T(8,128)(2,1)S(1)}, bf16[256,768]{1,0:T(8,128)(2,1)}, u32[]{:S(2)}, u32[]{:S(2)}) collective-permute-start(bf16[256,768]{1,0:T(8,128)(2,1)S(1)} %get-tuple-element.130), channel_id=1, source_target_pairs={{0,2},{1,3},{2,0},{3,1},{4,6},{5,7},{6,4},{7,5},{8,10},{9,11},{10,... | collective-permute-start | bytes 1179656 | tf_op jit(solution)/shard_map/ppermute | solution.py:848
  1250.3 30.5 %collective-permute-start.8 = (bf16[256,768]{1,0:T(8,128)(2,1)S(1)}, bf16[256,768]{1,0:T(8,128)(2,1)}, u32[]{:S(2)}, u32[]{:S(2)}) collective-permute-start(bf16[256,768]{1,0:T(8,128)(2,1)S(1)} %get-tuple-element.129), channel_id=1, source_target_pairs={{0,3},{1,0},{2,1},{3,2},{4,7},{5,4},{6,5},{7,6},{8,11},{9,8},{10,9... | collective-permute-start | bytes 1179656 | tf_op jit(solution)/shard_map/ppermute | solution.py:848
  (14 other events, 36.9 us)
Sparse Core Ops, SparseCore 0:
  11.4 93.0 all-gather.9
  114.8 78.9 all-gather.11
  202.2 100.3 all-gather.13
  304.3 138.4 all-gather.7
  751.4 80.3 reduce-scatter.4
  835.6 131.7 reduce-scatter.6
  971.3 74.8 reduce-scatter.10
  1049.7 92.3 reduce-scatter.8

commit v3 on v2

--- a/solution.py
+++ b/solution.py
@@ -584,6 +584,155 @@
     )(own_rows, *grad_rows, weights)
 
 
+def flip(index, bit):
+    return index + bit - 2 * bit * lax.rem(lax.div(index, bit), 2)
+
+
+def collect_kernel(
+    tp_count, dp_count, shard, gains, chunk, out, gains_out, chunk_out,
+    own_sem, ring_send, ring_recv, send, recv, gain_send, gain_recv, chunk_send, chunk_recv,
+):
+    my_dp = lax.axis_index("dp")
+    my_tp = lax.axis_index("tensor")
+    rows = shard.shape[0]
+    half = rows // 2
+    bits = [1 << b for b in reversed(range(dp_count.bit_length() - 1))]
+    orders = [bits, bits[:-1][::-1] + bits[-1:]]
+    steps = len(bits)
+
+    barrier = pltpu.get_barrier_semaphore()
+    for j in range(1, tp_count):
+        pl.semaphore_signal(
+            barrier, inc=1, device_id={"tensor": lax.rem(my_tp + j, tp_count)}, device_id_type=MESH
+        )
+    for j in range(1, dp_count):
+        pl.semaphore_signal(
+            barrier, inc=1, device_id={"dp": lax.rem(my_dp + j, dp_count)}, device_id_type=MESH
+        )
+    pl.semaphore_wait(barrier, tp_count + dp_count - 2)
+
+    home = out.at[my_tp, pl.ds(my_dp * rows, rows), :]
+    own = pltpu.make_async_copy(shard, home, own_sem.at[0])
+    own.start()
+    own_gain = pltpu.make_async_copy(gains, gains_out.at[my_dp], own_sem.at[1])
+    own_gain.start()
+
+    def across(j):
+        return pltpu.make_async_remote_copy(
+            src_ref=shard,
+            dst_ref=home,
+            send_sem=ring_send.at[j],
+            recv_sem=ring_recv.at[j],
+            device_id={"tensor": lax.rem(my_tp + j, tp_count)},
+            device_id_type=MESH,
+        )
+
+    def gain_copy(j):
+        return pltpu.make_async_remote_copy(
+            src_ref=gains,
+            dst_ref=gains_out.at[my_dp],
+            send_sem=gain_send.at[j],
+            recv_sem=gain_recv.at[j],
+            device_id={"dp": lax.rem(my_dp + j, dp_count)},
+            device_id_type=MESH,
+        )
+
+    onward = pltpu.make_async_remote_copy(
+        src_ref=chunk,
+        dst_ref=chunk_out,
+        send_sem=chunk_send,
+        recv_sem=chunk_recv,
+        device_id={"tensor": lax.rem(my_tp + 1, tp_count)},
+        device_id_type=MESH,
+    )
+
+    def within(j, s, k, m):
+        order = orders[s]
+        owner = my_dp
+        for b in range(k):
+            if m >> b & 1:
+                owner = flip(owner, order[b])
+        block = out.at[
+            lax.rem(my_tp - j + tp_count, tp_count), pl.ds(owner * rows + s * half, half), :
+        ]
+        at = (1 << k) - 1 + m
+        return pltpu.make_async_remote_copy(
+            src_ref=block,
+            dst_ref=block,
+            send_sem=send.at[j, s, at],
+            recv_sem=recv.at[j, s, at],
+            device_id={"dp": flip(my_dp, order[k])},
+            device_id_type=MESH,
+        )
+
+    for j in range(1, tp_count):
+        across(j).start()
+    for j in range(1, dp_count):
+        gain_copy(j).start()
+    onward.start()
+    own.wait()
+    for phase in range(tp_count + steps):
+        for k in reversed(range(steps + 1)):
+            j = phase - k
+            if not 0 <= j < tp_count:
+                continue
+            if k == 0:
+                if j > 0:
+                    across(j).wait_recv()
+            else:
+                for s in range(2):
+                    for m in range(1 << (k - 1)):
+                        within(j, s, k - 1, m).wait_recv()
+            if k < steps:
+                for s in range(2):
+                    for m in range(1 << k):
+                        within(j, s, k, m).start()
+    for j in range(tp_count):
+        if j > 0:
+            across(j).wait_send()
+        for s in range(2):
+            for k in range(steps):
+                for m in range(1 << k):
+                    within(j, s, k, m).wait_send()
+    own_gain.wait()
+    for j in range(1, dp_count):
+        gain_copy(j).wait()
+    onward.wait()
+
+
+def collect(shard, gains, chunk, tp_count, dp_count, collective_id):
+    rows, cols = shard.shape
+    dma = pltpu.SemaphoreType.DMA
+    vmem_spec = pl.BlockSpec(memory_space=pltpu.VMEM)
+    any_spec = pl.BlockSpec(memory_space=pl.ANY)
+    return pl.pallas_call(
+        functools.partial(collect_kernel, tp_count, dp_count),
+        out_shape=[
+            jax.ShapeDtypeStruct((tp_count, dp_count * rows, cols), shard.dtype),
+            jax.ShapeDtypeStruct((dp_count,) + gains.shape, gains.dtype),
+            jax.ShapeDtypeStruct(chunk.shape, chunk.dtype),
+        ],
+        in_specs=[vmem_spec, vmem_spec, any_spec],
+        out_specs=[any_spec] * 3,
+        scratch_shapes=[
+            dma((2,)),
+            dma((tp_count,)),
+            dma((tp_count,)),
+            dma((tp_count, 2, dp_count - 1)),
+            dma((tp_count, 2, dp_count - 1)),
+            dma((dp_count,)),
+            dma((dp_count,)),
+            dma,
+            dma,
+        ],
+        compiler_params=pltpu.CompilerParams(collective_id=collective_id, has_side_effects=True),
+        cost_estimate=pl.CostEstimate(
+            flops=0, bytes_accessed=16 * tp_count * dp_count * shard.size, transcendentals=0
+        ),
+        name="collect",
+    )(shard, gains, chunk)
+
+
 def spread_kernel(rows, weight, out):
     out[0] = dot_nn(rows[...], weight[0]).astype(out.dtype)
 
@@ -754,17 +903,18 @@
     per_group = q_cols // kv_cols
     group_q = per_group * HD
     groups = range(kv_heads)
-    qkv_shards = [
-        jnp.concatenate(
-            [
+    qkv_shard = jnp.concatenate(
+        [
+            part
+            for g in groups
+            for part in (
                 w_query[:, g * group_q : (g + 1) * group_q],
                 w_key[:, g * HD : (g + 1) * HD],
                 w_value[:, g * HD : (g + 1) * HD],
-            ],
-            axis=1,
-        )
-        for g in groups
-    ]
+            )
+        ],
+        axis=1,
+    )
 
     def gather_all(shard):
         full = lax.all_gather(shard, everyone, axis=0, tiled=False)
@@ -782,37 +932,36 @@
     def pass_on(value):
         return lax.ppermute(value, "tensor", ring_next)
 
-    gains = lax.all_gather(jnp.stack([attn_gain, mlp_gain]), "dp", axis=1, tiled=True)
-    gain_one, gain_two = gains[0].astype(f32), gains[1].astype(f32)
-
     grad_out = grad_top * valid_rows
     grad_chunks = [grad_out.astype(bf16)]
-    for _ in range(tp_count - 1):
+    mlp_shard = jnp.concatenate([w_gate, w_up, w_down.T], axis=1)
+    w_mlp = lax.all_gather(mlp_shard, "dp", axis=0, tiled=True)
+    w_qkv, gains, grad_chunk = collect(
+        qkv_shard, jnp.stack([attn_gain, mlp_gain]), grad_chunks[0], tp_count, dp_count, 1
+    )
+    grad_chunks.append(grad_chunk)
+    for _ in range(tp_count - 2):
         grad_chunks.append(pass_on(grad_chunks[-1]))
+    gains = gains.transpose(1, 0, 2).reshape(2, -1).astype(f32)
+    gain_one, gain_two = gains[0], gains[1]
 
     scale_one = rms_scale(hidden_in)
     normed_one = (hidden_in * scale_one * gain_one).astype(bf16)
-    w_qkv, qkv, slots = [], [], []
+    qkv, slots = [], []
     for g in groups:
-        if g == 0:
-            w_qkv.append(gather_all(qkv_shards[g]))
-            weight = after(w_qkv[g], grad_chunks[1])
-        else:
-            w_qkv.append(gather_all(after(qkv_shards[g], qkv[-1])))
-            weight = after(w_qkv[g], slots[-1])
-        qkv.append(spread(normed_one, weight, 0, group_q + 2 * HD))
+        qkv.append(spread(normed_one, w_qkv, g, group_q + 2 * HD))
         slots.append(trade(qkv[g]))
     out_shard = with_layout_constraint(w_out.T, Layout(major_to_minor=(0, 1)))
-    w_out_t = gather_all(after(out_shard, qkv[-1]))
-    mlp_shard = jnp.concatenate([w_gate, w_up, w_down.T], axis=1)
+    w_out_t = gather_all(after(out_shard, w_qkv))
     saved, mixed = [], []
     last = qkv[-1]
     for g in groups:
+        last = (last, grad_chunks[min(g + 1, tp_count - 1)])
+        if g == len(groups) - 1:
+            last = (last, w_mlp)
         q_t, k_t, k_rows, v_t, v_rows = prepare(
             after(slots[g], last), perm, cos_t, sin_t, per_group, 1
         )
-        if g == 0:
-            w_mlp = lax.all_gather(after(mlp_shard, q_t), "dp", axis=0, tiled=True)
         o_t, lse, last = attend_forward(
             q_t, k_rows, v_t, begin, first_block, perm, page_rows, block_len
         )
@@ -830,10 +979,11 @@
     grad_normed_two = grad_normed_two.astype(f32)
     grad_mid_norm, gain_two_part = norm_back(grad_normed_two, hidden_mid, scale_two, gain_two)
     grad_mid = grad_out + grad_mid_norm
-    branch_two = partial_two[1]
-    for s in range(2, tp_count):
-        branch_two = (pass_on(branch_two).astype(f32) + partial_two[s].astype(f32)).astype(bf16)
-    branch_two = pass_on(branch_two)
+
+    def add_on(arrived, s):
+        return (arrived.astype(f32) + partial_two[s].astype(f32)).astype(bf16)
+
+    branch_two = pass_on(partial_two[1])
 
     def reduce_dp(grad):
         return lax.psum_scatter(grad.astype(bf16), "dp", scatter_dimension=0, tiled=True)
@@ -855,7 +1005,7 @@
     sum_down = reduce_dp(grad_down_t)
     grad_gate_up = dot_tn(flat(mlp_rows), flat(after(grad_gate_up, grad_down_t))).astype(bf16)
     sum_gate_up = reduce_dp(grad_gate_up)
-    grad_z = after(grad_mid.astype(bf16), grad_gate_up)
+    grad_z = after(grad_mid.astype(bf16), (grad_gate_up, branch_two))
     grad_slots = [trade(spread(grad_z, w_out_t, g, group_q)) for g in groups]
     grad_qkv = []
     last = grad_z
@@ -867,7 +1017,10 @@
         )
         grad_qkv.append(trade_back(back))
         last = (back, sum_down)
-    grad_wout = outer(after(grad_z, back), jnp.concatenate(mixed, axis=2))
+    for s in range(2, tp_count - 1):
+        branch_two = pass_on(add_on(after(branch_two, grad_slots[-1]), s))
+    grad_wout = outer(after(grad_z, (back, branch_two)), jnp.concatenate(mixed, axis=2))
+    branch_two = pass_on(add_on(after(branch_two, grad_qkv[-1]), tp_count - 1))
     sum_out = reduce_dp(grad_wout)
     normed_late = after(normed_one, (sum_gate_up, grad_wout))
     hidden = sum_gate_up.shape[1] // 2
@@ -875,7 +1028,7 @@
     sum_qkv = reduce_tensor(reduce_dp(grad_wqkv))
     grad_normed_one = jnp.zeros((tok_dev, width), f32)
     for g in groups:
-        grad_normed_one = gather_sum(grad_qkv[g], w_qkv[g], 0, grad_normed_one)
+        grad_normed_one = gather_sum(grad_qkv[g], w_qkv, g, grad_normed_one)
     sum_out = reduce_tensor(sum_out)
     each = group_q + 2 * HD
     sum_qkv = [sum_qkv[:, g * each : (g + 1) * each] for g in groups]
@@ -885,9 +1038,13 @@
     grad_in_norm, gain_one_part = norm_back(grad_normed_one, hidden_in, scale_one, gain_one)
     grad_in = (grad_mid + grad_in_norm).astype(bf16)
 
-    gain_sums = lax.psum(jnp.stack([gain_one_part, gain_two_part]), everyone)
-    gain_shard = attn_gain.shape[0]
-    gain_sums = lax.dynamic_slice_in_dim(gain_sums, dp_index * gain_shard, gain_shard, 1)
+    gain_parts = jnp.stack([gain_one_part, gain_two_part]).reshape(2, dp_count, -1)
+    gain_parts = jnp.broadcast_to(
+        gain_parts.transpose(1, 0, 2)[None], (tp_count, dp_count, 2, gain_parts.shape[2])
+    ).reshape(group_pages, 2, -1)
+    gain_sums = jnp.sum(
+        lax.all_to_all(gain_parts, everyone, split_axis=0, concat_axis=0, tiled=True), axis=0
+    )
     return (
         reorder(result, dest_group),
         reorder(grad_in, dest_group),

time: 1310 us -> 1290 us (0.985)
  Pallas kernels: 524 us -> 631 us
  waiting for transfers between devices: 404 us -> 308 us
  blocking collectives: 138 us -> 89.8 us
    ppermute x6 -> x5, waiting for transfers between devices: 168 us -> 40.5 us  [pass_on(): return lax.ppermute(value, 'tensor', ring_next)]
    pallas_call x0 -> x1, Pallas kernels: none -> 119 us  [collect(): pl.pallas_call(functools.partial(collect_kernel, tp_count, dp_count), out...]
    psum x1 -> x0, blocking collectives: 41.8 us -> none  [local(): gain_sums = lax.psum(jnp.stack([gain_one_part, gain_two_part]), everyone)]
    all_to_all x6, waiting for transfers between devices: 186 us -> 227 us  [trade(): lax.all_to_all(blocks, everyone, split_axis=0, concat_axis=0, tiled=True)]
    all_gather x3 -> x1, waiting for transfers between devices: 24.7 us -> 0.01 us  [gather_all(): full = lax.all_gather(shard, everyone, axis=0, tiled=False)]
  transfers between devices with their start and end apart: 26 -> 24, of which waited for: 12 -> 11; matrix products, arithmetic and copies ran while one was open for 11% -> 11% of each run, Pallas kernels for 18% -> 28%
where the time goes in v3:
time: 1290 us; the launch traced here: 1270 us
  Pallas kernels  631 us (49%)
  waiting for transfers between devices  308 us (24%)
  blocking collectives  89.8 us (7%)
  other arithmetic  72.1 us (6%)
  matrix products  66.1 us (5%)
  starting transfers between devices  45.8 us (4%)
  local copies, waits for them, and re-layouts  39.3 us (3%)
  between operations  15.2 us (1%)
    pallas_call x1, Pallas kernels, feed(): pl.pallas_call(functools.partial(feed_kernel, ring, min(tile, hidden)), o...  278 us
    all_to_all x6, waiting for transfers between devices, trade(): lax.all_to_all(blocks, everyone, split_axis=0, concat_axis=0, tiled=True)  227 us
    pallas_call x1, Pallas kernels, collect(): pl.pallas_call(functools.partial(collect_kernel, tp_count, dp_count), out...  119 us
    all_to_all x2, blocking collectives, trade(): lax.all_to_all(blocks, everyone, split_axis=0, concat_axis=0, tiled=True)  89.8 us
    dot_general x2, matrix products, dot_tn(): lax.dot_general(left, right, (((0,), (0,)), ((), ())), preferred_element_...  66.1 us
    pallas_call x2, Pallas kernels, attend_backward(): pl.pallas_call(functools.partial(backward_kernel, q_heads, kv_heads, page...  62.3 us
    pallas_call x2, Pallas kernels, attend_forward(): pl.pallas_call(functools.partial(forward_kernel, q_heads, kv_heads, page_...  59.7 us
    pallas_call x4, Pallas kernels, gather_sum(): pl.pallas_call(gather_kernel, grid=(shards,), in_specs=[pl.BlockSpec((1,...  41 us
  transfers between devices with their start and end apart: 24, of which 11 were waited for; matrix products, arithmetic and copies ran while one was open for 11% of the time, Pallas kernels for 28%

profile of v3, /device:TPU:0, one launch (start us, length us, event | category | flops | bytes accessed | tf_op | source)
XLA Modules:
  0.0 1267.2 jit_solution(11588332218452099652)
XLA Ops:
  19.1 3.6 gather_fusion.2
  26.1 4.5 select_convert_fusion
  33.7 118.6 %collect.1 = (bf16[4,2048,768]{2,1,0:T(8,128)(2,1)}, bf16[8,2,256]{2,1,0:T(2,128)(2,1)}, bf16[512,2048]{1,0:T(8,128)(2,1)}) custom-call(bf16[256,768]{1,0:T(8,128)(2,1)} %concatenate.22.shard, bf16[2,256]{1,0:T(2,128)(2,1)} %pad_maximum_fusion.6.gains, bf16[512,2048]{1,0:T(8,128)(2,1)} %fusion.10.chunk.refs_0_), custom_call_target="tpu_custom_call" | custom-call | bytes 100663296 | tf_op jit(solution)/shard_map/collect/pallas_call | solution.py:708
  154.4 3.9 multiply_convert_fusion.1.rows
  158.3 8.2 spread.5
  166.6 5.5 all-to-all-start.1
  172.0 8.2 spread.4
  180.3 29.5 %all-to-all-done.1.refs_0_.refs_1_ = bf16[32,64,384]{2,1,0:T(8,128)(2,1)S(1)} async-done(((bf16[32,64,384]{2,1,0:T(8,128)(2,1)}), bf16[32,64,384]{2,1,0:T(8,128)(2,1)S(1)}, u32[]{:S(2)}, u32[]{:S(2)}) %all-to-all-start.1) | async-done | bytes 1572896 | tf_op jit(solution)/shard_map/all_to_all | solution.py:925
  209.8 3.8 all-to-all-start
  217.8 10.6 prepare.2
  228.4 29.8 %attend_forward.2 = (bf16[256,2048]{1,0:T(8,128)(2,1)}, f32[4,2048]{1,0:T(4,128)}, bf16[32,64,256]{2,1,0:T(8,128)(2,1)}) custom-call(s32[8]{0:T(128)} %get-tuple-element.172.first_block, s32[32]{0:T(128)} %fusion.13.perm, bf16[256,2048]{1,0:T(8,128)(2,1)} %get-tuple-element.53.q_t.refs_4_, bf16[1,2048,64]{2,1,0:T(8,128)(2,1)} %get-tuple-element.54.k_rows.refs_5_, ...), custom_call_target="tpu_custom_call" | custom-call | flops 1073741824 | bytes 4194304 | tf_op jit(solution)/shard_map/attend_forward/pallas_call | solution.py:163
  258.2 51.7 %all-to-all-done.refs_0_.refs_1_ = bf16[32,64,384]{2,1,0:T(8,128)(2,1)S(1)} async-done(((bf16[32,64,384]{2,1,0:T(8,128)(2,1)}), bf16[32,64,384]{2,1,0:T(8,128)(2,1)S(1)}, u32[]{:S(2)}, u32[]{:S(2)}) %all-to-all-start) | async-done | bytes 1572896 | tf_op jit(solution)/shard_map/all_to_all | solution.py:925
  312.6 10.6 prepare.3
  323.2 29.8 %attend_forward.3 = (bf16[256,2048]{1,0:T(8,128)(2,1)}, f32[4,2048]{1,0:T(4,128)}, bf16[32,64,256]{2,1,0:T(8,128)(2,1)}) custom-call(s32[8]{0:T(128)} %get-tuple-element.172.first_block, s32[32]{0:T(128)} %fusion.13.perm, bf16[256,2048]{1,0:T(8,128)(2,1)} %get-tuple-element.58.q_t.refs_4_, bf16[1,2048,64]{2,1,0:T(8,128)(2,1)} %get-tuple-element.59.k_rows.refs_5_, ...), custom_call_target="tpu_custom_call" | custom-call | flops 1073741824 | bytes 4194304 | tf_op jit(solution)/shard_map/attend_forward/pallas_call | solution.py:163
  356.0 6.7 all-to-all-start.2
  365.0 8.5 gather_sum.4.begin
  373.6 60.3 %all-to-all-done.2 = bf16[32,64,256]{2,1,0:T(8,128)(2,1)S(1)} async-done(((bf16[32,64,256]{2,1,0:T(8,128)(2,1)}), bf16[32,64,256]{2,1,0:T(8,128)(2,1)S(1)}, u32[]{:S(2)}, u32[]{:S(2)}) %all-to-all-start.2) | async-done | bytes 1048608 | tf_op jit(solution)/shard_map/all_to_all | solution.py:925
  434.8 8.5 gather_sum.5
  448.5 277.7 %feed_forward.1 = (bf16[4,512,2048]{2,1,0:T(8,128)(2,1)}, bf16[4,512,2048]{2,1,0:T(8,128)(2,1)}, bf16[4,512,2048]{2,1,0:T(8,128)(2,1)}, bf16[4,512,4096]{2,1,0:T...) custom-call(bf16[512,2048]{1,0:T(8,128)(2,1)} %multiply_convert_fusion.own_rows, ...), custom_call_target="tpu_custom_call" | custom-call | flops 103079215104 | bytes 33554432 | tf_op jit(solution)/shard_map/feed_forward/pallas_call | solution.py:542
  726.3 24.0 %bitcast_convert_fusion.1 = bf16[2048,2048]{1,0:T(8,128)(2,1)} fusion(bf16[4,512,2048]{2,1,0:T(8,128)(2,1)} %get-tuple-element.66, bf16[4,512,2048]{2,1,0:T(8,128)(2,1)} %get-tuple-element.67), kind=kOutput, calls=%fused_computation.8 | convolution fusion | flops 17184063488 | bytes 25165824 | tf_op jit(solution)/shard_map/dot_general | solution.py:33
  750.3 42.1 %bitcast_convert_fusion = bf16[2048,4096]{1,0:T(8,128)(2,1)} fusion(bf16[4,512,2048]{2,1,0:T(8,128)(2,1)} %get-tuple-element.64, bf16[4,512,4096]{2,1,0:T(8,128)(2,1)} %get-tuple-element.68), kind=kOutput, calls=%fused_computation.7 | convolution fusion | flops 34368126976 | bytes 41943040 | tf_op jit(solution)/shard_map/dot_general | solution.py:33
  801.8 40.5 %collective-permute-done.2 = bf16[512,2048]{1,0:T(8,128)(2,1)} collective-permute-done((bf16[512,2048]{1,0:T(8,128)(2,1)S(1)}, bf16[512,2048]{1,0:T(8,128)(2,1)}, u32[]{:S(2)}, u32[]{:S(2)}) %collective-permute-start.2) | collective-permute-done | bytes 2097184 | tf_op jit(solution)/shard_map/ppermute | solution.py:933
  842.3 7.0 spread.6
  852.2 6.3 spread.7
  858.6 19.9 %all-to-all-done.4.refs_0_.refs_1_.refs_2_.refs_3_ = bf16[32,64,256]{2,1,0:T(8,128)(2,1)S(1)} async-done(((bf16[32,64,256]{2,1,0:T(8,128)(2,1)}), bf16[32,64,256]{2,1,0:T(8,128)(2,1)S(1)}, u32[]{:S(2)}, u32[]{:S(2)}) %all-to-all-start.4) | async-done | bytes 1048608 | tf_op jit(solution)/shard_map/all_to_all | solution.py:925
  879.4 3.7 all-to-all-start.5
  883.2 4.7 fusion.9
  891.1 63.1 %all-to-all-done.5.refs_0_.refs_1_.refs_2_.refs_3_ = bf16[32,64,256]{2,1,0:T(8,128)(2,1)} async-done(((bf16[32,64,256]{2,1,0:T(8,128)(2,1)}), bf16[32,64,256]{2,1,0:T(8,128)(2,1)}, u32[]{:S(2)}, u32[]{:S(2)}) %all-to-all-start.5) | async-done | bytes 1048608 | tf_op jit(solution)/shard_map/all_to_all | solution.py:925
  954.3 31.3 %attend_backward.2 = bf16[32,64,384]{2,1,0:T(8,128)(2,1)} custom-call(s32[8]{0:T(128)} %get-tuple-element.172.first_block, s32[32]{0:T(128)} %fusion.13.perm, bf16[32,64,256]{2,1,0:T(8,128)(2,1)} %all-to-all-done.5.refs_0_.refs_1_.refs_2_.refs_3_, bf16[32,64,256]{2,1,0:T(8,128)(2,1)} %all-to-all-done.5.refs_0_.refs_1_.refs_2_.refs_3_, ...), custom_call_target="tpu_custom_call" | custom-call | flops 3221225472 | bytes 6291456 | tf_op jit(solution)/shard_map/attend_backward/pallas_call | solution.py:322
  985.6 31.1 %attend_backward.3 = bf16[32,64,384]{2,1,0:T(8,128)(2,1)} custom-call(s32[8]{0:T(128)} %get-tuple-element.172.first_block, s32[32]{0:T(128)} %fusion.13.perm, bf16[32,64,256]{2,1,0:T(8,128)(2,1)} %copy-done.15, bf16[32,64,256]{2,1,0:T(8,128)(2,1)} %copy-done.15, bf16[32,64,256]{2,1,0:T(8,128)(2,1)} %copy-done.15, bf16[32,64,256]{2,1,0:T(8,128)(2,1)} %copy-done.15, ...), custom_call_target="tpu_custom_call" | custom-call | flops 3221225472 | bytes 6291456 | tf_op jit(solution)/shard_map/attend_backward/pallas_call | solution.py:322
  1016.7 9.1 outer.2
  1025.9 48.9 %all_to_all.45 = bf16[32,64,384]{2,1,0:T(8,128)(2,1)S(1)} all-to-all(bf16[32,64,384]{2,1,0:T(8,128)(2,1)} %attend_backward.2), channel_id=1, replica_groups=mesh['dp'=8,'tensor'=4] {'tensor','dp'}, dimensions={0} | all-to-all | bytes 3145728 | tf_op jit(solution)/shard_map/all_to_all | solution.py:925
  1074.8 40.9 %all_to_all.46 = bf16[32,64,384]{2,1,0:T(8,128)(2,1)S(1)} all-to-all(bf16[32,64,384]{2,1,0:T(8,128)(2,1)S(1)} %copy-done.13), channel_id=1, replica_groups=mesh['dp'=8,'tensor'=4] {'tensor','dp'}, dimensions={0} | all-to-all | bytes 3145728 | tf_op jit(solution)/shard_map/all_to_all | solution.py:925
  1118.7 11.7 outer.3
  1131.2 4.4 fusion.8
  1136.9 3.2 broadcast_in_dim.57.begin
  1140.1 12.9 %gather_sum.6.begin = f32[512,2048]{1,0:T(8,128)} custom-call(bf16[4,512,384]{2,1,0:T(8,128)(2,1)} %bitcast.77, bf16[4,2048,768]{2,1,0:T(8,128)(2,1)} %get-tuple-element.50.weight, f32[512,2048]{1,0:T(8,128)} %broadcast_in_dim.57.begin), custom_call_target="tpu_custom_call" | custom-call | flops 3221225472 | bytes 6291456 | tf_op jit(solution)/shard_map/gather_sum/pallas_call | solution.py:772
  1157.4 11.1 gather_sum.7
  1168.5 4.9 multiply_reduce_fusion
  1174.0 4.1 all-to-all-start.8
  1178.1 9.2 all-to-all-done.8
  1188.0 10.2 add_convert_fusion
  1200.5 4.2 gather_fusion.4
  1205.9 4.0 broadcast_select_fusion
  1211.9 10.2 reduce-scatter.9.cloned.1.call-done
  1228.9 4.1 slice_convert_fusion
  1233.6 14.2 %collective-permute-done.9 = bf16[256,512]{1,0:T(8,128)(2,1)} collective-permute-done((bf16[256,512]{1,0:T(8,128)(2,1)S(1)}, bf16[256,512]{1,0:T(8,128)(2,1)}, u32[]{:S(2)}, u32[]{:S(2)}) %collective-permute-start.9) | collective-permute-done | bytes 262176 | tf_op jit(solution)/shard_map/ppermute | solution.py:998
  1250.2 6.0 collective-permute-done.6
  (183 shorter events, 84.9 us)
Async XLA Ops:
  7.2 305.4 %all-gather.4.cloned.1.call-start = ((), (), s32[]{:S(2)}) async-start(), calls=%async_computation.13 | async-start | bytes 28311552 | tf_op jit(solution)/shard_map/all_gather | solution.py:938
  11.8 353.2 %all-gather.6.cloned.1.call-start = ((), (), s32[]{:S(2)}) async-start(), calls=%async_computation.18 | async-start | bytes 8650752 | tf_op jit(solution)/shard_map/all_gather | solution.py:920
  12.7 10.0 copy-start.32
  16.7 6.8 copy-start.38
  16.7 6.8 copy-start.39
  16.7 6.8 copy-start.16
  16.7 7.7 copy-start.17
  16.8 7.7 copy-start.19
  16.8 7.7 copy-start.20
  23.5 7.0 copy-start.27
  153.1 13.4 %copy-start.29 = (f32[512]{0:T(512)}, f32[512]{0:T(512)S(1)}, u32[]{:S(2)}) copy-start(f32[512]{0:T(512)S(1)} %rsqrt.20) | copy-start | bytes 6148
  153.9 292.2 %copy-start.21 = (f32[1,8,256]{2,0,1:T(1,128)}, f32[1,8,256]{2,0,1:T(1,128)S(1)}, u32[]{:S(2)}) copy-start(f32[1,8,256]{2,0,1:T(1,128)S(1)} %get-tuple-element.159) | copy-start | bytes 24580
  166.6 43.2 %all-to-all-start.1 = ((bf16[32,64,384]{2,1,0:T(8,128)(2,1)}), bf16[32,64,384]{2,1,0:T(8,128)(2,1)S(1)}, u32[]{:S(2)}, u32[]{:S(2)}) async-start(bf16[32,64,384]{2,1,0:T(8,128)(2,1)} %bitcast.85), calls=%async_computation.1 | async-start | bytes 3145728 | tf_op jit(solution)/shard_map/all_to_all | solution.py:925
  172.0 43.4 %copy-start.31 = (s32[1,2048]{1,0:T(1,128)S(1)}, s32[1,2048]{1,0:T(1,128)}, u32[]{:S(2)}) copy-start(s32[1,2048]{1,0:T(1,128)} %param.19) | copy-start | bytes 24580
  209.8 8.1 copy-start.6
  209.8 100.2 %all-to-all-start = ((bf16[32,64,384]{2,1,0:T(8,128)(2,1)}), bf16[32,64,384]{2,1,0:T(8,128)(2,1)S(1)}, u32[]{:S(2)}, u32[]{:S(2)}) async-start(bf16[32,64,384]{2,1,0:T(8,128)(2,1)} %bitcast.84), calls=%async_computation | async-start | bytes 3145728 | tf_op jit(solution)/shard_map/all_to_all | solution.py:925
  213.5 99.0 %collective-permute-start = (bf16[512,2048]{1,0:T(8,128)(2,1)}, bf16[512,2048]{1,0:T(8,128)(2,1)}, u32[]{:S(2)}, u32[]{:S(2)}) collective-permute-start(bf16[512,2048]{1,0:T(8,128)(2,1)} %get-tuple-element.51.refs_1_), channel_id=1, source_target_pairs={{0,1},{1,2},{2,3},{3,0},{4,5},{5,6},{6,7},{7,4},{8,9},{9,10},{10,1... | collective-permute-start | bytes 6291464 | tf_op jit(solution)/shard_map/ppermute | solution.py:933
  309.9 46.1 %all-to-all-start.3 = ((bf16[32,64,256]{2,1,0:T(8,128)(2,1)}), bf16[32,64,256]{2,1,0:T(8,128)(2,1)S(1)}, u32[]{:S(2)}, u32[]{:S(2)}) async-start(bf16[32,64,256]{2,1,0:T(8,128)(2,1)} %get-tuple-element.56), calls=%async_computation.3 | async-start | bytes 2097152 | tf_op jit(solution)/shard_map/all_to_all | solution.py:925
  356.0 9.0 copy-start.9
  356.0 77.9 %all-to-all-start.2 = ((bf16[32,64,256]{2,1,0:T(8,128)(2,1)}), bf16[32,64,256]{2,1,0:T(8,128)(2,1)S(1)}, u32[]{:S(2)}, u32[]{:S(2)}) async-start(bf16[32,64,256]{2,1,0:T(8,128)(2,1)} %get-tuple-element.61), calls=%async_computation.2 | async-start | bytes 2097152 | tf_op jit(solution)/shard_map/all_to_all | solution.py:925
  362.7 622.9 %reduce-scatter.5.cloned.1.call-start = ((), (), s32[]{:S(2)}) async-start(), calls=%async_computation.14 | async-start | bytes 9437184 | tf_op jit(solution)/shard_map/reduce_scatter | solution.py:989
  362.7 85.8 %collective-permute-start.1 = (bf16[512,2048]{1,0:T(8,128)(2,1)}, bf16[512,2048]{1,0:T(8,128)(2,1)}, u32[]{:S(2)}, u32[]{:S(2)}) collective-permute-start(bf16[512,2048]{1,0:T(8,128)(2,1)} %collective-permute-done.refs_2_), channel_id=1, source_target_pairs={{0,1},{1,2},{2,3},{3,0},{4,5},{5,6},{6,7},{7,4},{8,9},{9,10},{10,1... | collective-permute-start | bytes 6291464 | tf_op jit(solution)/shard_map/ppermute | solution.py:933
  750.3 368.5 %reduce-scatter.7.cloned.1.call-start = ((), (), s32[]{:S(2)}) async-start(), calls=%async_computation.15 | async-start | bytes 18874368 | tf_op jit(solution)/shard_map/reduce_scatter | solution.py:989
  794.4 4.5 copy-start.3
  794.5 4.5 copy-start.4
  794.5 4.5 copy-start.28
  794.5 47.9 %collective-permute-start.2 = (bf16[512,2048]{1,0:T(8,128)(2,1)S(1)}, bf16[512,2048]{1,0:T(8,128)(2,1)}, u32[]{:S(2)}, u32[]{:S(2)}) collective-permute-start(bf16[512,2048]{1,0:T(8,128)(2,1)S(1)} %slice_bitcast_fusion), channel_id=1, source_target_pairs={{0,1},{1,2},{2,3},{3,0},{4,5},{5,6},{6,7},{7,4},{8,9},{9,10},{10,1... | collective-permute-start | bytes 6291464 | tf_op jit(solution)/shard_map/ppermute | solution.py:933
  849.4 29.1 %all-to-all-start.4 = ((bf16[32,64,256]{2,1,0:T(8,128)(2,1)}), bf16[32,64,256]{2,1,0:T(8,128)(2,1)S(1)}, u32[]{:S(2)}, u32[]{:S(2)}) async-start(bf16[32,64,256]{2,1,0:T(8,128)(2,1)} %bitcast.88), calls=%async_computation.4 | async-start | bytes 2097152 | tf_op jit(solution)/shard_map/all_to_all | solution.py:925
  879.4 10.2 copy-start.10
  879.4 74.8 %all-to-all-start.5 = ((bf16[32,64,256]{2,1,0:T(8,128)(2,1)}), bf16[32,64,256]{2,1,0:T(8,128)(2,1)}, u32[]{:S(2)}, u32[]{:S(2)}) async-start(bf16[32,64,256]{2,1,0:T(8,128)(2,1)} %bitcast.87), calls=%async_computation.5 | async-start | bytes 2097152 | tf_op jit(solution)/shard_map/all_to_all | solution.py:925
  883.1 321.5 %reduce-scatter.11.cloned.1.call-start = ((), (), s32[]{:S(2)}) async-start(), calls=%async_computation.17 | async-start | bytes 9437184 | tf_op jit(solution)/shard_map/reduce_scatter | solution.py:989
  883.2 6.5 copy-start.12
  887.9 128.7 %collective-permute-start.3 = (bf16[512,2048]{1,0:T(8,128)(2,1)}, bf16[512,2048]{1,0:T(8,128)(2,1)}, u32[]{:S(2)}, u32[]{:S(2)}) collective-permute-start(bf16[512,2048]{1,0:T(8,128)(2,1)} %fusion.9), channel_id=1, source_target_pairs={{0,1},{1,2},{2,3},{3,0},{4,5},{5,6},{6,7},{7,4},{8,9},{9,10},{10,1... | collective-permute-start | bytes 6291464 | tf_op jit(solution)/shard_map/ppermute | solution.py:933
  1025.8 196.3 %reduce-scatter.9.cloned.1.call-start = ((), (), s32[]{:S(2)}) async-start(), calls=%async_computation.16 | async-start | bytes 14155776 | tf_op jit(solution)/shard_map/reduce_scatter | solution.py:989
  1025.9 48.9 %copy-start.13 = (bf16[32,64,384]{2,1,0:T(8,128)(2,1)S(1)}, bf16[32,64,384]{2,1,0:T(8,128)(2,1)}, u32[]{:S(2)}) copy-start(bf16[32,64,384]{2,1,0:T(8,128)(2,1)} %attend_backward.3) | copy-start | bytes 4718596
  1074.8 40.9 %copy-start.8 = (bf16[32,64,384]{2,1,0:T(8,128)(2,1)}, bf16[32,64,384]{2,1,0:T(8,128)(2,1)S(1)}, u32[]{:S(2)}) copy-start(bf16[32,64,384]{2,1,0:T(8,128)(2,1)S(1)} %all_to_all.45) | copy-start | bytes 4718596
  1135.6 52.4 %collective-permute-start.4 = (bf16[512,2048]{1,0:T(8,128)(2,1)}, bf16[512,2048]{1,0:T(8,128)(2,1)}, u32[]{:S(2)}, u32[]{:S(2)}) collective-permute-start(bf16[512,2048]{1,0:T(8,128)(2,1)} %fusion.8), channel_id=1, source_target_pairs={{0,1},{1,2},{2,3},{3,0},{4,5},{5,6},{6,7},{7,4},{8,9},{9,10},{10,1... | collective-permute-start | bytes 6291464 | tf_op jit(solution)/shard_map/ppermute | solution.py:933
  1140.1 12.9 %copy-start.14 = (bf16[256,2048]{1,0:T(8,128)(2,1)S(1)}, bf16[256,2048]{1,0:T(8,128)(2,1)}, u32[]{:S(2)}) copy-start(bf16[256,2048]{1,0:T(8,128)(2,1)} %reduce-scatter.5.cloned.1.call-done) | copy-start | bytes 3145732
  1157.4 11.1 copy-start.24
  1157.4 11.1 copy-start.30
  1174.0 13.4 %all-to-all-start.8 = ((f32[32,2,256]{2,1,0:T(2,128)}), f32[32,2,256]{2,1,0:T(2,128)S(1)}, u32[]{:S(2)}, u32[]{:S(2)}) async-start(f32[32,2,256]{2,1,0:T(2,128)} %bitcast.36), calls=%async_computation.9 | async-start | bytes 131072 | tf_op jit(solution)/shard_map/all_to_all | solution.py:1046
  1198.2 7.7 copy-start.33
  1205.8 21.6 %collective-permute-start.10 = (bf16[256,512]{1,0:T(8,128)(2,1)S(1)}, bf16[256,512]{1,0:T(8,128)(2,1)}, u32[]{:S(2)}, u32[]{:S(2)}) collective-permute-start(bf16[256,512]{1,0:T(8,128)(2,1)S(1)} %get-tuple-element.145), channel_id=1, source_target_pairs={{0,3},{1,0},{2,1},{3,2},{4,7},{5,4},{6,5},{7,6},{8,11},{9,8},{10,9... | collective-permute-start | bytes 786440 | tf_op jit(solution)/shard_map/ppermute | solution.py:998
  1209.9 23.0 %collective-permute-start.8 = (bf16[256,512]{1,0:T(8,128)(2,1)S(1)}, bf16[256,512]{1,0:T(8,128)(2,1)S(1)}, u32[]{:S(2)}, u32[]{:S(2)}) collective-permute-start(bf16[256,512]{1,0:T(8,128)(2,1)S(1)} %get-tuple-element.144), channel_id=1, source_target_pairs={{0,1},{1,2},{2,3},{3,0},{4,5},{5,6},{6,7},{7,4},{8,9},{9,10},{10,1... | collective-permute-start | bytes 786440 | tf_op jit(solution)/shard_map/ppermute | solution.py:998
  1211.9 35.9 %collective-permute-start.9 = (bf16[256,512]{1,0:T(8,128)(2,1)S(1)}, bf16[256,512]{1,0:T(8,128)(2,1)}, u32[]{:S(2)}, u32[]{:S(2)}) collective-permute-start(bf16[256,512]{1,0:T(8,128)(2,1)S(1)} %get-tuple-element.146), channel_id=1, source_target_pairs={{0,2},{1,3},{2,0},{3,1},{4,6},{5,7},{6,4},{7,5},{8,10},{9,11},{10,... | collective-permute-start | bytes 786440 | tf_op jit(solution)/shard_map/ppermute | solution.py:998
  1223.5 26.7 %collective-permute-start.5 = (bf16[256,768]{1,0:T(8,128)(2,1)S(1)}, bf16[256,768]{1,0:T(8,128)(2,1)S(1)}, u32[]{:S(2)}, u32[]{:S(2)}) collective-permute-start(bf16[256,768]{1,0:T(8,128)(2,1)S(1)} %get-tuple-element.141), channel_id=1, source_target_pairs={{0,1},{1,2},{2,3},{3,0},{4,5},{5,6},{6,7},{7,4},{8,9},{9,10},{10,1... | collective-permute-start | bytes 1179656 | tf_op jit(solution)/shard_map/ppermute | solution.py:998
  1225.0 31.2 %collective-permute-start.6 = (bf16[256,768]{1,0:T(8,128)(2,1)S(1)}, bf16[256,768]{1,0:T(8,128)(2,1)S(1)}, u32[]{:S(2)}, u32[]{:S(2)}) collective-permute-start(bf16[256,768]{1,0:T(8,128)(2,1)S(1)} %get-tuple-element.143), channel_id=1, source_target_pairs={{0,2},{1,3},{2,0},{3,1},{4,6},{5,7},{6,4},{7,5},{8,10},{9,11},{10,... | collective-permute-start | bytes 1179656 | tf_op jit(solution)/shard_map/ppermute | solution.py:998
  1227.4 28.8 %collective-permute-start.7 = (bf16[256,768]{1,0:T(8,128)(2,1)S(1)}, bf16[256,768]{1,0:T(8,128)(2,1)S(1)}, u32[]{:S(2)}, u32[]{:S(2)}) collective-permute-start(bf16[256,768]{1,0:T(8,128)(2,1)S(1)} %get-tuple-element.142), channel_id=1, source_target_pairs={{0,3},{1,0},{2,1},{3,2},{4,7},{5,4},{6,5},{7,6},{8,11},{9,8},{10,9... | collective-permute-start | bytes 1179656 | tf_op jit(solution)/shard_map/ppermute | solution.py:998
  (16 other events, 35.4 us)
Sparse Core Ops, SparseCore 0:
  11.9 185.7 all-gather.3
  200.6 154.7 all-gather.5
  750.4 70.8 reduce-scatter.4
  825.1 132.4 reduce-scatter.6
  1025.9 95.9 reduce-scatter.10
  1130.6 91.4 reduce-scatter.8

commit v4 on v3

--- a/solution.py
+++ b/solution.py
@@ -589,7 +589,7 @@
 
 
 def collect_kernel(
-    tp_count, dp_count, shard, gains, chunk, out, gains_out, chunk_out,
+    tp_count, dp_count, hops, shard, gains, chunk, out, gains_out, chunks_out,
     own_sem, ring_send, ring_recv, send, recv, gain_send, gain_recv, chunk_send, chunk_recv,
 ):
     my_dp = lax.axis_index("dp")
@@ -637,14 +637,15 @@
             device_id_type=MESH,
         )
 
-    onward = pltpu.make_async_remote_copy(
-        src_ref=chunk,
-        dst_ref=chunk_out,
-        send_sem=chunk_send,
-        recv_sem=chunk_recv,
-        device_id={"tensor": lax.rem(my_tp + 1, tp_count)},
-        device_id_type=MESH,
-    )
+    def onward(hop):
+        return pltpu.make_async_remote_copy(
+            src_ref=chunk if hop == 0 else chunks_out.at[hop - 1],
+            dst_ref=chunks_out.at[hop],
+            send_sem=chunk_send.at[hop],
+            recv_sem=chunk_recv.at[hop],
+            device_id={"tensor": lax.rem(my_tp + 1, tp_count)},
+            device_id_type=MESH,
+        )
 
     def within(j, s, k, m):
         order = orders[s]
@@ -669,7 +670,7 @@
         across(j).start()
     for j in range(1, dp_count):
         gain_copy(j).start()
-    onward.start()
+    onward(0).start()
     own.wait()
     for phase in range(tp_count + steps):
         for k in reversed(range(steps + 1)):
@@ -687,6 +688,9 @@
                 for s in range(2):
                     for m in range(1 << k):
                         within(j, s, k, m).start()
+        if tp_count <= phase < tp_count + hops - 1:
+            onward(phase - tp_count).wait_recv()
+            onward(phase - tp_count + 1).start()
     for j in range(tp_count):
         if j > 0:
             across(j).wait_send()
@@ -697,20 +701,23 @@
     own_gain.wait()
     for j in range(1, dp_count):
         gain_copy(j).wait()
-    onward.wait()
-
-
-def collect(shard, gains, chunk, tp_count, dp_count, collective_id):
+    for hop in range(hops):
+        if hop == hops - 1:
+            onward(hop).wait_recv()
+        onward(hop).wait_send()
+
+
+def collect(shard, gains, chunk, tp_count, dp_count, hops, collective_id):
     rows, cols = shard.shape
     dma = pltpu.SemaphoreType.DMA
     vmem_spec = pl.BlockSpec(memory_space=pltpu.VMEM)
     any_spec = pl.BlockSpec(memory_space=pl.ANY)
     return pl.pallas_call(
-        functools.partial(collect_kernel, tp_count, dp_count),
+        functools.partial(collect_kernel, tp_count, dp_count, hops),
         out_shape=[
             jax.ShapeDtypeStruct((tp_count, dp_count * rows, cols), shard.dtype),
             jax.ShapeDtypeStruct((dp_count,) + gains.shape, gains.dtype),
-            jax.ShapeDtypeStruct(chunk.shape, chunk.dtype),
+            jax.ShapeDtypeStruct((hops,) + chunk.shape, chunk.dtype),
         ],
         in_specs=[vmem_spec, vmem_spec, any_spec],
         out_specs=[any_spec] * 3,
@@ -722,8 +729,8 @@
             dma((tp_count, 2, dp_count - 1)),
             dma((dp_count,)),
             dma((dp_count,)),
-            dma,
-            dma,
+            dma((hops,)),
+            dma((hops,)),
         ],
         compiler_params=pltpu.CompilerParams(collective_id=collective_id, has_side_effects=True),
         cost_estimate=pl.CostEstimate(
@@ -936,12 +943,11 @@
     grad_chunks = [grad_out.astype(bf16)]
     mlp_shard = jnp.concatenate([w_gate, w_up, w_down.T], axis=1)
     w_mlp = lax.all_gather(mlp_shard, "dp", axis=0, tiled=True)
-    w_qkv, gains, grad_chunk = collect(
-        qkv_shard, jnp.stack([attn_gain, mlp_gain]), grad_chunks[0], tp_count, dp_count, 1
+    hops = min(2, tp_count - 1)
+    w_qkv, gains, got_chunks = collect(
+        qkv_shard, jnp.stack([attn_gain, mlp_gain]), grad_chunks[0], tp_count, dp_count, hops, 1
     )
-    grad_chunks.append(grad_chunk)
-    for _ in range(tp_count - 2):
-        grad_chunks.append(pass_on(grad_chunks[-1]))
+    grad_chunks += [got_chunks[hop] for hop in range(hops)]
     gains = gains.transpose(1, 0, 2).reshape(2, -1).astype(f32)
     gain_one, gain_two = gains[0], gains[1]
 
@@ -955,8 +961,9 @@
     w_out_t = gather_all(after(out_shard, w_qkv))
     saved, mixed = [], []
     last = qkv[-1]
+    for hop in range(hops + 1, tp_count):
+        grad_chunks.append(pass_on(after(grad_chunks[-1], slots[-1])))
     for g in groups:
-        last = (last, grad_chunks[min(g + 1, tp_count - 1)])
         if g == len(groups) - 1:
             last = (last, w_mlp)
         q_t, k_t, k_rows, v_t, v_rows = prepare(
@@ -982,8 +989,6 @@
 
     def add_on(arrived, s):
         return (arrived.astype(f32) + partial_two[s].astype(f32)).astype(bf16)
-
-    branch_two = pass_on(partial_two[1])
 
     def reduce_dp(grad):
         return lax.psum_scatter(grad.astype(bf16), "dp", scatter_dimension=0, tiled=True)
@@ -1005,7 +1010,7 @@
     sum_down = reduce_dp(grad_down_t)
     grad_gate_up = dot_tn(flat(mlp_rows), flat(after(grad_gate_up, grad_down_t))).astype(bf16)
     sum_gate_up = reduce_dp(grad_gate_up)
-    grad_z = after(grad_mid.astype(bf16), (grad_gate_up, branch_two))
+    grad_z = after(grad_mid.astype(bf16), grad_gate_up)
     grad_slots = [trade(spread(grad_z, w_out_t, g, group_q)) for g in groups]
     grad_qkv = []
     last = grad_z
@@ -1017,10 +1022,10 @@
         )
         grad_qkv.append(trade_back(back))
         last = (back, sum_down)
-    for s in range(2, tp_count - 1):
-        branch_two = pass_on(add_on(after(branch_two, grad_slots[-1]), s))
+    branch_two = pass_on(after(partial_two[1], grad_slots[-1]))
     grad_wout = outer(after(grad_z, (back, branch_two)), jnp.concatenate(mixed, axis=2))
-    branch_two = pass_on(add_on(after(branch_two, grad_qkv[-1]), tp_count - 1))
+    for s in range(2, tp_count):
+        branch_two = pass_on(add_on(after(branch_two, grad_qkv[-1]), s))
     sum_out = reduce_dp(grad_wout)
     normed_late = after(normed_one, (sum_gate_up, grad_wout))
     hidden = sum_gate_up.shape[1] // 2

time: 1290 us -> 1300 us (level)
  Pallas kernels: 631 us -> 661 us
  waiting for transfers between devices: 308 us -> 286 us
    all_to_all x6, waiting for transfers between devices: 227 us -> 195 us  [trade(): lax.all_to_all(blocks, everyone, split_axis=0, concat_axis=0, tiled=True)]
    pallas_call x1, Pallas kernels: 119 us -> 138 us  [collect(): pl.pallas_call(functools.partial(collect_kernel, tp_count, dp_count, hops...]
    ppermute x5 -> x4, waiting for transfers between devices: 40.5 us -> 48.2 us  [pass_on(): return lax.ppermute(value, 'tensor', ring_next)]
  transfers between devices with their start and end apart: 24 -> 23, of which waited for: 11 -> 10; matrix products, arithmetic and copies ran while one was open for 11% -> 11% of each run, Pallas kernels for 28% -> 30%
where the time goes in v4:
time: 1300 us; the launch traced here: 1280 us
  Pallas kernels  661 us (51%)
  waiting for transfers between devices  286 us (22%)
  blocking collectives  83.1 us (6%)
  other arithmetic  73.6 us (6%)
  matrix products  66 us (5%)
  starting transfers between devices  51.3 us (4%)
  local copies, waits for them, and re-layouts  44.9 us (3%)
  between operations  15.2 us (1%)
    pallas_call x1, Pallas kernels, feed(): pl.pallas_call(functools.partial(feed_kernel, ring, min(tile, hidden)), o...  278 us
    all_to_all x6, waiting for transfers between devices, trade(): lax.all_to_all(blocks, everyone, split_axis=0, concat_axis=0, tiled=True)  195 us
    pallas_call x1, Pallas kernels, collect(): pl.pallas_call(functools.partial(collect_kernel, tp_count, dp_count, hops...  138 us
    all_to_all x2, blocking collectives, trade(): lax.all_to_all(blocks, everyone, split_axis=0, concat_axis=0, tiled=True)  83.1 us
    pallas_call x2, Pallas kernels, attend_backward(): pl.pallas_call(functools.partial(backward_kernel, q_heads, kv_heads, page...  69.1 us
    pallas_call x2, Pallas kernels, attend_forward(): pl.pallas_call(functools.partial(forward_kernel, q_heads, kv_heads, page_...  66.6 us
    dot_general x2, matrix products, dot_tn(): lax.dot_general(left, right, (((0,), (0,)), ((), ())), preferred_element_...  66 us
    ppermute x4, waiting for transfers between devices, pass_on(): return lax.ppermute(value, 'tensor', ring_next)  48.2 us
  transfers between devices with their start and end apart: 23, of which 10 were waited for; matrix products, arithmetic and copies ran while one was open for 11% of the time, Pallas kernels for 30%

profile of v4, /device:TPU:0, one launch (start us, length us, event | category | flops | bytes accessed | tf_op | source)
XLA Modules:
  0.0 1281.0 jit_solution(12000215898967106508)
XLA Ops:
  26.0 4.5 select_convert_fusion
  33.5 138.2 %collect.1 = (bf16[4,2048,768]{2,1,0:T(8,128)(2,1)}, bf16[8,2,256]{2,1,0:T(2,128)(2,1)}, bf16[2,512,2048]{2,1,0:T(8,128)(2,1)}) custom-call(bf16[256,768]{1,0:T(8,128)(2,1)} %concatenate.22.shard, bf16[2,256]{1,0:T(2,128)(2,1)} %pad_maximum_fusion.6.gains, bf16[512,2048]{1,0:T(8,128)(2,1)} %fusion.10.chunk.refs_0_), custom_call_target="tpu_custom_call" | custom-call | bytes 100663296 | tf_op jit(solution)/shard_map/collect/pallas_call | solution.py:715
  173.9 3.9 multiply_convert_fusion.1.rows
  177.8 8.2 spread.5
  186.1 9.8 all-to-all-start.1
  195.8 8.2 spread.4
  204.1 45.3 %all-to-all-done.1.refs_0_.refs_1_ = bf16[32,64,384]{2,1,0:T(8,128)(2,1)S(1)} async-done(((bf16[32,64,384]{2,1,0:T(8,128)(2,1)}), bf16[32,64,384]{2,1,0:T(8,128)(2,1)S(1)}, u32[]{:S(2)}, u32[]{:S(2)}) %all-to-all-start.1) | async-done | bytes 1572896 | tf_op jit(solution)/shard_map/all_to_all | solution.py:932
  255.2 10.5 prepare.2
  265.7 33.3 %attend_forward.2 = (bf16[256,2048]{1,0:T(8,128)(2,1)}, f32[4,2048]{1,0:T(4,128)}, bf16[32,64,256]{2,1,0:T(8,128)(2,1)}) custom-call(s32[8]{0:T(128)} %get-tuple-element.178.first_block, s32[32]{0:T(128)} %fusion.13.perm, bf16[256,2048]{1,0:T(8,128)(2,1)} %get-tuple-element.54.q_t.refs_4_, bf16[1,2048,64]{2,1,0:T(8,128)(2,1)} %get-tuple-element.55.k_rows.refs_5_, ...), custom_call_target="tpu_custom_call" | custom-call | flops 1073741824 | bytes 4194304 | tf_op jit(solution)/shard_map/attend_forward/pallas_call | solution.py:163
  299.0 9.8 all-to-all-done.refs_0_.refs_1_
  312.4 10.6 prepare.3
  323.0 33.3 %attend_forward.3 = (bf16[256,2048]{1,0:T(8,128)(2,1)}, f32[4,2048]{1,0:T(4,128)}, bf16[32,64,256]{2,1,0:T(8,128)(2,1)}) custom-call(s32[8]{0:T(128)} %get-tuple-element.178.first_block, s32[32]{0:T(128)} %fusion.13.perm, bf16[256,2048]{1,0:T(8,128)(2,1)} %get-tuple-element.59.q_t.refs_4_, bf16[1,2048,64]{2,1,0:T(8,128)(2,1)} %get-tuple-element.60.k_rows.refs_5_, ...), custom_call_target="tpu_custom_call" | custom-call | flops 1073741824 | bytes 4194304 | tf_op jit(solution)/shard_map/attend_forward/pallas_call | solution.py:163
  356.4 6.1 all-to-all-start.2
  362.5 4.8 slice_bitcast_fusion.1
  369.5 8.5 gather_sum.4.begin
  378.1 55.6 %all-to-all-done.2 = bf16[32,64,256]{2,1,0:T(8,128)(2,1)S(1)} async-done(((bf16[32,64,256]{2,1,0:T(8,128)(2,1)}), bf16[32,64,256]{2,1,0:T(8,128)(2,1)S(1)}, u32[]{:S(2)}, u32[]{:S(2)}) %all-to-all-start.2) | async-done | bytes 1048608 | tf_op jit(solution)/shard_map/all_to_all | solution.py:932
  434.6 8.5 gather_sum.5
  449.6 277.7 %feed_forward.1 = (bf16[4,512,2048]{2,1,0:T(8,128)(2,1)}, bf16[4,512,2048]{2,1,0:T(8,128)(2,1)}, bf16[4,512,2048]{2,1,0:T(8,128)(2,1)}, bf16[4,512,4096]{2,1,0:T...) custom-call(bf16[512,2048]{1,0:T(8,128)(2,1)} %multiply_convert_fusion.own_rows, ...), custom_call_target="tpu_custom_call" | custom-call | flops 103079215104 | bytes 33554432 | tf_op jit(solution)/shard_map/feed_forward/pallas_call | solution.py:542
  727.4 24.0 %bitcast_convert_fusion.1 = bf16[2048,2048]{1,0:T(8,128)(2,1)} fusion(bf16[4,512,2048]{2,1,0:T(8,128)(2,1)} %get-tuple-element.69, bf16[4,512,2048]{2,1,0:T(8,128)(2,1)} %get-tuple-element.70), kind=kOutput, calls=%fused_computation.8 | convolution fusion | flops 17184063488 | bytes 25165824 | tf_op jit(solution)/shard_map/dot_general | solution.py:33
  751.4 42.0 %bitcast_convert_fusion = bf16[2048,4096]{1,0:T(8,128)(2,1)} fusion(bf16[4,512,2048]{2,1,0:T(8,128)(2,1)} %get-tuple-element.67, bf16[4,512,4096]{2,1,0:T(8,128)(2,1)} %get-tuple-element.71), kind=kOutput, calls=%fused_computation.7 | convolution fusion | flops 34368126976 | bytes 41943040 | tf_op jit(solution)/shard_map/dot_general | solution.py:33
  794.2 4.4 fusion.5
  798.6 3.9 fusion.20.rows
  802.6 6.2 spread.6
  808.8 4.8 all-to-all-start.4
  813.5 6.2 spread.7
  819.8 19.9 %all-to-all-done.4.refs_0_.refs_1_.refs_2_.refs_3_ = bf16[32,64,256]{2,1,0:T(8,128)(2,1)} async-done(((bf16[32,64,256]{2,1,0:T(8,128)(2,1)}), bf16[32,64,256]{2,1,0:T(8,128)(2,1)}, u32[]{:S(2)}, u32[]{:S(2)}) %all-to-all-start.4) | async-done | bytes 1048608 | tf_op jit(solution)/shard_map/all_to_all | solution.py:932
  839.7 3.8 all-to-all-start.5
  850.4 64.2 %all-to-all-done.5.refs_0_.refs_1_.refs_2_.refs_3_ = bf16[32,64,256]{2,1,0:T(8,128)(2,1)} async-done(((bf16[32,64,256]{2,1,0:T(8,128)(2,1)}), bf16[32,64,256]{2,1,0:T(8,128)(2,1)}, u32[]{:S(2)}, u32[]{:S(2)}) %all-to-all-start.5) | async-done | bytes 1048608 | tf_op jit(solution)/shard_map/all_to_all | solution.py:932
  914.7 34.6 %attend_backward.2 = bf16[32,64,384]{2,1,0:T(8,128)(2,1)} custom-call(s32[8]{0:T(128)} %get-tuple-element.178.first_block, s32[32]{0:T(128)} %fusion.13.perm, bf16[32,64,256]{2,1,0:T(8,128)(2,1)} %all-to-all-done.5.refs_0_.refs_1_.refs_2_.refs_3_, bf16[32,64,256]{2,1,0:T(8,128)(2,1)} %all-to-all-done.5.refs_0_.refs_1_.refs_2_.refs_3_, ...), custom_call_target="tpu_custom_call" | custom-call | flops 3221225472 | bytes 6291456 | tf_op jit(solution)/shard_map/attend_backward/pallas_call | solution.py:322
  949.3 34.5 %attend_backward.3 = bf16[32,64,384]{2,1,0:T(8,128)(2,1)} custom-call(s32[8]{0:T(128)} %get-tuple-element.178.first_block, s32[32]{0:T(128)} %fusion.13.perm, bf16[32,64,256]{2,1,0:T(8,128)(2,1)} %all-to-all-done.4.refs_0_.refs_1_.refs_2_.refs_3_, bf16[32,64,256]{2,1,0:T(8,128)(2,1)} %all-to-all-done.4.refs_0_.refs_1_.refs_2_.refs_3_, ...), custom_call_target="tpu_custom_call" | custom-call | flops 3221225472 | bytes 6291456 | tf_op jit(solution)/shard_map/attend_backward/pallas_call | solution.py:322
  983.8 9.2 outer.2
  993.1 42.2 %all_to_all.45 = bf16[32,64,384]{2,1,0:T(8,128)(2,1)S(1)} all-to-all(bf16[32,64,384]{2,1,0:T(8,128)(2,1)} %attend_backward.2), channel_id=1, replica_groups=mesh['dp'=8,'tensor'=4] {'tensor','dp'}, dimensions={0} | all-to-all | bytes 3145728 | tf_op jit(solution)/shard_map/all_to_all | solution.py:932
  1035.4 40.9 %all_to_all.46 = bf16[32,64,384]{2,1,0:T(8,128)(2,1)S(1)} all-to-all(bf16[32,64,384]{2,1,0:T(8,128)(2,1)S(1)} %copy-done.12), channel_id=1, replica_groups=mesh['dp'=8,'tensor'=4] {'tensor','dp'}, dimensions={0} | all-to-all | bytes 3145728 | tf_op jit(solution)/shard_map/all_to_all | solution.py:932
  1079.3 11.6 outer.3
  1090.9 4.5 fusion.9
  1096.6 48.2 %collective-permute-done.2 = bf16[512,2048]{1,0:T(8,128)(2,1)} collective-permute-done((bf16[512,2048]{1,0:T(8,128)(2,1)}, bf16[512,2048]{1,0:T(8,128)(2,1)}, u32[]{:S(2)}, u32[]{:S(2)}) %collective-permute-start.2) | collective-permute-done | bytes 2097184 | tf_op jit(solution)/shard_map/ppermute | solution.py:940
  1144.8 4.4 fusion.8
  1151.7 10.9 gather_sum.6.begin
  1167.1 10.7 gather_sum.7
  1177.8 4.4 multiply_reduce_fusion
  1182.9 5.8 all-to-all-start.8
  1188.7 11.8 all-to-all-done.8
  1201.1 9.7 add_convert_fusion
  1218.6 4.0 broadcast_select_fusion
  1232.1 4.1 slice_convert_fusion
  1236.2 4.1 collective-permute-done.8
  1241.0 6.5 collective-permute-done.9
  1249.9 20.1 %collective-permute-done.5 = bf16[256,768]{1,0:T(8,128)(2,1)S(1)} collective-permute-done((bf16[256,768]{1,0:T(8,128)(2,1)S(1)}, bf16[256,768]{1,0:T(8,128)(2,1)S(1)}, u32[]{:S(2)}, u32[]{:S(2)}) %collective-permute-start.5) | collective-permute-done | bytes 393248 | tf_op jit(solution)/shard_map/ppermute | solution.py:1003
  (180 shorter events, 87.0 us)
Async XLA Ops:
  7.2 305.2 %all-gather.4.cloned.1.call-start = ((), (), s32[]{:S(2)}) async-start(), calls=%async_computation.13 | async-start | bytes 28311552 | tf_op jit(solution)/shard_map/all_gather | solution.py:945
  11.7 357.8 %all-gather.6.cloned.1.call-start = ((), (), s32[]{:S(2)}) async-start(), calls=%async_computation.18 | async-start | bytes 8650752 | tf_op jit(solution)/shard_map/all_gather | solution.py:927
  12.7 10.0 copy-start.30
  16.6 6.8 copy-start.37
  16.6 6.8 copy-start.38
  16.7 6.8 copy-start.14
  16.7 7.7 copy-start.15
  16.7 7.7 copy-start.17
  16.7 7.7 copy-start.18
  23.5 7.0 copy-start.25
  172.6 13.5 %copy-start.27 = (f32[512]{0:T(512)}, f32[512]{0:T(512)S(1)}, u32[]{:S(2)}) copy-start(f32[512]{0:T(512)S(1)} %rsqrt.20) | copy-start | bytes 6148
  173.3 272.5 %copy-start.19 = (f32[1,8,256]{2,0,1:T(1,128)}, f32[1,8,256]{2,0,1:T(1,128)S(1)}, u32[]{:S(2)}) copy-start(f32[1,8,256]{2,0,1:T(1,128)S(1)} %get-tuple-element.165) | copy-start | bytes 24580
  186.1 63.3 %all-to-all-start.1 = ((bf16[32,64,384]{2,1,0:T(8,128)(2,1)}), bf16[32,64,384]{2,1,0:T(8,128)(2,1)S(1)}, u32[]{:S(2)}, u32[]{:S(2)}) async-start(bf16[32,64,384]{2,1,0:T(8,128)(2,1)} %bitcast.89), calls=%async_computation.1 | async-start | bytes 3145728 | tf_op jit(solution)/shard_map/all_to_all | solution.py:932
  195.8 56.9 %copy-start.29 = (s32[1,2048]{1,0:T(1,128)S(1)}, s32[1,2048]{1,0:T(1,128)}, u32[]{:S(2)}) copy-start(s32[1,2048]{1,0:T(1,128)} %param.19) | copy-start | bytes 24580
  249.3 5.8 copy-start.5
  249.3 59.5 %all-to-all-start = ((bf16[32,64,384]{2,1,0:T(8,128)(2,1)}), bf16[32,64,384]{2,1,0:T(8,128)(2,1)S(1)}, u32[]{:S(2)}, u32[]{:S(2)}) async-start(bf16[32,64,384]{2,1,0:T(8,128)(2,1)} %bitcast.88), calls=%async_computation | async-start | bytes 3145728 | tf_op jit(solution)/shard_map/all_to_all | solution.py:932
  308.8 47.6 %all-to-all-start.3 = ((bf16[32,64,256]{2,1,0:T(8,128)(2,1)}), bf16[32,64,256]{2,1,0:T(8,128)(2,1)S(1)}, u32[]{:S(2)}, u32[]{:S(2)}) async-start(bf16[32,64,256]{2,1,0:T(8,128)(2,1)} %get-tuple-element.57), calls=%async_computation.3 | async-start | bytes 2097152 | tf_op jit(solution)/shard_map/all_to_all | solution.py:932
  356.4 11.0 copy-start.8
  356.4 77.3 %all-to-all-start.2 = ((bf16[32,64,256]{2,1,0:T(8,128)(2,1)}), bf16[32,64,256]{2,1,0:T(8,128)(2,1)S(1)}, u32[]{:S(2)}, u32[]{:S(2)}) async-start(bf16[32,64,256]{2,1,0:T(8,128)(2,1)} %get-tuple-element.62), calls=%async_computation.2 | async-start | bytes 2097152 | tf_op jit(solution)/shard_map/all_to_all | solution.py:932
  362.5 586.9 %reduce-scatter.5.cloned.1.call-start = ((), (), s32[]{:S(2)}) async-start(), calls=%async_computation.14 | async-start | bytes 9437184 | tf_op jit(solution)/shard_map/reduce_scatter | solution.py:994
  367.3 81.0 %collective-permute-start = (bf16[512,2048]{1,0:T(8,128)(2,1)}, bf16[512,2048]{1,0:T(8,128)(2,1)S(1)}, u32[]{:S(2)}, u32[]{:S(2)}) collective-permute-start(bf16[512,2048]{1,0:T(8,128)(2,1)} %get-tuple-element.65.refs_2_), channel_id=1, source_target_pairs={{0,1},{1,2},{2,3},{3,0},{4,5},{5,6},{6,7},{7,4},{8,9},{9,10},{10,1... | collective-permute-start | bytes 6291464 | tf_op jit(solution)/shard_map/ppermute | solution.py:940
  751.4 327.9 %reduce-scatter.7.cloned.1.call-start = ((), (), s32[]{:S(2)}) async-start(), calls=%async_computation.15 | async-start | bytes 18874368 | tf_op jit(solution)/shard_map/reduce_scatter | solution.py:994
  793.5 5.1 copy-start.1
  793.5 5.1 copy-start.3
  793.5 5.1 copy-start.26
  808.8 31.0 %all-to-all-start.4 = ((bf16[32,64,256]{2,1,0:T(8,128)(2,1)}), bf16[32,64,256]{2,1,0:T(8,128)(2,1)}, u32[]{:S(2)}, u32[]{:S(2)}) async-start(bf16[32,64,256]{2,1,0:T(8,128)(2,1)} %bitcast.92), calls=%async_computation.4 | async-start | bytes 2097152 | tf_op jit(solution)/shard_map/all_to_all | solution.py:932
  819.8 29.1 %copy-start.9 = (bf16[32,64,256]{2,1,0:T(8,128)(2,1)S(1)}, bf16[32,64,256]{2,1,0:T(8,128)(2,1)}, u32[]{:S(2)}) copy-start(bf16[32,64,256]{2,1,0:T(8,128)(2,1)} %copy-done.8) | copy-start | bytes 3145732
  839.7 74.9 %all-to-all-start.5 = ((bf16[32,64,256]{2,1,0:T(8,128)(2,1)}), bf16[32,64,256]{2,1,0:T(8,128)(2,1)}, u32[]{:S(2)}, u32[]{:S(2)}) async-start(bf16[32,64,256]{2,1,0:T(8,128)(2,1)} %bitcast.91), calls=%async_computation.5 | async-start | bytes 2097152 | tf_op jit(solution)/shard_map/all_to_all | solution.py:932
  843.5 373.2 %reduce-scatter.11.cloned.1.call-start = ((), (), s32[]{:S(2)}) async-start(), calls=%async_computation.17 | async-start | bytes 9437184 | tf_op jit(solution)/shard_map/reduce_scatter | solution.py:994
  843.6 5.4 copy-start.11
  847.2 136.6 %collective-permute-start.1 = (bf16[512,2048]{1,0:T(8,128)(2,1)}, bf16[512,2048]{1,0:T(8,128)(2,1)}, u32[]{:S(2)}, u32[]{:S(2)}) collective-permute-start(bf16[512,2048]{1,0:T(8,128)(2,1)} %slice_bitcast_fusion), channel_id=1, source_target_pairs={{0,1},{1,2},{2,3},{3,0},{4,5},{5,6},{6,7},{7,4},{8,9},{9,10},{10,1... | collective-permute-start | bytes 6291464 | tf_op jit(solution)/shard_map/ppermute | solution.py:940
  993.1 232.7 %reduce-scatter.9.cloned.1.call-start = ((), (), s32[]{:S(2)}) async-start(), calls=%async_computation.16 | async-start | bytes 14155776 | tf_op jit(solution)/shard_map/reduce_scatter | solution.py:994
  993.1 42.2 %copy-start.12 = (bf16[32,64,384]{2,1,0:T(8,128)(2,1)S(1)}, bf16[32,64,384]{2,1,0:T(8,128)(2,1)}, u32[]{:S(2)}) copy-start(bf16[32,64,384]{2,1,0:T(8,128)(2,1)} %attend_backward.3) | copy-start | bytes 4718596
  1035.3 40.9 %copy-start.7 = (bf16[32,64,384]{2,1,0:T(8,128)(2,1)}, bf16[32,64,384]{2,1,0:T(8,128)(2,1)S(1)}, u32[]{:S(2)}) copy-start(bf16[32,64,384]{2,1,0:T(8,128)(2,1)S(1)} %all_to_all.45) | copy-start | bytes 4718596
  1090.9 5.7 copy-start.33
  1095.4 49.4 %collective-permute-start.2 = (bf16[512,2048]{1,0:T(8,128)(2,1)}, bf16[512,2048]{1,0:T(8,128)(2,1)}, u32[]{:S(2)}, u32[]{:S(2)}) collective-permute-start(bf16[512,2048]{1,0:T(8,128)(2,1)} %fusion.9), channel_id=1, source_target_pairs={{0,1},{1,2},{2,3},{3,0},{4,5},{5,6},{6,7},{7,4},{8,9},{9,10},{10,1... | collective-permute-start | bytes 6291464 | tf_op jit(solution)/shard_map/ppermute | solution.py:940
  1149.2 51.9 %collective-permute-start.3 = (bf16[512,2048]{1,0:T(8,128)(2,1)}, bf16[512,2048]{1,0:T(8,128)(2,1)}, u32[]{:S(2)}, u32[]{:S(2)}) collective-permute-start(bf16[512,2048]{1,0:T(8,128)(2,1)} %fusion.8), channel_id=1, source_target_pairs={{0,1},{1,2},{2,3},{3,0},{4,5},{5,6},{6,7},{7,4},{8,9},{9,10},{10,1... | collective-permute-start | bytes 6291464 | tf_op jit(solution)/shard_map/ppermute | solution.py:940
  1151.7 10.9 copy-start.13
  1167.0 10.7 copy-start.22
  1167.1 10.7 copy-start.28
  1182.9 17.6 %all-to-all-start.8 = ((f32[32,2,256]{2,1,0:T(2,128)}), f32[32,2,256]{2,1,0:T(2,128)S(1)}, u32[]{:S(2)}, u32[]{:S(2)}) async-start(f32[32,2,256]{2,1,0:T(2,128)} %bitcast.38), calls=%async_computation.9 | async-start | bytes 131072 | tf_op jit(solution)/shard_map/all_to_all | solution.py:1051
  1210.8 7.8 copy-start.31
  1217.9 11.4 collective-permute-start.7
  1222.6 17.7 %collective-permute-start.8 = (bf16[256,512]{1,0:T(8,128)(2,1)S(1)}, bf16[256,512]{1,0:T(8,128)(2,1)S(1)}, u32[]{:S(2)}, u32[]{:S(2)}) collective-permute-start(bf16[256,512]{1,0:T(8,128)(2,1)S(1)} %get-tuple-element.152), channel_id=1, source_target_pairs={{0,2},{1,3},{2,0},{3,1},{4,6},{5,7},{6,4},{7,5},{8,10},{9,11},{10,... | collective-permute-start | bytes 786440 | tf_op jit(solution)/shard_map/ppermute | solution.py:1003
  1222.6 24.9 %collective-permute-start.9 = (bf16[256,512]{1,0:T(8,128)(2,1)S(1)}, bf16[256,512]{1,0:T(8,128)(2,1)}, u32[]{:S(2)}, u32[]{:S(2)}) collective-permute-start(bf16[256,512]{1,0:T(8,128)(2,1)S(1)} %get-tuple-element.151), channel_id=1, source_target_pairs={{0,3},{1,0},{2,1},{3,2},{4,7},{5,4},{6,5},{7,6},{8,11},{9,8},{10,9... | collective-permute-start | bytes 786440 | tf_op jit(solution)/shard_map/ppermute | solution.py:1003
  1227.1 22.8 %collective-permute-start.4 = (bf16[256,768]{1,0:T(8,128)(2,1)S(1)}, bf16[256,768]{1,0:T(8,128)(2,1)S(1)}, u32[]{:S(2)}, u32[]{:S(2)}) collective-permute-start(bf16[256,768]{1,0:T(8,128)(2,1)S(1)} %get-tuple-element.147), channel_id=1, source_target_pairs={{0,1},{1,2},{2,3},{3,0},{4,5},{5,6},{6,7},{7,4},{8,9},{9,10},{10,1... | collective-permute-start | bytes 1179656 | tf_op jit(solution)/shard_map/ppermute | solution.py:1003
  1227.7 42.3 %collective-permute-start.5 = (bf16[256,768]{1,0:T(8,128)(2,1)S(1)}, bf16[256,768]{1,0:T(8,128)(2,1)S(1)}, u32[]{:S(2)}, u32[]{:S(2)}) collective-permute-start(bf16[256,768]{1,0:T(8,128)(2,1)S(1)} %get-tuple-element.149), channel_id=1, source_target_pairs={{0,2},{1,3},{2,0},{3,1},{4,6},{5,7},{6,4},{7,5},{8,10},{9,11},{10,... | collective-permute-start | bytes 1179656 | tf_op jit(solution)/shard_map/ppermute | solution.py:1003
  1229.3 40.7 %collective-permute-start.6 = (bf16[256,768]{1,0:T(8,128)(2,1)S(1)}, bf16[256,768]{1,0:T(8,128)(2,1)S(1)}, u32[]{:S(2)}, u32[]{:S(2)}) collective-permute-start(bf16[256,768]{1,0:T(8,128)(2,1)S(1)} %get-tuple-element.148), channel_id=1, source_target_pairs={{0,3},{1,0},{2,1},{3,2},{4,7},{5,4},{6,5},{7,6},{8,11},{9,8},{10,9... | collective-permute-start | bytes 1179656 | tf_op jit(solution)/shard_map/ppermute | solution.py:1003
  (14 other events, 25.9 us)
Sparse Core Ops, SparseCore 0:
  11.9 172.5 all-gather.3
  187.4 112.7 all-gather.5
  751.5 79.8 reduce-scatter.4
  835.3 116.3 reduce-scatter.6
  993.2 89.2 reduce-scatter.10
  1091.0 90.7 reduce-scatter.8

commit v5 on v4

--- a/solution.py
+++ b/solution.py
@@ -296,7 +296,7 @@
 
 
 def attend_backward(
-    grad_slots, q_t, k_rows, k_t, v_rows, o_t, lse, begin, cos_t, sin_t, first_block, perm,
+    grad_slots, part, q_t, k_rows, k_t, v_rows, o_t, lse, begin, cos_t, sin_t, first_block, perm,
     page_rows, block_len,
 ):
     total_rows = q_t.shape[1]
@@ -310,7 +310,7 @@
     def page_spec(a):
         return pl.BlockSpec(
             (1, page_rows, q_cols),
-            lambda i, first_ref, perm_ref, a=a: (perm_ref[i * pages + a], 0, 0),
+            lambda i, first_ref, perm_ref, a=a: (perm_ref[i * pages + a], 0, part),
         )
 
     def whole(shape):
@@ -367,9 +367,9 @@
 ):
     grad_rows = refs[:ring]
     (
-        weights, grad_all, rows_all, act_all, grads_all, mixed_all, grad_own,
+        weights, grads_t, rows_t, act_all, grads_all, mixed_all, grad_own,
     held, grads_held, acc_n, acc_m, first_part, arrived, outgoing, mixed_stage, final_stage,
-    load_sem, keep_sem, grad_sem, mixed_sem, final_sem,
+    turned, load_sem, keep_sem, grad_sem, mixed_sem, final_sem,
     row_send, row_recv, sum_send, sum_recv, all_sem,
     ) = refs[ring:]
     me = lax.axis_index("tensor")
@@ -389,10 +389,12 @@
     def grad_load(s):
         return pltpu.make_async_copy(grad_rows[s], grads_held.at[s % 2], grad_sem.at[s % 2])
 
+    def part_of(array, s):
+        count = own_rows.shape[0]
+        return array.at[:, pl.ds(pl.multiple_of(s * count, 128), count)]
+
     def grad_keep(s):
-        return pltpu.make_async_copy(
-            grads_held.at[lax.rem(s, 2)], grad_all.at[s], all_sem.at[lax.rem(s, 2)]
-        )
+        return pltpu.make_async_copy(turned.at[1], part_of(grads_t, s), all_sem)
 
     grad_load(0).start()
     load.wait()
@@ -418,7 +420,7 @@
         )
 
     def keep(s):
-        return pltpu.make_async_copy(held.at[s], rows_all.at[s], keep_sem.at[s])
+        return pltpu.make_async_copy(turned.at[0], part_of(rows_t, s), keep_sem)
 
     def mixed_store(s):
         return pltpu.make_async_copy(mixed_stage, mixed_all.at[s], mixed_sem)
@@ -432,12 +434,13 @@
         def _():
             pass_rows(s).start()
 
-        keep(s).start()
-
         @pl.when(s > 0)
         def _():
+            keep(s - 1).wait()
             grad_keep(s - 1).wait()
 
+        turned[0] = held[s].T
+        keep(s).start()
         for k in range(ring):
 
             @pl.when(s == k)
@@ -446,8 +449,9 @@
                 if k < ring - 1:
                     grad_load(k + 1).start()
 
+        slot = lax.rem(s, 2)
+        turned[1] = grads_held[slot].T
         grad_keep(s).start()
-        slot = lax.rem(s, 2)
         acc_n[...] = jnp.zeros_like(acc_n)
         acc_m[...] = jnp.zeros_like(acc_m)
 
@@ -517,8 +521,6 @@
     final.start()
 
     def settle(s, carry):
-        keep(s).wait()
-
         @pl.when(s < ring - 1)
         def _():
             pass_rows(s).wait_send()
@@ -530,6 +532,7 @@
         return carry
 
     lax.fori_loop(0, ring, settle, 0)
+    keep(ring - 1).wait()
     grad_keep(ring - 1).wait()
     final.wait()
 
@@ -542,8 +545,8 @@
     return pl.pallas_call(
         functools.partial(feed_kernel, ring, min(tile, hidden)),
         out_shape=[
-            jax.ShapeDtypeStruct((ring, count, width), bf16),
-            jax.ShapeDtypeStruct((ring, count, width), bf16),
+            jax.ShapeDtypeStruct((width, ring * count), bf16),
+            jax.ShapeDtypeStruct((width, ring * count), bf16),
             jax.ShapeDtypeStruct((ring, count, hidden), bf16),
             jax.ShapeDtypeStruct((ring, count, 2 * hidden), bf16),
             jax.ShapeDtypeStruct((ring, count, width), bf16),
@@ -561,8 +564,9 @@
             pltpu.VMEM((ring - 1, count, width), bf16),
             pltpu.VMEM((count, width), bf16),
             pltpu.VMEM((count, width), bf16),
+            pltpu.VMEM((2, width, count), bf16),
             dma,
-            dma((ring,)),
+            dma,
             dma((2,)),
             dma,
             dma,
@@ -570,7 +574,7 @@
             dma((ring - 1,)),
             dma((ring - 1,)),
             dma((ring - 1,)),
-            dma((2,)),
+            dma,
         ],
         compiler_params=pltpu.CompilerParams(
             collective_id=collective_id, has_side_effects=True, vmem_limit_bytes=64 * 1024 * 1024 - 65536,
@@ -582,6 +586,126 @@
         ),
         name="feed_forward",
     )(own_rows, *grad_rows, weights)
+
+
+def weigh_kernel(
+    tp_count, dp_count, tile, grads, rows_t, grads_t, gate_up, act, slots, out,
+    left, left_sem, own_sem, send, recv,
+):
+    count = dp_count * tp_count
+    my_dp = lax.axis_index("dp")
+    my_tp = lax.axis_index("tensor")
+    me = my_dp * tp_count + my_tp
+    page_rows = slots.shape[1]
+
+    loads = [
+        pltpu.make_async_copy(source, left.at[k], left_sem.at[k])
+        for k, source in enumerate((rows_t, grads_t))
+    ]
+    for load in loads:
+        load.start()
+
+    barrier = pltpu.get_barrier_semaphore()
+
+    def place(peer):
+        return {"dp": lax.div(peer, tp_count), "tensor": lax.rem(peer, tp_count)}
+
+    def greet(j, carry):
+        peer = lax.rem(me + j, count)
+        pl.semaphore_signal(barrier, inc=1, device_id=place(peer), device_id_type=MESH)
+        return carry
+
+    lax.fori_loop(1, count, greet, 0)
+    pl.semaphore_wait(barrier, count - 1)
+
+    home = slots.at[my_tp * dp_count + my_dp]
+
+    def block(p_dp, p_tp):
+        return grads.at[p_tp, pl.ds(p_dp * page_rows, page_rows), :]
+
+    own = pltpu.make_async_copy(block(my_dp, my_tp), home, own_sem)
+    own.start()
+
+    def copy_to(j):
+        peer = lax.rem(me + j, count)
+        return pltpu.make_async_remote_copy(
+            src_ref=block(lax.div(peer, tp_count), lax.rem(peer, tp_count)),
+            dst_ref=home,
+            send_sem=send.at[j],
+            recv_sem=recv.at[j],
+            device_id=place(peer),
+            device_id_type=MESH,
+        )
+
+    def start(j, carry):
+        copy_to(j).start()
+        return carry
+
+    def finish(j, carry):
+        copy_to(j).wait()
+        return carry
+
+    lax.fori_loop(1, count, start, 0)
+
+    width = rows_t.shape[0]
+    step = min(512, width)
+
+    def multiply(k, right, first):
+        ring, rows, cols = right.shape
+
+        def body(part, result):
+            values = part[...].reshape(ring * rows, tile)
+            for m in range(0, width, step):
+                result[m : m + step, :] = dot_nn(left[k, m : m + step, :], values).astype(bf16)
+
+        pltpu.emit_pipeline(
+            body,
+            grid=(cols // tile,),
+            in_specs=[pl.BlockSpec((ring, rows, tile), lambda n: (0, 0, n))],
+            out_specs=[pl.BlockSpec((width, tile), lambda n: (0, n + first))],
+        )(right, out)
+
+    loads[0].wait()
+    multiply(0, gate_up, 0)
+    loads[1].wait()
+    multiply(1, act, gate_up.shape[2] // tile)
+    own.wait()
+    lax.fori_loop(1, count, finish, 0)
+
+
+def weigh(grads, rows_t, grads_t, gate_up, act, tp_count, dp_count, collective_id):
+    count = tp_count * dp_count
+    cols = grads.shape[2]
+    page_rows = grads.shape[1] // dp_count
+    width, rows = rows_t.shape
+    hidden = act.shape[2]
+    any_spec = pl.BlockSpec(memory_space=pl.ANY)
+    dma = pltpu.SemaphoreType.DMA
+    return pl.pallas_call(
+        functools.partial(weigh_kernel, tp_count, dp_count, min(512, hidden)),
+        out_shape=[
+            jax.ShapeDtypeStruct((count, page_rows, cols), bf16),
+            jax.ShapeDtypeStruct((width, 3 * hidden), bf16),
+        ],
+        in_specs=[any_spec] * 5,
+        out_specs=[any_spec] * 2,
+        scratch_shapes=[
+            pltpu.VMEM((2, width, rows), bf16),
+            dma((2,)),
+            dma,
+            dma((count,)),
+            dma((count,)),
+        ],
+        compiler_params=pltpu.CompilerParams(
+            collective_id=collective_id, has_side_effects=True, vmem_limit_bytes=48 * 1024 * 1024
+        ),
+        cost_estimate=pl.CostEstimate(
+            flops=6 * rows * width * hidden,
+            bytes_accessed=2 * width * (2 * rows + 3 * hidden),
+            transcendentals=0,
+        ),
+        name="weigh",
+    )(grads, rows_t, grads_t, gate_up, act)
 
 
 def flip(index, bit):
@@ -962,10 +1086,10 @@
     saved, mixed = [], []
     last = qkv[-1]
     for hop in range(hops + 1, tp_count):
-        grad_chunks.append(pass_on(after(grad_chunks[-1], slots[-1])))
+        grad_chunks.append(pass_on(after(grad_chunks[-1], slots[0])))
     for g in groups:
         if g == len(groups) - 1:
-            last = (last, w_mlp)
+            last = (last, w_mlp, grad_chunks[-1])
         q_t, k_t, k_rows, v_t, v_rows = prepare(
             after(slots[g], last), perm, cos_t, sin_t, per_group, 1
         )
@@ -980,7 +1104,7 @@
 
     scale_two = rms_scale(hidden_mid)
     normed_two = (hidden_mid * scale_two * gain_two).astype(bf16)
-    grad_mlp, mlp_rows, inner_act, grad_gate_up, partial_two, grad_normed_two = feed(
+    grads_t, rows_t, inner_act, grad_gate_up, partial_two, grad_normed_two = feed(
         normed_two, grad_chunks, w_mlp, tp_count
     )
     grad_normed_two = grad_normed_two.astype(f32)
@@ -1003,40 +1127,36 @@
             total = total + lax.ppermute(block, "tensor", pairs).astype(f32)
         return total
 
-    def flat(value):
-        return value.reshape(tok_group, value.shape[-1])
-
-    grad_down_t = dot_tn(flat(grad_mlp), flat(inner_act)).astype(bf16)
-    sum_down = reduce_dp(grad_down_t)
-    grad_gate_up = dot_tn(flat(mlp_rows), flat(after(grad_gate_up, grad_down_t))).astype(bf16)
-    sum_gate_up = reduce_dp(grad_gate_up)
-    grad_z = after(grad_mid.astype(bf16), grad_gate_up)
-    grad_slots = [trade(spread(grad_z, w_out_t, g, group_q)) for g in groups]
+    grad_z = grad_mid.astype(bf16)
+    grad_wout = outer(grad_z, jnp.concatenate(mixed, axis=2))
+    sum_out = reduce_dp(grad_wout)
+    grad_slots, grad_wmlp = weigh(
+        spread(after(grad_z, grad_wout), w_out_t, 0, q_cols),
+        rows_t, grads_t, grad_gate_up, inner_act, tp_count, dp_count, 2,
+    )
+    sum_mlp = reduce_dp(grad_wmlp)
+    branch_two = pass_on(after(partial_two[1], grad_slots))
     grad_qkv = []
-    last = grad_z
     for g in groups:
         q_t, k_rows, k_t, v_rows, o_t, lse = saved[g]
         back = attend_backward(
-            after(grad_slots[g], last), q_t, k_rows, k_t, v_rows, o_t, lse, begin, cos_t, sin_t,
-            first_block, perm, page_rows, block_len,
-        )
-        grad_qkv.append(trade_back(back))
-        last = (back, sum_down)
-    branch_two = pass_on(after(partial_two[1], grad_slots[-1]))
-    grad_wout = outer(after(grad_z, (back, branch_two)), jnp.concatenate(mixed, axis=2))
-    for s in range(2, tp_count):
-        branch_two = pass_on(add_on(after(branch_two, grad_qkv[-1]), s))
-    sum_out = reduce_dp(grad_wout)
-    normed_late = after(normed_one, (sum_gate_up, grad_wout))
-    hidden = sum_gate_up.shape[1] // 2
-    grad_wqkv = outer(normed_late, jnp.concatenate(grad_qkv, axis=2))
+            grad_slots if g == 0 else after(grad_slots, (back, sum_out)), g, q_t, k_rows, k_t,
+            v_rows, o_t, lse, begin, cos_t, sin_t, first_block, perm, page_rows, block_len,
+        )
+        grad_qkv.append(trade_back(after(back, branch_two) if g == len(groups) - 1 else back))
+    hidden = sum_mlp.shape[1] // 3
+    grad_wqkv = outer(after(normed_one, sum_mlp), jnp.concatenate(grad_qkv, axis=2))
     sum_qkv = reduce_tensor(reduce_dp(grad_wqkv))
+    each = group_q + 2 * HD
+    sum_qkv = [sum_qkv[:, g * each : (g + 1) * each] for g in groups]
+    branch_two = add_on(after(branch_two, grad_qkv[-1]), 2)
     grad_normed_one = jnp.zeros((tok_dev, width), f32)
     for g in groups:
-        grad_normed_one = gather_sum(grad_qkv[g], w_qkv, g, grad_normed_one)
+        grad_normed_one = gather_sum(after(grad_qkv[g], grad_wqkv), w_qkv, g, grad_normed_one)
+    for s in range(3, tp_count):
+        branch_two = add_on(after(pass_on(branch_two), grad_normed_one), s)
+    branch_two = pass_on(branch_two)
     sum_out = reduce_tensor(sum_out)
-    each = group_q + 2 * HD
-    sum_qkv = [sum_qkv[:, g * each : (g + 1) * each] for g in groups]
     result = (
         (after(hidden_mid, back) + branch_two.astype(f32) + partial_two[0].astype(f32)) * valid_rows
     ).astype(bf16)
@@ -1059,9 +1179,9 @@
         jnp.concatenate([part[:, group_q + HD :] for part in sum_qkv], axis=1),
         sum_out.T,
         gain_sums[1],
-        sum_gate_up[:, :hidden].astype(f32),
-        sum_gate_up[:, hidden:].astype(f32),
-        sum_down.astype(f32).T,
+        sum_mlp[:, :hidden].astype(f32),
+        sum_mlp[:, hidden : 2 * hidden].astype(f32),
+        sum_mlp[:, 2 * hidden :].astype(f32).T,
     )
 
 

time: 1300 us -> 1240 us (0.954)
  Pallas kernels: 661 us -> 728 us
  matrix products: 66 us -> 0 us
  waiting for transfers between devices: 286 us -> 223 us
  starting transfers between devices: 51.3 us -> 94.7 us
  blocking collectives: 83.1 us -> 41.1 us
    all_to_all x6 -> x5, waiting for transfers between devices: 195 us -> 119 us  [trade(): lax.all_to_all(blocks, everyone, split_axis=0, concat_axis=0, tiled=True)]
    pallas_call x0 -> x1, Pallas kernels: none -> 67.3 us  [weigh(): pl.pallas_call(functools.partial(weigh_kernel, tp_count, dp_count, min(51...]
    dot_general x2 -> x0, matrix products: 66 us -> none  [dot_tn(): lax.dot_general(left, right, (((0,), (0,)), ((), ())), preferred_element_...]
    all_to_all x1, starting transfers between devices: 5.79 us -> 51.4 us  [local(): lax.all_to_all(gain_parts, everyone, split_axis=0, concat_axis=0, tiled=T...]
    all_to_all x2 -> x1, blocking collectives: 83.1 us -> 41.1 us  [trade(): lax.all_to_all(blocks, everyone, split_axis=0, concat_axis=0, tiled=True)]
    reduce_scatter x4 -> x3, waiting for transfers between devices: 0.03 us -> 19.4 us  [reduce_dp(): lax.psum_scatter(grad.astype(bf16), 'dp', scatter_dimension=0, tiled=True)]
    all_to_all x6 -> x5, starting transfers between devices: 31.3 us -> 27.1 us  [trade(): lax.all_to_all(blocks, everyone, split_axis=0, concat_axis=0, tiled=True)]
    pallas_call x4 -> x3, Pallas kernels: 28.9 us -> 25.7 us  [spread(): pl.pallas_call(spread_kernel, grid=(shards,), in_specs=[pl.BlockSpec((cou...]
  transfers between devices with their start and end apart: 23 -> 21, of which waited for: 10 -> 11; matrix products, arithmetic and copies ran while one was open for 11% -> 7% of each run, Pallas kernels for 30% -> 34%
where the time goes in v5:
time: 1240 us; the launch traced here: 1220 us
  Pallas kernels  728 us (59%)
  waiting for transfers between devices  223 us (18%)
  starting transfers between devices  94.7 us (8%)
  other arithmetic  75.5 us (6%)
  local copies, waits for them, and re-layouts  45.2 us (4%)
  blocking collectives  41.1 us (3%)
  between operations  14.6 us (1%)
    pallas_call x1, Pallas kernels, feed(): pl.pallas_call(functools.partial(feed_kernel, ring, min(tile, hidden)), o...  279 us
    pallas_call x1, Pallas kernels, collect(): pl.pallas_call(functools.partial(collect_kernel, tp_count, dp_count, hops...  138 us
    all_to_all x5, waiting for transfers between devices, trade(): lax.all_to_all(blocks, everyone, split_axis=0, concat_axis=0, tiled=True)  119 us
    pallas_call x2, Pallas kernels, attend_backward(): pl.pallas_call(functools.partial(backward_kernel, q_heads, kv_heads, page...  68.8 us
    pallas_call x1, Pallas kernels, weigh(): pl.pallas_call(functools.partial(weigh_kernel, tp_count, dp_count, min(51...  67.3 us
    pallas_call x2, Pallas kernels, attend_forward(): pl.pallas_call(functools.partial(forward_kernel, q_heads, kv_heads, page_...  66.7 us
    ppermute x4, waiting for transfers between devices, pass_on(): return lax.ppermute(value, 'tensor', ring_next)  52.5 us
    all_to_all x1, starting transfers between devices, local(): lax.all_to_all(gain_parts, everyone, split_axis=0, concat_axis=0, tiled=T...  51.4 us
  transfers between devices with their start and end apart: 21, of which 11 were waited for; matrix products, arithmetic and copies ran while one was open for 7% of the time, Pallas kernels for 34%

profile of v5, /device:TPU:0, one launch (start us, length us, event | category | flops | bytes accessed | tf_op | source)
XLA Modules:
  0.0 1222.3 jit_solution(3532427444681506285)
XLA Ops:
  19.0 3.6 gather_fusion.2
  25.9 4.5 select_convert_fusion
  33.5 138.3 %collect.1 = (bf16[4,2048,768]{2,1,0:T(8,128)(2,1)}, bf16[8,2,256]{2,1,0:T(2,128)(2,1)}, bf16[2,512,2048]{2,1,0:T(8,128)(2,1)}) custom-call(bf16[256,768]{1,0:T(8,128)(2,1)} %concatenate.22.shard, bf16[2,256]{1,0:T(2,128)(2,1)} %pad_maximum_fusion.6.gains, bf16[512,2048]{1,0:T(8,128)(2,1)} %fusion.10.chunk.refs_0_), custom_call_target="tpu_custom_call" | custom-call | bytes 100663296 | tf_op jit(solution)/shard_map/collect/pallas_call | solution.py:839
  174.0 3.9 multiply_convert_fusion.1.rows
  177.9 8.2 spread.4
  186.2 9.7 all-to-all-start.1
  195.9 8.2 spread.3
  204.1 45.3 %all-to-all-done.1.refs_0_.refs_1_ = bf16[32,64,384]{2,1,0:T(8,128)(2,1)S(1)} async-done(((bf16[32,64,384]{2,1,0:T(8,128)(2,1)}), bf16[32,64,384]{2,1,0:T(8,128)(2,1)S(1)}, u32[]{:S(2)}, u32[]{:S(2)}) %all-to-all-start.1) | async-done | bytes 1572896 | tf_op jit(solution)/shard_map/all_to_all | solution.py:1056
  249.4 3.4 all-to-all-start
  254.7 4.8 slice_bitcast_fusion.1
  261.9 10.5 prepare.2
  272.4 33.4 %attend_forward.2 = (bf16[256,2048]{1,0:T(8,128)(2,1)}, f32[4,2048]{1,0:T(4,128)}, bf16[32,64,256]{2,1,0:T(8,128)(2,1)}) custom-call(s32[8]{0:T(128)} %get-tuple-element.183.first_block, s32[32]{0:T(128)} %fusion.13.perm, bf16[256,2048]{1,0:T(8,128)(2,1)} %get-tuple-element.56.q_t.refs_4_, bf16[1,2048,64]{2,1,0:T(8,128)(2,1)} %get-tuple-element.57.k_rows.refs_5_, ...), custom_call_target="tpu_custom_call" | custom-call | flops 1073741824 | bytes 4194304 | tf_op jit(solution)/shard_map/attend_forward/pallas_call | solution.py:163
  305.8 48.0 %all-to-all-done.refs_0_.refs_1_ = bf16[32,64,384]{2,1,0:T(8,128)(2,1)S(1)} async-done(((bf16[32,64,384]{2,1,0:T(8,128)(2,1)}), bf16[32,64,384]{2,1,0:T(8,128)(2,1)S(1)}, u32[]{:S(2)}, u32[]{:S(2)}) %all-to-all-start) | async-done | bytes 1572896 | tf_op jit(solution)/shard_map/all_to_all | solution.py:1056
  356.6 10.6 prepare.3
  367.2 33.3 %attend_forward.3 = (bf16[256,2048]{1,0:T(8,128)(2,1)}, f32[4,2048]{1,0:T(4,128)}, bf16[32,64,256]{2,1,0:T(8,128)(2,1)}) custom-call(s32[8]{0:T(128)} %get-tuple-element.183.first_block, s32[32]{0:T(128)} %fusion.13.perm, bf16[256,2048]{1,0:T(8,128)(2,1)} %get-tuple-element.63.q_t.refs_4_, bf16[1,2048,64]{2,1,0:T(8,128)(2,1)} %get-tuple-element.64.k_rows.refs_5_, ...), custom_call_target="tpu_custom_call" | custom-call | flops 1073741824 | bytes 4194304 | tf_op jit(solution)/shard_map/attend_forward/pallas_call | solution.py:163
  400.5 6.8 all-to-all-start.2
  407.6 8.5 gather_sum.4.begin
  416.1 17.4 %all-to-all-done.2 = bf16[32,64,256]{2,1,0:T(8,128)(2,1)S(1)} async-done(((bf16[32,64,256]{2,1,0:T(8,128)(2,1)}), bf16[32,64,256]{2,1,0:T(8,128)(2,1)S(1)}, u32[]{:S(2)}, u32[]{:S(2)}) %all-to-all-start.2) | async-done | bytes 1048608 | tf_op jit(solution)/shard_map/all_to_all | solution.py:1056
  436.6 8.5 gather_sum.5
  450.3 278.5 %feed_forward.1 = (bf16[2048,2048]{1,0:T(8,128)(2,1)}, bf16[2048,2048]{1,0:T(8,128)(2,1)}, bf16[4,512,2048]{2,1,0:T(8,128)(2,1)}, bf16[4,512,4096]{2,1,0:T(8,128...) custom-call(bf16[512,2048]{1,0:T(8,128)(2,1)} %multiply_convert_fusion.own_rows, ...), custom_call_target="tpu_custom_call" | custom-call | flops 103079215104 | bytes 33554432 | tf_op jit(solution)/shard_map/feed_forward/pallas_call | solution.py:545
  728.9 4.2 fusion.5
  733.6 3.9 fusion.20.rows
  737.5 9.4 outer.2
  747.0 9.3 spread.5.grads
  758.2 67.3 %weigh.1 = (bf16[32,64,512]{2,1,0:T(8,128)(2,1)S(1)}, bf16[2048,6144]{1,0:T(8,128)(2,1)}) custom-call(bf16[4,512,512]{2,1,0:T(8,128)(2,1)S(1)} %copy-done.1, bf16[2048,2048]{1,0:T(8,128)(2,1)} %get-tuple-element.70.rows_t, bf16[2048,2048]{1,0:T(8,128)(2,1)} %get-tuple-element.71.grads_t, bf16[4,512,4096]{2,1,0:T(8,128)(2,1)} %get-tuple-element.72.gate_up, ...), custom_call_target="tpu_custom_call" | custom-call | flops 51539607552 | bytes 41943040 | tf_op jit(solution)/shard_map/weigh/pallas_call | solution.py:684
  826.9 34.4 %attend_backward.2 = bf16[32,64,384]{2,1,0:T(8,128)(2,1)} custom-call(s32[8]{0:T(128)} %get-tuple-element.183.first_block, s32[32]{0:T(128)} %fusion.13.perm, bf16[32,64,512]{2,1,0:T(8,128)(2,1)} %copy-done, bf16[32,64,512]{2,1,0:T(8,128)(2,1)} %copy-done, bf16[32,64,512]{2,1,0:T(8,128)(2,1)} %copy-done, bf16[32,64,512]{2,1,0:T(8,128)(2,1)} %copy-done, ...), custom_call_target="tpu_custom_call" | custom-call | flops 3221225472 | bytes 6291456 | tf_op jit(solution)/shard_map/attend_backward/pallas_call | solution.py:322
  861.3 4.5 all-to-all-start.5
  865.9 3.6 slice_bitcast_fusion
  871.3 34.4 %attend_backward.3 = bf16[32,64,384]{2,1,0:T(8,128)(2,1)} custom-call(s32[8]{0:T(128)} %get-tuple-element.183.first_block, s32[32]{0:T(128)} %fusion.13.perm, bf16[32,64,512]{2,1,0:T(8,128)(2,1)} %copy-done, bf16[32,64,512]{2,1,0:T(8,128)(2,1)} %copy-done, bf16[32,64,512]{2,1,0:T(8,128)(2,1)} %copy-done, bf16[32,64,512]{2,1,0:T(8,128)(2,1)} %copy-done, ...), custom_call_target="tpu_custom_call" | custom-call | flops 3221225472 | bytes 6291456 | tf_op jit(solution)/shard_map/attend_backward/pallas_call | solution.py:322
  905.7 35.2 %collective-permute-done.1 = bf16[512,2048]{1,0:T(8,128)(2,1)} collective-permute-done((bf16[512,2048]{1,0:T(8,128)(2,1)}, bf16[512,2048]{1,0:T(8,128)(2,1)}, u32[]{:S(2)}, u32[]{:S(2)}) %collective-permute-start.1) | collective-permute-done | bytes 2097184 | tf_op jit(solution)/shard_map/ppermute | solution.py:1064
  940.9 7.9 all-to-all-done.5
  948.7 41.1 %all_to_all.35 = bf16[32,64,384]{2,1,0:T(8,128)(2,1)S(1)} all-to-all(bf16[32,64,384]{2,1,0:T(8,128)(2,1)} %attend_backward.3), channel_id=1, replica_groups=mesh['dp'=8,'tensor'=4] {'tensor','dp'}, dimensions={0} | all-to-all | bytes 3145728 | tf_op jit(solution)/shard_map/all_to_all | solution.py:1056
  994.4 19.4 %reduce-scatter.6.cloned.1.call-done = bf16[256,6144]{1,0:T(8,128)(2,1)} async-done(((bf16[2048,6144]{1,0:T(8,128)(2,1)}), bf16[256,6144]{1,0:T(8,128)(2,1)}) %reduce-scatter.6.cloned.1.call-update) | async-done | bytes 3145744 | tf_op jit(solution)/shard_map/reduce_scatter | solution.py:1118
  1013.8 11.7 outer.3
  1025.6 4.5 fusion.9
  1040.4 11.7 gather_sum.6.begin
  1052.1 11.5 gather_sum.7
  1063.6 17.3 %collective-permute-done.2 = bf16[512,2048]{1,0:T(8,128)(2,1)} collective-permute-done((bf16[512,2048]{1,0:T(8,128)(2,1)}, bf16[512,2048]{1,0:T(8,128)(2,1)}, u32[]{:S(2)}, u32[]{:S(2)}) %collective-permute-start.2) | collective-permute-done | bytes 2097184 | tf_op jit(solution)/shard_map/ppermute | solution.py:1064
  1080.9 4.4 fusion.8
  1086.4 11.2 collective-permute-done.8
  1099.8 4.5 multiply_reduce_fusion
  1104.9 51.4 %all-to-all-start.6 = ((f32[32,2,256]{2,1,0:T(2,128)}), f32[32,2,256]{2,1,0:T(2,128)S(1)}, u32[]{:S(2)}, u32[]{:S(2)}) async-start(f32[32,2,256]{2,1,0:T(2,128)} %bitcast.34), calls=%async_computation.8 | async-start | bytes 131072 | tf_op jit(solution)/shard_map/all_to_all | solution.py:1171
  1156.3 4.8 convert_bitcast_fusion
  1164.7 9.7 add_convert_fusion
  1176.6 3.6 gather_fusion.4
  1187.3 4.0 broadcast_select_fusion
  1191.3 4.1 collective-permute-done.4
  1195.5 16.3 %collective-permute-done.5 = bf16[256,768]{1,0:T(8,128)(2,1)S(1)} collective-permute-done((bf16[256,768]{1,0:T(8,128)(2,1)S(1)}, bf16[256,768]{1,0:T(8,128)(2,1)S(1)}, u32[]{:S(2)}, u32[]{:S(2)}) %collective-permute-start.5) | collective-permute-done | bytes 393248 | tf_op jit(solution)/shard_map/ppermute | solution.py:1127
  (163 shorter events, 76.6 us)
Async XLA Ops:
  7.2 349.4 %all-gather.4.cloned.1.call-start = ((), (), s32[]{:S(2)}) async-start(), calls=%async_computation.10 | async-start | bytes 28311552 | tf_op jit(solution)/shard_map/all_gather | solution.py:1069
  8.7 3.1 copy-start.32
  8.7 4.1 copy-start.31
  11.7 395.8 %all-gather.6.cloned.1.call-start = ((), (), s32[]{:S(2)}) async-start(), calls=%async_computation.14 | async-start | bytes 8650752 | tf_op jit(solution)/shard_map/all_gather | solution.py:1051
  12.7 9.9 copy-start.20
  16.6 6.8 copy-start.33
  16.6 6.8 copy-start.34
  16.6 6.8 copy-start.12
  16.6 7.7 copy-start.13
  16.6 7.7 copy-start.14
  16.6 7.7 copy-start.15
  23.4 7.0 copy-start.23
  172.7 13.5 %copy-start.25 = (f32[512]{0:T(512)}, f32[512]{0:T(512)S(1)}, u32[]{:S(2)}) copy-start(f32[512]{0:T(512)S(1)} %rsqrt.20) | copy-start | bytes 6148
  173.4 274.4 %copy-start.16 = (f32[1,8,256]{2,0,1:T(1,128)}, f32[1,8,256]{2,0,1:T(1,128)S(1)}, u32[]{:S(2)}) copy-start(f32[1,8,256]{2,0,1:T(1,128)S(1)} %get-tuple-element.170) | copy-start | bytes 24580
  186.2 63.2 %all-to-all-start.1 = ((bf16[32,64,384]{2,1,0:T(8,128)(2,1)}), bf16[32,64,384]{2,1,0:T(8,128)(2,1)S(1)}, u32[]{:S(2)}, u32[]{:S(2)}) async-start(bf16[32,64,384]{2,1,0:T(8,128)(2,1)} %bitcast.76), calls=%async_computation.1 | async-start | bytes 3145728 | tf_op jit(solution)/shard_map/all_to_all | solution.py:1056
  195.9 56.9 %copy-start.27 = (s32[1,2048]{1,0:T(1,128)S(1)}, s32[1,2048]{1,0:T(1,128)}, u32[]{:S(2)}) copy-start(s32[1,2048]{1,0:T(1,128)} %param.19) | copy-start | bytes 24580
  249.4 10.1 copy-start.7
  249.4 104.4 %all-to-all-start = ((bf16[32,64,384]{2,1,0:T(8,128)(2,1)}), bf16[32,64,384]{2,1,0:T(8,128)(2,1)S(1)}, u32[]{:S(2)}, u32[]{:S(2)}) async-start(bf16[32,64,384]{2,1,0:T(8,128)(2,1)} %bitcast.75), calls=%async_computation | async-start | bytes 3145728 | tf_op jit(solution)/shard_map/all_to_all | solution.py:1056
  259.5 97.0 %collective-permute-start = (bf16[512,2048]{1,0:T(8,128)(2,1)}, bf16[512,2048]{1,0:T(8,128)(2,1)}, u32[]{:S(2)}, u32[]{:S(2)}) collective-permute-start(bf16[512,2048]{1,0:T(8,128)(2,1)} %get-tuple-element.61.refs_2_), channel_id=1, source_target_pairs={{0,1},{1,2},{2,3},{3,0},{4,5},{5,6},{6,7},{7,4},{8,9},{9,10},{10,1... | collective-permute-start | bytes 6291464 | tf_op jit(solution)/shard_map/ppermute | solution.py:1064
  353.8 46.7 %all-to-all-start.3 = ((bf16[32,64,256]{2,1,0:T(8,128)(2,1)}), bf16[32,64,256]{2,1,0:T(8,128)(2,1)S(1)}, u32[]{:S(2)}, u32[]{:S(2)}) async-start(bf16[32,64,256]{2,1,0:T(8,128)(2,1)} %get-tuple-element.59), calls=%async_computation.3 | async-start | bytes 2097152 | tf_op jit(solution)/shard_map/all_to_all | solution.py:1056
  400.5 7.1 copy-start.9
  400.5 33.0 %all-to-all-start.2 = ((bf16[32,64,256]{2,1,0:T(8,128)(2,1)}), bf16[32,64,256]{2,1,0:T(8,128)(2,1)S(1)}, u32[]{:S(2)}, u32[]{:S(2)}) async-start(bf16[32,64,256]{2,1,0:T(8,128)(2,1)} %get-tuple-element.66), calls=%async_computation.2 | async-start | bytes 2097152 | tf_op jit(solution)/shard_map/all_to_all | solution.py:1056
  407.3 464.0 %reduce-scatter.4.cloned.1.call-start = ((), (), s32[]{:S(2)}) async-start(), calls=%async_computation.11 | async-start | bytes 9437184 | tf_op jit(solution)/shard_map/reduce_scatter | solution.py:1118
  433.5 3.1 copy-start.10
  445.2 3.4 copy-start.2
  728.9 4.2 copy-start.3
  728.9 4.7 copy-start.5
  728.9 4.7 copy-start.17
  728.9 4.7 copy-start.22
  728.9 4.7 copy-start.24
  747.0 266.8 %reduce-scatter.6.cloned.1.call-start = ((), (), s32[]{:S(2)}) async-start(), calls=%async_computation.12 | async-start | bytes 28311552 | tf_op jit(solution)/shard_map/reduce_scatter | solution.py:1118
  861.3 87.4 %all-to-all-start.5 = ((bf16[32,64,384]{2,1,0:T(8,128)(2,1)}), bf16[32,64,384]{2,1,0:T(8,128)(2,1)}, u32[]{:S(2)}, u32[]{:S(2)}) async-start(bf16[32,64,384]{2,1,0:T(8,128)(2,1)} %attend_backward.2), calls=%async_computation.7 | async-start | bytes 3145728 | tf_op jit(solution)/shard_map/all_to_all | solution.py:1056
  865.9 314.3 %reduce-scatter.8.cloned.1.call-start = ((), (), s32[]{:S(2)}) async-start(), calls=%async_computation.13 | async-start | bytes 14155776 | tf_op jit(solution)/shard_map/reduce_scatter | solution.py:1118
  869.6 71.3 %collective-permute-start.1 = (bf16[512,2048]{1,0:T(8,128)(2,1)}, bf16[512,2048]{1,0:T(8,128)(2,1)}, u32[]{:S(2)}, u32[]{:S(2)}) collective-permute-start(bf16[512,2048]{1,0:T(8,128)(2,1)} %slice_bitcast_fusion), channel_id=1, source_target_pairs={{0,1},{1,2},{2,3},{3,0},{4,5},{5,6},{6,7},{7,4},{8,9},{9,10},{10,1... | collective-permute-start | bytes 6291464 | tf_op jit(solution)/shard_map/ppermute | solution.py:1064
  1025.5 6.6 copy-start.11
  1030.1 50.8 %collective-permute-start.2 = (bf16[512,2048]{1,0:T(8,128)(2,1)}, bf16[512,2048]{1,0:T(8,128)(2,1)}, u32[]{:S(2)}, u32[]{:S(2)}) collective-permute-start(bf16[512,2048]{1,0:T(8,128)(2,1)} %fusion.9), channel_id=1, source_target_pairs={{0,1},{1,2},{2,3},{3,0},{4,5},{5,6},{6,7},{7,4},{8,9},{9,10},{10,1... | collective-permute-start | bytes 6291464 | tf_op jit(solution)/shard_map/ppermute | solution.py:1064
  1033.0 53.4 %collective-permute-start.7 = (bf16[256,512]{1,0:T(8,128)(2,1)}, bf16[256,512]{1,0:T(8,128)(2,1)S(1)}, u32[]{:S(2)}, u32[]{:S(2)}) collective-permute-start(bf16[256,512]{1,0:T(8,128)(2,1)} %get-tuple-element.155), channel_id=1, source_target_pairs={{0,1},{1,2},{2,3},{3,0},{4,5},{5,6},{6,7},{7,4},{8,9},{9,10},{10,1... | collective-permute-start | bytes 786440 | tf_op jit(solution)/shard_map/ppermute | solution.py:1127
  1034.4 63.2 %collective-permute-start.8 = (bf16[256,512]{1,0:T(8,128)(2,1)}, bf16[256,512]{1,0:T(8,128)(2,1)S(1)}, u32[]{:S(2)}, u32[]{:S(2)}) collective-permute-start(bf16[256,512]{1,0:T(8,128)(2,1)} %get-tuple-element.157), channel_id=1, source_target_pairs={{0,2},{1,3},{2,0},{3,1},{4,6},{5,7},{6,4},{7,5},{8,10},{9,11},{10,... | collective-permute-start | bytes 786440 | tf_op jit(solution)/shard_map/ppermute | solution.py:1127
  1035.3 62.3 %collective-permute-start.9 = (bf16[256,512]{1,0:T(8,128)(2,1)S(1)}, bf16[256,512]{1,0:T(8,128)(2,1)}, u32[]{:S(2)}, u32[]{:S(2)}) collective-permute-start(bf16[256,512]{1,0:T(8,128)(2,1)S(1)} %get-tuple-element.156), channel_id=1, source_target_pairs={{0,3},{1,0},{2,1},{3,2},{4,7},{5,4},{6,5},{7,6},{8,11},{9,8},{10,9... | collective-permute-start | bytes 786440 | tf_op jit(solution)/shard_map/ppermute | solution.py:1127
  1063.6 21.8 %copy-start.30 = (s32[8]{0:T(128)S(1)}, s32[8]{0:T(128)}, u32[]{:S(2)}) copy-start(s32[8]{0:T(128)} %copy-done.29) | copy-start | bytes 100
  1063.6 36.1 %copy-start.19 = (f32[1,8,256]{2,0,1:T(1,128)S(1)}, f32[1,8,256]{2,0,1:T(1,128)}, u32[]{:S(2)}) copy-start(f32[1,8,256]{2,0,1:T(1,128)} %copy-done.18) | copy-start | bytes 24580
  1063.6 36.1 %copy-start.26 = (f32[512]{0:T(512)S(1)}, f32[512]{0:T(512)}, u32[]{:S(2)}) copy-start(f32[512]{0:T(512)} %copy-done.25) | copy-start | bytes 6148
  1085.3 79.3 %collective-permute-start.3 = (bf16[512,2048]{1,0:T(8,128)(2,1)}, bf16[512,2048]{1,0:T(8,128)(2,1)}, u32[]{:S(2)}, u32[]{:S(2)}) collective-permute-start(bf16[512,2048]{1,0:T(8,128)(2,1)} %fusion.8), channel_id=1, source_target_pairs={{0,1},{1,2},{2,3},{3,0},{4,5},{5,6},{6,7},{7,4},{8,9},{9,10},{10,1... | collective-permute-start | bytes 6291464 | tf_op jit(solution)/shard_map/ppermute | solution.py:1064
  1104.9 59.1 %all-to-all-start.6 = ((f32[32,2,256]{2,1,0:T(2,128)}), f32[32,2,256]{2,1,0:T(2,128)S(1)}, u32[]{:S(2)}, u32[]{:S(2)}) async-start(f32[32,2,256]{2,1,0:T(2,128)} %bitcast.34), calls=%async_computation.8 | async-start | bytes 131072 | tf_op jit(solution)/shard_map/all_to_all | solution.py:1171
  1176.6 10.7 copy-start.28
  1181.5 13.9 %collective-permute-start.4 = (bf16[256,768]{1,0:T(8,128)(2,1)S(1)}, bf16[256,768]{1,0:T(8,128)(2,1)S(1)}, u32[]{:S(2)}, u32[]{:S(2)}) collective-permute-start(bf16[256,768]{1,0:T(8,128)(2,1)S(1)} %get-tuple-element.152), channel_id=1, source_target_pairs={{0,1},{1,2},{2,3},{3,0},{4,5},{5,6},{6,7},{7,4},{8,9},{9,10},{10,1... | collective-permute-start | bytes 1179656 | tf_op jit(solution)/shard_map/ppermute | solution.py:1127
  1183.5 28.3 %collective-permute-start.5 = (bf16[256,768]{1,0:T(8,128)(2,1)S(1)}, bf16[256,768]{1,0:T(8,128)(2,1)S(1)}, u32[]{:S(2)}, u32[]{:S(2)}) collective-permute-start(bf16[256,768]{1,0:T(8,128)(2,1)S(1)} %get-tuple-element.154), channel_id=1, source_target_pairs={{0,2},{1,3},{2,0},{3,1},{4,6},{5,7},{6,4},{7,5},{8,10},{9,11},{10,... | collective-permute-start | bytes 1179656 | tf_op jit(solution)/shard_map/ppermute | solution.py:1127
  1185.9 25.9 %collective-permute-start.6 = (bf16[256,768]{1,0:T(8,128)(2,1)S(1)}, bf16[256,768]{1,0:T(8,128)(2,1)S(1)}, u32[]{:S(2)}, u32[]{:S(2)}) collective-permute-start(bf16[256,768]{1,0:T(8,128)(2,1)S(1)} %get-tuple-element.153), channel_id=1, source_target_pairs={{0,3},{1,0},{2,1},{3,2},{4,7},{5,4},{6,5},{7,6},{8,11},{9,8},{10,9... | collective-permute-start | bytes 1179656 | tf_op jit(solution)/shard_map/ppermute | solution.py:1127
  (8 other events, 13.4 us)
Sparse Core Ops, SparseCore 0:
  11.9 172.6 all-gather.3
  187.4 112.8 all-gather.5
  747.1 86.1 reduce-scatter.3
  837.2 176.5 reduce-scatter.5
  1025.7 91.8 reduce-scatter.7

commit v6 on v5

--- a/solution.py
+++ b/solution.py
@@ -4,7 +4,6 @@
 import jax.numpy as jnp
 from jax import lax
 from jax.experimental import pallas as pl
-from jax.experimental.layout import Layout, with_layout_constraint
 from jax.experimental.pallas import tpu as pltpu
 from jax.sharding import PartitionSpec as P
 
@@ -60,7 +59,7 @@
 def prepare(slots, perm, cos_t, sin_t, q_heads, kv_heads):
     page_rows, cols = slots.shape[1:]
     total_rows = slots.shape[0] * page_rows
-    lanes = 128
+    lanes = min(256, total_rows)
     pages_per = lanes // page_rows
 
     def page_spec(a):
@@ -713,8 +712,8 @@
 
 
 def collect_kernel(
-    tp_count, dp_count, hops, shard, gains, chunk, out, gains_out, chunks_out,
-    own_sem, ring_send, ring_recv, send, recv, gain_send, gain_recv, chunk_send, chunk_recv,
+    tp_count, dp_count, hops, shard, second, gains, chunk, out, second_out, gains_out, chunks_out,
+    second_send, second_recv, own_sem, ring_send, ring_recv, send, recv, gain_send, gain_recv, chunk_send, chunk_recv,
 ):
     my_dp = lax.axis_index("dp")
     my_tp = lax.axis_index("tensor")
@@ -740,6 +739,18 @@
     own.start()
     own_gain = pltpu.make_async_copy(gains, gains_out.at[my_dp], own_sem.at[1])
     own_gain.start()
+    own_second = pltpu.make_async_copy(second, second_out.at[my_tp], own_sem.at[2])
+    own_second.start()
+
+    def second_copy(j):
+        return pltpu.make_async_remote_copy(
+            src_ref=second,
+            dst_ref=second_out.at[my_tp],
+            send_sem=second_send.at[j],
+            recv_sem=second_recv.at[j],
+            device_id={"tensor": lax.rem(my_tp + j, tp_count)},
+            device_id_type=MESH,
+        )
 
     def across(j):
         return pltpu.make_async_remote_copy(
@@ -812,6 +823,9 @@
                 for s in range(2):
                     for m in range(1 << k):
                         within(j, s, k, m).start()
+        if phase == tp_count:
+            for j in range(1, tp_count):
+                second_copy(j).start()
         if tp_count <= phase < tp_count + hops - 1:
             onward(phase - tp_count).wait_recv()
             onward(phase - tp_count + 1).start()
@@ -823,6 +837,9 @@
                 for m in range(1 << k):
                     within(j, s, k, m).wait_send()
     own_gain.wait()
+    own_second.wait()
+    for j in range(1, tp_count):
+        second_copy(j).wait()
     for j in range(1, dp_count):
         gain_copy(j).wait()
     for hop in range(hops):
@@ -831,7 +848,7 @@
         onward(hop).wait_send()
 
 
-def collect(shard, gains, chunk, tp_count, dp_count, hops, collective_id):
+def collect(shard, second, gains, chunk, tp_count, dp_count, hops, collective_id):
     rows, cols = shard.shape
     dma = pltpu.SemaphoreType.DMA
     vmem_spec = pl.BlockSpec(memory_space=pltpu.VMEM)
@@ -840,13 +857,16 @@
         functools.partial(collect_kernel, tp_count, dp_count, hops),
         out_shape=[
             jax.ShapeDtypeStruct((tp_count, dp_count * rows, cols), shard.dtype),
+            jax.ShapeDtypeStruct((tp_count,) + second.shape, second.dtype),
             jax.ShapeDtypeStruct((dp_count,) + gains.shape, gains.dtype),
             jax.ShapeDtypeStruct((hops,) + chunk.shape, chunk.dtype),
         ],
-        in_specs=[vmem_spec, vmem_spec, any_spec],
-        out_specs=[any_spec] * 3,
+        in_specs=[vmem_spec, vmem_spec, vmem_spec, any_spec],
+        out_specs=[any_spec] * 4,
         scratch_shapes=[
-            dma((2,)),
+            dma((tp_count,)),
+            dma((tp_count,)),
+            dma((3,)),
             dma((tp_count,)),
             dma((tp_count,)),
             dma((tp_count, 2, dp_count - 1)),
@@ -861,7 +881,7 @@
             flops=0, bytes_accessed=16 * tp_count * dp_count * shard.size, transcendentals=0
         ),
         name="collect",
-    )(shard, gains, chunk)
+    )(shard, second, gains, chunk)
 
 
 def spread_kernel(rows, weight, out):
@@ -889,10 +909,12 @@
     )(rows, weights)
 
 
-def gather_kernel(part, weight, begin, out):
+def gather_kernel(has_begin, part, weight, *refs):
+    out = refs[-1]
+
     @pl.when(pl.program_id(0) == 0)
     def _():
-        out[...] = begin[...]
+        out[...] = refs[0][...] if has_begin else jnp.zeros_like(out)
 
     out[...] += dot_nt(part[0], weight[0])
 
@@ -900,15 +922,17 @@
 def gather_sum(parts, weights, part, begin):
     shards, count, cols = parts.shape
     width = weights.shape[1]
+    whole = pl.BlockSpec((count, width), lambda t: (0, 0))
+    begins = [] if begin is None else [begin]
     return pl.pallas_call(
-        gather_kernel,
+        functools.partial(gather_kernel, begin is not None),
         grid=(shards,),
         in_specs=[
             pl.BlockSpec((1, count, cols), lambda t: (t, 0, 0)),
             pl.BlockSpec((1, width, cols), lambda t: (t, 0, part)),
-            pl.BlockSpec((count, width), lambda t: (0, 0)),
-        ],
-        out_specs=pl.BlockSpec((count, width), lambda t: (0, 0)),
+        ]
+        + [whole] * len(begins),
+        out_specs=whole,
         out_shape=jax.ShapeDtypeStruct((count, width), f32),
         cost_estimate=pl.CostEstimate(
             flops=2 * shards * count * width * cols,
@@ -916,27 +940,32 @@
             transcendentals=0,
         ),
         name="gather_sum",
-    )(parts, weights, begin)
-
-
-def outer_kernel(rows, part, out, turned):
+    )(parts, weights, *begins)
+
+
+def outer_kernel(rows, *refs):
+    parts, out, turned = refs[:-2], refs[-2], refs[-1]
+
     @pl.when(pl.program_id(0) == 0)
     def _():
         turned[...] = rows[...].T
 
-    out[...] = dot_nn(turned[...], part[0]).astype(out.dtype)
+    at = 0
+    for part in parts:
+        cols = part.shape[2]
+        out[:, at : at + cols] = dot_nn(turned[...], part[0]).astype(out.dtype)
+        at += cols
 
 
 def outer(rows, parts):
-    shards, count, cols = parts.shape
+    shards, count, _ = parts[0].shape
+    cols = sum(part.shape[2] for part in parts)
     width = rows.shape[1]
     return pl.pallas_call(
         outer_kernel,
         grid=(shards,),
-        in_specs=[
-            pl.BlockSpec((count, width), lambda t: (0, 0)),
-            pl.BlockSpec((1, count, cols), lambda t: (t, 0, 0)),
-        ],
+        in_specs=[pl.BlockSpec((count, width), lambda t: (0, 0))]
+        + [pl.BlockSpec((1, count, part.shape[2]), lambda t: (t, 0, 0)) for part in parts],
         out_specs=pl.BlockSpec((width, cols), lambda t: (0, t)),
         out_shape=jax.ShapeDtypeStruct((width, shards * cols), bf16),
         scratch_shapes=[pltpu.VMEM((width, count), bf16)],
@@ -946,7 +975,7 @@
             transcendentals=0,
         ),
         name="outer",
-    )(rows, parts)
+    )(rows, *parts)
 
 
 def rms_scale(hidden):
@@ -1008,13 +1037,13 @@
 
     def reorder(rows, order):
         blocks = rows.reshape(dp_count, page_rows, rows.shape[1])
-        return jnp.take(blocks, order, axis=0).reshape(rows.shape)
+        return jnp.take(blocks, order, axis=0, mode="clip").reshape(rows.shape)
 
     hidden_in = reorder(tokens, send_order).astype(f32)
     grad_top = reorder(upstream, send_order).astype(f32)
     seq_lens = lengths[0]
     seq_ends = jnp.cumsum(seq_lens)
-    place = (jnp.take(dealt, send_order) % group_pages) * page_rows
+    place = (jnp.take(dealt, send_order, mode="clip") % group_pages) * page_rows
     place_rows = (place[:, None] + jnp.arange(page_rows, dtype=jnp.int32)[None, :]).reshape(-1)
     valid_rows = (place_rows < seq_ends[-1]).astype(f32)[:, None]
 
@@ -1047,10 +1076,6 @@
         axis=1,
     )
 
-    def gather_all(shard):
-        full = lax.all_gather(shard, everyone, axis=0, tiled=False)
-        return full.reshape(tp_count, dp_count * shard.shape[0], shard.shape[1])
-
     def trade(value):
         blocks = value.reshape(group_pages, page_rows, value.shape[-1])
         return lax.all_to_all(blocks, everyone, split_axis=0, concat_axis=0, tiled=True)
@@ -1068,9 +1093,11 @@
     mlp_shard = jnp.concatenate([w_gate, w_up, w_down.T], axis=1)
     w_mlp = lax.all_gather(mlp_shard, "dp", axis=0, tiled=True)
     hops = min(2, tp_count - 1)
-    w_qkv, gains, got_chunks = collect(
-        qkv_shard, jnp.stack([attn_gain, mlp_gain]), grad_chunks[0], tp_count, dp_count, hops, 1
+    w_qkv, out_shards, gains, got_chunks = collect(
+        qkv_shard, w_out.T, jnp.stack([attn_gain, mlp_gain]), grad_chunks[0], tp_count, dp_count,
+        hops, 1,
     )
+    w_out_t = lax.all_gather(out_shards, "dp", axis=1, tiled=True)
     grad_chunks += [got_chunks[hop] for hop in range(hops)]
     gains = gains.transpose(1, 0, 2).reshape(2, -1).astype(f32)
     gain_one, gain_two = gains[0], gains[1]
@@ -1081,8 +1108,6 @@
     for g in groups:
         qkv.append(spread(normed_one, w_qkv, g, group_q + 2 * HD))
         slots.append(trade(qkv[g]))
-    out_shard = with_layout_constraint(w_out.T, Layout(major_to_minor=(0, 1)))
-    w_out_t = gather_all(after(out_shard, w_qkv))
     saved, mixed = [], []
     last = qkv[-1]
     for hop in range(hops + 1, tp_count):
@@ -1128,7 +1153,7 @@
         return total
 
     grad_z = grad_mid.astype(bf16)
-    grad_wout = outer(grad_z, jnp.concatenate(mixed, axis=2))
+    grad_wout = outer(grad_z, mixed)
     sum_out = reduce_dp(grad_wout)
     grad_slots, grad_wmlp = weigh(
         spread(after(grad_z, grad_wout), w_out_t, 0, q_cols),
@@ -1140,23 +1165,23 @@
     for g in groups:
         q_t, k_rows, k_t, v_rows, o_t, lse = saved[g]
         back = attend_backward(
-            grad_slots if g == 0 else after(grad_slots, (back, sum_out)), g, q_t, k_rows, k_t,
-            v_rows, o_t, lse, begin, cos_t, sin_t, first_block, perm, page_rows, block_len,
-        )
-        grad_qkv.append(trade_back(after(back, branch_two) if g == len(groups) - 1 else back))
+            grad_slots if g == 0 else after(grad_slots, (back, sum_out)), g, q_t,
+            k_rows, k_t, v_rows, o_t, lse, begin, cos_t, sin_t, first_block, perm, page_rows,
+            block_len,
+        )
+        grad_qkv.append(trade_back(after(back, (grad_qkv[-1], branch_two)) if grad_qkv else back))
     hidden = sum_mlp.shape[1] // 3
-    grad_wqkv = outer(after(normed_one, sum_mlp), jnp.concatenate(grad_qkv, axis=2))
+    sum_out = reduce_tensor(sum_out)
+    for s in range(2, tp_count - 1):
+        branch_two = pass_on(add_on(after(branch_two, tuple(grad_qkv)), s))
+    grad_wqkv = outer(after(normed_one, (sum_mlp, sum_out)), grad_qkv)
     sum_qkv = reduce_tensor(reduce_dp(grad_wqkv))
     each = group_q + 2 * HD
     sum_qkv = [sum_qkv[:, g * each : (g + 1) * each] for g in groups]
-    branch_two = add_on(after(branch_two, grad_qkv[-1]), 2)
-    grad_normed_one = jnp.zeros((tok_dev, width), f32)
+    grad_normed_one = None
     for g in groups:
         grad_normed_one = gather_sum(after(grad_qkv[g], grad_wqkv), w_qkv, g, grad_normed_one)
-    for s in range(3, tp_count):
-        branch_two = add_on(after(pass_on(branch_two), grad_normed_one), s)
-    branch_two = pass_on(branch_two)
-    sum_out = reduce_tensor(sum_out)
+    branch_two = pass_on(add_on(after(branch_two, grad_normed_one), tp_count - 1))
     result = (
         (after(hidden_mid, back) + branch_two.astype(f32) + partial_two[0].astype(f32)) * valid_rows
     ).astype(bf16)

time: 1240 us -> 1160 us (0.935)
  starting transfers between devices: 94.7 us -> 49.7 us
  blocking collectives: 41.1 us -> 0 us
  Pallas kernels: 728 us -> 746 us
  waiting for transfers between devices: 223 us -> 239 us
  other arithmetic: 75.5 us -> 59.9 us
    all_to_all x1, starting transfers between devices: 51.4 us -> 5.1 us  [local(): lax.all_to_all(gain_parts, everyone, split_axis=0, concat_axis=0, tiled=T...]
    all_to_all x1 -> x0, blocking collectives: 41.1 us -> none  [trade(): lax.all_to_all(blocks, everyone, split_axis=0, concat_axis=0, tiled=True)]
    all_to_all x5 -> x6, waiting for transfers between devices: 119 us -> 83.7 us  [trade(): lax.all_to_all(blocks, everyone, split_axis=0, concat_axis=0, tiled=True)]
    all_to_all x1, waiting for transfers between devices: 0.01 us -> 33.1 us  [local(): lax.all_to_all(gain_parts, everyone, split_axis=0, concat_axis=0, tiled=T...]
    ppermute x6, waiting for transfers between devices: 32.6 us -> 59.1 us  [reduce_tensor(): total = total + lax.ppermute(block, 'tensor', pairs).astype(f32)]
    pallas_call x1, Pallas kernels: 138 us -> 159 us  [collect(): pl.pallas_call(functools.partial(collect_kernel, tp_count, dp_count, hops...]
    reduce_scatter x3, waiting for transfers between devices: 19.4 us -> 3.25 us  [reduce_dp(): lax.psum_scatter(grad.astype(bf16), 'dp', scatter_dimension=0, tiled=True)]
    all_to_all x5 -> x6, starting transfers between devices: 27.1 us -> 28.2 us  [trade(): lax.all_to_all(blocks, everyone, split_axis=0, concat_axis=0, tiled=True)]
  transfers between devices with their start and end apart: 21 -> 22, of which waited for: 11 -> 11; matrix products, arithmetic and copies ran while one was open for 7% -> 6% of each run, Pallas kernels for 34% -> 38%
where the time goes in v6:
time: 1160 us; the launch traced here: 1150 us
  Pallas kernels  746 us (64%)
  waiting for transfers between devices  239 us (21%)
  other arithmetic  59.9 us (5%)
  starting transfers between devices  49.7 us (4%)
  local copies, waits for them, and re-layouts  41.1 us (4%)
  between operations  14.9 us (1%)
    pallas_call x1, Pallas kernels, feed(): pl.pallas_call(functools.partial(feed_kernel, ring, min(tile, hidden)), o...  279 us
    pallas_call x1, Pallas kernels, collect(): pl.pallas_call(functools.partial(collect_kernel, tp_count, dp_count, hops...  159 us
    all_to_all x6, waiting for transfers between devices, trade(): lax.all_to_all(blocks, everyone, split_axis=0, concat_axis=0, tiled=True)  83.7 us
    pallas_call x2, Pallas kernels, attend_backward(): pl.pallas_call(functools.partial(backward_kernel, q_heads, kv_heads, page...  71.1 us
    pallas_call x2, Pallas kernels, attend_forward(): pl.pallas_call(functools.partial(forward_kernel, q_heads, kv_heads, page_...  69.1 us
    pallas_call x1, Pallas kernels, weigh(): pl.pallas_call(functools.partial(weigh_kernel, tp_count, dp_count, min(51...  67.4 us
    ppermute x4, waiting for transfers between devices, pass_on(): return lax.ppermute(value, 'tensor', ring_next)  59.7 us
    ppermute x6, waiting for transfers between devices, reduce_tensor(): total = total + lax.ppermute(block, 'tensor', pairs).astype(f32)  59.1 us
  transfers between devices with their start and end apart: 22, of which 11 were waited for; matrix products, arithmetic and copies ran while one was open for 6% of the time, Pallas kernels for 38%

profile of v6, /device:TPU:0, one launch (start us, length us, event | category | flops | bytes accessed | tf_op | source)
XLA Modules:
  0.0 1150.1 jit_solution(2145900791369262098)
XLA Ops:
  8.7 3.0 pad_maximum_fusion
  23.5 158.7 %collect.1 = (bf16[4,2048,768]{2,1,0:T(8,128)(2,1)}, bf16[4,256,512]{2,1,0:T(8,128)(2,1)}, bf16[8,2,256]{2,1,0:T(2,128)(2,1)}, bf16[2,512,2048]{2,1,0:T(8,128)(2,1)}) custom-call(bf16[256,768]{1,0:T(8,128)(2,1)} %concatenate.16.shard, bf16[256,512]{1,0:T(8,128)(2,1)} %bitcast.79, bf16[2,256]{1,0:T(2,128)(2,1)} %pad_maximum_fusion.4.gains, ...), custom_call_target="tpu_custom_call" | custom-call | bytes 100663296 | tf_op jit(solution)/shard_map/collect/pallas_call | solution.py:856
  187.2 8.2 spread.4
  195.5 8.7 all-to-all-start.1
  204.1 8.2 spread.3
  212.4 29.5 %all-to-all-done.1.refs_0_.refs_1_.refs_2_.refs_3_ = bf16[32,64,384]{2,1,0:T(8,128)(2,1)} async-done(((bf16[32,64,384]{2,1,0:T(8,128)(2,1)}), bf16[32,64,384]{2,1,0:T(8,128)(2,1)}, u32[]{:S(2)}, u32[]{:S(2)}) %all-to-all-start.1) | async-done | bytes 1572896 | tf_op jit(solution)/shard_map/all_to_all | solution.py:1081
  241.9 3.9 all-to-all-start
  248.4 4.8 slice_bitcast_fusion.1
  255.5 6.7 prepare.2
  262.2 34.6 %attend_forward.2 = (bf16[256,2048]{1,0:T(8,128)(2,1)}, f32[4,2048]{1,0:T(4,128)}, bf16[32,64,256]{2,1,0:T(8,128)(2,1)}) custom-call(s32[8]{0:T(128)} %and_select_fusion.4.first_block, s32[32]{0:T(128)} %fusion.13.perm, bf16[256,2048]{1,0:T(8,128)(2,1)} %get-tuple-element.55.q_t.refs_4_, bf16[1,2048,64]{2,1,0:T(8,128)(2,1)} %get-tuple-element.56.k_rows.refs_5_, ...), custom_call_target="tpu_custom_call" | custom-call | flops 1073741824 | bytes 4194304 | tf_op jit(solution)/shard_map/attend_forward/pallas_call | solution.py:162
  296.8 31.7 %all-to-all-done.refs_0_.refs_1_.refs_2_.refs_3_ = bf16[32,64,384]{2,1,0:T(8,128)(2,1)} async-done(((bf16[32,64,384]{2,1,0:T(8,128)(2,1)}), bf16[32,64,384]{2,1,0:T(8,128)(2,1)}, u32[]{:S(2)}, u32[]{:S(2)}) %all-to-all-start) | async-done | bytes 1572896 | tf_op jit(solution)/shard_map/all_to_all | solution.py:1081
  331.2 6.7 prepare.3
  337.8 34.5 %attend_forward.3 = (bf16[256,2048]{1,0:T(8,128)(2,1)}, f32[4,2048]{1,0:T(4,128)}, bf16[32,64,256]{2,1,0:T(8,128)(2,1)}) custom-call(s32[8]{0:T(128)} %and_select_fusion.4.first_block, s32[32]{0:T(128)} %fusion.13.perm, bf16[256,2048]{1,0:T(8,128)(2,1)} %get-tuple-element.62.q_t.refs_4_, bf16[1,2048,64]{2,1,0:T(8,128)(2,1)} %get-tuple-element.63.k_rows.refs_5_, ...), custom_call_target="tpu_custom_call" | custom-call | flops 1073741824 | bytes 4194304 | tf_op jit(solution)/shard_map/attend_forward/pallas_call | solution.py:162
  372.3 6.0 all-to-all-start.2
  381.2 8.6 gather_sum.4.refs_0_
  389.8 14.8 %all-to-all-done.2 = bf16[32,64,256]{2,1,0:T(8,128)(2,1)} async-done(((bf16[32,64,256]{2,1,0:T(8,128)(2,1)}), bf16[32,64,256]{2,1,0:T(8,128)(2,1)}, u32[]{:S(2)}, u32[]{:S(2)}) %all-to-all-start.2) | async-done | bytes 1048608 | tf_op jit(solution)/shard_map/all_to_all | solution.py:1081
  404.5 8.5 gather_sum.5
  418.3 278.5 %feed_forward.1 = (bf16[2048,2048]{1,0:T(8,128)(2,1)}, bf16[2048,2048]{1,0:T(8,128)(2,1)}, bf16[4,512,2048]{2,1,0:T(8,128)(2,1)}, bf16[4,512,4096]{2,1,0:T(8,128...) custom-call(bf16[512,2048]{1,0:T(8,128)(2,1)} %multiply_convert_fusion.own_rows, ...), custom_call_target="tpu_custom_call" | custom-call | flops 103079215104 | bytes 33554432 | tf_op jit(solution)/shard_map/feed_forward/pallas_call | solution.py:544
  696.8 4.2 fusion.5
  701.5 3.9 fusion.20.rows
  705.4 9.3 outer.2
  714.8 9.3 spread.5.grads
  726.0 67.4 %weigh.1 = (bf16[32,64,512]{2,1,0:T(8,128)(2,1)S(1)}, bf16[2048,6144]{1,0:T(8,128)(2,1)}) custom-call(bf16[4,512,512]{2,1,0:T(8,128)(2,1)S(1)} %copy-done.1, bf16[2048,2048]{1,0:T(8,128)(2,1)} %get-tuple-element.69.rows_t, bf16[2048,2048]{1,0:T(8,128)(2,1)} %get-tuple-element.70.grads_t, bf16[4,512,4096]{2,1,0:T(8,128)(2,1)} %get-tuple-element.71.gate_up, ...), custom_call_target="tpu_custom_call" | custom-call | flops 51539607552 | bytes 41943040 | tf_op jit(solution)/shard_map/weigh/pallas_call | solution.py:683
  794.7 35.5 %attend_backward.2 = bf16[32,64,384]{2,1,0:T(8,128)(2,1)} custom-call(s32[8]{0:T(128)} %and_select_fusion.4.first_block, s32[32]{0:T(128)} %fusion.13.perm, bf16[32,64,512]{2,1,0:T(8,128)(2,1)} %copy-done, bf16[32,64,512]{2,1,0:T(8,128)(2,1)} %copy-done, bf16[32,64,512]{2,1,0:T(8,128)(2,1)} %copy-done, bf16[32,64,512]{2,1,0:T(8,128)(2,1)} %copy-done, ...), custom_call_target="tpu_custom_call" | custom-call | flops 3221225472 | bytes 6291456 | tf_op jit(solution)/shard_map/attend_backward/pallas_call | solution.py:321
  830.3 4.1 all-to-all-start.4
  834.4 3.7 slice_bitcast_fusion
  839.8 35.5 %attend_backward.3 = bf16[32,64,384]{2,1,0:T(8,128)(2,1)} custom-call(s32[8]{0:T(128)} %and_select_fusion.4.first_block, s32[32]{0:T(128)} %fusion.13.perm, bf16[32,64,512]{2,1,0:T(8,128)(2,1)} %copy-done, bf16[32,64,512]{2,1,0:T(8,128)(2,1)} %copy-done, bf16[32,64,512]{2,1,0:T(8,128)(2,1)} %copy-done, bf16[32,64,512]{2,1,0:T(8,128)(2,1)} %copy-done, ...), custom_call_target="tpu_custom_call" | custom-call | flops 3221225472 | bytes 6291456 | tf_op jit(solution)/shard_map/attend_backward/pallas_call | solution.py:321
  875.4 34.1 %collective-permute-done.1 = bf16[512,2048]{1,0:T(8,128)(2,1)} collective-permute-done((bf16[512,2048]{1,0:T(8,128)(2,1)}, bf16[512,2048]{1,0:T(8,128)(2,1)}, u32[]{:S(2)}, u32[]{:S(2)}) %collective-permute-start.1) | collective-permute-done | bytes 2097184 | tf_op jit(solution)/shard_map/ppermute | solution.py:1089
  909.5 7.8 all-to-all-done.4
  917.3 2.9 all-to-all-start.5
  927.8 28.6 %collective-permute-done.3 = bf16[256,512]{1,0:T(8,128)(2,1)} collective-permute-done((bf16[256,512]{1,0:T(8,128)(2,1)}, bf16[256,512]{1,0:T(8,128)(2,1)}, u32[]{:S(2)}, u32[]{:S(2)}) %collective-permute-start.3) | collective-permute-done | bytes 262176 | tf_op jit(solution)/shard_map/ppermute | solution.py:1152
  956.4 19.1 %collective-permute-done.4 = bf16[256,512]{1,0:T(8,128)(2,1)} collective-permute-done((bf16[256,512]{1,0:T(8,128)(2,1)}, bf16[256,512]{1,0:T(8,128)(2,1)}, u32[]{:S(2)}, u32[]{:S(2)}) %collective-permute-start.4) | collective-permute-done | bytes 262176 | tf_op jit(solution)/shard_map/ppermute | solution.py:1152
  977.7 3.2 reduce-scatter.6.cloned.1.call-done
  982.1 13.9 %outer.3 = bf16[2048,3072]{1,0:T(8,128)(2,1)} custom-call(bf16[512,2048]{1,0:T(8,128)(2,1)} %multiply_convert_fusion.1.rows, bf16[4,512,384]{2,1,0:T(8,128)(2,1)} %bitcast.65, bf16[4,512,384]{2,1,0:T(8,128)(2,1)} %bitcast.67), custom_call_target="tpu_custom_call" | custom-call | flops 6442450944 | bytes 12582912 | tf_op jit(solution)/shard_map/outer/pallas_call | solution.py:964
  996.0 4.4 fusion.9
  1003.0 10.2 gather_sum.6.refs_0_
  1013.2 11.3 gather_sum.7
  1024.6 25.6 %collective-permute-done.2 = bf16[512,2048]{1,0:T(8,128)(2,1)} collective-permute-done((bf16[512,2048]{1,0:T(8,128)(2,1)}, bf16[512,2048]{1,0:T(8,128)(2,1)}, u32[]{:S(2)}, u32[]{:S(2)}) %collective-permute-start.2) | collective-permute-done | bytes 2097184 | tf_op jit(solution)/shard_map/ppermute | solution.py:1089
  1050.1 4.5 fusion.8
  1056.3 3.3 multiply_reduce_fusion
  1060.2 5.1 all-to-all-start.6
  1065.3 5.2 convert_bitcast_fusion
  1070.5 2.9 copy.43
  1073.4 33.1 %all-to-all-done.6 = f32[32,2,256]{2,1,0:T(2,128)S(1)} async-done(((f32[32,2,256]{2,1,0:T(2,128)}), f32[32,2,256]{2,1,0:T(2,128)S(1)}, u32[]{:S(2)}, u32[]{:S(2)}) %all-to-all-start.6) | async-done | bytes 65568 | tf_op jit(solution)/shard_map/all_to_all | solution.py:1196
  1109.8 3.2 collective-permute-start.9
  1113.0 9.0 add_convert_fusion
  1122.0 3.7 gather_fusion.4
  1127.7 11.4 collective-permute-done.8
  (160 shorter events, 64.4 us)
Async XLA Ops:
  7.2 324.0 %all-gather.3.cloned.1.call-start = ((), (), s32[]{:S(2)}) async-start(), calls=%async_computation.10 | async-start | bytes 28311552 | tf_op jit(solution)/shard_map/all_gather | solution.py:1094
  11.7 7.3 copy-start.13
  11.7 8.3 copy-start.33
  11.7 8.4 copy-start.34
  11.7 8.4 copy-start.14
  11.7 8.4 copy-start.15
  11.8 8.4 copy-start.16
  11.8 369.4 %all-gather.5.cloned.1.call-start = ((), (), s32[]{:S(2)}) async-start(), calls=%async_computation.11 | async-start | bytes 9437184 | tf_op jit(solution)/shard_map/all_gather | solution.py:1100
  16.8 6.7 copy-start.24
  19.1 163.1 %copy-start.6 = (bf16[8,64,2048]{2,1,0:T(8,128)(2,1)}, bf16[8,64,2048]{2,1,0:T(8,128)(2,1)S(1)}, u32[]{:S(2)}) copy-start(bf16[8,64,2048]{2,1,0:T(8,128)(2,1)S(1)} %gather_fusion.1) | copy-start | bytes 6291460
  184.7 193.8 %copy-start.4 = (bf16[8,64,2048]{2,1,0:T(8,128)(2,1)}, bf16[8,64,2048]{2,1,0:T(8,128)(2,1)S(1)}, u32[]{:S(2)}) copy-start(bf16[8,64,2048]{2,1,0:T(8,128)(2,1)S(1)} %gather_fusion) | copy-start | bytes 6291460
  185.3 10.1 copy-start.26
  185.4 10.1 copy-start.19
  185.4 230.4 %copy-start.17 = (f32[1,8,256]{2,0,1:T(1,128)}, f32[1,8,256]{2,0,1:T(1,128)S(1)}, u32[]{:S(2)}) copy-start(f32[1,8,256]{2,0,1:T(1,128)S(1)} %get-tuple-element.167) | copy-start | bytes 24580
  195.5 46.5 %all-to-all-start.1 = ((bf16[32,64,384]{2,1,0:T(8,128)(2,1)}), bf16[32,64,384]{2,1,0:T(8,128)(2,1)}, u32[]{:S(2)}, u32[]{:S(2)}) async-start(bf16[32,64,384]{2,1,0:T(8,128)(2,1)} %bitcast.70), calls=%async_computation.1 | async-start | bytes 3145728 | tf_op jit(solution)/shard_map/all_to_all | solution.py:1081
  204.1 41.7 %copy-start.29 = (s32[1,2048]{1,0:T(1,128)S(1)}, s32[1,2048]{1,0:T(1,128)}, u32[]{:S(2)}) copy-start(s32[1,2048]{1,0:T(1,128)} %param.17) | copy-start | bytes 24580
  241.9 86.5 %all-to-all-start = ((bf16[32,64,384]{2,1,0:T(8,128)(2,1)}), bf16[32,64,384]{2,1,0:T(8,128)(2,1)}, u32[]{:S(2)}, u32[]{:S(2)}) async-start(bf16[32,64,384]{2,1,0:T(8,128)(2,1)} %bitcast.69), calls=%async_computation | async-start | bytes 3145728 | tf_op jit(solution)/shard_map/all_to_all | solution.py:1081
  245.9 7.3 copy-start.21
  253.2 77.9 %collective-permute-start = (bf16[512,2048]{1,0:T(8,128)(2,1)}, bf16[512,2048]{1,0:T(8,128)(2,1)}, u32[]{:S(2)}, u32[]{:S(2)}) collective-permute-start(bf16[512,2048]{1,0:T(8,128)(2,1)} %get-tuple-element.60.refs_2_), channel_id=1, source_target_pairs={{0,1},{1,2},{2,3},{3,0},{4,5},{5,6},{6,7},{7,4},{8,9},{9,10},{10,1... | collective-permute-start | bytes 6291464 | tf_op jit(solution)/shard_map/ppermute | solution.py:1089
  328.5 43.9 %all-to-all-start.3 = ((bf16[32,64,256]{2,1,0:T(8,128)(2,1)}), bf16[32,64,256]{2,1,0:T(8,128)(2,1)S(1)}, u32[]{:S(2)}, u32[]{:S(2)}) async-start(bf16[32,64,256]{2,1,0:T(8,128)(2,1)} %get-tuple-element.58), calls=%async_computation.3 | async-start | bytes 2097152 | tf_op jit(solution)/shard_map/all_to_all | solution.py:1081
  372.3 8.9 copy-start.11
  372.3 32.2 %all-to-all-start.2 = ((bf16[32,64,256]{2,1,0:T(8,128)(2,1)}), bf16[32,64,256]{2,1,0:T(8,128)(2,1)}, u32[]{:S(2)}, u32[]{:S(2)}) async-start(bf16[32,64,256]{2,1,0:T(8,128)(2,1)} %get-tuple-element.65), calls=%async_computation.2 | async-start | bytes 2097152 | tf_op jit(solution)/shard_map/all_to_all | solution.py:1081
  378.3 461.5 %reduce-scatter.4.cloned.1.call-start = ((), (), s32[]{:S(2)}) async-start(), calls=%async_computation.12 | async-start | bytes 9437184 | tf_op jit(solution)/shard_map/reduce_scatter | solution.py:1143
  696.8 4.2 copy-start.3
  696.8 4.7 copy-start.7
  696.8 4.7 copy-start.18
  696.8 4.7 copy-start.23
  696.8 4.7 copy-start.25
  714.7 266.2 %reduce-scatter.6.cloned.1.call-start = ((), (), s32[]{:S(2)}) async-start(), calls=%async_computation.13 | async-start | bytes 28311552 | tf_op jit(solution)/shard_map/reduce_scatter | solution.py:1143
  830.3 87.0 %all-to-all-start.4 = ((bf16[32,64,384]{2,1,0:T(8,128)(2,1)}), bf16[32,64,384]{2,1,0:T(8,128)(2,1)S(1)}, u32[]{:S(2)}, u32[]{:S(2)}) async-start(bf16[32,64,384]{2,1,0:T(8,128)(2,1)} %attend_backward.2), calls=%async_computation.5 | async-start | bytes 3145728 | tf_op jit(solution)/shard_map/all_to_all | solution.py:1081
  838.0 71.5 %collective-permute-start.1 = (bf16[512,2048]{1,0:T(8,128)(2,1)}, bf16[512,2048]{1,0:T(8,128)(2,1)}, u32[]{:S(2)}, u32[]{:S(2)}) collective-permute-start(bf16[512,2048]{1,0:T(8,128)(2,1)} %slice_bitcast_fusion), channel_id=1, source_target_pairs={{0,1},{1,2},{2,3},{3,0},{4,5},{5,6},{6,7},{7,4},{8,9},{9,10},{10,1... | collective-permute-start | bytes 6291464 | tf_op jit(solution)/shard_map/ppermute | solution.py:1089
  917.3 63.7 %copy-start.9 = (bf16[32,64,384]{2,1,0:T(8,128)(2,1)}, bf16[32,64,384]{2,1,0:T(8,128)(2,1)S(1)}, u32[]{:S(2)}) copy-start(bf16[32,64,384]{2,1,0:T(8,128)(2,1)S(1)} %all-to-all-done.4) | copy-start | bytes 4718596
  917.3 63.7 %all-to-all-start.5 = ((bf16[32,64,384]{2,1,0:T(8,128)(2,1)}), bf16[32,64,384]{2,1,0:T(8,128)(2,1)S(1)}, u32[]{:S(2)}, u32[]{:S(2)}) async-start(bf16[32,64,384]{2,1,0:T(8,128)(2,1)} %attend_backward.3), calls=%async_computation.6 | async-start | bytes 3145728 | tf_op jit(solution)/shard_map/all_to_all | solution.py:1081
  920.2 186.9 %reduce-scatter.8.cloned.1.call-start = ((), (), s32[]{:S(2)}) async-start(), calls=%async_computation.14 | async-start | bytes 14155776 | tf_op jit(solution)/shard_map/reduce_scatter | solution.py:1143
  922.2 34.2 %collective-permute-start.3 = (bf16[256,512]{1,0:T(8,128)(2,1)}, bf16[256,512]{1,0:T(8,128)(2,1)}, u32[]{:S(2)}, u32[]{:S(2)}) collective-permute-start(bf16[256,512]{1,0:T(8,128)(2,1)} %get-tuple-element.152), channel_id=1, source_target_pairs={{0,1},{1,2},{2,3},{3,0},{4,5},{5,6},{6,7},{7,4},{8,9},{9,10},{10,1... | collective-permute-start | bytes 786440 | tf_op jit(solution)/shard_map/ppermute | solution.py:1152
  924.0 51.5 %collective-permute-start.4 = (bf16[256,512]{1,0:T(8,128)(2,1)}, bf16[256,512]{1,0:T(8,128)(2,1)}, u32[]{:S(2)}, u32[]{:S(2)}) collective-permute-start(bf16[256,512]{1,0:T(8,128)(2,1)} %get-tuple-element.154), channel_id=1, source_target_pairs={{0,2},{1,3},{2,0},{3,1},{4,6},{5,7},{6,4},{7,5},{8,10},{9,11},{10,... | collective-permute-start | bytes 786440 | tf_op jit(solution)/shard_map/ppermute | solution.py:1152
  926.4 49.1 %collective-permute-start.5 = (bf16[256,512]{1,0:T(8,128)(2,1)S(1)}, bf16[256,512]{1,0:T(8,128)(2,1)}, u32[]{:S(2)}, u32[]{:S(2)}) collective-permute-start(bf16[256,512]{1,0:T(8,128)(2,1)S(1)} %get-tuple-element.153), channel_id=1, source_target_pairs={{0,3},{1,0},{2,1},{3,2},{4,7},{5,4},{6,5},{7,6},{8,11},{9,8},{10,9... | collective-permute-start | bytes 786440 | tf_op jit(solution)/shard_map/ppermute | solution.py:1152
  1000.4 49.7 %collective-permute-start.2 = (bf16[512,2048]{1,0:T(8,128)(2,1)}, bf16[512,2048]{1,0:T(8,128)(2,1)}, u32[]{:S(2)}, u32[]{:S(2)}) collective-permute-start(bf16[512,2048]{1,0:T(8,128)(2,1)} %fusion.9), channel_id=1, source_target_pairs={{0,1},{1,2},{2,3},{3,0},{4,5},{5,6},{6,7},{7,4},{8,9},{9,10},{10,1... | collective-permute-start | bytes 6291464 | tf_op jit(solution)/shard_map/ppermute | solution.py:1089
  1024.5 30.7 %copy-start.30 = (s32[8]{0:T(128)S(1)}, s32[8]{0:T(128)}, u32[]{:S(2)}) copy-start(s32[8]{0:T(128)} %get-tuple-element.142) | copy-start | bytes 100
  1024.5 30.7 %copy-start.12 = (f32[256,512]{1,0:T(8,128)S(1)}, f32[256,512]{1,0:T(8,128)}, u32[]{:S(2)}) copy-start(f32[256,512]{1,0:T(8,128)} %convert_add_fusion.4) | copy-start | bytes 1572868
  1024.5 31.7 %copy-start.5 = (bf16[8,64,2048]{2,1,0:T(8,128)(2,1)S(1)}, bf16[8,64,2048]{2,1,0:T(8,128)(2,1)}, u32[]{:S(2)}) copy-start(bf16[8,64,2048]{2,1,0:T(8,128)(2,1)} %copy-done.4) | copy-start | bytes 6291460
  1024.5 31.7 %copy-start.20 = (f32[1,8,256]{2,0,1:T(1,128)S(1)}, f32[1,8,256]{2,0,1:T(1,128)}, u32[]{:S(2)}) copy-start(f32[1,8,256]{2,0,1:T(1,128)} %copy-done.19) | copy-start | bytes 24580
  1024.6 31.7 %copy-start.27 = (f32[512]{0:T(512)S(1)}, f32[512]{0:T(512)}, u32[]{:S(2)}) copy-start(f32[512]{0:T(512)} %copy-done.26) | copy-start | bytes 6148
  1054.7 58.3 %collective-permute-start.6 = (bf16[512,2048]{1,0:T(8,128)(2,1)}, bf16[512,2048]{1,0:T(8,128)(2,1)}, u32[]{:S(2)}, u32[]{:S(2)}) collective-permute-start(bf16[512,2048]{1,0:T(8,128)(2,1)} %fusion.8), channel_id=1, source_target_pairs={{0,1},{1,2},{2,3},{3,0},{4,5},{5,6},{6,7},{7,4},{8,9},{9,10},{10,1... | collective-permute-start | bytes 6291464 | tf_op jit(solution)/shard_map/ppermute | solution.py:1089
  1060.2 46.2 %all-to-all-start.6 = ((f32[32,2,256]{2,1,0:T(2,128)}), f32[32,2,256]{2,1,0:T(2,128)S(1)}, u32[]{:S(2)}, u32[]{:S(2)}) async-start(f32[32,2,256]{2,1,0:T(2,128)} %bitcast.33), calls=%async_computation.8 | async-start | bytes 131072 | tf_op jit(solution)/shard_map/all_to_all | solution.py:1196
  1109.1 18.6 %collective-permute-start.7 = (bf16[256,768]{1,0:T(8,128)(2,1)}, bf16[256,768]{1,0:T(8,128)(2,1)S(1)}, u32[]{:S(2)}, u32[]{:S(2)}) collective-permute-start(bf16[256,768]{1,0:T(8,128)(2,1)} %get-tuple-element.149), channel_id=1, source_target_pairs={{0,1},{1,2},{2,3},{3,0},{4,5},{5,6},{6,7},{7,4},{8,9},{9,10},{10,1... | collective-permute-start | bytes 1179656 | tf_op jit(solution)/shard_map/ppermute | solution.py:1152
  1109.8 29.3 %collective-permute-start.8 = (bf16[256,768]{1,0:T(8,128)(2,1)S(1)}, bf16[256,768]{1,0:T(8,128)(2,1)}, u32[]{:S(2)}, u32[]{:S(2)}) collective-permute-start(bf16[256,768]{1,0:T(8,128)(2,1)S(1)} %get-tuple-element.151), channel_id=1, source_target_pairs={{0,2},{1,3},{2,0},{3,1},{4,6},{5,7},{6,4},{7,5},{8,10},{9,11},{10,... | collective-permute-start | bytes 1179656 | tf_op jit(solution)/shard_map/ppermute | solution.py:1152
  1109.8 29.3 %collective-permute-start.9 = (bf16[256,768]{1,0:T(8,128)(2,1)S(1)}, bf16[256,768]{1,0:T(8,128)(2,1)}, u32[]{:S(2)}, u32[]{:S(2)}) collective-permute-start(bf16[256,768]{1,0:T(8,128)(2,1)S(1)} %get-tuple-element.150), channel_id=1, source_target_pairs={{0,3},{1,0},{2,1},{3,2},{4,7},{5,4},{6,5},{7,6},{8,11},{9,8},{10,9... | collective-permute-start | bytes 1179656 | tf_op jit(solution)/shard_map/ppermute | solution.py:1152
  (9 other events, 24.2 us)
Sparse Core Ops, SparseCore 0:
  11.9 172.5 all-gather.2
  186.5 82.6 all-gather.4
  714.8 86.1 reduce-scatter.3
  804.9 175.9 reduce-scatter.5
  996.1 93.2 reduce-scatter.7

commit v7 on v6

--- a/solution.py
+++ b/solution.py
@@ -14,7 +14,8 @@
 theta_base = 500000.0
 masked_score = -1e30
 score_scale = HD**-0.5
-block_rows = 256
+block_rows = 512
+key_rows = 256
 MESH = pl.DeviceIdType.MESH
 f32 = jnp.float32
 bf16 = jnp.bfloat16
@@ -56,15 +57,16 @@
         v_rows[g] = rows[:, v_base + g * HD : v_base + (g + 1) * HD].astype(bf16)
 
 
-def prepare(slots, perm, cos_t, sin_t, q_heads, kv_heads):
-    page_rows, cols = slots.shape[1:]
+def prepare(slots, part, perm, cos_t, sin_t, q_heads, kv_heads):
+    page_rows = slots.shape[1]
+    cols = (q_heads + 2 * kv_heads) * HD
     total_rows = slots.shape[0] * page_rows
     lanes = min(256, total_rows)
     pages_per = lanes // page_rows
 
     def page_spec(a):
         return pl.BlockSpec(
-            (1, page_rows, cols), lambda i, perm_ref, a=a: (perm_ref[i * pages_per + a], 0, 0)
+            (1, page_rows, cols), lambda i, perm_ref, a=a: (perm_ref[i * pages_per + a], 0, part)
         )
 
     table = pl.BlockSpec((HALF, lanes), lambda i, perm_ref: (0, i))
@@ -96,51 +98,61 @@
     )(perm, *([slots] * pages_per), cos_t, sin_t)
 
 
-def block_bias(i, j, begin_row, block_len):
-    keys = j * block_len + lax.broadcasted_iota(jnp.int32, (block_len, block_len), 0)
-    queries = i * block_len + lax.broadcasted_iota(jnp.int32, (block_len, block_len), 1)
+def block_bias(i, j, begin_row, block_len, key_len):
+    keys = j * key_len + lax.broadcasted_iota(jnp.int32, (key_len, block_len), 0)
+    queries = i * block_len + lax.broadcasted_iota(jnp.int32, (key_len, block_len), 1)
     allowed = (keys >= begin_row) & (keys <= queries)
     return jnp.where(allowed, 0.0, masked_score)
 
 
 def forward_kernel(
     q_heads, kv_heads, page_rows, first_block, perm,
-    q_t, k_rows, v_t, begin, o_t, lse, o_slots, acc, top, total, stage, sems,
+    q_t, k_rows, v_t, begin, o_t, lse, o_slots, acc, stage, sems,
 ):
     i = pl.program_id(0)
     block_len = q_t.shape[1]
+    key_len = min(key_rows, k_rows.shape[1])
     per_group = q_heads // kv_heads
     acc[...] = jnp.zeros_like(acc)
-    top[...] = jnp.full_like(top, masked_score)
-    total[...] = jnp.zeros_like(total)
     begin_row = begin[...]
 
     def visit(j, carry):
-        bias = block_bias(i, j, begin_row, block_len)
-        at = pl.ds(pl.multiple_of(j * block_len, block_len), block_len)
+        bias = block_bias(i, j, begin_row, block_len, key_len)
+        at = pl.ds(pl.multiple_of(j * key_len, key_len), key_len)
+        scores = [
+            dot_nn(k_rows[h // per_group, at, :], q_t[h * HD : (h + 1) * HD, :]) + bias
+            for h in range(q_heads)
+        ]
+        tops = [
+            jnp.maximum(carry[h][0], jnp.max(scores[h], axis=0, keepdims=True))
+            for h in range(q_heads)
+        ]
+        weights = [jnp.exp(scores[h] - tops[h]) for h in range(q_heads)]
+        fades = [jnp.exp(carry[h][0] - tops[h]) for h in range(q_heads)]
+        totals = [
+            carry[h][1] * fades[h] + jnp.sum(weights[h], axis=0, keepdims=True)
+            for h in range(q_heads)
+        ]
         for h in range(q_heads):
             g = h // per_group
             span = slice(h * HD, (h + 1) * HD)
-            scores = dot_nn(k_rows[g, at, :], q_t[span, :]) + bias
-            old = top[h : h + 1, :]
-            new = jnp.maximum(old, jnp.max(scores, axis=0, keepdims=True))
-            weights = jnp.exp(scores - new)
-            fade = jnp.exp(old - new)
-            total[h : h + 1, :] = total[h : h + 1, :] * fade + jnp.sum(
-                weights, axis=0, keepdims=True
+            acc[span, :] = acc[span, :] * fades[h] + dot_nn(
+                v_t[g * HD : (g + 1) * HD, at], weights[h].astype(bf16)
             )
-            top[h : h + 1, :] = new
-            acc[span, :] = acc[span, :] * fade + dot_nn(
-                v_t[g * HD : (g + 1) * HD, at], weights.astype(bf16)
-            )
-        return carry
-
-    lax.fori_loop(first_block[i], i + 1, visit, 0)
-    lse[...] = top[...] + jnp.log(total[...])
-    scaled = [
-        acc[h * HD : (h + 1) * HD, :] / total[h : h + 1, :] for h in range(q_heads)
-    ]
-    mixed = jnp.concatenate(scaled, axis=0)
+        return tuple(zip(tops, totals))
+
+    start = tuple(
+        (jnp.full((1, block_len), masked_score, f32), jnp.zeros((1, block_len), f32))
+        for _ in range(q_heads)
+    )
+    stats = lax.fori_loop(
+        first_block[i], lax.div((i + 1) * block_len - 1, key_len) + 1, visit, start
+    )
+    for h in range(q_heads):
+        lse[h : h + 1, :] = stats[h][0] + jnp.log(stats[h][1])
+    mixed = jnp.concatenate(
+        [acc[h * HD : (h + 1) * HD, :] / stats[h][1] for h in range(q_heads)], axis=0
+    )
     o_t[...] = mixed.astype(bf16)
     pages = block_len // page_rows
     stage[...] = mixed.T.astype(bf16).reshape(pages, page_rows, q_heads * HD)
@@ -177,8 +189,6 @@
             ],
             scratch_shapes=[
                 pltpu.VMEM((q_heads * HD, block_len), f32),
-                pltpu.VMEM((q_heads, block_len), f32),
-                pltpu.VMEM((q_heads, block_len), f32),
                 pltpu.VMEM((pages, page_rows, q_heads * HD), bf16),
                 pltpu.SemaphoreType.DMA((pages,)),
             ],
@@ -208,6 +218,7 @@
     i = pl.program_id(0)
     steps = pl.num_programs(0)
     block_len = q_t.shape[1]
+    key_len = min(key_rows, k_rows.shape[1])
     per_group = q_heads // kv_heads
     q_cols = q_heads * HD
     kv_cols = kv_heads * HD
@@ -232,28 +243,31 @@
     begin_row = begin[...]
 
     def visit(j, carry):
-        bias = block_bias(i, j, begin_row, block_len)
-        at = pl.ds(pl.multiple_of(j * block_len, block_len), block_len)
+        bias = block_bias(i, j, begin_row, block_len, key_len)
+        at = pl.ds(pl.multiple_of(j * key_len, key_len), key_len)
         for g in range(kv_heads):
             kv_span = slice(g * HD, (g + 1) * HD)
             keys, vals, keys_t = k_rows[g, at, :], v_rows[g, at, :], k_t[kv_span, at]
-            add_k = jnp.zeros((HD, block_len), f32)
-            add_v = jnp.zeros((HD, block_len), f32)
-            for h in range(g * per_group, (g + 1) * per_group):
-                span = slice(h * HD, (h + 1) * HD)
-                queries = q_t[span, :]
-                probs = jnp.exp(dot_nn(keys, queries) + bias - lse[h : h + 1, :])
-                grad_h = grad_low[span]
-                grad_probs = dot_nn(vals, grad_h)
-                grad_scores = (probs * (grad_probs - inner[h])).astype(bf16)
-                add_v = add_v + dot_nt(grad_h, probs.astype(bf16))
-                add_k = add_k + dot_nt(queries, grad_scores)
-                grad_q[span, :] = grad_q[span, :] + dot_nn(keys_t, grad_scores)
-            grad_k[kv_span, at] = grad_k[kv_span, at] + add_k
-            grad_v[kv_span, at] = grad_v[kv_span, at] + add_v
+            heads = range(g * per_group, (g + 1) * per_group)
+            spans = [slice(h * HD, (h + 1) * HD) for h in heads]
+            scores = [dot_nn(keys, q_t[span, :]) + bias for span in spans]
+            grad_probs = [dot_nn(vals, grad_low[span]) for span in spans]
+            probs = [jnp.exp(s - lse[h : h + 1, :]) for s, h in zip(scores, heads)]
+            grad_scores = [
+                (p * (d - inner[h])).astype(bf16) for p, d, h in zip(probs, grad_probs, heads)
+            ]
+            low_probs = [p.astype(bf16) for p in probs]
+            grad_v[kv_span, at] += sum(
+                dot_nt(grad_low[span], p) for span, p in zip(spans, low_probs)
+            )
+            grad_k[kv_span, at] += sum(
+                dot_nt(q_t[span, :], d) for span, d in zip(spans, grad_scores)
+            )
+            for span, d in zip(spans, grad_scores):
+                grad_q[span, :] += dot_nn(keys_t, d)
         return carry
 
-    lax.fori_loop(first_block[i], i + 1, visit, 0)
+    lax.fori_loop(first_block[i], lax.div((i + 1) * block_len - 1, key_len) + 1, visit, 0)
 
     def unrope(value, cos, sin):
         first, second = value[:HALF], value[HALF:]
@@ -359,6 +373,102 @@
         first_block, perm, *([grad_slots] * pages), q_t, k_rows, k_t, v_rows, o_t, lse, begin,
         cos_t, sin_t, cos_t, sin_t,
     )
+
+
+def project_kernel(
+    tp_count, dp_count, rows, weights, slots, held, stage, load_sem, own_sem, send, recv
+):
+    count = dp_count * tp_count
+    my_dp = lax.axis_index("dp")
+    my_tp = lax.axis_index("tensor")
+    me = my_dp * tp_count + my_tp
+    page_rows = slots.shape[1]
+
+    def load(j):
+        shard = lax.rem(my_tp + 1 + j, tp_count)
+        return pltpu.make_async_copy(weights.at[shard], held.at[j % 2], load_sem.at[j % 2])
+
+    load(0).start()
+    barrier = pltpu.get_barrier_semaphore()
+
+    def greet(j, carry):
+        peer = lax.rem(me + j, count)
+        pl.semaphore_signal(
+            barrier,
+            inc=1,
+            device_id={"dp": lax.div(peer, tp_count), "tensor": lax.rem(peer, tp_count)},
+            device_id_type=MESH,
+        )
+        return carry
+
+    lax.fori_loop(1, count, greet, 0)
+    pl.semaphore_wait(barrier, count - 1)
+    home = slots.at[my_tp * dp_count + my_dp]
+
+    def copy_to(j, off):
+        p_dp = lax.rem(my_dp + off, dp_count)
+        return pltpu.make_async_remote_copy(
+            src_ref=stage.at[j, pl.ds(p_dp * page_rows, page_rows), :],
+            dst_ref=home,
+            send_sem=send.at[j, off],
+            recv_sem=recv.at[j, off],
+            device_id={"dp": p_dp, "tensor": lax.rem(my_tp + 1 + j, tp_count)},
+            device_id_type=MESH,
+        )
+
+    def each(j, act):
+        def one(off, carry):
+            act(copy_to(j, off))
+            return carry
+
+        lax.fori_loop(1 if j == tp_count - 1 else 0, dp_count, one, 0)
+
+    for j in range(tp_count):
+        load(j).wait()
+        if j + 1 < tp_count:
+            load(j + 1).start()
+        stage[j] = dot_nn(rows[...], held[j % 2]).astype(bf16)
+        if j > 0:
+            each(j - 1, lambda copy: copy.start())
+    each(tp_count - 1, lambda copy: copy.start())
+    own = pltpu.make_async_copy(
+        stage.at[tp_count - 1, pl.ds(my_dp * page_rows, page_rows), :], home, own_sem
+    )
+    own.start()
+    own.wait()
+    for j in range(tp_count):
+        each(j, lambda copy: copy.wait())
+
+
+def project(rows, weights, dp_count, collective_id):
+    tp_count, width, cols = weights.shape
+    total = rows.shape[0]
+    page_rows = total // dp_count
+    any_spec = pl.BlockSpec(memory_space=pl.ANY)
+    dma = pltpu.SemaphoreType.DMA
+    return pl.pallas_call(
+        functools.partial(project_kernel, tp_count, dp_count),
+        out_shape=jax.ShapeDtypeStruct((tp_count * dp_count, page_rows, cols), bf16),
+        in_specs=[pl.BlockSpec(memory_space=pltpu.VMEM), any_spec],
+        out_specs=any_spec,
+        scratch_shapes=[
+            pltpu.VMEM((2, width, cols), bf16),
+            pltpu.VMEM((tp_count, total, cols), bf16),
+            dma((2,)),
+            dma,
+            dma((tp_count, dp_count)),
+            dma((tp_count, dp_count)),
+        ],
+        compiler_params=pltpu.CompilerParams(
+            collective_id=collective_id, has_side_effects=True, vmem_limit_bytes=32 * 1024 * 1024
+        ),
+        cost_estimate=pl.CostEstimate(
+            flops=2 * tp_count * total * width * cols,
+            bytes_accessed=16 * tp_count * width * cols,
+            transcendentals=0,
+        ),
+        name="project",
+    )(rows, weights)
 
 
 def feed_kernel(
@@ -1052,7 +1162,7 @@
         jnp.where(row_ids[:, None] >= seq_ends[None, :], seq_ends[None, :], 0), axis=1
     ).astype(jnp.int32)
     block_len = min(block_rows, tok_group)
-    first_block = begin[::block_len] // block_len
+    first_block = begin[::block_len] // min(key_rows, tok_group)
     begin = begin[None, :]
     inverse_freq = theta_base ** (-(jnp.arange(HALF, dtype=f32) * 2.0) / HD)
     angles = inverse_freq[:, None] * positions.astype(f32)
@@ -1104,25 +1214,19 @@
 
     scale_one = rms_scale(hidden_in)
     normed_one = (hidden_in * scale_one * gain_one).astype(bf16)
-    qkv, slots = [], []
+    slots = project(normed_one, w_qkv, dp_count, 3)
+    for hop in range(hops + 1, tp_count):
+        grad_chunks.append(pass_on(after(grad_chunks[-1], slots)))
+    saved, mixed = [], []
     for g in groups:
-        qkv.append(spread(normed_one, w_qkv, g, group_q + 2 * HD))
-        slots.append(trade(qkv[g]))
-    saved, mixed = [], []
-    last = qkv[-1]
-    for hop in range(hops + 1, tp_count):
-        grad_chunks.append(pass_on(after(grad_chunks[-1], slots[0])))
-    for g in groups:
-        if g == len(groups) - 1:
-            last = (last, w_mlp, grad_chunks[-1])
         q_t, k_t, k_rows, v_t, v_rows = prepare(
-            after(slots[g], last), perm, cos_t, sin_t, per_group, 1
-        )
-        o_t, lse, last = attend_forward(
+            after(slots, (o_slots, w_mlp)) if g else slots, g, perm, cos_t, sin_t, per_group, 1
+        )
+        o_t, lse, o_slots = attend_forward(
             q_t, k_rows, v_t, begin, first_block, perm, page_rows, block_len
         )
         saved.append((q_t, k_rows, k_t, v_rows, o_t, lse))
-        mixed.append(trade_back(last))
+        mixed.append(trade_back(after(o_slots, grad_chunks[-1]) if g else o_slots))
     hidden_mid = hidden_in
     for g in groups:
         hidden_mid = gather_sum(mixed[g], w_out_t, g, hidden_mid)

time: 1160 us -> 1140 us (0.983)
  waiting for transfers between devices: 239 us -> 203 us
    pallas_call x0 -> x1, Pallas kernels: none -> 69.1 us  [project(): pl.pallas_call(functools.partial(project_kernel, tp_count, dp_count), out...]
    all_to_all x6 -> x4, waiting for transfers between devices: 83.7 us -> 33.7 us  [trade(): lax.all_to_all(blocks, everyone, split_axis=0, concat_axis=0, tiled=True)]
    pallas_call x2, Pallas kernels: 69.1 us -> 35.8 us  [attend_forward(): pl.pallas_call(functools.partial(forward_kernel, q_heads, kv_heads, page_...]
    pallas_call x2, Pallas kernels: 71.1 us -> 52.3 us  [attend_backward(): pl.pallas_call(functools.partial(backward_kernel, q_heads, kv_heads, page...]
    pallas_call x3 -> x1, Pallas kernels: 25.7 us -> 9.2 us  [spread(): pl.pallas_call(spread_kernel, grid=(shards,), in_specs=[pl.BlockSpec((cou...]
    ppermute x4, starting transfers between devices: 6.61 us -> 21.5 us  [pass_on(): return lax.ppermute(value, 'tensor', ring_next)]
    all_to_all x6 -> x4, starting transfers between devices: 28.2 us -> 21.5 us  [trade(): lax.all_to_all(blocks, everyone, split_axis=0, concat_axis=0, tiled=True)]
  transfers between devices with their start and end apart: 22 -> 20, of which waited for: 11 -> 10; matrix products, arithmetic and copies ran while one was open for 6% -> 6% of each run, Pallas kernels for 38% -> 39%
where the time goes in v7:
time: 1140 us; the launch traced here: 1120 us
  Pallas kernels  746 us (65%)
  waiting for transfers between devices  203 us (18%)
  other arithmetic  58.1 us (5%)
  starting transfers between devices  57.7 us (5%)
  local copies, waits for them, and re-layouts  44.6 us (4%)
  between operations  14.9 us (1%)
    pallas_call x1, Pallas kernels, feed(): pl.pallas_call(functools.partial(feed_kernel, ring, min(tile, hidden)), o...  278 us
    pallas_call x1, Pallas kernels, collect(): pl.pallas_call(functools.partial(collect_kernel, tp_count, dp_count, hops...  159 us
    ppermute x4, waiting for transfers between devices, pass_on(): return lax.ppermute(value, 'tensor', ring_next)  69.6 us
    pallas_call x1, Pallas kernels, project(): pl.pallas_call(functools.partial(project_kernel, tp_count, dp_count), out...  69.1 us
    pallas_call x1, Pallas kernels, weigh(): pl.pallas_call(functools.partial(weigh_kernel, tp_count, dp_count, min(51...  67.5 us
    ppermute x6, waiting for transfers between devices, reduce_tensor(): total = total + lax.ppermute(block, 'tensor', pairs).astype(f32)  59.3 us
    pallas_call x2, Pallas kernels, attend_backward(): pl.pallas_call(functools.partial(backward_kernel, q_heads, kv_heads, page...  52.3 us
    pallas_call x4, Pallas kernels, gather_sum(): pl.pallas_call(functools.partial(gather_kernel, begin is not None), grid=...  38.6 us
  transfers between devices with their start and end apart: 20, of which 10 were waited for; matrix products, arithmetic and copies ran while one was open for 6% of the time, Pallas kernels for 39%

profile of v7, /device:TPU:0, one launch (start us, length us, event | category | flops | bytes accessed | tf_op | source)
XLA Modules:
  0.0 1123.8 jit_solution(3998574340849063910)
XLA Ops:
  8.7 3.0 pad_maximum_fusion
  23.5 158.7 %collect.1 = (bf16[4,2048,768]{2,1,0:T(8,128)(2,1)}, bf16[4,256,512]{2,1,0:T(8,128)(2,1)}, bf16[8,2,256]{2,1,0:T(2,128)(2,1)}, bf16[2,512,2048]{2,1,0:T(8,128)(2,1)}) custom-call(bf16[256,768]{1,0:T(8,128)(2,1)} %concatenate.16.shard, bf16[256,512]{1,0:T(8,128)(2,1)} %bitcast.75, bf16[2,256]{1,0:T(2,128)(2,1)} %pad_maximum_fusion.4.gains, ...), custom_call_target="tpu_custom_call" | custom-call | bytes 100663296 | tf_op jit(solution)/shard_map/collect/pallas_call | solution.py:966
  186.0 5.3 copy-done.2
  191.3 69.1 %project.1.refs_0_.refs_1_.refs_2_.refs_3_ = bf16[32,64,768]{2,1,0:T(8,128)(2,1)S(1)} custom-call(bf16[512,2048]{1,0:T(8,128)(2,1)S(1)} %multiply_convert_fusion.1.rows, bf16[4,2048,768]{2,1,0:T(8,128)(2,1)S(1)} %copy-done.2), custom_call_target="tpu_custom_call" | custom-call | flops 6442450944 | bytes 100663296 | tf_op jit(solution)/shard_map/project/pallas_call | solution.py:449
  260.5 3.0 slice_bitcast_fusion.1
  263.5 17.6 %collective-permute-start = (bf16[512,2048]{1,0:T(8,128)(2,1)}, bf16[512,2048]{1,0:T(8,128)(2,1)}, u32[]{:S(2)}, u32[]{:S(2)}) collective-permute-start(bf16[512,2048]{1,0:T(8,128)(2,1)} %get-tuple-element.64.refs_2_), channel_id=1, source_target_pairs={{0,1},{1,2},{2,3},{3,0},{4,5},{5,6},{6,7},{7,4},{8,9},{9,10},{10,1... | collective-permute-start | bytes 6291464 | tf_op jit(solution)/shard_map/ppermute | solution.py:1199
  283.7 6.7 prepare.2
  290.9 18.0 %attend_forward.2 = (bf16[256,2048]{1,0:T(8,128)(2,1)}, f32[4,2048]{1,0:T(4,128)}, bf16[32,64,256]{2,1,0:T(8,128)(2,1)}) custom-call(s32[4]{0:T(128)} %and_select_fusion.4.first_block, s32[32]{0:T(128)} %fusion.13.perm, bf16[256,2048]{1,0:T(8,128)(2,1)} %get-tuple-element.54.q_t.refs_8_, bf16[1,2048,64]{2,1,0:T(8,128)(2,1)} %get-tuple-element.55.k_rows.refs_9_, ...), custom_call_target="tpu_custom_call" | custom-call | flops 1073741824 | bytes 4194304 | tf_op jit(solution)/shard_map/attend_forward/pallas_call | solution.py:174
  308.9 5.8 all-to-all-start.1
  314.7 6.7 prepare.3
  321.4 17.8 %attend_forward.3 = (bf16[256,2048]{1,0:T(8,128)(2,1)}, f32[4,2048]{1,0:T(4,128)}, bf16[32,64,256]{2,1,0:T(8,128)(2,1)}) custom-call(s32[4]{0:T(128)} %and_select_fusion.4.first_block, s32[32]{0:T(128)} %fusion.13.perm, bf16[256,2048]{1,0:T(8,128)(2,1)} %get-tuple-element.59.q_t.refs_8_, bf16[1,2048,64]{2,1,0:T(8,128)(2,1)} %get-tuple-element.60.k_rows.refs_9_, ...), custom_call_target="tpu_custom_call" | custom-call | flops 1073741824 | bytes 4194304 | tf_op jit(solution)/shard_map/attend_forward/pallas_call | solution.py:174
  339.3 11.0 all-to-all-done.1
  350.3 3.4 all-to-all-start
  356.4 8.6 gather_sum.4.refs_0_
  365.0 14.9 %all-to-all-done = bf16[32,64,256]{2,1,0:T(8,128)(2,1)} async-done(((bf16[32,64,256]{2,1,0:T(8,128)(2,1)}), bf16[32,64,256]{2,1,0:T(8,128)(2,1)}, u32[]{:S(2)}, u32[]{:S(2)}) %all-to-all-start) | async-done | bytes 1048608 | tf_op jit(solution)/shard_map/all_to_all | solution.py:1191
  379.9 8.5 gather_sum.5
  388.4 2.7 multiply_reduce_fusion.2
  393.6 278.3 %feed_forward.1 = (bf16[2048,2048]{1,0:T(8,128)(2,1)}, bf16[2048,2048]{1,0:T(8,128)(2,1)}, bf16[4,512,2048]{2,1,0:T(8,128)(2,1)}, bf16[4,512,4096]{2,1,0:T(8,128...) custom-call(bf16[512,2048]{1,0:T(8,128)(2,1)} %multiply_convert_fusion.own_rows, ...), custom_call_target="tpu_custom_call" | custom-call | flops 103079215104 | bytes 33554432 | tf_op jit(solution)/shard_map/feed_forward/pallas_call | solution.py:654
  671.9 4.2 fusion.5
  676.6 3.9 fusion.20.rows
  680.5 9.2 outer.2
  689.8 9.2 spread.1.grads
  701.0 67.5 %weigh.1 = (bf16[32,64,512]{2,1,0:T(8,128)(2,1)S(1)}, bf16[2048,6144]{1,0:T(8,128)(2,1)}) custom-call(bf16[4,512,512]{2,1,0:T(8,128)(2,1)S(1)} %copy-done.4, bf16[2048,2048]{1,0:T(8,128)(2,1)} %get-tuple-element.69.rows_t, bf16[2048,2048]{1,0:T(8,128)(2,1)} %get-tuple-element.70.grads_t, bf16[4,512,4096]{2,1,0:T(8,128)(2,1)} %get-tuple-element.71.gate_up, ...), custom_call_target="tpu_custom_call" | custom-call | flops 51539607552 | bytes 41943040 | tf_op jit(solution)/shard_map/weigh/pallas_call | solution.py:793
  769.8 26.0 %attend_backward.2 = bf16[32,64,384]{2,1,0:T(8,128)(2,1)} custom-call(s32[4]{0:T(128)} %and_select_fusion.4.first_block, s32[32]{0:T(128)} %fusion.13.perm, bf16[32,64,512]{2,1,0:T(8,128)(2,1)} %copy-done, bf16[32,64,512]{2,1,0:T(8,128)(2,1)} %copy-done, bf16[32,64,512]{2,1,0:T(8,128)(2,1)} %copy-done, bf16[32,64,512]{2,1,0:T(8,128)(2,1)} %copy-done, ...), custom_call_target="tpu_custom_call" | custom-call | flops 3221225472 | bytes 6291456 | tf_op jit(solution)/shard_map/attend_backward/pallas_call | solution.py:335
  795.9 9.4 all-to-all-start.2
  805.3 3.7 slice_bitcast_fusion
  810.6 26.2 %attend_backward.3 = bf16[32,64,384]{2,1,0:T(8,128)(2,1)} custom-call(s32[4]{0:T(128)} %and_select_fusion.4.first_block, s32[32]{0:T(128)} %fusion.13.perm, bf16[32,64,512]{2,1,0:T(8,128)(2,1)} %copy-done, bf16[32,64,512]{2,1,0:T(8,128)(2,1)} %copy-done, bf16[32,64,512]{2,1,0:T(8,128)(2,1)} %copy-done, bf16[32,64,512]{2,1,0:T(8,128)(2,1)} %copy-done, ...), custom_call_target="tpu_custom_call" | custom-call | flops 3221225472 | bytes 6291456 | tf_op jit(solution)/shard_map/attend_backward/pallas_call | solution.py:335
  836.9 43.5 %collective-permute-done.1 = bf16[512,2048]{1,0:T(8,128)(2,1)} collective-permute-done((bf16[512,2048]{1,0:T(8,128)(2,1)}, bf16[512,2048]{1,0:T(8,128)(2,1)}, u32[]{:S(2)}, u32[]{:S(2)}) %collective-permute-start.1) | collective-permute-done | bytes 2097184 | tf_op jit(solution)/shard_map/ppermute | solution.py:1199
  880.3 7.8 all-to-all-done.2
  888.1 2.9 all-to-all-start.3
  898.7 28.6 %collective-permute-done.3 = bf16[256,512]{1,0:T(8,128)(2,1)} collective-permute-done((bf16[256,512]{1,0:T(8,128)(2,1)}, bf16[256,512]{1,0:T(8,128)(2,1)}, u32[]{:S(2)}, u32[]{:S(2)}) %collective-permute-start.3) | collective-permute-done | bytes 262176 | tf_op jit(solution)/shard_map/ppermute | solution.py:1256
  927.3 19.0 %collective-permute-done.4 = bf16[256,512]{1,0:T(8,128)(2,1)} collective-permute-done((bf16[256,512]{1,0:T(8,128)(2,1)}, bf16[256,512]{1,0:T(8,128)(2,1)}, u32[]{:S(2)}, u32[]{:S(2)}) %collective-permute-start.4) | collective-permute-done | bytes 262176 | tf_op jit(solution)/shard_map/ppermute | solution.py:1256
  948.4 7.6 reduce-scatter.6.cloned.1.call-done
  957.1 13.6 %outer.3 = bf16[2048,3072]{1,0:T(8,128)(2,1)} custom-call(bf16[512,2048]{1,0:T(8,128)(2,1)} %copy-done.3, bf16[4,512,384]{2,1,0:T(8,128)(2,1)} %bitcast.63, bf16[4,512,384]{2,1,0:T(8,128)(2,1)} %bitcast.65), custom_call_target="tpu_custom_call" | custom-call | flops 6442450944 | bytes 12582912 | tf_op jit(solution)/shard_map/outer/pallas_call | solution.py:1074
  970.8 4.4 fusion.9
  977.0 10.4 gather_sum.6.refs_0_
  987.4 11.1 gather_sum.7
  998.5 26.1 %collective-permute-done.2 = bf16[512,2048]{1,0:T(8,128)(2,1)} collective-permute-done((bf16[512,2048]{1,0:T(8,128)(2,1)}, bf16[512,2048]{1,0:T(8,128)(2,1)}, u32[]{:S(2)}, u32[]{:S(2)}) %collective-permute-start.2) | collective-permute-done | bytes 2097184 | tf_op jit(solution)/shard_map/ppermute | solution.py:1199
  1024.7 4.4 fusion.8
  1030.5 3.3 multiply_reduce_fusion
  1034.5 4.8 all-to-all-start.4
  1039.3 5.1 convert_bitcast_fusion
  1044.4 2.9 copy.43
  1047.3 32.7 %all-to-all-done.4 = f32[32,2,256]{2,1,0:T(2,128)S(1)} async-done(((f32[32,2,256]{2,1,0:T(2,128)}), f32[32,2,256]{2,1,0:T(2,128)S(1)}, u32[]{:S(2)}, u32[]{:S(2)}) %all-to-all-start.4) | async-done | bytes 65568 | tf_op jit(solution)/shard_map/all_to_all | solution.py:1300
  1083.3 3.4 collective-permute-start.9
  1086.7 8.7 add_convert_fusion
  1095.4 3.7 gather_fusion.4
  1101.1 11.7 %collective-permute-done.8 = bf16[256,768]{1,0:T(8,128)(2,1)} collective-permute-done((bf16[256,768]{1,0:T(8,128)(2,1)S(1)}, bf16[256,768]{1,0:T(8,128)(2,1)}, u32[]{:S(2)}, u32[]{:S(2)}) %collective-permute-start.8) | collective-permute-done | bytes 393248 | tf_op jit(solution)/shard_map/ppermute | solution.py:1256
  (163 shorter events, 54.8 us)
Async XLA Ops:
  7.2 307.6 %all-gather.3.cloned.1.call-start = ((), (), s32[]{:S(2)}) async-start(), calls=%async_computation.8 | async-start | bytes 28311552 | tf_op jit(solution)/shard_map/all_gather | solution.py:1204
  11.7 7.3 copy-start.17
  11.7 8.4 copy-start.37
  11.7 8.4 copy-start.38
  11.7 8.4 copy-start.18
  11.7 8.4 copy-start.19
  11.8 8.4 copy-start.20
  11.8 344.6 %all-gather.5.cloned.1.call-start = ((), (), s32[]{:S(2)}) async-start(), calls=%async_computation.9 | async-start | bytes 9437184 | tf_op jit(solution)/shard_map/all_gather | solution.py:1210
  16.8 6.7 copy-start.28
  19.1 163.2 %copy-start.9 = (bf16[8,64,2048]{2,1,0:T(8,128)(2,1)}, bf16[8,64,2048]{2,1,0:T(8,128)(2,1)S(1)}, u32[]{:S(2)}) copy-start(bf16[8,64,2048]{2,1,0:T(8,128)(2,1)S(1)} %gather_fusion.1) | copy-start | bytes 6291460
  184.8 169.0 %copy-start.7 = (bf16[8,64,2048]{2,1,0:T(8,128)(2,1)}, bf16[8,64,2048]{2,1,0:T(8,128)(2,1)S(1)}, u32[]{:S(2)}) copy-start(bf16[8,64,2048]{2,1,0:T(8,128)(2,1)S(1)} %gather_fusion) | copy-start | bytes 6291460
  185.3 75.1 %copy-start.30 = (f32[512]{0:T(512)}, f32[512]{0:T(512)S(1)}, u32[]{:S(2)}) copy-start(f32[512]{0:T(512)S(1)} %rsqrt.20) | copy-start | bytes 6148
  185.4 75.0 %copy-start.23 = (f32[1,8,256]{2,0,1:T(1,128)}, f32[1,8,256]{2,0,1:T(1,128)S(1)}, u32[]{:S(2)}) copy-start(f32[1,8,256]{2,0,1:T(1,128)S(1)} %get-tuple-element.168) | copy-start | bytes 24580
  185.4 205.7 %copy-start.21 = (f32[1,8,256]{2,0,1:T(1,128)}, f32[1,8,256]{2,0,1:T(1,128)S(1)}, u32[]{:S(2)}) copy-start(f32[1,8,256]{2,0,1:T(1,128)S(1)} %get-tuple-element.167) | copy-start | bytes 24580
  186.0 74.5 %copy-start.3 = (bf16[512,2048]{1,0:T(8,128)(2,1)}, bf16[512,2048]{1,0:T(8,128)(2,1)S(1)}, u32[]{:S(2)}) copy-start(bf16[512,2048]{1,0:T(8,128)(2,1)S(1)} %multiply_convert_fusion.1.rows) | copy-start | bytes 6291460
  186.0 5.3 copy-start.2
  191.3 69.1 %copy-start.15 = (bf16[2,512,2048]{2,1,0:T(8,128)(2,1)S(1)}, bf16[2,512,2048]{2,1,0:T(8,128)(2,1)}, u32[]{:S(2)}) copy-start(bf16[2,512,2048]{2,1,0:T(8,128)(2,1)} %get-tuple-element.63) | copy-start | bytes 12582916
  260.4 20.6 %copy-start.33 = (s32[1,2048]{1,0:T(1,128)S(1)}, s32[1,2048]{1,0:T(1,128)}, u32[]{:S(2)}) copy-start(s32[1,2048]{1,0:T(1,128)} %param.17) | copy-start | bytes 24580
  263.5 75.8 %collective-permute-start = (bf16[512,2048]{1,0:T(8,128)(2,1)}, bf16[512,2048]{1,0:T(8,128)(2,1)}, u32[]{:S(2)}, u32[]{:S(2)}) collective-permute-start(bf16[512,2048]{1,0:T(8,128)(2,1)} %get-tuple-element.64.refs_2_), channel_id=1, source_target_pairs={{0,1},{1,2},{2,3},{3,0},{4,5},{5,6},{6,7},{7,4},{8,9},{9,10},{10,1... | collective-permute-start | bytes 6291464 | tf_op jit(solution)/shard_map/ppermute | solution.py:1199
  281.2 9.2 copy-start.25
  308.9 41.4 %all-to-all-start.1 = ((bf16[32,64,256]{2,1,0:T(8,128)(2,1)}), bf16[32,64,256]{2,1,0:T(8,128)(2,1)S(1)}, u32[]{:S(2)}, u32[]{:S(2)}) async-start(bf16[32,64,256]{2,1,0:T(8,128)(2,1)} %get-tuple-element.57), calls=%async_computation.1 | async-start | bytes 2097152 | tf_op jit(solution)/shard_map/all_to_all | solution.py:1191
  350.3 6.1 copy-start.14
  350.3 29.6 %all-to-all-start = ((bf16[32,64,256]{2,1,0:T(8,128)(2,1)}), bf16[32,64,256]{2,1,0:T(8,128)(2,1)}, u32[]{:S(2)}, u32[]{:S(2)}) async-start(bf16[32,64,256]{2,1,0:T(8,128)(2,1)} %get-tuple-element.65), calls=%async_computation | async-start | bytes 2097152 | tf_op jit(solution)/shard_map/all_to_all | solution.py:1191
  353.7 456.9 %reduce-scatter.4.cloned.1.call-start = ((), (), s32[]{:S(2)}) async-start(), calls=%async_computation.10 | async-start | bytes 9437184 | tf_op jit(solution)/shard_map/reduce_scatter | solution.py:1247
  671.9 4.7 copy-start.10
  671.9 4.7 copy-start.22
  671.9 4.7 copy-start.27
  671.9 4.7 copy-start.29
  689.8 266.2 %reduce-scatter.6.cloned.1.call-start = ((), (), s32[]{:S(2)}) async-start(), calls=%async_computation.11 | async-start | bytes 28311552 | tf_op jit(solution)/shard_map/reduce_scatter | solution.py:1247
  795.9 92.2 %all-to-all-start.2 = ((bf16[32,64,384]{2,1,0:T(8,128)(2,1)}), bf16[32,64,384]{2,1,0:T(8,128)(2,1)S(1)}, u32[]{:S(2)}, u32[]{:S(2)}) async-start(bf16[32,64,384]{2,1,0:T(8,128)(2,1)} %attend_backward.2), calls=%async_computation.3 | async-start | bytes 3145728 | tf_op jit(solution)/shard_map/all_to_all | solution.py:1191
  808.9 71.4 %collective-permute-start.1 = (bf16[512,2048]{1,0:T(8,128)(2,1)}, bf16[512,2048]{1,0:T(8,128)(2,1)}, u32[]{:S(2)}, u32[]{:S(2)}) collective-permute-start(bf16[512,2048]{1,0:T(8,128)(2,1)} %slice_bitcast_fusion), channel_id=1, source_target_pairs={{0,1},{1,2},{2,3},{3,0},{4,5},{5,6},{6,7},{7,4},{8,9},{9,10},{10,1... | collective-permute-start | bytes 6291464 | tf_op jit(solution)/shard_map/ppermute | solution.py:1199
  888.1 67.9 %copy-start.12 = (bf16[32,64,384]{2,1,0:T(8,128)(2,1)}, bf16[32,64,384]{2,1,0:T(8,128)(2,1)S(1)}, u32[]{:S(2)}) copy-start(bf16[32,64,384]{2,1,0:T(8,128)(2,1)S(1)} %all-to-all-done.2) | copy-start | bytes 4718596
  888.1 67.9 %all-to-all-start.3 = ((bf16[32,64,384]{2,1,0:T(8,128)(2,1)}), bf16[32,64,384]{2,1,0:T(8,128)(2,1)S(1)}, u32[]{:S(2)}, u32[]{:S(2)}) async-start(bf16[32,64,384]{2,1,0:T(8,128)(2,1)} %attend_backward.3), calls=%async_computation.4 | async-start | bytes 3145728 | tf_op jit(solution)/shard_map/all_to_all | solution.py:1191
  891.0 189.5 %reduce-scatter.8.cloned.1.call-start = ((), (), s32[]{:S(2)}) async-start(), calls=%async_computation.12 | async-start | bytes 14155776 | tf_op jit(solution)/shard_map/reduce_scatter | solution.py:1247
  893.1 34.2 %collective-permute-start.3 = (bf16[256,512]{1,0:T(8,128)(2,1)}, bf16[256,512]{1,0:T(8,128)(2,1)}, u32[]{:S(2)}, u32[]{:S(2)}) collective-permute-start(bf16[256,512]{1,0:T(8,128)(2,1)} %get-tuple-element.152), channel_id=1, source_target_pairs={{0,1},{1,2},{2,3},{3,0},{4,5},{5,6},{6,7},{7,4},{8,9},{9,10},{10,1... | collective-permute-start | bytes 786440 | tf_op jit(solution)/shard_map/ppermute | solution.py:1256
  894.9 51.4 %collective-permute-start.4 = (bf16[256,512]{1,0:T(8,128)(2,1)}, bf16[256,512]{1,0:T(8,128)(2,1)}, u32[]{:S(2)}, u32[]{:S(2)}) collective-permute-start(bf16[256,512]{1,0:T(8,128)(2,1)} %get-tuple-element.154), channel_id=1, source_target_pairs={{0,2},{1,3},{2,0},{3,1},{4,6},{5,7},{6,4},{7,5},{8,10},{9,11},{10,... | collective-permute-start | bytes 786440 | tf_op jit(solution)/shard_map/ppermute | solution.py:1256
  897.3 49.0 %collective-permute-start.5 = (bf16[256,512]{1,0:T(8,128)(2,1)S(1)}, bf16[256,512]{1,0:T(8,128)(2,1)}, u32[]{:S(2)}, u32[]{:S(2)}) collective-permute-start(bf16[256,512]{1,0:T(8,128)(2,1)S(1)} %get-tuple-element.153), channel_id=1, source_target_pairs={{0,3},{1,0},{2,1},{3,2},{4,7},{5,4},{6,5},{7,6},{8,11},{9,8},{10,9... | collective-permute-start | bytes 786440 | tf_op jit(solution)/shard_map/ppermute | solution.py:1256
  975.2 49.5 %collective-permute-start.2 = (bf16[512,2048]{1,0:T(8,128)(2,1)}, bf16[512,2048]{1,0:T(8,128)(2,1)}, u32[]{:S(2)}, u32[]{:S(2)}) collective-permute-start(bf16[512,2048]{1,0:T(8,128)(2,1)} %fusion.9), channel_id=1, source_target_pairs={{0,1},{1,2},{2,3},{3,0},{4,5},{5,6},{6,7},{7,4},{8,9},{9,10},{10,1... | collective-permute-start | bytes 6291464 | tf_op jit(solution)/shard_map/ppermute | solution.py:1199
  998.5 31.0 %copy-start.34 = (s32[8]{0:T(128)S(1)}, s32[8]{0:T(128)}, u32[]{:S(2)}) copy-start(s32[8]{0:T(128)} %get-tuple-element.142) | copy-start | bytes 100
  998.5 31.0 %copy-start.16 = (f32[256,512]{1,0:T(8,128)S(1)}, f32[256,512]{1,0:T(8,128)}, u32[]{:S(2)}) copy-start(f32[256,512]{1,0:T(8,128)} %convert_add_fusion.4) | copy-start | bytes 1572868
  998.5 32.0 %copy-start.8 = (bf16[8,64,2048]{2,1,0:T(8,128)(2,1)S(1)}, bf16[8,64,2048]{2,1,0:T(8,128)(2,1)}, u32[]{:S(2)}) copy-start(bf16[8,64,2048]{2,1,0:T(8,128)(2,1)} %copy-done.7) | copy-start | bytes 6291460
  998.5 32.0 %copy-start.24 = (f32[1,8,256]{2,0,1:T(1,128)S(1)}, f32[1,8,256]{2,0,1:T(1,128)}, u32[]{:S(2)}) copy-start(f32[1,8,256]{2,0,1:T(1,128)} %copy-done.23) | copy-start | bytes 24580
  998.5 32.0 %copy-start.31 = (f32[512]{0:T(512)S(1)}, f32[512]{0:T(512)}, u32[]{:S(2)}) copy-start(f32[512]{0:T(512)} %copy-done.30) | copy-start | bytes 6148
  1029.1 57.6 %collective-permute-start.6 = (bf16[512,2048]{1,0:T(8,128)(2,1)}, bf16[512,2048]{1,0:T(8,128)(2,1)}, u32[]{:S(2)}, u32[]{:S(2)}) collective-permute-start(bf16[512,2048]{1,0:T(8,128)(2,1)} %fusion.8), channel_id=1, source_target_pairs={{0,1},{1,2},{2,3},{3,0},{4,5},{5,6},{6,7},{7,4},{8,9},{9,10},{10,1... | collective-permute-start | bytes 6291464 | tf_op jit(solution)/shard_map/ppermute | solution.py:1199
  1034.5 45.5 %all-to-all-start.4 = ((f32[32,2,256]{2,1,0:T(2,128)}), f32[32,2,256]{2,1,0:T(2,128)S(1)}, u32[]{:S(2)}, u32[]{:S(2)}) async-start(f32[32,2,256]{2,1,0:T(2,128)} %bitcast.31), calls=%async_computation.6 | async-start | bytes 131072 | tf_op jit(solution)/shard_map/all_to_all | solution.py:1300
  1082.6 18.5 %collective-permute-start.7 = (bf16[256,768]{1,0:T(8,128)(2,1)}, bf16[256,768]{1,0:T(8,128)(2,1)S(1)}, u32[]{:S(2)}, u32[]{:S(2)}) collective-permute-start(bf16[256,768]{1,0:T(8,128)(2,1)} %get-tuple-element.149), channel_id=1, source_target_pairs={{0,1},{1,2},{2,3},{3,0},{4,5},{5,6},{6,7},{7,4},{8,9},{9,10},{10,1... | collective-permute-start | bytes 1179656 | tf_op jit(solution)/shard_map/ppermute | solution.py:1256
  1083.3 29.6 %collective-permute-start.8 = (bf16[256,768]{1,0:T(8,128)(2,1)S(1)}, bf16[256,768]{1,0:T(8,128)(2,1)}, u32[]{:S(2)}, u32[]{:S(2)}) collective-permute-start(bf16[256,768]{1,0:T(8,128)(2,1)S(1)} %get-tuple-element.151), channel_id=1, source_target_pairs={{0,2},{1,3},{2,0},{3,1},{4,6},{5,7},{6,4},{7,5},{8,10},{9,11},{10,... | collective-permute-start | bytes 1179656 | tf_op jit(solution)/shard_map/ppermute | solution.py:1256
  1083.3 29.6 %collective-permute-start.9 = (bf16[256,768]{1,0:T(8,128)(2,1)S(1)}, bf16[256,768]{1,0:T(8,128)(2,1)}, u32[]{:S(2)}, u32[]{:S(2)}) collective-permute-start(bf16[256,768]{1,0:T(8,128)(2,1)S(1)} %get-tuple-element.150), channel_id=1, source_target_pairs={{0,3},{1,0},{2,1},{3,2},{4,7},{5,4},{6,5},{7,6},{8,11},{9,8},{10,9... | collective-permute-start | bytes 1179656 | tf_op jit(solution)/shard_map/ppermute | solution.py:1256
  (11 other events, 31.5 us)
Sparse Core Ops, SparseCore 0:
  11.9 172.6 all-gather.2
  186.5 85.1 all-gather.4
  689.9 86.3 reduce-scatter.3
  780.2 175.7 reduce-scatter.5
  970.9 92.1 reduce-scatter.7

commit v8 on v7

--- a/solution.py
+++ b/solution.py
@@ -1088,6 +1088,198 @@
     )(rows, *parts)
 
 
+def total_kernel(
+    tp_count, dp_count, hops, groups, rows, *refs
+):
+    parts = refs[:groups]
+    running = refs[groups]
+    addends = refs[groups + 1 : groups + hops]
+    (
+        weights, out, grad_rows, last_chunk,
+        turned, mine, got, got_across, held, chunks, onward,
+        load_sem, send, recv, across_send, across_recv, chunk_send, chunk_recv,
+    ) = refs[groups + hops :]
+    my_dp = lax.axis_index("dp")
+    my_tp = lax.axis_index("tensor")
+    own_rows = out.shape[0]
+    half = own_rows // 2
+    bits = [1 << b for b in range(dp_count.bit_length() - 1)]
+    orders = [bits, bits[:1] + bits[1:][::-1]]
+    steps = len(bits)
+
+    def shard_of(j):
+        return lax.rem(my_tp + 1 + j, tp_count)
+
+    def load(j):
+        return pltpu.make_async_copy(weights.at[shard_of(j)], held.at[j % 2], load_sem.at[j % 2])
+
+    load(0).start()
+    barrier = pltpu.get_barrier_semaphore()
+    for j in range(1, tp_count):
+        pl.semaphore_signal(
+            barrier, inc=1, device_id={"tensor": lax.rem(my_tp + j, tp_count)}, device_id_type=MESH
+        )
+    for bit in bits:
+        pl.semaphore_signal(
+            barrier, inc=1, device_id={"dp": flip(my_dp, bit)}, device_id_type=MESH
+        )
+    pl.semaphore_wait(barrier, tp_count - 1 + steps)
+
+    def hop(n):
+        source = running if n == 0 else onward.at[n - 1]
+        return pltpu.make_async_remote_copy(
+            src_ref=source,
+            dst_ref=last_chunk if n == hops - 1 else chunks.at[n],
+            send_sem=chunk_send.at[n],
+            recv_sem=chunk_recv.at[n],
+            device_id={"tensor": lax.rem(my_tp + 1, tp_count)},
+            device_id_type=MESH,
+        )
+
+    hop(0).start()
+
+    def block(j, s, owner):
+        return j, pl.ds(pl.multiple_of(owner * own_rows + s * half, half), half)
+
+    def place(k, m):
+        return sum(1 << (steps - 1 - e) for e in range(k)) + m
+
+    def fellow(s, k, m, start):
+        owner = start
+        for b in range(steps - 1 - k):
+            if m >> b & 1:
+                owner = flip(owner, orders[s][k + 1 + b])
+        return owner
+
+    def exchange_part(j, s, k, m):
+        partner = flip(my_dp, orders[s][k])
+        at = place(k, m)
+        index, span = block(j, s, fellow(s, k, m, partner))
+        return pltpu.make_async_remote_copy(
+            src_ref=mine.at[index, span, :],
+            dst_ref=got.at[j, s, at],
+            send_sem=send.at[j, s, at],
+            recv_sem=recv.at[j, s, at],
+            device_id={"dp": partner},
+            device_id_type=MESH,
+        )
+
+    def across(j):
+        return pltpu.make_async_remote_copy(
+            src_ref=mine.at[j, pl.ds(pl.multiple_of(my_dp * own_rows, own_rows), own_rows), :],
+            dst_ref=got_across.at[j],
+            send_sem=across_send.at[j],
+            recv_sem=across_recv.at[j],
+            device_id={"tensor": shard_of(j)},
+            device_id_type=MESH,
+        )
+
+    def every(k):
+        return [(s, m) for s in range(2) for m in range(1 << (steps - 1 - k))]
+
+    turned[...] = rows[...].T
+    for phase in range(tp_count + steps + 1):
+        if phase < tp_count:
+            shard = shard_of(phase)
+            at = 0
+            load(phase).wait()
+            if phase + 1 < tp_count:
+                load(phase + 1).start()
+            for g, part in enumerate(parts):
+                cols = part.shape[2]
+                value = part[shard]
+                mine[phase, :, at : at + cols] = dot_nn(turned[...], value).astype(bf16)
+                product = dot_nt(value, held[phase % 2, :, at : at + cols])
+                if phase == 0 and g == 0:
+                    grad_rows[...] = product
+                else:
+                    grad_rows[...] += product
+                at += cols
+        for k in reversed(range(steps + 1)):
+            j = phase - k
+            if not 0 <= j < tp_count:
+                continue
+            if k > 0:
+                for s, m in every(k - 1):
+                    exchange_part(j, s, k - 1, m).wait_recv()
+                    index, span = block(j, s, fellow(s, k - 1, m, my_dp))
+                    mine[index, span, :] = (
+                        mine[index, span, :].astype(f32)
+                        + got[j, s, place(k - 1, m)].astype(f32)
+                    ).astype(bf16)
+            if k < steps:
+                for s, m in every(k):
+                    exchange_part(j, s, k, m).start()
+            elif j < tp_count - 1:
+                across(j).start()
+        if tp_count <= phase < tp_count + hops - 1:
+            n = phase - tp_count
+            hop(n).wait_recv()
+            onward[n] = (chunks[n].astype(f32) + addends[n][...].astype(f32)).astype(bf16)
+            hop(n + 1).start()
+    total = mine[
+        tp_count - 1, pl.ds(pl.multiple_of(my_dp * own_rows, own_rows), own_rows), :
+    ].astype(f32)
+    for j in range(tp_count - 1):
+        across(j).wait_recv()
+        total += got_across[j].astype(f32)
+    out[...] = total
+    hop(hops - 1).wait_recv()
+    for n in range(hops):
+        hop(n).wait_send()
+    for j in range(tp_count):
+        if j < tp_count - 1:
+            across(j).wait_send()
+        for k in range(steps):
+            for s, m in every(k):
+                exchange_part(j, s, k, m).wait_send()
+
+
+def total_grads(rows, parts, running, addends, weights, dp_count, collective_id):
+    tp_count, width, cols = weights.shape
+    count = rows.shape[0]
+    own_rows = width // dp_count
+    hops = len(addends) + 1
+    vmem_spec = pl.BlockSpec(memory_space=pltpu.VMEM)
+    any_spec = pl.BlockSpec(memory_space=pl.ANY)
+    dma = pltpu.SemaphoreType.DMA
+    return pl.pallas_call(
+        functools.partial(total_kernel, tp_count, dp_count, hops, len(parts)),
+        out_shape=[
+            jax.ShapeDtypeStruct((own_rows, cols), f32),
+            jax.ShapeDtypeStruct((count, width), f32),
+            jax.ShapeDtypeStruct((count, width), bf16),
+        ],
+        in_specs=[vmem_spec] * (1 + len(parts) + hops) + [any_spec],
+        out_specs=[vmem_spec, vmem_spec, any_spec],
+        scratch_shapes=[
+            pltpu.VMEM((width, count), bf16),
+            pltpu.VMEM((tp_count, width, cols), bf16),
+            pltpu.VMEM((tp_count, 2, dp_count - 1, own_rows // 2, cols), bf16),
+            pltpu.VMEM((tp_count - 1, own_rows, cols), bf16),
+            pltpu.VMEM((2, width, cols), bf16),
+            pltpu.VMEM((max(hops - 1, 1), count, width), bf16),
+            pltpu.VMEM((max(hops - 1, 1), count, width), bf16),
+            dma((2,)),
+            dma((tp_count, 2, dp_count - 1)),
+            dma((tp_count, 2, dp_count - 1)),
+            dma((tp_count,)),
+            dma((tp_count,)),
+            dma((hops,)),
+            dma((hops,)),
+        ],
+        compiler_params=pltpu.CompilerParams(
+            collective_id=collective_id, has_side_effects=True, vmem_limit_bytes=62 * 1024 * 1024
+        ),
+        cost_estimate=pl.CostEstimate(
+            flops=4 * tp_count * count * width * cols,
+            bytes_accessed=16 * tp_count * width * cols,
+            transcendentals=0,
+        ),
+        name="total_grads",
+    )(rows, *parts, running, *addends, weights)
+
+
 def rms_scale(hidden):
     return lax.rsqrt(jnp.mean(hidden * hidden, axis=1, keepdims=True) + epsilon)
 
@@ -1264,28 +1456,32 @@
         rows_t, grads_t, grad_gate_up, inner_act, tp_count, dp_count, 2,
     )
     sum_mlp = reduce_dp(grad_wmlp)
-    branch_two = pass_on(after(partial_two[1], grad_slots))
+    first_part = after(partial_two[1], grad_slots)
+    branch_two = pass_on(first_part)
     grad_qkv = []
     for g in groups:
         q_t, k_rows, k_t, v_rows, o_t, lse = saved[g]
         back = attend_backward(
-            grad_slots if g == 0 else after(grad_slots, (back, sum_out)), g, q_t,
-            k_rows, k_t, v_rows, o_t, lse, begin, cos_t, sin_t, first_block, perm, page_rows,
-            block_len,
-        )
-        grad_qkv.append(trade_back(after(back, (grad_qkv[-1], branch_two)) if grad_qkv else back))
+            after(grad_slots, (back, sum_out) if g else first_part), g, q_t, k_rows, k_t, v_rows,
+            o_t, lse, begin, cos_t, sin_t, first_block, perm, page_rows, block_len,
+        )
+        grad_qkv.append(trade_back(after(back, (grad_qkv[-1], branch_two)) if g else back))
     hidden = sum_mlp.shape[1] // 3
-    sum_out = reduce_tensor(sum_out)
-    for s in range(2, tp_count - 1):
-        branch_two = pass_on(add_on(after(branch_two, tuple(grad_qkv)), s))
-    grad_wqkv = outer(after(normed_one, (sum_mlp, sum_out)), grad_qkv)
-    sum_qkv = reduce_tensor(reduce_dp(grad_wqkv))
+    hops = min(2, tp_count - 2)
+    sum_qkv, grad_normed_one, branch_two = total_grads(
+        normed_one,
+        grad_qkv,
+        add_on(branch_two, 2),
+        [partial_two[2 + n] for n in range(1, hops)],
+        w_qkv,
+        dp_count,
+        4,
+    )
     each = group_q + 2 * HD
     sum_qkv = [sum_qkv[:, g * each : (g + 1) * each] for g in groups]
-    grad_normed_one = None
-    for g in groups:
-        grad_normed_one = gather_sum(after(grad_qkv[g], grad_wqkv), w_qkv, g, grad_normed_one)
-    branch_two = pass_on(add_on(after(branch_two, grad_normed_one), tp_count - 1))
+    for s in range(2 + hops, tp_count):
+        branch_two = pass_on(add_on(branch_two, s))
+    sum_out = reduce_tensor(sum_out)
     result = (
         (after(hidden_mid, back) + branch_two.astype(f32) + partial_two[0].astype(f32)) * valid_rows
     ).astype(bf16)

time: 1140 us -> 1140 us (level)
  Pallas kernels: 746 us -> 842 us
  waiting for transfers between devices: 203 us -> 126 us
    pallas_call x0 -> x1, Pallas kernels: none -> 131 us  [total_grads(): pl.pallas_call(functools.partial(total_kernel, tp_count, dp_count, hops,...]
    all_to_all x1, waiting for transfers between devices: 32.7 us -> 0.01 us  [local(): lax.all_to_all(gain_parts, everyone, split_axis=0, concat_axis=0, tiled=T...]
    ppermute x4 -> x2, waiting for transfers between devices: 69.6 us -> 46.6 us  [pass_on(): return lax.ppermute(value, 'tensor', ring_next)]
    pallas_call x4 -> x2, Pallas kernels: 38.6 us -> 17.1 us  [gather_sum(): pl.pallas_call(functools.partial(gather_kernel, begin is not None), grid=...]
    ppermute x6 -> x3, waiting for transfers between devices: 59.3 us -> 45.7 us  [reduce_tensor(): total = total + lax.ppermute(block, 'tensor', pairs).astype(f32)]
    pallas_call x2 -> x1, Pallas kernels: 22.8 us -> 9.37 us  [outer(): pl.pallas_call(outer_kernel, grid=(shards,), in_specs=[pl.BlockSpec((coun...]
  transfers between devices with their start and end apart: 20 -> 14, of which waited for: 10 -> 6; matrix products, arithmetic and copies ran while one was open for 6% -> 5% of each run, Pallas kernels for 39% -> 48%
where the time goes in v8:
time: 1140 us; the launch traced here: 1130 us
  Pallas kernels  842 us (74%)
  waiting for transfers between devices  126 us (11%)
  starting transfers between devices  58.8 us (5%)
  other arithmetic  50 us (4%)
  local copies, waits for them, and re-layouts  39.5 us (3%)
  between operations  14.7 us (1%)
    pallas_call x1, Pallas kernels, feed(): pl.pallas_call(functools.partial(feed_kernel, ring, min(tile, hidden)), o...  278 us
    pallas_call x1, Pallas kernels, collect(): pl.pallas_call(functools.partial(collect_kernel, tp_count, dp_count, hops...  159 us
    pallas_call x1, Pallas kernels, total_grads(): pl.pallas_call(functools.partial(total_kernel, tp_count, dp_count, hops,...  131 us
    pallas_call x1, Pallas kernels, project(): pl.pallas_call(functools.partial(project_kernel, tp_count, dp_count), out...  69.1 us
    pallas_call x1, Pallas kernels, weigh(): pl.pallas_call(functools.partial(weigh_kernel, tp_count, dp_count, min(51...  67.7 us
    pallas_call x2, Pallas kernels, attend_backward(): pl.pallas_call(functools.partial(backward_kernel, q_heads, kv_heads, page...  52.6 us
    ppermute x2, waiting for transfers between devices, pass_on(): return lax.ppermute(value, 'tensor', ring_next)  46.6 us
    ppermute x3, waiting for transfers between devices, reduce_tensor(): total = total + lax.ppermute(block, 'tensor', pairs).astype(f32)  45.7 us
  transfers between devices with their start and end apart: 14, of which 6 were waited for; matrix products, arithmetic and copies ran while one was open for 5% of the time, Pallas kernels for 48%

profile of v8, /device:TPU:0, one launch (start us, length us, event | category | flops | bytes accessed | tf_op | source)
XLA Modules:
  0.0 1131.3 jit_solution(9317580798079970497)
XLA Ops:
  8.7 3.0 pad_maximum_fusion
  16.7 2.3 gather_fusion.1
  23.5 158.8 %collect.1 = (bf16[4,2048,768]{2,1,0:T(8,128)(2,1)}, bf16[4,256,512]{2,1,0:T(8,128)(2,1)}, bf16[8,2,256]{2,1,0:T(2,128)(2,1)}, bf16[2,512,2048]{2,1,0:T(8,128)(2,1)}) custom-call(bf16[256,768]{1,0:T(8,128)(2,1)} %concatenate.16.shard, bf16[256,512]{1,0:T(8,128)(2,1)} %bitcast.70, bf16[2,256]{1,0:T(2,128)(2,1)} %pad_maximum_fusion.4.gains, ...), custom_call_target="tpu_custom_call" | custom-call | bytes 100663296 | tf_op jit(solution)/shard_map/collect/pallas_call | solution.py:966
  182.3 2.5 gather_fusion
  186.0 5.3 copy-done.3
  191.3 69.1 %project.1.refs_0_.refs_1_.refs_2_.refs_3_ = bf16[32,64,768]{2,1,0:T(8,128)(2,1)S(1)} custom-call(bf16[512,2048]{1,0:T(8,128)(2,1)S(1)} %multiply_convert_fusion.1.rows, bf16[4,2048,768]{2,1,0:T(8,128)(2,1)S(1)} %copy-done.3), custom_call_target="tpu_custom_call" | custom-call | flops 6442450944 | bytes 100663296 | tf_op jit(solution)/shard_map/project/pallas_call | solution.py:449
  260.4 3.0 slice_bitcast_fusion.2
  263.5 17.7 %collective-permute-start = (bf16[512,2048]{1,0:T(8,128)(2,1)}, bf16[512,2048]{1,0:T(8,128)(2,1)}, u32[]{:S(2)}, u32[]{:S(2)}) collective-permute-start(bf16[512,2048]{1,0:T(8,128)(2,1)} %get-tuple-element.63.refs_2_), channel_id=1, source_target_pairs={{0,1},{1,2},{2,3},{3,0},{4,5},{5,6},{6,7},{7,4},{8,9},{9,10},{10,1... | collective-permute-start | bytes 6291464 | tf_op jit(solution)/shard_map/ppermute | solution.py:1391
  282.1 1.8 multiply_sine_fusion
  283.9 6.6 prepare.2
  291.0 17.9 %attend_forward.2 = (bf16[256,2048]{1,0:T(8,128)(2,1)}, f32[4,2048]{1,0:T(4,128)}, bf16[32,64,256]{2,1,0:T(8,128)(2,1)}) custom-call(s32[4]{0:T(128)} %and_select_fusion.4.first_block, s32[32]{0:T(128)} %fusion.12.perm, bf16[256,2048]{1,0:T(8,128)(2,1)} %get-tuple-element.53.q_t.refs_8_, bf16[1,2048,64]{2,1,0:T(8,128)(2,1)} %get-tuple-element.54.k_rows.refs_9_, ...), custom_call_target="tpu_custom_call" | custom-call | flops 1073741824 | bytes 4194304 | tf_op jit(solution)/shard_map/attend_forward/pallas_call | solution.py:174
  309.0 5.8 all-to-all-start.1
  314.8 6.7 prepare.3
  321.5 17.9 %attend_forward.3 = (bf16[256,2048]{1,0:T(8,128)(2,1)}, f32[4,2048]{1,0:T(4,128)}, bf16[32,64,256]{2,1,0:T(8,128)(2,1)}) custom-call(s32[4]{0:T(128)} %and_select_fusion.4.first_block, s32[32]{0:T(128)} %fusion.12.perm, bf16[256,2048]{1,0:T(8,128)(2,1)} %get-tuple-element.58.q_t.refs_8_, bf16[1,2048,64]{2,1,0:T(8,128)(2,1)} %get-tuple-element.59.k_rows.refs_9_, ...), custom_call_target="tpu_custom_call" | custom-call | flops 1073741824 | bytes 4194304 | tf_op jit(solution)/shard_map/attend_forward/pallas_call | solution.py:174
  339.4 11.1 all-to-all-done.1
  350.4 3.4 all-to-all-start
  353.9 2.7 bitcast_convert_fusion.refs_0_
  356.6 8.5 gather_sum.2.refs_0_
  365.1 14.9 %all-to-all-done = bf16[32,64,256]{2,1,0:T(8,128)(2,1)} async-done(((bf16[32,64,256]{2,1,0:T(8,128)(2,1)}), bf16[32,64,256]{2,1,0:T(8,128)(2,1)}, u32[]{:S(2)}, u32[]{:S(2)}) %all-to-all-start) | async-done | bytes 1048608 | tf_op jit(solution)/shard_map/all_to_all | solution.py:1383
  380.0 8.6 gather_sum.3
  388.6 2.7 multiply_reduce_fusion.2
  393.8 278.2 %feed_forward.1 = (bf16[2048,2048]{1,0:T(8,128)(2,1)}, bf16[2048,2048]{1,0:T(8,128)(2,1)}, bf16[4,512,2048]{2,1,0:T(8,128)(2,1)}, bf16[4,512,4096]{2,1,0:T(8,128...) custom-call(bf16[512,2048]{1,0:T(8,128)(2,1)} %multiply_convert_fusion.own_rows, ...), custom_call_target="tpu_custom_call" | custom-call | flops 103079215104 | bytes 33554432 | tf_op jit(solution)/shard_map/feed_forward/pallas_call | solution.py:654
  672.0 4.2 fusion.5
  676.7 3.9 fusion.19.rows
  680.6 9.4 outer.1
  690.0 9.1 spread.1.grads
  699.2 1.9 copy-done.4
  701.1 67.7 %weigh.1 = (bf16[32,64,512]{2,1,0:T(8,128)(2,1)S(1)}, bf16[2048,6144]{1,0:T(8,128)(2,1)}) custom-call(bf16[4,512,512]{2,1,0:T(8,128)(2,1)S(1)} %copy-done.4, bf16[2048,2048]{1,0:T(8,128)(2,1)} %get-tuple-element.68.rows_t, bf16[2048,2048]{1,0:T(8,128)(2,1)} %get-tuple-element.69.grads_t, bf16[4,512,4096]{2,1,0:T(8,128)(2,1)} %get-tuple-element.70.gate_up, ...), custom_call_target="tpu_custom_call" | custom-call | flops 51539607552 | bytes 41943040 | tf_op jit(solution)/shard_map/weigh/pallas_call | solution.py:793
  770.2 4.9 slice_bitcast_fusion
  775.1 26.1 %attend_backward.2 = bf16[32,64,384]{2,1,0:T(8,128)(2,1)} custom-call(s32[4]{0:T(128)} %and_select_fusion.4.first_block, s32[32]{0:T(128)} %fusion.12.perm, bf16[32,64,512]{2,1,0:T(8,128)(2,1)} %copy-done, bf16[32,64,512]{2,1,0:T(8,128)(2,1)} %copy-done, bf16[32,64,512]{2,1,0:T(8,128)(2,1)} %copy-done, bf16[32,64,512]{2,1,0:T(8,128)(2,1)} %copy-done, ...), custom_call_target="tpu_custom_call" | custom-call | flops 3221225472 | bytes 6291456 | tf_op jit(solution)/shard_map/attend_backward/pallas_call | solution.py:335
  801.2 9.5 all-to-all-start.2
  810.7 1.8 collective-permute-start.1
  812.4 26.5 %attend_backward.3 = bf16[32,64,384]{2,1,0:T(8,128)(2,1)} custom-call(s32[4]{0:T(128)} %and_select_fusion.4.first_block, s32[32]{0:T(128)} %fusion.12.perm, bf16[32,64,512]{2,1,0:T(8,128)(2,1)} %copy-done, bf16[32,64,512]{2,1,0:T(8,128)(2,1)} %copy-done, bf16[32,64,512]{2,1,0:T(8,128)(2,1)} %copy-done, bf16[32,64,512]{2,1,0:T(8,128)(2,1)} %copy-done, ...), custom_call_target="tpu_custom_call" | custom-call | flops 3221225472 | bytes 6291456 | tf_op jit(solution)/shard_map/attend_backward/pallas_call | solution.py:335
  839.0 46.6 %collective-permute-done.1 = bf16[512,2048]{1,0:T(8,128)(2,1)S(1)} collective-permute-done((bf16[512,2048]{1,0:T(8,128)(2,1)}, bf16[512,2048]{1,0:T(8,128)(2,1)S(1)}, u32[]{:S(2)}, u32[]{:S(2)}) %collective-permute-start.1) | collective-permute-done | bytes 2097184 | tf_op jit(solution)/shard_map/ppermute | solution.py:1391
  885.6 8.0 all-to-all-done.2
  893.5 3.4 all-to-all-start.3
  898.8 2.5 collective-permute-start.3
  902.9 3.7 fusion.8.refs_2_
  906.5 26.5 %collective-permute-done.2 = bf16[256,512]{1,0:T(8,128)(2,1)S(1)} collective-permute-done((bf16[256,512]{1,0:T(8,128)(2,1)S(1)}, bf16[256,512]{1,0:T(8,128)(2,1)S(1)}, u32[]{:S(2)}, u32[]{:S(2)}) %collective-permute-start.2) | collective-permute-done | bytes 262176 | tf_op jit(solution)/shard_map/ppermute | solution.py:1448
  933.0 19.2 %collective-permute-done.3 = bf16[256,512]{1,0:T(8,128)(2,1)S(1)} collective-permute-done((bf16[256,512]{1,0:T(8,128)(2,1)S(1)}, bf16[256,512]{1,0:T(8,128)(2,1)S(1)}, u32[]{:S(2)}, u32[]{:S(2)}) %collective-permute-start.3) | collective-permute-done | bytes 262176 | tf_op jit(solution)/shard_map/ppermute | solution.py:1448
  953.4 131.0 %total_grads.1 = (f32[256,768]{1,0:T(8,128)}, f32[512,2048]{1,0:T(8,128)}, bf16[512,2048]{1,0:T(8,128)(2,1)}) custom-call(bf16[512,2048]{1,0:T(8,128)(2,1)} %copy-done.2, bf16[4,512,384]{2,1,0:T(8,128)(2,1)} %bitcast.19.refs_0_, bf16[4,512,384]{2,1,0:T(8,128)(2,1)} %bitcast.20.refs_1_, bf16[512,2048]{1,0:T(8,128)(2,1)} %fusion.8.refs_2_, ...), custom_call_target="tpu_custom_call" | custom-call | flops 12884901888 | bytes 100663296 | tf_op jit(solution)/shard_map/total_grads/pallas_call | solution.py:1246
  1084.4 4.1 multiply_reduce_fusion
  1089.2 11.4 %all-to-all-start.4 = ((f32[32,2,256]{2,1,0:T(2,128)}), f32[32,2,256]{2,1,0:T(2,128)S(1)}, u32[]{:S(2)}, u32[]{:S(2)}) async-start(f32[32,2,256]{2,1,0:T(2,128)} %bitcast.31), calls=%async_computation.5 | async-start | bytes 131072 | tf_op jit(solution)/shard_map/all_to_all | solution.py:1496
  1101.5 8.8 add_convert_fusion
  1111.0 3.6 gather_fusion.4
  1114.6 2.0 gather_fusion.3
  1118.1 4.7 convert_bitcast_fusion
  1122.8 1.8 copy.43
  (143 shorter events, 26.3 us)
Async XLA Ops:
  7.2 307.6 %all-gather.3.cloned.1.call-start = ((), (), s32[]{:S(2)}) async-start(), calls=%async_computation.7 | async-start | bytes 28311552 | tf_op jit(solution)/shard_map/all_gather | solution.py:1396
  8.7 3.1 copy-start.35
  8.7 3.9 copy-start.34
  11.7 7.3 copy-start.16
  11.7 8.3 copy-start.36
  11.7 8.3 copy-start.37
  11.7 8.4 copy-start.17
  11.7 8.4 copy-start.18
  11.8 8.4 copy-start.19
  11.8 344.8 %all-gather.5.cloned.1.call-start = ((), (), s32[]{:S(2)}) async-start(), calls=%async_computation.8 | async-start | bytes 9437184 | tf_op jit(solution)/shard_map/all_gather | solution.py:1402
  16.7 6.8 copy-start.27
  19.0 163.2 %copy-start.9 = (bf16[8,64,2048]{2,1,0:T(8,128)(2,1)}, bf16[8,64,2048]{2,1,0:T(8,128)(2,1)S(1)}, u32[]{:S(2)}) copy-start(bf16[8,64,2048]{2,1,0:T(8,128)(2,1)S(1)} %gather_fusion.1) | copy-start | bytes 6291460
  182.3 3.1 copy-start.31
  184.8 169.1 %copy-start.7 = (bf16[8,64,2048]{2,1,0:T(8,128)(2,1)}, bf16[8,64,2048]{2,1,0:T(8,128)(2,1)S(1)}, u32[]{:S(2)}) copy-start(bf16[8,64,2048]{2,1,0:T(8,128)(2,1)S(1)} %gather_fusion) | copy-start | bytes 6291460
  185.3 75.1 %copy-start.29 = (f32[512]{0:T(512)}, f32[512]{0:T(512)S(1)}, u32[]{:S(2)}) copy-start(f32[512]{0:T(512)S(1)} %rsqrt.20) | copy-start | bytes 6148
  185.4 75.0 %copy-start.22 = (f32[1,8,256]{2,0,1:T(1,128)}, f32[1,8,256]{2,0,1:T(1,128)S(1)}, u32[]{:S(2)}) copy-start(f32[1,8,256]{2,0,1:T(1,128)S(1)} %get-tuple-element.165) | copy-start | bytes 24580
  185.4 205.9 %copy-start.20 = (f32[1,8,256]{2,0,1:T(1,128)}, f32[1,8,256]{2,0,1:T(1,128)S(1)}, u32[]{:S(2)}) copy-start(f32[1,8,256]{2,0,1:T(1,128)S(1)} %get-tuple-element.164) | copy-start | bytes 24580
  185.9 74.5 %copy-start.2 = (bf16[512,2048]{1,0:T(8,128)(2,1)}, bf16[512,2048]{1,0:T(8,128)(2,1)S(1)}, u32[]{:S(2)}) copy-start(bf16[512,2048]{1,0:T(8,128)(2,1)S(1)} %multiply_convert_fusion.1.rows) | copy-start | bytes 6291460
  186.0 5.3 copy-start.3
  191.3 69.1 %copy-start.13 = (bf16[2,512,2048]{2,1,0:T(8,128)(2,1)S(1)}, bf16[2,512,2048]{2,1,0:T(8,128)(2,1)}, u32[]{:S(2)}) copy-start(bf16[2,512,2048]{2,1,0:T(8,128)(2,1)} %get-tuple-element.62) | copy-start | bytes 12582916
  260.4 20.8 %copy-start.32 = (s32[1,2048]{1,0:T(1,128)S(1)}, s32[1,2048]{1,0:T(1,128)}, u32[]{:S(2)}) copy-start(s32[1,2048]{1,0:T(1,128)} %param.17) | copy-start | bytes 24580
  263.5 75.9 %collective-permute-start = (bf16[512,2048]{1,0:T(8,128)(2,1)}, bf16[512,2048]{1,0:T(8,128)(2,1)}, u32[]{:S(2)}, u32[]{:S(2)}) collective-permute-start(bf16[512,2048]{1,0:T(8,128)(2,1)} %get-tuple-element.63.refs_2_), channel_id=1, source_target_pairs={{0,1},{1,2},{2,3},{3,0},{4,5},{5,6},{6,7},{7,4},{8,9},{9,10},{10,1... | collective-permute-start | bytes 6291464 | tf_op jit(solution)/shard_map/ppermute | solution.py:1391
  281.3 9.2 copy-start.24
  309.0 41.4 %all-to-all-start.1 = ((bf16[32,64,256]{2,1,0:T(8,128)(2,1)}), bf16[32,64,256]{2,1,0:T(8,128)(2,1)S(1)}, u32[]{:S(2)}, u32[]{:S(2)}) async-start(bf16[32,64,256]{2,1,0:T(8,128)(2,1)} %get-tuple-element.56), calls=%async_computation.1 | async-start | bytes 2097152 | tf_op jit(solution)/shard_map/all_to_all | solution.py:1383
  350.4 6.2 copy-start.12
  350.4 29.6 %all-to-all-start = ((bf16[32,64,256]{2,1,0:T(8,128)(2,1)}), bf16[32,64,256]{2,1,0:T(8,128)(2,1)}, u32[]{:S(2)}, u32[]{:S(2)}) async-start(bf16[32,64,256]{2,1,0:T(8,128)(2,1)} %get-tuple-element.64), calls=%async_computation | async-start | bytes 2097152 | tf_op jit(solution)/shard_map/all_to_all | solution.py:1383
  353.8 458.6 %reduce-scatter.3.cloned.1.call-start = ((), (), s32[]{:S(2)}) async-start(), calls=%async_computation.9 | async-start | bytes 9437184 | tf_op jit(solution)/shard_map/reduce_scatter | solution.py:1439
  388.6 3.4 copy-start.5
  671.9 4.2 copy-start.6
  672.0 4.7 copy-start.10
  672.0 4.7 copy-start.21
  672.0 4.7 copy-start.26
  672.0 4.7 copy-start.28
  690.0 428.1 %reduce-scatter.5.cloned.1.call-start = ((), (), s32[]{:S(2)}) async-start(), calls=%async_computation.10 | async-start | bytes 28311552 | tf_op jit(solution)/shard_map/reduce_scatter | solution.py:1439
  801.2 92.4 %all-to-all-start.2 = ((bf16[32,64,384]{2,1,0:T(8,128)(2,1)}), bf16[32,64,384]{2,1,0:T(8,128)(2,1)}, u32[]{:S(2)}, u32[]{:S(2)}) async-start(bf16[32,64,384]{2,1,0:T(8,128)(2,1)} %attend_backward.2), calls=%async_computation.3 | async-start | bytes 3145728 | tf_op jit(solution)/shard_map/all_to_all | solution.py:1383
  810.7 74.9 %collective-permute-start.1 = (bf16[512,2048]{1,0:T(8,128)(2,1)}, bf16[512,2048]{1,0:T(8,128)(2,1)S(1)}, u32[]{:S(2)}, u32[]{:S(2)}) collective-permute-start(bf16[512,2048]{1,0:T(8,128)(2,1)} %get-tuple-element.74), channel_id=1, source_target_pairs={{0,1},{1,2},{2,3},{3,0},{4,5},{5,6},{6,7},{7,4},{8,9},{9,10},{10,1... | collective-permute-start | bytes 6291464 | tf_op jit(solution)/shard_map/ppermute | solution.py:1391
  812.4 84.6 %copy-start.33 = (s32[8]{0:T(128)S(1)}, s32[8]{0:T(128)}, u32[]{:S(2)}) copy-start(s32[8]{0:T(128)} %get-tuple-element.140) | copy-start | bytes 100
  812.4 84.6 %copy-start.15 = (bf16[256,2048]{1,0:T(8,128)(2,1)S(1)}, bf16[256,2048]{1,0:T(8,128)(2,1)}, u32[]{:S(2)}) copy-start(bf16[256,2048]{1,0:T(8,128)(2,1)} %reduce-scatter.3.cloned.1.call-done) | copy-start | bytes 3145732
  893.5 59.8 %all-to-all-start.3 = ((bf16[32,64,384]{2,1,0:T(8,128)(2,1)}), bf16[32,64,384]{2,1,0:T(8,128)(2,1)}, u32[]{:S(2)}, u32[]{:S(2)}) async-start(bf16[32,64,384]{2,1,0:T(8,128)(2,1)} %attend_backward.3), calls=%async_computation.4 | async-start | bytes 3145728 | tf_op jit(solution)/shard_map/all_to_all | solution.py:1383
  897.1 35.9 %collective-permute-start.2 = (bf16[256,512]{1,0:T(8,128)(2,1)S(1)}, bf16[256,512]{1,0:T(8,128)(2,1)S(1)}, u32[]{:S(2)}, u32[]{:S(2)}) collective-permute-start(bf16[256,512]{1,0:T(8,128)(2,1)S(1)} %get-tuple-element.149), channel_id=1, source_target_pairs={{0,1},{1,2},{2,3},{3,0},{4,5},{5,6},{6,7},{7,4},{8,9},{9,10},{10,1... | collective-permute-start | bytes 786440 | tf_op jit(solution)/shard_map/ppermute | solution.py:1448
  898.8 53.4 %collective-permute-start.3 = (bf16[256,512]{1,0:T(8,128)(2,1)S(1)}, bf16[256,512]{1,0:T(8,128)(2,1)S(1)}, u32[]{:S(2)}, u32[]{:S(2)}) collective-permute-start(bf16[256,512]{1,0:T(8,128)(2,1)S(1)} %get-tuple-element.151), channel_id=1, source_target_pairs={{0,2},{1,3},{2,0},{3,1},{4,6},{5,7},{6,4},{7,5},{8,10},{9,11},{10,... | collective-permute-start | bytes 786440 | tf_op jit(solution)/shard_map/ppermute | solution.py:1448
  901.3 50.9 %collective-permute-start.4 = (bf16[256,512]{1,0:T(8,128)(2,1)S(1)}, bf16[256,512]{1,0:T(8,128)(2,1)S(1)}, u32[]{:S(2)}, u32[]{:S(2)}) collective-permute-start(bf16[256,512]{1,0:T(8,128)(2,1)S(1)} %get-tuple-element.150), channel_id=1, source_target_pairs={{0,3},{1,0},{2,1},{3,2},{4,7},{5,4},{6,5},{7,6},{8,11},{9,8},{10,9... | collective-permute-start | bytes 786440 | tf_op jit(solution)/shard_map/ppermute | solution.py:1448
  953.4 131.0 %copy-start.23 = (f32[1,8,256]{2,0,1:T(1,128)S(1)}, f32[1,8,256]{2,0,1:T(1,128)}, u32[]{:S(2)}) copy-start(f32[1,8,256]{2,0,1:T(1,128)} %copy-done.22) | copy-start | bytes 24580
  953.4 131.0 %copy-start.30 = (f32[512]{0:T(512)S(1)}, f32[512]{0:T(512)}, u32[]{:S(2)}) copy-start(f32[512]{0:T(512)} %copy-done.29) | copy-start | bytes 6148
  1084.3 16.2 %copy-start.14 = (f32[256,768]{1,0:T(8,128)S(1)}, f32[256,768]{1,0:T(8,128)}, u32[]{:S(2)}) copy-start(f32[256,768]{1,0:T(8,128)} %get-tuple-element.89) | copy-start | bytes 2359300
  1084.4 17.1 %copy-start.8 = (bf16[8,64,2048]{2,1,0:T(8,128)(2,1)S(1)}, bf16[8,64,2048]{2,1,0:T(8,128)(2,1)}, u32[]{:S(2)}) copy-start(bf16[8,64,2048]{2,1,0:T(8,128)(2,1)} %copy-done.7) | copy-start | bytes 6291460
  1089.2 28.3 %all-to-all-start.4 = ((f32[32,2,256]{2,1,0:T(2,128)}), f32[32,2,256]{2,1,0:T(2,128)S(1)}, u32[]{:S(2)}, u32[]{:S(2)}) async-start(f32[32,2,256]{2,1,0:T(2,128)} %bitcast.31), calls=%async_computation.5 | async-start | bytes 131072 | tf_op jit(solution)/shard_map/all_to_all | solution.py:1496
  1110.3 4.4 copy-start.11
  (4 other events, 8.8 us)
Sparse Core Ops, SparseCore 0:
  11.9 172.5 all-gather.2
  186.5 85.1 all-gather.4
  690.1 86.3 reduce-scatter.2
  780.5 175.4 reduce-scatter.4

commit v9 on v8

--- a/solution.py
+++ b/solution.py
@@ -474,13 +474,13 @@
 def feed_kernel(
     ring, tile, own_rows, *refs
 ):
-    grad_rows = refs[:ring]
+    grad_rows = refs[: 2 * ring - 1]
     (
         weights, grads_t, rows_t, act_all, grads_all, mixed_all, grad_own,
     held, grads_held, acc_n, acc_m, first_part, arrived, outgoing, mixed_stage, final_stage,
     turned, load_sem, keep_sem, grad_sem, mixed_sem, final_sem,
     row_send, row_recv, sum_send, sum_recv, all_sem,
-    ) = refs[ring:]
+    ) = refs[2 * ring - 1 :]
     me = lax.axis_index("tensor")
     right = lax.rem(me + 1, ring)
     left = lax.rem(me + ring - 1, ring)
@@ -496,7 +496,25 @@
     load.start()
 
     def grad_load(s):
-        return pltpu.make_async_copy(grad_rows[s], grads_held.at[s % 2], grad_sem.at[s % 2])
+        def copy_of(source):
+            return pltpu.make_async_copy(
+                grad_rows[source], grads_held.at[s % 2], grad_sem.at[s % 2]
+            )
+
+        if s == 0:
+            copy_of(0).start()
+            return
+
+        @pl.when(me >= s)
+        def _():
+            copy_of(s).start()
+
+        @pl.when(me < s)
+        def _():
+            copy_of(ring - 1 + ring - s).start()
+
+    def grad_wait(s):
+        pltpu.make_async_copy(grad_rows[0], grads_held.at[s % 2], grad_sem.at[s % 2]).wait()
 
     def part_of(array, s):
         count = own_rows.shape[0]
@@ -505,7 +523,7 @@
     def grad_keep(s):
         return pltpu.make_async_copy(turned.at[1], part_of(grads_t, s), all_sem)
 
-    grad_load(0).start()
+    grad_load(0)
     load.wait()
 
     def pass_rows(s):
@@ -554,9 +572,9 @@
 
             @pl.when(s == k)
             def _(k=k):
-                grad_load(k).wait()
+                grad_wait(k)
                 if k < ring - 1:
-                    grad_load(k + 1).start()
+                    grad_load(k + 1)
 
         slot = lax.rem(s, 2)
         turned[1] = grads_held[slot].T
@@ -661,7 +679,7 @@
             jax.ShapeDtypeStruct((ring, count, width), bf16),
             jax.ShapeDtypeStruct((count, width), bf16),
         ],
-        in_specs=[any_spec] * (2 + ring),
+        in_specs=[any_spec] * (1 + 2 * ring),
         out_specs=[any_spec] * 6,
         scratch_shapes=[
             pltpu.VMEM((ring, count, width), bf16),
@@ -822,7 +840,7 @@
 
 
 def collect_kernel(
-    tp_count, dp_count, hops, shard, second, gains, chunk, out, second_out, gains_out, chunks_out,
+    tp_count, dp_count, shard, second, gains, chunk, out, second_out, gains_out, chunks_out,
     second_send, second_recv, own_sem, ring_send, ring_recv, send, recv, gain_send, gain_recv, chunk_send, chunk_recv,
 ):
     my_dp = lax.axis_index("dp")
@@ -882,15 +900,17 @@
             device_id_type=MESH,
         )
 
-    def onward(hop):
+    def step(way):
         return pltpu.make_async_remote_copy(
-            src_ref=chunk if hop == 0 else chunks_out.at[hop - 1],
-            dst_ref=chunks_out.at[hop],
-            send_sem=chunk_send.at[hop],
-            recv_sem=chunk_recv.at[hop],
-            device_id={"tensor": lax.rem(my_tp + 1, tp_count)},
+            src_ref=chunk,
+            dst_ref=chunks_out.at[way],
+            send_sem=chunk_send.at[way],
+            recv_sem=chunk_recv.at[way],
+            device_id={"tensor": lax.rem(my_tp + (1, tp_count - 1)[way], tp_count)},
             device_id_type=MESH,
         )
+
+    has_right, has_left = my_tp < tp_count - 1, my_tp > 0
 
     def within(j, s, k, m):
         order = orders[s]
@@ -915,7 +935,15 @@
         across(j).start()
     for j in range(1, dp_count):
         gain_copy(j).start()
-    onward(0).start()
+
+    @pl.when(has_right)
+    def _():
+        step(0).start()
+
+    @pl.when(has_left)
+    def _():
+        step(1).start()
+
     own.wait()
     for phase in range(tp_count + steps):
         for k in reversed(range(steps + 1)):
@@ -936,9 +964,6 @@
         if phase == tp_count:
             for j in range(1, tp_count):
                 second_copy(j).start()
-        if tp_count <= phase < tp_count + hops - 1:
-            onward(phase - tp_count).wait_recv()
-            onward(phase - tp_count + 1).start()
     for j in range(tp_count):
         if j > 0:
             across(j).wait_send()
@@ -952,24 +977,30 @@
         second_copy(j).wait()
     for j in range(1, dp_count):
         gain_copy(j).wait()
-    for hop in range(hops):
-        if hop == hops - 1:
-            onward(hop).wait_recv()
-        onward(hop).wait_send()
-
-
-def collect(shard, second, gains, chunk, tp_count, dp_count, hops, collective_id):
+
+    @pl.when(has_right)
+    def _():
+        step(0).wait_send()
+        step(1).wait_recv()
+
+    @pl.when(has_left)
+    def _():
+        step(1).wait_send()
+        step(0).wait_recv()
+
+
+def collect(shard, second, gains, chunk, tp_count, dp_count, collective_id):
     rows, cols = shard.shape
     dma = pltpu.SemaphoreType.DMA
     vmem_spec = pl.BlockSpec(memory_space=pltpu.VMEM)
     any_spec = pl.BlockSpec(memory_space=pl.ANY)
     return pl.pallas_call(
-        functools.partial(collect_kernel, tp_count, dp_count, hops),
+        functools.partial(collect_kernel, tp_count, dp_count),
         out_shape=[
             jax.ShapeDtypeStruct((tp_count, dp_count * rows, cols), shard.dtype),
             jax.ShapeDtypeStruct((tp_count,) + second.shape, second.dtype),
             jax.ShapeDtypeStruct((dp_count,) + gains.shape, gains.dtype),
-            jax.ShapeDtypeStruct((hops,) + chunk.shape, chunk.dtype),
+            jax.ShapeDtypeStruct((2,) + chunk.shape, chunk.dtype),
         ],
         in_specs=[vmem_spec, vmem_spec, vmem_spec, any_spec],
         out_specs=[any_spec] * 4,
@@ -983,8 +1014,8 @@
             dma((tp_count, 2, dp_count - 1)),
             dma((dp_count,)),
             dma((dp_count,)),
-            dma((hops,)),
-            dma((hops,)),
+            dma((2,)),
+            dma((2,)),
         ],
         compiler_params=pltpu.CompilerParams(collective_id=collective_id, has_side_effects=True),
         cost_estimate=pl.CostEstimate(
@@ -1089,16 +1120,14 @@
 
 
 def total_kernel(
-    tp_count, dp_count, hops, groups, rows, *refs
+    tp_count, dp_count, groups, rows, *refs
 ):
     parts = refs[:groups]
-    running = refs[groups]
-    addends = refs[groups + 1 : groups + hops]
     (
-        weights, out, grad_rows, last_chunk,
-        turned, mine, got, got_across, held, chunks, onward,
-        load_sem, send, recv, across_send, across_recv, chunk_send, chunk_recv,
-    ) = refs[groups + hops :]
+        to_right, to_left, weights, out, grad_rows, from_sides,
+        turned, mine, got, got_across, held, load_sem, send, recv,
+        across_send, across_recv, chunk_send, chunk_recv,
+    ) = refs[groups:]
     my_dp = lax.axis_index("dp")
     my_tp = lax.axis_index("tensor")
     own_rows = out.shape[0]
@@ -1125,18 +1154,25 @@
         )
     pl.semaphore_wait(barrier, tp_count - 1 + steps)
 
-    def hop(n):
-        source = running if n == 0 else onward.at[n - 1]
+    def step(way):
         return pltpu.make_async_remote_copy(
-            src_ref=source,
-            dst_ref=last_chunk if n == hops - 1 else chunks.at[n],
-            send_sem=chunk_send.at[n],
-            recv_sem=chunk_recv.at[n],
-            device_id={"tensor": lax.rem(my_tp + 1, tp_count)},
+            src_ref=(to_right, to_left)[way],
+            dst_ref=from_sides.at[way],
+            send_sem=chunk_send.at[way],
+            recv_sem=chunk_recv.at[way],
+            device_id={"tensor": lax.rem(my_tp + (1, tp_count - 1)[way], tp_count)},
             device_id_type=MESH,
         )
 
-    hop(0).start()
+    has_right, has_left = my_tp < tp_count - 1, my_tp > 0
+
+    @pl.when(has_right)
+    def _():
+        step(0).start()
+
+    @pl.when(has_left)
+    def _():
+        step(1).start()
 
     def block(j, s, owner):
         return j, pl.ds(pl.multiple_of(owner * own_rows + s * half, half), half)
@@ -1212,11 +1248,6 @@
                     exchange_part(j, s, k, m).start()
             elif j < tp_count - 1:
                 across(j).start()
-        if tp_count <= phase < tp_count + hops - 1:
-            n = phase - tp_count
-            hop(n).wait_recv()
-            onward[n] = (chunks[n].astype(f32) + addends[n][...].astype(f32)).astype(bf16)
-            hop(n + 1).start()
     total = mine[
         tp_count - 1, pl.ds(pl.multiple_of(my_dp * own_rows, own_rows), own_rows), :
     ].astype(f32)
@@ -1224,9 +1255,17 @@
         across(j).wait_recv()
         total += got_across[j].astype(f32)
     out[...] = total
-    hop(hops - 1).wait_recv()
-    for n in range(hops):
-        hop(n).wait_send()
+
+    @pl.when(has_right)
+    def _():
+        step(0).wait_send()
+        step(1).wait_recv()
+
+    @pl.when(has_left)
+    def _():
+        step(1).wait_send()
+        step(0).wait_recv()
+
     for j in range(tp_count):
         if j < tp_count - 1:
             across(j).wait_send()
@@ -1235,22 +1274,21 @@
                 exchange_part(j, s, k, m).wait_send()
 
 
-def total_grads(rows, parts, running, addends, weights, dp_count, collective_id):
+def total_grads(rows, parts, to_right, to_left, weights, dp_count, collective_id):
     tp_count, width, cols = weights.shape
     count = rows.shape[0]
     own_rows = width // dp_count
-    hops = len(addends) + 1
     vmem_spec = pl.BlockSpec(memory_space=pltpu.VMEM)
     any_spec = pl.BlockSpec(memory_space=pl.ANY)
     dma = pltpu.SemaphoreType.DMA
     return pl.pallas_call(
-        functools.partial(total_kernel, tp_count, dp_count, hops, len(parts)),
+        functools.partial(total_kernel, tp_count, dp_count, len(parts)),
         out_shape=[
             jax.ShapeDtypeStruct((own_rows, cols), f32),
             jax.ShapeDtypeStruct((count, width), f32),
-            jax.ShapeDtypeStruct((count, width), bf16),
+            jax.ShapeDtypeStruct((2, count, width), bf16),
         ],
-        in_specs=[vmem_spec] * (1 + len(parts) + hops) + [any_spec],
+        in_specs=[vmem_spec] * (1 + len(parts)) + [any_spec] * 3,
         out_specs=[vmem_spec, vmem_spec, any_spec],
         scratch_shapes=[
             pltpu.VMEM((width, count), bf16),
@@ -1258,15 +1296,13 @@
             pltpu.VMEM((tp_count, 2, dp_count - 1, own_rows // 2, cols), bf16),
             pltpu.VMEM((tp_count - 1, own_rows, cols), bf16),
             pltpu.VMEM((2, width, cols), bf16),
-            pltpu.VMEM((max(hops - 1, 1), count, width), bf16),
-            pltpu.VMEM((max(hops - 1, 1), count, width), bf16),
             dma((2,)),
             dma((tp_count, 2, dp_count - 1)),
             dma((tp_count, 2, dp_count - 1)),
             dma((tp_count,)),
             dma((tp_count,)),
-            dma((hops,)),
-            dma((hops,)),
+            dma((2,)),
+            dma((2,)),
         ],
         compiler_params=pltpu.CompilerParams(
             collective_id=collective_id, has_side_effects=True, vmem_limit_bytes=62 * 1024 * 1024
@@ -1277,7 +1313,7 @@
             transcendentals=0,
         ),
         name="total_grads",
-    )(rows, *parts, running, *addends, weights)
+    )(rows, *parts, to_right, to_left, weights)
 
 
 def rms_scale(hidden):
@@ -1385,30 +1421,30 @@
     def trade_back(value):
         return trade(value).reshape(tp_count, tok_dev, value.shape[-1])
 
-    ring_next = [(t, (t + 1) % tp_count) for t in range(tp_count)]
-
-    def pass_on(value):
-        return lax.ppermute(value, "tensor", ring_next)
+    def pass_on(values, first, last):
+        return (
+            lax.ppermute(values[0], "tensor", [(t, t + 1) for t in range(*first)]),
+            lax.ppermute(values[1], "tensor", [(t, t - 1) for t in range(*last)]),
+        )
 
     grad_out = grad_top * valid_rows
-    grad_chunks = [grad_out.astype(bf16)]
+    own_chunk = grad_out.astype(bf16)
     mlp_shard = jnp.concatenate([w_gate, w_up, w_down.T], axis=1)
     w_mlp = lax.all_gather(mlp_shard, "dp", axis=0, tiled=True)
-    hops = min(2, tp_count - 1)
-    w_qkv, out_shards, gains, got_chunks = collect(
-        qkv_shard, w_out.T, jnp.stack([attn_gain, mlp_gain]), grad_chunks[0], tp_count, dp_count,
-        hops, 1,
+    w_qkv, out_shards, gains, sides = collect(
+        qkv_shard, w_out.T, jnp.stack([attn_gain, mlp_gain]), own_chunk, tp_count, dp_count, 1
     )
     w_out_t = lax.all_gather(out_shards, "dp", axis=1, tiled=True)
-    grad_chunks += [got_chunks[hop] for hop in range(hops)]
+    chunks = [(sides[0], sides[1])]
     gains = gains.transpose(1, 0, 2).reshape(2, -1).astype(f32)
     gain_one, gain_two = gains[0], gains[1]
 
     scale_one = rms_scale(hidden_in)
     normed_one = (hidden_in * scale_one * gain_one).astype(bf16)
     slots = project(normed_one, w_qkv, dp_count, 3)
-    for hop in range(hops + 1, tp_count):
-        grad_chunks.append(pass_on(after(grad_chunks[-1], slots)))
+    for n in range(2, tp_count):
+        passed = after(chunks[-1], slots) if n == 2 else chunks[-1]
+        chunks.append(pass_on(passed, (n - 1, tp_count - 1), (1, tp_count - n + 1)))
     saved, mixed = [], []
     for g in groups:
         q_t, k_t, k_rows, v_t, v_rows = prepare(
@@ -1418,7 +1454,7 @@
             q_t, k_rows, v_t, begin, first_block, perm, page_rows, block_len
         )
         saved.append((q_t, k_rows, k_t, v_rows, o_t, lse))
-        mixed.append(trade_back(after(o_slots, grad_chunks[-1]) if g else o_slots))
+        mixed.append(trade_back(after(o_slots, chunks[1]) if g else o_slots))
     hidden_mid = hidden_in
     for g in groups:
         hidden_mid = gather_sum(mixed[g], w_out_t, g, hidden_mid)
@@ -1426,14 +1462,17 @@
     scale_two = rms_scale(hidden_mid)
     normed_two = (hidden_mid * scale_two * gain_two).astype(bf16)
     grads_t, rows_t, inner_act, grad_gate_up, partial_two, grad_normed_two = feed(
-        normed_two, grad_chunks, w_mlp, tp_count
+        normed_two, [own_chunk] + [c[0] for c in chunks] + [c[1] for c in chunks], w_mlp, tp_count
     )
     grad_normed_two = grad_normed_two.astype(f32)
     grad_mid_norm, gain_two_part = norm_back(grad_normed_two, hidden_mid, scale_two, gain_two)
     grad_mid = grad_out + grad_mid_norm
 
     def add_on(arrived, s):
-        return (arrived.astype(f32) + partial_two[s].astype(f32)).astype(bf16)
+        return tuple(
+            (value.astype(f32) + partial_two[at].astype(f32)).astype(bf16)
+            for value, at in zip(arrived, (s, tp_count - s))
+        )
 
     def reduce_dp(grad):
         return lax.psum_scatter(grad.astype(bf16), "dp", scatter_dimension=0, tiled=True)
@@ -1456,8 +1495,8 @@
         rows_t, grads_t, grad_gate_up, inner_act, tp_count, dp_count, 2,
     )
     sum_mlp = reduce_dp(grad_wmlp)
-    first_part = after(partial_two[1], grad_slots)
-    branch_two = pass_on(first_part)
+    first_part = after((partial_two[1], partial_two[tp_count - 1]), grad_slots)
+    passing = pass_on(first_part, (0, 1), (tp_count - 1, tp_count))
     grad_qkv = []
     for g in groups:
         q_t, k_rows, k_t, v_rows, o_t, lse = saved[g]
@@ -1465,25 +1504,21 @@
             after(grad_slots, (back, sum_out) if g else first_part), g, q_t, k_rows, k_t, v_rows,
             o_t, lse, begin, cos_t, sin_t, first_block, perm, page_rows, block_len,
         )
-        grad_qkv.append(trade_back(after(back, (grad_qkv[-1], branch_two)) if g else back))
+        grad_qkv.append(trade_back(after(back, (grad_qkv[-1], passing)) if g else back))
     hidden = sum_mlp.shape[1] // 3
-    hops = min(2, tp_count - 2)
-    sum_qkv, grad_normed_one, branch_two = total_grads(
-        normed_one,
-        grad_qkv,
-        add_on(branch_two, 2),
-        [partial_two[2 + n] for n in range(1, hops)],
-        w_qkv,
-        dp_count,
-        4,
+    for s in range(2, tp_count - 1):
+        passing = pass_on(add_on(passing, s), (0, s), (tp_count - s, tp_count))
+    passing = add_on(passing, tp_count - 1)
+    sum_qkv, grad_normed_one, sides = total_grads(
+        normed_one, grad_qkv, passing[0], passing[1], w_qkv, dp_count, 4
     )
+    branch_two = jnp.where(tp_index > 0, sides[0].astype(f32), 0.0)
+    branch_two += jnp.where(tp_index < tp_count - 1, sides[1].astype(f32), 0.0)
     each = group_q + 2 * HD
     sum_qkv = [sum_qkv[:, g * each : (g + 1) * each] for g in groups]
-    for s in range(2 + hops, tp_count):
-        branch_two = pass_on(add_on(branch_two, s))
     sum_out = reduce_tensor(sum_out)
     result = (
-        (after(hidden_mid, back) + branch_two.astype(f32) + partial_two[0].astype(f32)) * valid_rows
+        (after(hidden_mid, back) + branch_two + partial_two[0].astype(f32)) * valid_rows
     ).astype(bf16)
     grad_in_norm, gain_one_part = norm_back(grad_normed_one, hidden_in, scale_one, gain_one)
     grad_in = (grad_mid + grad_in_norm).astype(bf16)

time: 1140 us -> 1080 us (0.947)
  Pallas kernels: 842 us -> 765 us
  starting transfers between devices: 58.8 us -> 70.7 us
    pallas_call x2, Pallas kernels: 290 us -> 199 us  [the longest x1 118 us: collect(): pl.pallas_call(functools.partial(collect_kernel, tp_count, dp_count), out...]
    all_to_all x4, waiting for transfers between devices: 33.9 us -> 19.1 us  [trade(): lax.all_to_all(blocks, everyone, split_axis=0, concat_axis=0, tiled=True)]
    all_to_all x4, starting transfers between devices: 22 us -> 34.6 us  [trade(): lax.all_to_all(blocks, everyone, split_axis=0, concat_axis=0, tiled=True)]
    ppermute x2 -> x8, waiting for transfers between devices: 46.6 us -> 53.5 us  [the longest x4 29 us: pass_on(): lax.ppermute(values[0], 'tensor', [(t, t + 1) for t in range(*first)])]
  transfers between devices with their start and end apart: 14 -> 20, of which waited for: 6 -> 8; matrix products, arithmetic and copies ran while one was open for 5% -> 7% of each run, Pallas kernels for 48% -> 44%
where the time goes in v9:
time: 1080 us; the launch traced here: 1070 us
  Pallas kernels  765 us (71%)
  waiting for transfers between devices  122 us (11%)
  starting transfers between devices  70.7 us (7%)
  other arithmetic  60.9 us (6%)
  local copies, waits for them, and re-layouts  41.1 us (4%)
  between operations  14.8 us (1%)
    pallas_call x1, Pallas kernels, feed(): pl.pallas_call(functools.partial(feed_kernel, ring, min(tile, hidden)), o...  277 us
    pallas_call x1, Pallas kernels, collect(): pl.pallas_call(functools.partial(collect_kernel, tp_count, dp_count), out...  118 us
    pallas_call x1, Pallas kernels, total_grads(): pl.pallas_call(functools.partial(total_kernel, tp_count, dp_count, len(pa...  81.2 us
    pallas_call x1, Pallas kernels, weigh(): pl.pallas_call(functools.partial(weigh_kernel, tp_count, dp_count, min(51...  67.8 us
    pallas_call x1, Pallas kernels, project(): pl.pallas_call(functools.partial(project_kernel, tp_count, dp_count), out...  63.9 us
    pallas_call x2, Pallas kernels, attend_backward(): pl.pallas_call(functools.partial(backward_kernel, q_heads, kv_heads, page...  58.4 us
    ppermute x3, waiting for transfers between devices, reduce_tensor(): total = total + lax.ppermute(block, 'tensor', pairs).astype(f32)  48.9 us
    pallas_call x2, Pallas kernels, attend_forward(): pl.pallas_call(functools.partial(forward_kernel, q_heads, kv_heads, page_...  39.7 us
  transfers between devices with their start and end apart: 20, of which 8 were waited for; matrix products, arithmetic and copies ran while one was open for 7% of the time, Pallas kernels for 44%

profile of v9, /device:TPU:0, one launch (start us, length us, event | category | flops | bytes accessed | tf_op | source)
XLA Modules:
  0.0 1074.1 jit_solution(15235216292450411421)
XLA Ops:
  8.7 3.0 pad_maximum_fusion
  16.7 2.3 gather_fusion.1
  23.5 117.6 %collect.1 = (bf16[4,2048,768]{2,1,0:T(8,128)(2,1)}, bf16[4,256,512]{2,1,0:T(8,128)(2,1)}, bf16[8,2,256]{2,1,0:T(2,128)(2,1)}, bf16[2,512,2048]{2,1,0:T(8,128)(2,1)}) custom-call(bf16[256,768]{1,0:T(8,128)(2,1)} %concatenate.16.shard, bf16[256,512]{1,0:T(8,128)(2,1)} %bitcast.79, bf16[2,256]{1,0:T(2,128)(2,1)} %pad_maximum_fusion.4.gains, ...), custom_call_target="tpu_custom_call" | custom-call | bytes 100663296 | tf_op jit(solution)/shard_map/collect/pallas_call | solution.py:997
  141.1 2.3 gather_fusion
  144.6 5.7 copy-done.3
  150.3 63.9 %project.1.refs_0_.refs_1_.refs_2_.refs_3_ = bf16[32,64,768]{2,1,0:T(8,128)(2,1)S(1)} custom-call(bf16[512,2048]{1,0:T(8,128)(2,1)S(1)} %multiply_convert_fusion.1.rows, bf16[4,2048,768]{2,1,0:T(8,128)(2,1)S(1)} %copy-done.3), custom_call_target="tpu_custom_call" | custom-call | flops 6442450944 | bytes 100663296 | tf_op jit(solution)/shard_map/project/pallas_call | solution.py:449
  214.3 3.0 slice_bitcast_fusion.2
  223.6 6.9 prepare.2
  231.0 19.9 %attend_forward.2 = (bf16[256,2048]{1,0:T(8,128)(2,1)}, f32[4,2048]{1,0:T(4,128)}, bf16[32,64,256]{2,1,0:T(8,128)(2,1)}) custom-call(s32[4]{0:T(128)} %and_select_fusion.4.first_block, s32[32]{0:T(128)} %fusion.13.perm, bf16[256,2048]{1,0:T(8,128)(2,1)} %get-tuple-element.55.q_t.refs_8_, bf16[1,2048,64]{2,1,0:T(8,128)(2,1)} %get-tuple-element.56.k_rows.refs_9_, ...), custom_call_target="tpu_custom_call" | custom-call | flops 1073741824 | bytes 4194304 | tf_op jit(solution)/shard_map/attend_forward/pallas_call | solution.py:174
  250.9 24.0 %all-to-all-start.1 = ((bf16[32,64,256]{2,1,0:T(8,128)(2,1)}), bf16[32,64,256]{2,1,0:T(8,128)(2,1)S(1)}, u32[]{:S(2)}, u32[]{:S(2)}) async-start(bf16[32,64,256]{2,1,0:T(8,128)(2,1)} %get-tuple-element.58), calls=%async_computation.1 | async-start | bytes 2097152 | tf_op jit(solution)/shard_map/all_to_all | solution.py:1419
  274.9 6.7 prepare.3
  281.6 19.8 %attend_forward.3 = (bf16[256,2048]{1,0:T(8,128)(2,1)}, f32[4,2048]{1,0:T(4,128)}, bf16[32,64,256]{2,1,0:T(8,128)(2,1)}) custom-call(s32[4]{0:T(128)} %and_select_fusion.4.first_block, s32[32]{0:T(128)} %fusion.13.perm, bf16[256,2048]{1,0:T(8,128)(2,1)} %get-tuple-element.60.q_t.refs_8_, bf16[1,2048,64]{2,1,0:T(8,128)(2,1)} %get-tuple-element.61.k_rows.refs_9_, ...), custom_call_target="tpu_custom_call" | custom-call | flops 1073741824 | bytes 4194304 | tf_op jit(solution)/shard_map/attend_forward/pallas_call | solution.py:174
  301.4 7.4 all-to-all-done.1
  308.8 3.4 all-to-all-start
  315.5 2.7 bitcast_convert_fusion.refs_0_
  318.2 8.5 gather_sum.2.refs_0_
  326.7 11.8 %all-to-all-done = bf16[32,64,256]{2,1,0:T(8,128)(2,1)} async-done(((bf16[32,64,256]{2,1,0:T(8,128)(2,1)}), bf16[32,64,256]{2,1,0:T(8,128)(2,1)}, u32[]{:S(2)}, u32[]{:S(2)}) %all-to-all-start) | async-done | bytes 1048608 | tf_op jit(solution)/shard_map/all_to_all | solution.py:1419
  338.5 8.6 gather_sum.3
  347.1 2.7 multiply_reduce_fusion.2
  352.2 24.5 %collective-permute-done.3.refs_6_ = bf16[512,2048]{1,0:T(8,128)(2,1)} collective-permute-done((bf16[512,2048]{1,0:T(8,128)(2,1)}, bf16[512,2048]{1,0:T(8,128)(2,1)}, u32[]{:S(2)}, u32[]{:S(2)}) %collective-permute-start.3) | collective-permute-done | bytes 2097184 | tf_op jit(solution)/shard_map/ppermute | solution.py:1427
  376.7 277.5 %feed_forward.1 = (bf16[2048,2048]{1,0:T(8,128)(2,1)}, bf16[2048,2048]{1,0:T(8,128)(2,1)}, bf16[4,512,2048]{2,1,0:T(8,128)(2,1)}, bf16[4,512,4096]{2,1,0:T(8,128...) custom-call(bf16[512,2048]{1,0:T(8,128)(2,1)} %multiply_convert_fusion.own_rows, ...), custom_call_target="tpu_custom_call" | custom-call | flops 103079215104 | bytes 33554432 | tf_op jit(solution)/shard_map/feed_forward/pallas_call | solution.py:672
  654.2 4.2 fusion.5
  658.9 3.9 fusion.20.rows
  662.8 19.1 %outer.1 = bf16[2048,2048]{1,0:T(8,128)(2,1)} custom-call(bf16[512,2048]{1,0:T(8,128)(2,1)} %fusion.20.rows, bf16[4,512,256]{2,1,0:T(8,128)(2,1)} %bitcast.73, bf16[4,512,256]{2,1,0:T(8,128)(2,1)} %bitcast.15.part.refs_1_), custom_call_target="tpu_custom_call" | custom-call | flops 4294967296 | bytes 8388608 | tf_op jit(solution)/shard_map/outer/pallas_call | solution.py:1105
  682.0 9.2 spread.1.grads
  691.3 2.0 copy-done.4
  693.3 67.8 %weigh.1 = (bf16[32,64,512]{2,1,0:T(8,128)(2,1)S(1)}, bf16[2048,6144]{1,0:T(8,128)(2,1)}) custom-call(bf16[4,512,512]{2,1,0:T(8,128)(2,1)S(1)} %copy-done.4, bf16[2048,2048]{1,0:T(8,128)(2,1)} %get-tuple-element.71.rows_t, bf16[2048,2048]{1,0:T(8,128)(2,1)} %get-tuple-element.72.grads_t, bf16[4,512,4096]{2,1,0:T(8,128)(2,1)} %get-tuple-element.73.gate_up, ...), custom_call_target="tpu_custom_call" | custom-call | flops 51539607552 | bytes 41943040 | tf_op jit(solution)/shard_map/weigh/pallas_call | solution.py:811
  762.5 4.9 slice_bitcast_fusion
  767.4 3.5 collective-permute-start.4
  772.9 29.0 %attend_backward.2 = bf16[32,64,384]{2,1,0:T(8,128)(2,1)} custom-call(s32[4]{0:T(128)} %and_select_fusion.4.first_block, s32[32]{0:T(128)} %fusion.13.perm, bf16[32,64,512]{2,1,0:T(8,128)(2,1)} %copy-done, bf16[32,64,512]{2,1,0:T(8,128)(2,1)} %copy-done, bf16[32,64,512]{2,1,0:T(8,128)(2,1)} %copy-done, bf16[32,64,512]{2,1,0:T(8,128)(2,1)} %copy-done, ...), custom_call_target="tpu_custom_call" | custom-call | flops 3221225472 | bytes 6291456 | tf_op jit(solution)/shard_map/attend_backward/pallas_call | solution.py:335
  801.9 3.8 all-to-all-start.2
  805.7 11.4 %collective-permute-done.4 = bf16[512,2048]{1,0:T(8,128)(2,1)S(1)} collective-permute-done((bf16[512,2048]{1,0:T(8,128)(2,1)}, bf16[512,2048]{1,0:T(8,128)(2,1)S(1)}, u32[]{:S(2)}, u32[]{:S(2)}) %collective-permute-start.4) | collective-permute-done | bytes 2097184 | tf_op jit(solution)/shard_map/ppermute | solution.py:1426
  818.5 5.8 fusion.7
  824.3 5.6 collective-permute-start.6
  831.9 29.4 %attend_backward.3 = bf16[32,64,384]{2,1,0:T(8,128)(2,1)} custom-call(s32[4]{0:T(128)} %and_select_fusion.4.first_block, s32[32]{0:T(128)} %fusion.13.perm, bf16[32,64,512]{2,1,0:T(8,128)(2,1)} %copy-done, bf16[32,64,512]{2,1,0:T(8,128)(2,1)} %copy-done, bf16[32,64,512]{2,1,0:T(8,128)(2,1)} %copy-done, bf16[32,64,512]{2,1,0:T(8,128)(2,1)} %copy-done, ...), custom_call_target="tpu_custom_call" | custom-call | flops 3221225472 | bytes 6291456 | tf_op jit(solution)/shard_map/attend_backward/pallas_call | solution.py:335
  861.3 3.4 all-to-all-start.3
  864.9 3.6 collective-permute-start.10
  870.0 17.5 %collective-permute-done.6 = bf16[512,2048]{1,0:T(8,128)(2,1)} collective-permute-done((bf16[512,2048]{1,0:T(8,128)(2,1)}, bf16[512,2048]{1,0:T(8,128)(2,1)}, u32[]{:S(2)}, u32[]{:S(2)}) %collective-permute-start.6) | collective-permute-done | bytes 2097184 | tf_op jit(solution)/shard_map/ppermute | solution.py:1426
  887.5 7.8 add_convert_fusion.1
  895.3 23.1 %collective-permute-done.10 = bf16[256,512]{1,0:T(8,128)(2,1)S(1)} collective-permute-done((bf16[256,512]{1,0:T(8,128)(2,1)S(1)}, bf16[256,512]{1,0:T(8,128)(2,1)S(1)}, u32[]{:S(2)}, u32[]{:S(2)}) %collective-permute-start.10) | collective-permute-done | bytes 262176 | tf_op jit(solution)/shard_map/ppermute | solution.py:1487
  918.4 8.6 collective-permute-done.8
  927.1 17.1 %collective-permute-done.9 = bf16[256,512]{1,0:T(8,128)(2,1)S(1)} collective-permute-done((bf16[256,512]{1,0:T(8,128)(2,1)S(1)}, bf16[256,512]{1,0:T(8,128)(2,1)S(1)}, u32[]{:S(2)}, u32[]{:S(2)}) %collective-permute-start.9) | collective-permute-done | bytes 262176 | tf_op jit(solution)/shard_map/ppermute | solution.py:1487
  945.3 81.2 %total_grads.1 = (f32[256,768]{1,0:T(8,128)}, f32[512,2048]{1,0:T(8,128)}, bf16[2,512,2048]{2,1,0:T(8,128)(2,1)}) custom-call(bf16[512,2048]{1,0:T(8,128)(2,1)} %copy-done.2, bf16[4,512,384]{2,1,0:T(8,128)(2,1)} %bitcast.20.refs_0_, bf16[4,512,384]{2,1,0:T(8,128)(2,1)} %bitcast.21.refs_1_, bf16[512,2048]{1,0:T(8,128)(2,1)} %get-tuple-element.147.refs_2_, ...), custom_call_target="tpu_custom_call" | custom-call | flops 12884901888 | bytes 100663296 | tf_op jit(solution)/shard_map/total_grads/pallas_call | solution.py:1284
  1026.6 4.1 multiply_reduce_fusion
  1031.4 11.0 %all-to-all-start.4 = ((f32[32,2,256]{2,1,0:T(2,128)}), f32[32,2,256]{2,1,0:T(2,128)S(1)}, u32[]{:S(2)}, u32[]{:S(2)}) async-start(f32[32,2,256]{2,1,0:T(2,128)} %bitcast.33), calls=%async_computation.5 | async-start | bytes 131072 | tf_op jit(solution)/shard_map/all_to_all | solution.py:1531
  1043.3 9.6 add_convert_fusion
  1053.7 3.6 gather_fusion.4
  1060.8 4.7 convert_bitcast_fusion
  (158 shorter events, 42.1 us)
Async XLA Ops:
  7.2 267.7 %all-gather.3.cloned.1.call-start = ((), (), s32[]{:S(2)}) async-start(), calls=%async_computation.7 | async-start | bytes 28311552 | tf_op jit(solution)/shard_map/all_gather | solution.py:1433
  11.8 7.3 copy-start.17
  11.8 8.3 copy-start.37
  11.8 8.3 copy-start.38
  11.8 8.3 copy-start.18
  11.8 8.4 copy-start.19
  11.8 8.4 copy-start.20
  11.8 306.4 %all-gather.5.cloned.1.call-start = ((), (), s32[]{:S(2)}) async-start(), calls=%async_computation.8 | async-start | bytes 9437184 | tf_op jit(solution)/shard_map/all_gather | solution.py:1437
  16.7 6.8 copy-start.28
  19.0 122.0 %copy-start.9 = (bf16[8,64,2048]{2,1,0:T(8,128)(2,1)}, bf16[8,64,2048]{2,1,0:T(8,128)(2,1)S(1)}, u32[]{:S(2)}) copy-start(bf16[8,64,2048]{2,1,0:T(8,128)(2,1)S(1)} %gather_fusion.1) | copy-start | bytes 6291460
  143.4 172.1 %copy-start.7 = (bf16[8,64,2048]{2,1,0:T(8,128)(2,1)}, bf16[8,64,2048]{2,1,0:T(8,128)(2,1)S(1)}, u32[]{:S(2)}) copy-start(bf16[8,64,2048]{2,1,0:T(8,128)(2,1)S(1)} %gather_fusion) | copy-start | bytes 6291460
  144.0 70.3 %copy-start.30 = (f32[512]{0:T(512)}, f32[512]{0:T(512)S(1)}, u32[]{:S(2)}) copy-start(f32[512]{0:T(512)S(1)} %rsqrt.20) | copy-start | bytes 6148
  144.0 70.2 %copy-start.23 = (f32[1,8,256]{2,0,1:T(1,128)}, f32[1,8,256]{2,0,1:T(1,128)S(1)}, u32[]{:S(2)}) copy-start(f32[1,8,256]{2,0,1:T(1,128)S(1)} %get-tuple-element.173) | copy-start | bytes 24580
  144.0 205.7 %copy-start.21 = (f32[1,8,256]{2,0,1:T(1,128)}, f32[1,8,256]{2,0,1:T(1,128)S(1)}, u32[]{:S(2)}) copy-start(f32[1,8,256]{2,0,1:T(1,128)S(1)} %get-tuple-element.172) | copy-start | bytes 24580
  144.6 69.7 %copy-start.2 = (bf16[512,2048]{1,0:T(8,128)(2,1)}, bf16[512,2048]{1,0:T(8,128)(2,1)S(1)}, u32[]{:S(2)}) copy-start(bf16[512,2048]{1,0:T(8,128)(2,1)S(1)} %multiply_convert_fusion.1.rows) | copy-start | bytes 6291460
  144.6 5.7 copy-start.3
  150.3 64.0 %copy-start.13 = (bf16[2,512,2048]{2,1,0:T(8,128)(2,1)S(1)}, bf16[2,512,2048]{2,1,0:T(8,128)(2,1)}, u32[]{:S(2)}) copy-start(bf16[2,512,2048]{2,1,0:T(8,128)(2,1)} %get-tuple-element.64) | copy-start | bytes 12582916
  214.3 6.6 copy-start.33
  217.3 84.1 %collective-permute-start = (bf16[512,2048]{1,0:T(8,128)(2,1)}, bf16[512,2048]{1,0:T(8,128)(2,1)}, u32[]{:S(2)}, u32[]{:S(2)}) collective-permute-start(bf16[512,2048]{1,0:T(8,128)(2,1)} %get-tuple-element.65.refs_1_), channel_id=1, source_target_pairs={{1,2},{2,3},{5,6},{6,7},{9,10},{10,11},{13,14},{14,15},{17,18},{18... | collective-permute-start | bytes 6291464 | tf_op jit(solution)/shard_map/ppermute | solution.py:1426
  219.3 82.1 %collective-permute-start.1 = (bf16[512,2048]{1,0:T(8,128)(2,1)}, bf16[512,2048]{1,0:T(8,128)(2,1)}, u32[]{:S(2)}, u32[]{:S(2)}) collective-permute-start(bf16[512,2048]{1,0:T(8,128)(2,1)} %get-tuple-element.66.refs_4_), channel_id=1, source_target_pairs={{1,0},{2,1},{5,4},{6,5},{9,8},{10,9},{13,12},{14,13},{17,16},{18,1... | collective-permute-start | bytes 6291464 | tf_op jit(solution)/shard_map/ppermute | solution.py:1427
  221.0 9.4 copy-start.25
  250.9 57.9 %all-to-all-start.1 = ((bf16[32,64,256]{2,1,0:T(8,128)(2,1)}), bf16[32,64,256]{2,1,0:T(8,128)(2,1)S(1)}, u32[]{:S(2)}, u32[]{:S(2)}) async-start(bf16[32,64,256]{2,1,0:T(8,128)(2,1)} %get-tuple-element.58), calls=%async_computation.1 | async-start | bytes 2097152 | tf_op jit(solution)/shard_map/all_to_all | solution.py:1419
  308.8 9.4 copy-start.12
  308.8 29.7 %all-to-all-start = ((bf16[32,64,256]{2,1,0:T(8,128)(2,1)}), bf16[32,64,256]{2,1,0:T(8,128)(2,1)}, u32[]{:S(2)}, u32[]{:S(2)}) async-start(bf16[32,64,256]{2,1,0:T(8,128)(2,1)} %get-tuple-element.67), calls=%async_computation | async-start | bytes 2097152 | tf_op jit(solution)/shard_map/all_to_all | solution.py:1419
  312.2 519.7 %reduce-scatter.3.cloned.1.call-start = ((), (), s32[]{:S(2)}) async-start(), calls=%async_computation.9 | async-start | bytes 9437184 | tf_op jit(solution)/shard_map/reduce_scatter | solution.py:1478
  312.2 40.0 %collective-permute-start.2 = (bf16[512,2048]{1,0:T(8,128)(2,1)}, bf16[512,2048]{1,0:T(8,128)(2,1)}, u32[]{:S(2)}, u32[]{:S(2)}) collective-permute-start(bf16[512,2048]{1,0:T(8,128)(2,1)} %collective-permute-done.refs_2_), channel_id=1, source_target_pairs={{2,3},{6,7},{10,11},{14,15},{18,19},{22,23},{26,27},{30,31}} | collective-permute-start | bytes 6291464 | tf_op jit(solution)/shard_map/ppermute | solution.py:1426
  314.2 62.5 %collective-permute-start.3 = (bf16[512,2048]{1,0:T(8,128)(2,1)}, bf16[512,2048]{1,0:T(8,128)(2,1)}, u32[]{:S(2)}, u32[]{:S(2)}) collective-permute-start(bf16[512,2048]{1,0:T(8,128)(2,1)} %collective-permute-done.1.refs_5_), channel_id=1, source_target_pairs={{1,0},{5,4},{9,8},{13,12},{17,16},{21,20},{25,24},{29,28}} | collective-permute-start | bytes 6291464 | tf_op jit(solution)/shard_map/ppermute | solution.py:1427
  654.2 4.7 copy-start.10
  654.2 4.7 copy-start.22
  654.2 4.7 copy-start.27
  654.2 4.7 copy-start.29
  682.0 378.8 %reduce-scatter.5.cloned.1.call-start = ((), (), s32[]{:S(2)}) async-start(), calls=%async_computation.10 | async-start | bytes 28311552 | tf_op jit(solution)/shard_map/reduce_scatter | solution.py:1478
  767.4 49.7 %collective-permute-start.4 = (bf16[512,2048]{1,0:T(8,128)(2,1)}, bf16[512,2048]{1,0:T(8,128)(2,1)S(1)}, u32[]{:S(2)}, u32[]{:S(2)}) collective-permute-start(bf16[512,2048]{1,0:T(8,128)(2,1)} %get-tuple-element.77), channel_id=1, source_target_pairs={{0,1},{4,5},{8,9},{12,13},{16,17},{20,21},{24,25},{28,29}} | collective-permute-start | bytes 6291464 | tf_op jit(solution)/shard_map/ppermute | solution.py:1426
  770.9 47.6 %collective-permute-start.5 = (bf16[512,2048]{1,0:T(8,128)(2,1)}, bf16[512,2048]{1,0:T(8,128)(2,1)}, u32[]{:S(2)}, u32[]{:S(2)}) collective-permute-start(bf16[512,2048]{1,0:T(8,128)(2,1)} %get-tuple-element.78), channel_id=1, source_target_pairs={{3,2},{7,6},{11,10},{15,14},{19,18},{23,22},{27,26},{31,30}} | collective-permute-start | bytes 6291464 | tf_op jit(solution)/shard_map/ppermute | solution.py:1427
  801.9 59.4 %all-to-all-start.2 = ((bf16[32,64,384]{2,1,0:T(8,128)(2,1)}), bf16[32,64,384]{2,1,0:T(8,128)(2,1)}, u32[]{:S(2)}, u32[]{:S(2)}) async-start(bf16[32,64,384]{2,1,0:T(8,128)(2,1)} %attend_backward.2), calls=%async_computation.3 | async-start | bytes 3145728 | tf_op jit(solution)/shard_map/all_to_all | solution.py:1419
  824.3 63.2 %collective-permute-start.6 = (bf16[512,2048]{1,0:T(8,128)(2,1)}, bf16[512,2048]{1,0:T(8,128)(2,1)}, u32[]{:S(2)}, u32[]{:S(2)}) collective-permute-start(bf16[512,2048]{1,0:T(8,128)(2,1)} %get-tuple-element.149), channel_id=1, source_target_pairs={{0,1},{1,2},{4,5},{5,6},{8,9},{9,10},{12,13},{13,14},{16,17},{17,1... | collective-permute-start | bytes 6291464 | tf_op jit(solution)/shard_map/ppermute | solution.py:1426
  829.9 57.6 %collective-permute-start.7 = (bf16[512,2048]{1,0:T(8,128)(2,1)S(1)}, bf16[512,2048]{1,0:T(8,128)(2,1)}, u32[]{:S(2)}, u32[]{:S(2)}) collective-permute-start(bf16[512,2048]{1,0:T(8,128)(2,1)S(1)} %get-tuple-element.148), channel_id=1, source_target_pairs={{2,1},{3,2},{6,5},{7,6},{10,9},{11,10},{14,13},{15,14},{18,17},{19... | collective-permute-start | bytes 6291464 | tf_op jit(solution)/shard_map/ppermute | solution.py:1427
  831.9 32.9 %copy-start.34 = (s32[8]{0:T(128)S(1)}, s32[8]{0:T(128)}, u32[]{:S(2)}) copy-start(s32[8]{0:T(128)} %get-tuple-element.144) | copy-start | bytes 100
  831.9 32.9 %copy-start.16 = (bf16[256,2048]{1,0:T(8,128)(2,1)S(1)}, bf16[256,2048]{1,0:T(8,128)(2,1)}, u32[]{:S(2)}) copy-start(bf16[256,2048]{1,0:T(8,128)(2,1)} %reduce-scatter.3.cloned.1.call-done) | copy-start | bytes 3145732
  861.3 84.0 %all-to-all-start.3 = ((bf16[32,64,384]{2,1,0:T(8,128)(2,1)}), bf16[32,64,384]{2,1,0:T(8,128)(2,1)}, u32[]{:S(2)}, u32[]{:S(2)}) async-start(bf16[32,64,384]{2,1,0:T(8,128)(2,1)} %attend_backward.3), calls=%async_computation.4 | async-start | bytes 3145728 | tf_op jit(solution)/shard_map/all_to_all | solution.py:1419
  864.9 53.5 %collective-permute-start.10 = (bf16[256,512]{1,0:T(8,128)(2,1)S(1)}, bf16[256,512]{1,0:T(8,128)(2,1)S(1)}, u32[]{:S(2)}, u32[]{:S(2)}) collective-permute-start(bf16[256,512]{1,0:T(8,128)(2,1)S(1)} %get-tuple-element.158), channel_id=1, source_target_pairs={{0,3},{1,0},{2,1},{3,2},{4,7},{5,4},{6,5},{7,6},{8,11},{9,8},{10,9... | collective-permute-start | bytes 786440 | tf_op jit(solution)/shard_map/ppermute | solution.py:1487
  868.6 58.5 %collective-permute-start.8 = (bf16[256,512]{1,0:T(8,128)(2,1)S(1)}, bf16[256,512]{1,0:T(8,128)(2,1)S(1)}, u32[]{:S(2)}, u32[]{:S(2)}) collective-permute-start(bf16[256,512]{1,0:T(8,128)(2,1)S(1)} %get-tuple-element.157), channel_id=1, source_target_pairs={{0,1},{1,2},{2,3},{3,0},{4,5},{5,6},{6,7},{7,4},{8,9},{9,10},{10,1... | collective-permute-start | bytes 786440 | tf_op jit(solution)/shard_map/ppermute | solution.py:1487
  868.9 75.2 %collective-permute-start.9 = (bf16[256,512]{1,0:T(8,128)(2,1)S(1)}, bf16[256,512]{1,0:T(8,128)(2,1)S(1)}, u32[]{:S(2)}, u32[]{:S(2)}) collective-permute-start(bf16[256,512]{1,0:T(8,128)(2,1)S(1)} %get-tuple-element.159), channel_id=1, source_target_pairs={{0,2},{1,3},{2,0},{3,1},{4,6},{5,7},{6,4},{7,5},{8,10},{9,11},{10,... | collective-permute-start | bytes 786440 | tf_op jit(solution)/shard_map/ppermute | solution.py:1487
  945.3 81.3 %copy-start.24 = (f32[1,8,256]{2,0,1:T(1,128)S(1)}, f32[1,8,256]{2,0,1:T(1,128)}, u32[]{:S(2)}) copy-start(f32[1,8,256]{2,0,1:T(1,128)} %copy-done.23) | copy-start | bytes 24580
  945.3 81.3 %copy-start.31 = (f32[512]{0:T(512)S(1)}, f32[512]{0:T(512)}, u32[]{:S(2)}) copy-start(f32[512]{0:T(512)} %copy-done.30) | copy-start | bytes 6148
  1026.6 15.8 %copy-start.15 = (f32[256,768]{1,0:T(8,128)S(1)}, f32[256,768]{1,0:T(8,128)}, u32[]{:S(2)}) copy-start(f32[256,768]{1,0:T(8,128)} %get-tuple-element.93) | copy-start | bytes 2359300
  1026.6 16.7 %copy-start.8 = (bf16[8,64,2048]{2,1,0:T(8,128)(2,1)S(1)}, bf16[8,64,2048]{2,1,0:T(8,128)(2,1)}, u32[]{:S(2)}) copy-start(bf16[8,64,2048]{2,1,0:T(8,128)(2,1)} %copy-done.7) | copy-start | bytes 6291460
  1031.4 28.8 %all-to-all-start.4 = ((f32[32,2,256]{2,1,0:T(2,128)}), f32[32,2,256]{2,1,0:T(2,128)S(1)}, u32[]{:S(2)}, u32[]{:S(2)}) async-start(f32[32,2,256]{2,1,0:T(2,128)} %bitcast.33), calls=%async_computation.5 | async-start | bytes 131072 | tf_op jit(solution)/shard_map/all_to_all | solution.py:1531
  (11 other events, 32.2 us)
Sparse Core Ops, SparseCore 0:
  11.9 206.9 all-gather.2
  220.9 53.3 all-gather.4
  682.1 87.3 reduce-scatter.2
  773.4 181.7 reduce-scatter.4

commit v10 on v9

--- a/solution.py
+++ b/solution.py
@@ -449,7 +449,10 @@
     return pl.pallas_call(
         functools.partial(project_kernel, tp_count, dp_count),
         out_shape=jax.ShapeDtypeStruct((tp_count * dp_count, page_rows, cols), bf16),
-        in_specs=[pl.BlockSpec(memory_space=pltpu.VMEM), any_spec],
+        in_specs=[
+            pl.BlockSpec(memory_space=pltpu.VMEM),
+            pl.BlockSpec(memory_space=pltpu.HBM),
+        ],
         out_specs=any_spec,
         scratch_shapes=[
             pltpu.VMEM((2, width, cols), bf16),
@@ -475,12 +478,13 @@
     ring, tile, own_rows, *refs
 ):
     grad_rows = refs[: 2 * ring - 1]
+    weights, grads_t, rows_t, act_all, grads_all = refs[2 * ring - 1 : 2 * ring + 4]
+    mixed_all = refs[2 * ring + 4 : 3 * ring + 4]
     (
-        weights, grads_t, rows_t, act_all, grads_all, mixed_all, grad_own,
-    held, grads_held, acc_n, acc_m, first_part, arrived, outgoing, mixed_stage, final_stage,
-    turned, load_sem, keep_sem, grad_sem, mixed_sem, final_sem,
-    row_send, row_recv, sum_send, sum_recv, all_sem,
-    ) = refs[2 * ring - 1 :]
+        grad_own, held, grads_held, acc_n, acc_m, first_part, arrived, outgoing, mixed_stage,
+        final_stage, turned, load_sem, keep_sem, grad_sem, mixed_sem, final_sem,
+        row_send, row_recv, sum_send, sum_recv, all_sem,
+    ) = refs[3 * ring + 4 :]
     me = lax.axis_index("tensor")
     right = lax.rem(me + 1, ring)
     left = lax.rem(me + ring - 1, ring)
@@ -550,7 +554,7 @@
         return pltpu.make_async_copy(turned.at[0], part_of(rows_t, s), keep_sem)
 
     def mixed_store(s):
-        return pltpu.make_async_copy(mixed_stage, mixed_all.at[s], mixed_sem)
+        return pltpu.make_async_copy(mixed_stage, mixed_all[s], mixed_sem)
 
     def chunk(s, carry):
         @pl.when(s > 0)
@@ -616,10 +620,14 @@
 
         @pl.when(s > 0)
         def _():
-            mixed_store(s - 1).wait()
+            mixed_store(0).wait()
 
         mixed_stage[...] = acc_m[...].astype(bf16)
-        mixed_store(s).start()
+        for k in range(ring):
+
+            @pl.when(s == k)
+            def _(k=k):
+                mixed_store(k).start()
 
         @pl.when(s == 0)
         def _():
@@ -641,7 +649,7 @@
         return carry
 
     lax.fori_loop(0, ring, chunk, 0)
-    mixed_store(ring - 1).wait()
+    mixed_store(0).wait()
     pass_sum(ring - 1).wait_recv()
     final_stage[...] = (first_part[...] + arrived[ring - 2].astype(f32)).astype(bf16)
     final = pltpu.make_async_copy(final_stage, grad_own, final_sem)
@@ -676,11 +684,10 @@
             jax.ShapeDtypeStruct((width, ring * count), bf16),
             jax.ShapeDtypeStruct((ring, count, hidden), bf16),
             jax.ShapeDtypeStruct((ring, count, 2 * hidden), bf16),
-            jax.ShapeDtypeStruct((ring, count, width), bf16),
-            jax.ShapeDtypeStruct((count, width), bf16),
-        ],
+        ]
+        + [jax.ShapeDtypeStruct((count, width), bf16)] * (ring + 1),
         in_specs=[any_spec] * (1 + 2 * ring),
-        out_specs=[any_spec] * 6,
+        out_specs=[any_spec] * (5 + ring),
         scratch_shapes=[
             pltpu.VMEM((ring, count, width), bf16),
             pltpu.VMEM((2, count, width), bf16),
@@ -814,7 +821,7 @@
             jax.ShapeDtypeStruct((count, page_rows, cols), bf16),
             jax.ShapeDtypeStruct((width, 3 * hidden), bf16),
         ],
-        in_specs=[any_spec] * 5,
+        in_specs=[pl.BlockSpec(memory_space=pltpu.HBM)] * 5,
         out_specs=[any_spec] * 2,
         scratch_shapes=[
             pltpu.VMEM((2, width, rows), bf16),
@@ -840,7 +847,7 @@
 
 
 def collect_kernel(
-    tp_count, dp_count, shard, second, gains, chunk, out, second_out, gains_out, chunks_out,
+    tp_count, dp_count, shard, second, gains, chunk, out, second_out, gains_out, from_left, from_right,
     second_send, second_recv, own_sem, ring_send, ring_recv, send, recv, gain_send, gain_recv, chunk_send, chunk_recv,
 ):
     my_dp = lax.axis_index("dp")
@@ -903,7 +910,7 @@
     def step(way):
         return pltpu.make_async_remote_copy(
             src_ref=chunk,
-            dst_ref=chunks_out.at[way],
+            dst_ref=(from_left, from_right)[way],
             send_sem=chunk_send.at[way],
             recv_sem=chunk_recv.at[way],
             device_id={"tensor": lax.rem(my_tp + (1, tp_count - 1)[way], tp_count)},
@@ -1000,10 +1007,11 @@
             jax.ShapeDtypeStruct((tp_count, dp_count * rows, cols), shard.dtype),
             jax.ShapeDtypeStruct((tp_count,) + second.shape, second.dtype),
             jax.ShapeDtypeStruct((dp_count,) + gains.shape, gains.dtype),
-            jax.ShapeDtypeStruct((2,) + chunk.shape, chunk.dtype),
+            jax.ShapeDtypeStruct(chunk.shape, chunk.dtype),
+            jax.ShapeDtypeStruct(chunk.shape, chunk.dtype),
         ],
         in_specs=[vmem_spec, vmem_spec, vmem_spec, any_spec],
-        out_specs=[any_spec] * 4,
+        out_specs=[any_spec] * 5,
         scratch_shapes=[
             dma((tp_count,)),
             dma((tp_count,)),
@@ -1431,7 +1439,7 @@
     own_chunk = grad_out.astype(bf16)
     mlp_shard = jnp.concatenate([w_gate, w_up, w_down.T], axis=1)
     w_mlp = lax.all_gather(mlp_shard, "dp", axis=0, tiled=True)
-    w_qkv, out_shards, gains, sides = collect(
+    w_qkv, out_shards, gains, *sides = collect(
         qkv_shard, w_out.T, jnp.stack([attn_gain, mlp_gain]), own_chunk, tp_count, dp_count, 1
     )
     w_out_t = lax.all_gather(out_shards, "dp", axis=1, tiled=True)
@@ -1448,7 +1456,7 @@
     saved, mixed = [], []
     for g in groups:
         q_t, k_t, k_rows, v_t, v_rows = prepare(
-            after(slots, (o_slots, w_mlp)) if g else slots, g, perm, cos_t, sin_t, per_group, 1
+            after(slots, (o_slots, w_mlp, chunks[1])) if g else slots, g, perm, cos_t, sin_t, per_group, 1
         )
         o_t, lse, o_slots = attend_forward(
             q_t, k_rows, v_t, begin, first_block, perm, page_rows, block_len
@@ -1456,12 +1464,13 @@
         saved.append((q_t, k_rows, k_t, v_rows, o_t, lse))
         mixed.append(trade_back(after(o_slots, chunks[1]) if g else o_slots))
     hidden_mid = hidden_in
+    mixed[0] = after(mixed[0], chunks[-1])
     for g in groups:
         hidden_mid = gather_sum(mixed[g], w_out_t, g, hidden_mid)
 
     scale_two = rms_scale(hidden_mid)
     normed_two = (hidden_mid * scale_two * gain_two).astype(bf16)
-    grads_t, rows_t, inner_act, grad_gate_up, partial_two, grad_normed_two = feed(
+    grads_t, rows_t, inner_act, grad_gate_up, *partial_two, grad_normed_two = feed(
         normed_two, [own_chunk] + [c[0] for c in chunks] + [c[1] for c in chunks], w_mlp, tp_count
     )
     grad_normed_two = grad_normed_two.astype(f32)
@@ -1504,9 +1513,15 @@
             after(grad_slots, (back, sum_out) if g else first_part), g, q_t, k_rows, k_t, v_rows,
             o_t, lse, begin, cos_t, sin_t, first_block, perm, page_rows, block_len,
         )
-        grad_qkv.append(trade_back(after(back, (grad_qkv[-1], passing)) if g else back))
+        if g == len(groups) - 1:
+            steps = 2
+            if tp_count > 3:
+                passing = pass_on(add_on(passing, 2), (0, 2), (tp_count - 2, tp_count))
+                steps = 3
+            back = after(back, (grad_qkv, passing))
+        grad_qkv.append(trade_back(back))
     hidden = sum_mlp.shape[1] // 3
-    for s in range(2, tp_count - 1):
+    for s in range(steps, tp_count - 1):
         passing = pass_on(add_on(passing, s), (0, s), (tp_count - s, tp_count))
     passing = add_on(passing, tp_count - 1)
     sum_qkv, grad_normed_one, sides = total_grads(
@@ -1516,7 +1531,7 @@
     branch_two += jnp.where(tp_index < tp_count - 1, sides[1].astype(f32), 0.0)
     each = group_q + 2 * HD
     sum_qkv = [sum_qkv[:, g * each : (g + 1) * each] for g in groups]
-    sum_out = reduce_tensor(sum_out)
+    sum_out = reduce_tensor(after(sum_out, grad_normed_one))
     result = (
         (after(hidden_mid, back) + branch_two + partial_two[0].astype(f32)) * valid_rows
     ).astype(bf16)

time: 1080 us -> 1080 us (level)
  waiting for transfers between devices: 122 us -> 98.5 us
  Pallas kernels: 765 us -> 779 us
    ppermute x3, waiting for transfers between devices: 48.9 us -> 0.01 us  [reduce_tensor(): total = total + lax.ppermute(block, 'tensor', pairs).astype(f32)]
    ppermute x4, waiting for transfers between devices: 24.5 us -> 39.7 us  [pass_on(): lax.ppermute(values[1], 'tensor', [(t, t - 1) for t in range(*last)])]
    all_to_all x4, starting transfers between devices: 34.6 us -> 49.3 us  [trade(): lax.all_to_all(blocks, everyone, split_axis=0, concat_axis=0, tiled=True)]
  transfers between devices with their start and end apart: 20 -> 20, of which waited for: 8 -> 5; matrix products, arithmetic and copies ran while one was open for 7% -> 6% of each run, Pallas kernels for 44% -> 45%
where the time goes in v10:
time: 1080 us; the launch traced here: 1070 us
  Pallas kernels  779 us (72%)
  waiting for transfers between devices  98.5 us (9%)
  starting transfers between devices  80.7 us (7%)
  other arithmetic  62.7 us (6%)
  local copies, waits for them, and re-layouts  35.9 us (3%)
  between operations  14.7 us (1%)
    pallas_call x1, Pallas kernels, feed(): pl.pallas_call(functools.partial(feed_kernel, ring, min(tile, hidden)), o...  275 us
    pallas_call x1, Pallas kernels, collect(): pl.pallas_call(functools.partial(collect_kernel, tp_count, dp_count), out...  118 us
    pallas_call x1, Pallas kernels, total_grads(): pl.pallas_call(functools.partial(total_kernel, tp_count, dp_count, len(pa...  85.8 us
    pallas_call x1, Pallas kernels, weigh(): pl.pallas_call(functools.partial(weigh_kernel, tp_count, dp_count, min(51...  71.3 us
    pallas_call x2, Pallas kernels, attend_backward(): pl.pallas_call(functools.partial(backward_kernel, q_heads, kv_heads, page...  64.4 us
    pallas_call x1, Pallas kernels, project(): pl.pallas_call(functools.partial(project_kernel, tp_count, dp_count), out...  63.9 us
    all_to_all x4, starting transfers between devices, trade(): lax.all_to_all(blocks, everyone, split_axis=0, concat_axis=0, tiled=True)  49.3 us
    pallas_call x2, Pallas kernels, attend_forward(): pl.pallas_call(functools.partial(forward_kernel, q_heads, kv_heads, page_...  43.6 us
  transfers between devices with their start and end apart: 20, of which 5 were waited for; matrix products, arithmetic and copies ran while one was open for 6% of the time, Pallas kernels for 45%

profile of v10, /device:TPU:0, one launch (start us, length us, event | category | flops | bytes accessed | tf_op | source)
XLA Modules:
  0.0 1071.4 jit_solution(3813127024375099726)
XLA Ops:
  8.7 3.0 pad_maximum_fusion
  16.7 2.3 gather_fusion.1
  23.5 117.5 %collect.1 = (bf16[4,2048,768]{2,1,0:T(8,128)(2,1)}, bf16[4,256,512]{2,1,0:T(8,128)(2,1)}, bf16[8,2,256]{2,1,0:T(2,128)(2,1)}, bf16[512,2048]{1,0:T(8,128)(2,1)}, bf16[512,2048]{1,0:T(8,128)(2,1)}) custom-call(bf16[256,768]{1,0:T(8,128)(2,1)} %concatenate.16.shard, bf16[256,512]{1,0:T(8,128)(2,1)} %bitcast.64, bf16[2,256]{1,0:T(2,128)(2,1)} %pad_maximum_fusion.4.gains, ...), custom_call_target="tpu_custom_call" | custom-call | bytes 100663296 | tf_op jit(solution)/shard_map/collect/pallas_call | solution.py:1004
  141.0 2.3 gather_fusion
  144.5 5.7 copy-done.3
  150.3 63.9 %project.1.refs_0_.refs_1_.refs_2_.refs_3_ = bf16[32,64,768]{2,1,0:T(8,128)(2,1)S(1)} custom-call(bf16[512,2048]{1,0:T(8,128)(2,1)S(1)} %multiply_convert_fusion.1.rows, bf16[4,2048,768]{2,1,0:T(8,128)(2,1)S(1)} %copy-done.3), custom_call_target="tpu_custom_call" | custom-call | flops 6442450944 | bytes 100663296 | tf_op jit(solution)/shard_map/project/pallas_call | solution.py:449
  222.1 6.8 prepare.2
  229.4 21.8 %attend_forward.2 = (bf16[256,2048]{1,0:T(8,128)(2,1)}, f32[4,2048]{1,0:T(4,128)}, bf16[32,64,256]{2,1,0:T(8,128)(2,1)}) custom-call(s32[4]{0:T(128)} %and_select_fusion.4.first_block, s32[32]{0:T(128)} %fusion.14.perm, bf16[256,2048]{1,0:T(8,128)(2,1)} %get-tuple-element.61.q_t.refs_8_, bf16[1,2048,64]{2,1,0:T(8,128)(2,1)} %get-tuple-element.62.k_rows.refs_9_, ...), custom_call_target="tpu_custom_call" | custom-call | flops 1073741824 | bytes 4194304 | tf_op jit(solution)/shard_map/attend_forward/pallas_call | solution.py:174
  251.2 22.4 %all-to-all-start.1 = ((bf16[32,64,256]{2,1,0:T(8,128)(2,1)}), bf16[32,64,256]{2,1,0:T(8,128)(2,1)S(1)}, u32[]{:S(2)}, u32[]{:S(2)}) async-start(bf16[32,64,256]{2,1,0:T(8,128)(2,1)} %get-tuple-element.64), calls=%async_computation.1 | async-start | bytes 2097152 | tf_op jit(solution)/shard_map/all_to_all | solution.py:1427
  273.6 2.0 collective-permute-start.2
  275.6 12.1 %collective-permute-done.1.refs_5_ = bf16[512,2048]{1,0:T(8,128)(2,1)} collective-permute-done((bf16[512,2048]{1,0:T(8,128)(2,1)}, bf16[512,2048]{1,0:T(8,128)(2,1)}, u32[]{:S(2)}, u32[]{:S(2)}) %collective-permute-start.1) | collective-permute-done | bytes 2097184 | tf_op jit(solution)/shard_map/ppermute | solution.py:1435
  289.1 6.7 prepare.3
  295.8 21.7 %attend_forward.3 = (bf16[256,2048]{1,0:T(8,128)(2,1)}, f32[4,2048]{1,0:T(4,128)}, bf16[32,64,256]{2,1,0:T(8,128)(2,1)}) custom-call(s32[4]{0:T(128)} %and_select_fusion.4.first_block, s32[32]{0:T(128)} %fusion.14.perm, bf16[256,2048]{1,0:T(8,128)(2,1)} %get-tuple-element.70.q_t.refs_8_, bf16[1,2048,64]{2,1,0:T(8,128)(2,1)} %get-tuple-element.71.k_rows.refs_9_, ...), custom_call_target="tpu_custom_call" | custom-call | flops 1073741824 | bytes 4194304 | tf_op jit(solution)/shard_map/attend_forward/pallas_call | solution.py:174
  317.6 12.4 %all-to-all-start = ((bf16[32,64,256]{2,1,0:T(8,128)(2,1)}), bf16[32,64,256]{2,1,0:T(8,128)(2,1)}, u32[]{:S(2)}, u32[]{:S(2)}) async-start(bf16[32,64,256]{2,1,0:T(8,128)(2,1)} %get-tuple-element.74), calls=%async_computation | async-start | bytes 2097152 | tf_op jit(solution)/shard_map/all_to_all | solution.py:1427
  330.0 2.7 bitcast_convert_fusion.refs_0_
  332.8 27.6 %collective-permute-done.3.refs_6_ = bf16[512,2048]{1,0:T(8,128)(2,1)} collective-permute-done((bf16[512,2048]{1,0:T(8,128)(2,1)}, bf16[512,2048]{1,0:T(8,128)(2,1)}, u32[]{:S(2)}, u32[]{:S(2)}) %collective-permute-start.3) | collective-permute-done | bytes 2097184 | tf_op jit(solution)/shard_map/ppermute | solution.py:1435
  360.3 8.5 gather_sum.2.refs_0_
  368.8 8.5 gather_sum.3
  377.3 2.7 multiply_reduce_fusion.2
  382.5 274.6 %feed_forward.1 = (bf16[2048,2048]{1,0:T(8,128)(2,1)}, bf16[2048,2048]{1,0:T(8,128)(2,1)}, bf16[4,512,2048]{2,1,0:T(8,128)(2,1)}, bf16[4,512,4096]{2,1,0:T(8,128...) custom-call(bf16[512,2048]{1,0:T(8,128)(2,1)} %multiply_convert_fusi, ...), custom_call_target="tpu_custom_call" | custom-call | flops 103079215104 | bytes 33554432 | tf_op jit(solution)/shard_map/feed_forward/pallas_call | solution.py:680
  657.2 4.2 fusion.5
  661.9 3.9 fusion.21.rows
  665.8 18.7 %outer.1 = bf16[2048,2048]{1,0:T(8,128)(2,1)} custom-call(bf16[512,2048]{1,0:T(8,128)(2,1)} %fusion.21.rows, bf16[4,512,256]{2,1,0:T(8,128)(2,1)} %bitcast.58, bf16[4,512,256]{2,1,0:T(8,128)(2,1)} %bitcast.13.part.refs_1_), custom_call_target="tpu_custom_call" | custom-call | flops 4294967296 | bytes 8388608 | tf_op jit(solution)/shard_map/outer/pallas_call | solution.py:1113
  684.6 8.7 spread.1.grads
  695.1 71.3 %weigh.1 = (bf16[32,64,512]{2,1,0:T(8,128)(2,1)S(1)}, bf16[2048,6144]{1,0:T(8,128)(2,1)}) custom-call(bf16[4,512,512]{2,1,0:T(8,128)(2,1)S(1)} %copy-done.4, bf16[2048,2048]{1,0:T(8,128)(2,1)} %get-tuple-element.79.rows_t, bf16[2048,2048]{1,0:T(8,128)(2,1)} %get-tuple-element.80.grads_t, bf16[4,512,4096]{2,1,0:T(8,128)(2,1)} %get-tuple-element.81.gate_up, ...), custom_call_target="tpu_custom_call" | custom-call | flops 51539607552 | bytes 41943040 | tf_op jit(solution)/shard_map/weigh/pallas_call | solution.py:818
  767.7 4.0 collective-permute-start.4
  771.7 2.0 collective-permute-start.6
  773.6 32.2 %attend_backward.2 = bf16[32,64,384]{2,1,0:T(8,128)(2,1)} custom-call(s32[4]{0:T(128)} %and_select_fusion.4.first_block, s32[32]{0:T(128)} %fusion.14.perm, bf16[32,64,512]{2,1,0:T(8,128)(2,1)} %copy-done, bf16[32,64,512]{2,1,0:T(8,128)(2,1)} %copy-done, bf16[32,64,512]{2,1,0:T(8,128)(2,1)} %copy-done, bf16[32,64,512]{2,1,0:T(8,128)(2,1)} %copy-done, ...), custom_call_target="tpu_custom_call" | custom-call | flops 3221225472 | bytes 6291456 | tf_op jit(solution)/shard_map/attend_backward/pallas_call | solution.py:335
  805.8 4.6 all-to-all-start.2
  810.4 6.2 collective-permute-done.4
  816.6 6.8 fusion.7
  823.4 2.0 collective-permute-start.7
  825.3 5.4 collective-permute-start.5
  830.7 32.2 %attend_backward.3 = bf16[32,64,384]{2,1,0:T(8,128)(2,1)} custom-call(s32[4]{0:T(128)} %and_select_fusion.4.first_block, s32[32]{0:T(128)} %fusion.14.perm, bf16[32,64,512]{2,1,0:T(8,128)(2,1)} %copy-done, bf16[32,64,512]{2,1,0:T(8,128)(2,1)} %copy-done, bf16[32,64,512]{2,1,0:T(8,128)(2,1)} %copy-done, bf16[32,64,512]{2,1,0:T(8,128)(2,1)} %copy-done, ...), custom_call_target="tpu_custom_call" | custom-call | flops 3221225472 | bytes 6291456 | tf_op jit(solution)/shard_map/attend_backward/pallas_call | solution.py:335
  863.0 23.2 %collective-permute-done.5 = bf16[512,2048]{1,0:T(8,128)(2,1)} collective-permute-done((bf16[512,2048]{1,0:T(8,128)(2,1)}, bf16[512,2048]{1,0:T(8,128)(2,1)}, u32[]{:S(2)}, u32[]{:S(2)}) %collective-permute-start.5) | collective-permute-done | bytes 2097184 | tf_op jit(solution)/shard_map/ppermute | solution.py:1434
  886.2 10.0 all-to-all-start.3
  896.2 4.5 add_convert_fusion.1.refs_3_
  900.8 3.7 add_convert_fusion.2.refs_2_
  904.4 29.2 %all-to-all-done.3 = bf16[32,64,384]{2,1,0:T(8,128)(2,1)} async-done(((bf16[32,64,384]{2,1,0:T(8,128)(2,1)}), bf16[32,64,384]{2,1,0:T(8,128)(2,1)}, u32[]{:S(2)}, u32[]{:S(2)}) %all-to-all-start.3) | async-done | bytes 1572896 | tf_op jit(solution)/shard_map/all_to_all | solution.py:1427
  933.7 85.8 %total_grads.1 = (f32[256,768]{1,0:T(8,128)}, f32[512,2048]{1,0:T(8,128)}, bf16[2,512,2048]{2,1,0:T(8,128)(2,1)}) custom-call(bf16[512,2048]{1,0:T(8,128)(2,1)} %copy-done.2, bf16[4,512,384]{2,1,0:T(8,128)(2,1)} %bitcast.16.refs_0_, bf16[4,512,384]{2,1,0:T(8,128)(2,1)} %bitcast.17.refs_1_, bf16[512,2048]{1,0:T(8,128)(2,1)} %add_convert_fusion.2.refs_2_, ...), custom_call_target="tpu_custom_call" | custom-call | flops 12884901888 | bytes 100663296 | tf_op jit(solution)/shard_map/total_grads/pallas_call | solution.py:1292
  1019.4 2.0 constant_dynamic-slice_fusion.2
  1021.4 4.4 collective-permute-start.10
  1026.5 4.0 multiply_reduce_fusion
  1031.1 6.1 all-to-all-start.4
  1039.0 9.1 add_convert_fusion
  1049.6 3.6 gather_fusion.4
  1053.2 2.0 gather_fusion.3
  1058.1 4.7 convert_bitcast_fusion
  (155 shorter events, 37.3 us)
Async XLA Ops:
  7.2 281.9 %all-gather.3.cloned.1.call-start = ((), (), s32[]{:S(2)}) async-start(), calls=%async_computation.7 | async-start | bytes 28311552 | tf_op jit(solution)/shard_map/all_gather | solution.py:1441
  11.7 7.3 copy-start.16
  11.7 8.3 copy-start.36
  11.7 8.3 copy-start.37
  11.7 8.3 copy-start.17
  11.7 8.4 copy-start.18
  11.8 8.4 copy-start.19
  11.8 348.6 %all-gather.5.cloned.1.call-start = ((), (), s32[]{:S(2)}) async-start(), calls=%async_computation.8 | async-start | bytes 9437184 | tf_op jit(solution)/shard_map/all_gather | solution.py:1445
  16.7 6.7 copy-start.27
  19.0 122.0 %copy-start.9 = (bf16[8,64,2048]{2,1,0:T(8,128)(2,1)}, bf16[8,64,2048]{2,1,0:T(8,128)(2,1)S(1)}, u32[]{:S(2)}) copy-start(bf16[8,64,2048]{2,1,0:T(8,128)(2,1)S(1)} %gather_fusion.1) | copy-start | bytes 6291460
  143.3 186.7 %copy-start.7 = (bf16[8,64,2048]{2,1,0:T(8,128)(2,1)}, bf16[8,64,2048]{2,1,0:T(8,128)(2,1)S(1)}, u32[]{:S(2)}) copy-start(bf16[8,64,2048]{2,1,0:T(8,128)(2,1)S(1)} %gather_fusion) | copy-start | bytes 6291460
  143.9 70.2 %copy-start.29 = (f32[512]{0:T(512)}, f32[512]{0:T(512)S(1)}, u32[]{:S(2)}) copy-start(f32[512]{0:T(512)S(1)} %rsqrt.20) | copy-start | bytes 6148
  143.9 70.2 %copy-start.22 = (f32[1,8,256]{2,0,1:T(1,128)}, f32[1,8,256]{2,0,1:T(1,128)S(1)}, u32[]{:S(2)}) copy-start(f32[1,8,256]{2,0,1:T(1,128)S(1)} %get-tuple-element.179) | copy-start | bytes 24580
  144.0 236.1 %copy-start.20 = (f32[1,8,256]{2,0,1:T(1,128)}, f32[1,8,256]{2,0,1:T(1,128)S(1)}, u32[]{:S(2)}) copy-start(f32[1,8,256]{2,0,1:T(1,128)S(1)} %get-tuple-element.178) | copy-start | bytes 24580
  144.5 69.6 %copy-start.2 = (bf16[512,2048]{1,0:T(8,128)(2,1)}, bf16[512,2048]{1,0:T(8,128)(2,1)S(1)}, u32[]{:S(2)}) copy-start(bf16[512,2048]{1,0:T(8,128)(2,1)S(1)} %multiply_convert_fusion.1.rows) | copy-start | bytes 6291460
  144.5 5.7 copy-start.3
  150.3 69.1 %copy-start.32 = (s32[1,2048]{1,0:T(1,128)S(1)}, s32[1,2048]{1,0:T(1,128)}, u32[]{:S(2)}) copy-start(s32[1,2048]{1,0:T(1,128)} %param.17) | copy-start | bytes 24580
  215.8 57.8 %collective-permute-start = (bf16[512,2048]{1,0:T(8,128)(2,1)}, bf16[512,2048]{1,0:T(8,128)(2,1)}, u32[]{:S(2)}, u32[]{:S(2)}) collective-permute-start(bf16[512,2048]{1,0:T(8,128)(2,1)} %get-tuple-element.67.refs_1_), channel_id=1, source_target_pairs={{1,2},{2,3},{5,6},{6,7},{9,10},{10,11},{13,14},{14,15},{17,18},{18... | collective-permute-start | bytes 6291464 | tf_op jit(solution)/shard_map/ppermute | solution.py:1434
  217.8 70.0 %collective-permute-start.1 = (bf16[512,2048]{1,0:T(8,128)(2,1)}, bf16[512,2048]{1,0:T(8,128)(2,1)}, u32[]{:S(2)}, u32[]{:S(2)}) collective-permute-start(bf16[512,2048]{1,0:T(8,128)(2,1)} %get-tuple-element.68.refs_4_), channel_id=1, source_target_pairs={{1,0},{2,1},{5,4},{6,5},{9,8},{10,9},{13,12},{14,13},{17,16},{18,1... | collective-permute-start | bytes 6291464 | tf_op jit(solution)/shard_map/ppermute | solution.py:1435
  219.5 9.4 copy-start.24
  251.2 66.3 %all-to-all-start.1 = ((bf16[32,64,256]{2,1,0:T(8,128)(2,1)}), bf16[32,64,256]{2,1,0:T(8,128)(2,1)S(1)}, u32[]{:S(2)}, u32[]{:S(2)}) async-start(bf16[32,64,256]{2,1,0:T(8,128)(2,1)} %get-tuple-element.64), calls=%async_computation.1 | async-start | bytes 2097152 | tf_op jit(solution)/shard_map/all_to_all | solution.py:1427
  273.6 59.1 %collective-permute-start.2 = (bf16[512,2048]{1,0:T(8,128)(2,1)}, bf16[512,2048]{1,0:T(8,128)(2,1)}, u32[]{:S(2)}, u32[]{:S(2)}) collective-permute-start(bf16[512,2048]{1,0:T(8,128)(2,1)} %collective-permute-done.refs_2_), channel_id=1, source_target_pairs={{2,3},{6,7},{10,11},{14,15},{18,19},{22,23},{26,27},{30,31}} | collective-permute-start | bytes 6291464 | tf_op jit(solution)/shard_map/ppermute | solution.py:1434
  287.8 72.6 %collective-permute-start.3 = (bf16[512,2048]{1,0:T(8,128)(2,1)}, bf16[512,2048]{1,0:T(8,128)(2,1)}, u32[]{:S(2)}, u32[]{:S(2)}) collective-permute-start(bf16[512,2048]{1,0:T(8,128)(2,1)} %collective-permute-done.1.refs_5_), channel_id=1, source_target_pairs={{1,0},{5,4},{9,8},{13,12},{17,16},{21,20},{25,24},{29,28}} | collective-permute-start | bytes 6291464 | tf_op jit(solution)/shard_map/ppermute | solution.py:1435
  317.6 15.2 %copy-start.13 = (bf16[32,64,256]{2,1,0:T(8,128)(2,1)}, bf16[32,64,256]{2,1,0:T(8,128)(2,1)S(1)}, u32[]{:S(2)}) copy-start(bf16[32,64,256]{2,1,0:T(8,128)(2,1)S(1)} %all-to-all-done.1) | copy-start | bytes 3145732
  317.6 51.3 %all-to-all-start = ((bf16[32,64,256]{2,1,0:T(8,128)(2,1)}), bf16[32,64,256]{2,1,0:T(8,128)(2,1)}, u32[]{:S(2)}, u32[]{:S(2)}) async-start(bf16[32,64,256]{2,1,0:T(8,128)(2,1)} %get-tuple-element.74), calls=%async_computation | async-start | bytes 2097152 | tf_op jit(solution)/shard_map/all_to_all | solution.py:1427
  330.0 500.8 %reduce-scatter.3.cloned.1.call-start = ((), (), s32[]{:S(2)}) async-start(), calls=%async_computation.9 | async-start | bytes 9437184 | tf_op jit(solution)/shard_map/reduce_scatter | solution.py:1487
  657.1 4.2 copy-start.6
  657.1 4.7 copy-start.10
  657.1 4.7 copy-start.21
  657.2 4.7 copy-start.26
  657.2 4.7 copy-start.28
  684.5 373.6 %reduce-scatter.5.cloned.1.call-start = ((), (), s32[]{:S(2)}) async-start(), calls=%async_computation.10 | async-start | bytes 28311552 | tf_op jit(solution)/shard_map/reduce_scatter | solution.py:1487
  767.7 48.9 %collective-permute-start.4 = (bf16[512,2048]{1,0:T(8,128)(2,1)}, bf16[512,2048]{1,0:T(8,128)(2,1)}, u32[]{:S(2)}, u32[]{:S(2)}) collective-permute-start(bf16[512,2048]{1,0:T(8,128)(2,1)} %get-tuple-element.86), channel_id=1, source_target_pairs={{0,1},{4,5},{8,9},{12,13},{16,17},{20,21},{24,25},{28,29}} | collective-permute-start | bytes 6291464 | tf_op jit(solution)/shard_map/ppermute | solution.py:1434
  771.7 44.9 %collective-permute-start.6 = (bf16[512,2048]{1,0:T(8,128)(2,1)S(1)}, bf16[512,2048]{1,0:T(8,128)(2,1)}, u32[]{:S(2)}, u32[]{:S(2)}) collective-permute-start(bf16[512,2048]{1,0:T(8,128)(2,1)S(1)} %copy-done.14), channel_id=1, source_target_pairs={{3,2},{7,6},{11,10},{15,14},{19,18},{23,22},{27,26},{31,30}} | collective-permute-start | bytes 6291464 | tf_op jit(solution)/shard_map/ppermute | solution.py:1435
  805.8 57.1 %all-to-all-start.2 = ((bf16[32,64,384]{2,1,0:T(8,128)(2,1)}), bf16[32,64,384]{2,1,0:T(8,128)(2,1)}, u32[]{:S(2)}, u32[]{:S(2)}) async-start(bf16[32,64,384]{2,1,0:T(8,128)(2,1)} %attend_backward.2), calls=%async_computation.3 | async-start | bytes 3145728 | tf_op jit(solution)/shard_map/all_to_all | solution.py:1427
  823.4 39.6 %collective-permute-start.7 = (bf16[512,2048]{1,0:T(8,128)(2,1)}, bf16[512,2048]{1,0:T(8,128)(2,1)}, u32[]{:S(2)}, u32[]{:S(2)}) collective-permute-start(bf16[512,2048]{1,0:T(8,128)(2,1)} %get-tuple-element.161), channel_id=1, source_target_pairs={{2,1},{3,2},{6,5},{7,6},{10,9},{11,10},{14,13},{15,14},{18,17},{19... | collective-permute-start | bytes 6291464 | tf_op jit(solution)/shard_map/ppermute | solution.py:1435
  825.3 60.8 %collective-permute-start.5 = (bf16[512,2048]{1,0:T(8,128)(2,1)}, bf16[512,2048]{1,0:T(8,128)(2,1)}, u32[]{:S(2)}, u32[]{:S(2)}) collective-permute-start(bf16[512,2048]{1,0:T(8,128)(2,1)} %get-tuple-element.162), channel_id=1, source_target_pairs={{0,1},{1,2},{4,5},{5,6},{8,9},{9,10},{12,13},{13,14},{16,17},{17,1... | collective-permute-start | bytes 6291464 | tf_op jit(solution)/shard_map/ppermute | solution.py:1434
  830.7 65.5 %copy-start.33 = (s32[8]{0:T(128)S(1)}, s32[8]{0:T(128)}, u32[]{:S(2)}) copy-start(s32[8]{0:T(128)} %get-tuple-element.156) | copy-start | bytes 100
  886.2 47.5 %all-to-all-start.3 = ((bf16[32,64,384]{2,1,0:T(8,128)(2,1)}), bf16[32,64,384]{2,1,0:T(8,128)(2,1)}, u32[]{:S(2)}, u32[]{:S(2)}) async-start(bf16[32,64,384]{2,1,0:T(8,128)(2,1)} %attend_backward.3), calls=%async_computation.4 | async-start | bytes 3145728 | tf_op jit(solution)/shard_map/all_to_all | solution.py:1427
  933.7 92.8 %copy-start.23 = (f32[1,8,256]{2,0,1:T(1,128)S(1)}, f32[1,8,256]{2,0,1:T(1,128)}, u32[]{:S(2)}) copy-start(f32[1,8,256]{2,0,1:T(1,128)} %copy-done.22) | copy-start | bytes 24580
  933.7 92.8 %copy-start.30 = (f32[512]{0:T(512)S(1)}, f32[512]{0:T(512)}, u32[]{:S(2)}) copy-start(f32[512]{0:T(512)} %copy-done.29) | copy-start | bytes 6148
  1019.4 17.8 %copy-start.15 = (f32[256,768]{1,0:T(8,128)S(1)}, f32[256,768]{1,0:T(8,128)}, u32[]{:S(2)}) copy-start(f32[256,768]{1,0:T(8,128)} %get-tuple-element.104) | copy-start | bytes 2359300
  1021.4 34.4 %collective-permute-start.10 = (bf16[256,512]{1,0:T(8,128)(2,1)}, bf16[256,512]{1,0:T(8,128)(2,1)}, u32[]{:S(2)}, u32[]{:S(2)}) collective-permute-start(bf16[256,512]{1,0:T(8,128)(2,1)} %get-tuple-element.164), channel_id=1, source_target_pairs={{0,3},{1,0},{2,1},{3,2},{4,7},{5,4},{6,5},{7,6},{8,11},{9,8},{10,9... | collective-permute-start | bytes 786440 | tf_op jit(solution)/shard_map/ppermute | solution.py:1496
  1025.8 30.0 %collective-permute-start.8 = (bf16[256,512]{1,0:T(8,128)(2,1)S(1)}, bf16[256,512]{1,0:T(8,128)(2,1)}, u32[]{:S(2)}, u32[]{:S(2)}) collective-permute-start(bf16[256,512]{1,0:T(8,128)(2,1)S(1)} %get-tuple-element.163), channel_id=1, source_target_pairs={{0,1},{1,2},{2,3},{3,0},{4,5},{5,6},{6,7},{7,4},{8,9},{9,10},{10,1... | collective-permute-start | bytes 786440 | tf_op jit(solution)/shard_map/ppermute | solution.py:1496
  1025.8 12.4 %copy-start.8 = (bf16[8,64,2048]{2,1,0:T(8,128)(2,1)S(1)}, bf16[8,64,2048]{2,1,0:T(8,128)(2,1)}, u32[]{:S(2)}) copy-start(bf16[8,64,2048]{2,1,0:T(8,128)(2,1)} %copy-done.7) | copy-start | bytes 6291460
  1025.9 30.0 %collective-permute-start.9 = (bf16[256,512]{1,0:T(8,128)(2,1)S(1)}, bf16[256,512]{1,0:T(8,128)(2,1)}, u32[]{:S(2)}, u32[]{:S(2)}) collective-permute-start(bf16[256,512]{1,0:T(8,128)(2,1)S(1)} %get-tuple-element.165), channel_id=1, source_target_pairs={{0,2},{1,3},{2,0},{3,1},{4,6},{5,7},{6,4},{7,5},{8,10},{9,11},{10,... | collective-permute-start | bytes 786440 | tf_op jit(solution)/shard_map/ppermute | solution.py:1496
  1031.1 24.0 %all-to-all-start.4 = ((f32[32,2,256]{2,1,0:T(2,128)}), f32[32,2,256]{2,1,0:T(2,128)S(1)}, u32[]{:S(2)}, u32[]{:S(2)}) async-start(f32[32,2,256]{2,1,0:T(2,128)} %bitcast.26), calls=%async_computation.5 | async-start | bytes 131072 | tf_op jit(solution)/shard_map/all_to_all | solution.py:1546
  1048.1 5.1 copy-start.12
  (10 other events, 24.6 us)
Sparse Core Ops, SparseCore 0:
  11.9 206.9 all-gather.2
  220.8 53.4 all-gather.4
  684.6 91.7 reduce-scatter.2
  780.3 182.9 reduce-scatter.4

commit v11 on v10

--- a/solution.py
+++ b/solution.py
@@ -463,7 +463,7 @@
             dma((tp_count, dp_count)),
         ],
         compiler_params=pltpu.CompilerParams(
-            collective_id=collective_id, has_side_effects=True, vmem_limit_bytes=32 * 1024 * 1024
+            collective_id=collective_id, has_side_effects=True, vmem_limit_bytes=62 * 1024 * 1024
         ),
         cost_estimate=pl.CostEstimate(
             flops=2 * tp_count * total * width * cols,
@@ -831,7 +831,7 @@
             dma((count,)),
         ],
         compiler_params=pltpu.CompilerParams(
-            collective_id=collective_id, has_side_effects=True, vmem_limit_bytes=48 * 1024 * 1024
+            collective_id=collective_id, has_side_effects=True, vmem_limit_bytes=62 * 1024 * 1024
         ),
         cost_estimate=pl.CostEstimate(
             flops=6 * rows * width * hidden,
@@ -1438,11 +1438,11 @@
     grad_out = grad_top * valid_rows
     own_chunk = grad_out.astype(bf16)
     mlp_shard = jnp.concatenate([w_gate, w_up, w_down.T], axis=1)
-    w_mlp = lax.all_gather(mlp_shard, "dp", axis=0, tiled=True)
     w_qkv, out_shards, gains, *sides = collect(
         qkv_shard, w_out.T, jnp.stack([attn_gain, mlp_gain]), own_chunk, tp_count, dp_count, 1
     )
     w_out_t = lax.all_gather(out_shards, "dp", axis=1, tiled=True)
+    w_mlp = lax.all_gather(after(mlp_shard, gains), "dp", axis=0, tiled=True)
     chunks = [(sides[0], sides[1])]
     gains = gains.transpose(1, 0, 2).reshape(2, -1).astype(f32)
     gain_one, gain_two = gains[0], gains[1]
@@ -1456,7 +1456,7 @@
     saved, mixed = [], []
     for g in groups:
         q_t, k_t, k_rows, v_t, v_rows = prepare(
-            after(slots, (o_slots, w_mlp, chunks[1])) if g else slots, g, perm, cos_t, sin_t, per_group, 1
+            after(slots, (o_slots, w_out_t, chunks[1])) if g else slots, g, perm, cos_t, sin_t, per_group, 1
         )
         o_t, lse, o_slots = attend_forward(
             q_t, k_rows, v_t, begin, first_block, perm, page_rows, block_len

time: 1080 us -> 1060 us (0.981)
  Pallas kernels: 779 us -> 760 us
  starting transfers between devices: 80.7 us -> 92.9 us
    all_to_all x4, starting transfers between devices: 49.3 us -> 62.1 us  [trade(): lax.all_to_all(blocks, everyone, split_axis=0, concat_axis=0, tiled=True)]
    pallas_call x1, Pallas kernels: 118 us -> 106 us  [collect(): pl.pallas_call(functools.partial(collect_kernel, tp_count, dp_count), out...]
  transfers between devices with their start and end apart: 20 -> 20, of which waited for: 5 -> 5; matrix products, arithmetic and copies ran while one was open for 6% -> 6% of each run, Pallas kernels for 45% -> 34%
where the time goes in v11:
time: 1060 us
  Pallas kernels  760 us (72%)
  waiting for transfers between devices  98.1 us (9%)
  starting transfers between devices  92.9 us (9%)
  other arithmetic  65.5 us (6%)
  local copies, waits for them, and re-layouts  27.6 us (3%)
  between operations  14.7 us (1%)
    pallas_call x1, Pallas kernels, feed(): pl.pallas_call(functools.partial(feed_kernel, ring, min(tile, hidden)), o...  275 us
    pallas_call x1, Pallas kernels, collect(): pl.pallas_call(functools.partial(collect_kernel, tp_count, dp_count), out...  106 us
    pallas_call x1, Pallas kernels, total_grads(): pl.pallas_call(functools.partial(total_kernel, tp_count, dp_count, len(pa...  84.9 us
    pallas_call x1, Pallas kernels, weigh(): pl.pallas_call(functools.partial(weigh_kernel, tp_count, dp_count, min(51...  69.2 us
    pallas_call x1, Pallas kernels, project(): pl.pallas_call(functools.partial(project_kernel, tp_count, dp_count), out...  68.5 us
    all_to_all x4, starting transfers between devices, trade(): lax.all_to_all(blocks, everyone, split_axis=0, concat_axis=0, tiled=True)  62.1 us
    pallas_call x2, Pallas kernels, attend_backward(): pl.pallas_call(functools.partial(backward_kernel, q_heads, kv_heads, page...  58.5 us
    pallas_call x2, Pallas kernels, attend_forward(): pl.pallas_call(functools.partial(forward_kernel, q_heads, kv_heads, page_...  39.9 us
  transfers between devices with their start and end apart: 20, of which 5 were waited for; matrix products, arithmetic and copies ran while one was open for 6% of the time, Pallas kernels for 34%

profile of v11, /device:TPU:0, one launch (start us, length us, event | category | flops | bytes accessed | tf_op | source)
XLA Modules:
  0.0 1058.9 jit_solution(5479722247038787799)
XLA Ops:
  13.5 2.3 gather_fusion.1
  22.6 106.1 %collect.1 = (bf16[4,2048,768]{2,1,0:T(8,128)(2,1)}, bf16[4,256,512]{2,1,0:T(8,128)(2,1)}, bf16[8,2,256]{2,1,0:T(2,128)(2,1)}, bf16[512,2048]{1,0:T(8,128)(2,1)}, bf16[512,2048]{1,0:T(8,128)(2,1)}) custom-call(bf16[256,768]{1,0:T(8,128)(2,1)} %concatenate.16.shard, bf16[256,512]{1,0:T(8,128)(2,1)} %bitcast.64, bf16[2,256]{1,0:T(2,128)(2,1)} %pad_maximum_fusion.4.gains, ...), custom_call_target="tpu_custom_call" | custom-call | bytes 100663296 | tf_op jit(solution)/shard_map/collect/pallas_call | solution.py:1004
  129.5 3.1 pad_maximum_fusion
  132.6 2.3 gather_fusion
  138.1 68.5 %project.1.refs_0_.refs_1_.refs_2_.refs_3_ = bf16[32,64,768]{2,1,0:T(8,128)(2,1)} custom-call(bf16[512,2048]{1,0:T(8,128)(2,1)} %multiply_convert_fusion.1.rows, bf16[4,2048,768]{2,1,0:T(8,128)(2,1)} %get-tuple-element.61.weights.refs_4_), custom_call_target="tpu_custom_call" | custom-call | flops 6442450944 | bytes 100663296 | tf_op jit(solution)/shard_map/project/pallas_call | solution.py:449
  206.6 2.0 collective-permute-start
  212.9 6.7 prepare.2
  220.1 19.9 %attend_forward.2 = (bf16[256,2048]{1,0:T(8,128)(2,1)}, f32[4,2048]{1,0:T(4,128)}, bf16[32,64,256]{2,1,0:T(8,128)(2,1)}) custom-call(s32[4]{0:T(128)} %and_select_fusion.4.first_block, s32[32]{0:T(128)} %fusion.14.perm, bf16[256,2048]{1,0:T(8,128)(2,1)} %get-tuple-element.62.q_t.refs_8_, bf16[1,2048,64]{2,1,0:T(8,128)(2,1)} %get-tuple-element.63.k_rows.refs_9_, ...), custom_call_target="tpu_custom_call" | custom-call | flops 1073741824 | bytes 4194304 | tf_op jit(solution)/shard_map/attend_forward/pallas_call | solution.py:174
  240.1 24.6 %all-to-all-start.1 = ((bf16[32,64,256]{2,1,0:T(8,128)(2,1)}), bf16[32,64,256]{2,1,0:T(8,128)(2,1)S(1)}, u32[]{:S(2)}, u32[]{:S(2)}) async-start(bf16[32,64,256]{2,1,0:T(8,128)(2,1)} %get-tuple-element.65), calls=%async_computation.1 | async-start | bytes 2097152 | tf_op jit(solution)/shard_map/all_to_all | solution.py:1427
  264.6 2.0 collective-permute-start.2
  266.7 11.8 %collective-permute-done.1.refs_5_ = bf16[512,2048]{1,0:T(8,128)(2,1)} collective-permute-done((bf16[512,2048]{1,0:T(8,128)(2,1)}, bf16[512,2048]{1,0:T(8,128)(2,1)}, u32[]{:S(2)}, u32[]{:S(2)}) %collective-permute-start.1) | collective-permute-done | bytes 2097184 | tf_op jit(solution)/shard_map/ppermute | solution.py:1435
  279.8 6.7 prepare.3
  286.5 20.0 %attend_forward.3 = (bf16[256,2048]{1,0:T(8,128)(2,1)}, f32[4,2048]{1,0:T(4,128)}, bf16[32,64,256]{2,1,0:T(8,128)(2,1)}) custom-call(s32[4]{0:T(128)} %and_select_fusion.4.first_block, s32[32]{0:T(128)} %fusion.14.perm, bf16[256,2048]{1,0:T(8,128)(2,1)} %get-tuple-element.72.q_t.refs_8_, bf16[1,2048,64]{2,1,0:T(8,128)(2,1)} %get-tuple-element.73.k_rows.refs_9_, ...), custom_call_target="tpu_custom_call" | custom-call | flops 1073741824 | bytes 4194304 | tf_op jit(solution)/shard_map/attend_forward/pallas_call | solution.py:174
  306.5 14.4 %all-to-all-start = ((bf16[32,64,256]{2,1,0:T(8,128)(2,1)}), bf16[32,64,256]{2,1,0:T(8,128)(2,1)}, u32[]{:S(2)}, u32[]{:S(2)}) async-start(bf16[32,64,256]{2,1,0:T(8,128)(2,1)} %get-tuple-element.76), calls=%async_computation | async-start | bytes 2097152 | tf_op jit(solution)/shard_map/all_to_all | solution.py:1427
  320.9 2.6 bitcast_convert_fusion.refs_0_
  323.6 27.2 %collective-permute-done.3.refs_6_ = bf16[512,2048]{1,0:T(8,128)(2,1)} collective-permute-done((bf16[512,2048]{1,0:T(8,128)(2,1)}, bf16[512,2048]{1,0:T(8,128)(2,1)}, u32[]{:S(2)}, u32[]{:S(2)}) %collective-permute-start.3) | collective-permute-done | bytes 2097184 | tf_op jit(solution)/shard_map/ppermute | solution.py:1435
  350.8 8.6 gather_sum.2.refs_0_
  359.4 8.5 gather_sum.3
  368.0 2.7 multiply_reduce_fusion.2
  373.1 274.9 %feed_forward.1 = (bf16[2048,2048]{1,0:T(8,128)(2,1)}, bf16[2048,2048]{1,0:T(8,128)(2,1)}, bf16[4,512,2048]{2,1,0:T(8,128)(2,1)}, bf16[4,512,4096]{2,1,0:T(8,128...) custom-call(bf16[512,2048]{1,0:T(8,128)(2,1)} %multiply_convert_fusi, ...), custom_call_target="tpu_custom_call" | custom-call | flops 103079215104 | bytes 33554432 | tf_op jit(solution)/shard_map/feed_forward/pallas_call | solution.py:680
  648.1 4.2 fusion.5
  652.8 3.9 fusion.21.rows
  656.7 18.7 %outer.1 = bf16[2048,2048]{1,0:T(8,128)(2,1)} custom-call(bf16[512,2048]{1,0:T(8,128)(2,1)} %fusion.21.rows, bf16[4,512,256]{2,1,0:T(8,128)(2,1)} %bitcast.58, bf16[4,512,256]{2,1,0:T(8,128)(2,1)} %bitcast.12.part.refs_1_), custom_call_target="tpu_custom_call" | custom-call | flops 4294967296 | bytes 8388608 | tf_op jit(solution)/shard_map/outer/pallas_call | solution.py:1113
  675.5 8.7 spread.1.grads
  684.2 69.2 %weigh.1 = (bf16[32,64,512]{2,1,0:T(8,128)(2,1)}, bf16[2048,6144]{1,0:T(8,128)(2,1)}) custom-call(bf16[4,512,512]{2,1,0:T(8,128)(2,1)} %spread.1.grads, bf16[2048,2048]{1,0:T(8,128)(2,1)} %get-tuple-element.81.rows_t, bf16[2048,2048]{1,0:T(8,128)(2,1)} %get-tuple-element.82.grads_t, bf16[4,512,4096]{2,1,0:T(8,128)(2,1)} %get-tuple-element.83.gate_up, ...), custom_call_target="tpu_custom_call" | custom-call | flops 51539607552 | bytes 41943040 | tf_op jit(solution)/shard_map/weigh/pallas_call | solution.py:818
  753.5 3.0 collective-permute-start.4
  756.5 1.9 collective-permute-start.6
  758.4 29.2 %attend_backward.2 = bf16[32,64,384]{2,1,0:T(8,128)(2,1)} custom-call(s32[4]{0:T(128)} %and_select_fusion.4.first_block, s32[32]{0:T(128)} %fusion.14.perm, bf16[32,64,512]{2,1,0:T(8,128)(2,1)} %get-tuple-element.95.refs_0_.refs_1_.refs_2_.refs_3_.refs_4_.refs_5_.refs_6_.refs_7_, ...), custom_call_target="tpu_custom_call" | custom-call | flops 3221225472 | bytes 6291456 | tf_op jit(solution)/shard_map/attend_backward/pallas_call | solution.py:335
  787.6 10.2 all-to-all-start.2
  797.9 3.5 collective-permute-done.4
  801.4 6.9 fusion.7
  808.3 1.9 collective-permute-start.7
  810.2 4.9 collective-permute-start.5
  815.1 29.3 %attend_backward.3 = bf16[32,64,384]{2,1,0:T(8,128)(2,1)} custom-call(s32[4]{0:T(128)} %and_select_fusion.4.first_block, s32[32]{0:T(128)} %fusion.14.perm, bf16[32,64,512]{2,1,0:T(8,128)(2,1)} %get-tuple-element.95.refs_0_.refs_1_.refs_2_.refs_3_.refs_4_.refs_5_.refs_6_.refs_7_, ...), custom_call_target="tpu_custom_call" | custom-call | flops 3221225472 | bytes 6291456 | tf_op jit(solution)/shard_map/attend_backward/pallas_call | solution.py:335
  844.5 26.3 %collective-permute-done.5 = bf16[512,2048]{1,0:T(8,128)(2,1)} collective-permute-done((bf16[512,2048]{1,0:T(8,128)(2,1)}, bf16[512,2048]{1,0:T(8,128)(2,1)}, u32[]{:S(2)}, u32[]{:S(2)}) %collective-permute-start.5) | collective-permute-done | bytes 2097184 | tf_op jit(solution)/shard_map/ppermute | solution.py:1434
  870.8 12.9 %all-to-all-start.3 = ((bf16[32,64,384]{2,1,0:T(8,128)(2,1)}), bf16[32,64,384]{2,1,0:T(8,128)(2,1)}, u32[]{:S(2)}, u32[]{:S(2)}) async-start(bf16[32,64,384]{2,1,0:T(8,128)(2,1)} %attend_backward.3), calls=%async_computation.4 | async-start | bytes 3145728 | tf_op jit(solution)/shard_map/all_to_all | solution.py:1427
  883.7 4.6 add_convert_fusion.1.refs_3_
  888.3 3.7 add_convert_fusion.2.refs_2_
  892.0 29.2 %all-to-all-done.3 = bf16[32,64,384]{2,1,0:T(8,128)(2,1)} async-done(((bf16[32,64,384]{2,1,0:T(8,128)(2,1)}), bf16[32,64,384]{2,1,0:T(8,128)(2,1)}, u32[]{:S(2)}, u32[]{:S(2)}) %all-to-all-start.3) | async-done | bytes 1572896 | tf_op jit(solution)/shard_map/all_to_all | solution.py:1427
  921.2 84.9 %total_grads.1 = (f32[256,768]{1,0:T(8,128)}, f32[512,2048]{1,0:T(8,128)}, bf16[2,512,2048]{2,1,0:T(8,128)(2,1)}) custom-call(bf16[512,2048]{1,0:T(8,128)(2,1)} %multiply_convert_fusion.1.rows, bf16[4,512,384]{2,1,0:T(8,128)(2,1)} %bitcast.16.refs_0_, bf16[4,512,384]{2,1,0:T(8,128)(2,1)} %bitcast.17.refs_1_, bf16[512,2048]{1,0:T(8,128)(2,1)} %add_convert_fusion.2.refs_2_, ...), custom_call_target="tpu_custom_call" | custom-call | flops 12884901888 | bytes 100663296 | tf_op jit(solution)/shard_map/total_grads/pallas_call | solution.py:1292
  1006.1 2.0 constant_dynamic-slice_fusion.2
  1008.1 5.2 collective-permute-start.10
  1014.0 4.0 multiply_reduce_fusion
  1018.6 6.1 all-to-all-start.4
  1026.5 9.1 add_convert_fusion
  1037.1 3.6 gather_fusion.4
  1040.7 2.0 gather_fusion.3
  1045.6 4.7 convert_bitcast_fusion
  (143 shorter events, 35.5 us)
Async XLA Ops:
  7.2 8.6 copy-start.13
  7.2 8.6 copy-start.14
  7.2 9.6 copy-start.30
  7.2 9.6 copy-start.31
  7.2 272.5 %all-gather.3.cloned.1.call-start = ((), (), s32[]{:S(2)}) async-start(), calls=%async_computation.7 | async-start | bytes 9437184 | tf_op jit(solution)/shard_map/all_gather | solution.py:1444
  13.5 3.4 copy-start.22
  15.8 113.0 %copy-start.5 = (bf16[8,64,2048]{2,1,0:T(8,128)(2,1)}, bf16[8,64,2048]{2,1,0:T(8,128)(2,1)S(1)}, u32[]{:S(2)}) copy-start(bf16[8,64,2048]{2,1,0:T(8,128)(2,1)S(1)} %gather_fusion.1) | copy-start | bytes 6291460
  16.9 112.0 %copy-start.12 = (bf16[2048,256]{1,0:T(8,128)(2,1)S(1)}, bf16[2048,256]{1,0:T(8,128)(2,1)}, u32[]{:S(2)}) copy-start(bf16[2048,256]{1,0:T(8,128)(2,1)} %param.27) | copy-start | bytes 3145732
  128.8 244.4 %all-gather.5.cloned.1.call-start = ((), (), s32[]{:S(2)}) async-start(), calls=%async_computation.8 | async-start | bytes 28311552 | tf_op jit(solution)/shard_map/all_gather | solution.py:1445
  135.5 71.2 %copy-start.24 = (f32[512]{0:T(512)}, f32[512]{0:T(512)S(1)}, u32[]{:S(2)}) copy-start(f32[512]{0:T(512)S(1)} %rsqrt.20) | copy-start | bytes 6148
  135.5 71.1 %copy-start.17 = (f32[1,8,256]{2,0,1:T(1,128)}, f32[1,8,256]{2,0,1:T(1,128)S(1)}, u32[]{:S(2)}) copy-start(f32[1,8,256]{2,0,1:T(1,128)S(1)} %get-tuple-element.181) | copy-start | bytes 24580
  135.5 235.2 %copy-start.15 = (f32[1,8,256]{2,0,1:T(1,128)}, f32[1,8,256]{2,0,1:T(1,128)S(1)}, u32[]{:S(2)}) copy-start(f32[1,8,256]{2,0,1:T(1,128)S(1)} %get-tuple-element.180) | copy-start | bytes 24580
  138.0 72.2 %copy-start.27 = (s32[1,2048]{1,0:T(1,128)S(1)}, s32[1,2048]{1,0:T(1,128)}, u32[]{:S(2)}) copy-start(s32[1,2048]{1,0:T(1,128)} %param.17) | copy-start | bytes 24580
  138.1 74.1 %copy-start.29 = (s32[256]{0:T(256)S(1)}, s32[256]{0:T(256)}, u32[]{:S(2)}) copy-start(s32[256]{0:T(256)} %param.18) | copy-start | bytes 3076
  206.6 58.0 %collective-permute-start = (bf16[512,2048]{1,0:T(8,128)(2,1)}, bf16[512,2048]{1,0:T(8,128)(2,1)}, u32[]{:S(2)}, u32[]{:S(2)}) collective-permute-start(bf16[512,2048]{1,0:T(8,128)(2,1)} %get-tuple-element.69.refs_1_), channel_id=1, source_target_pairs={{1,2},{2,3},{5,6},{6,7},{9,10},{10,11},{13,14},{14,15},{17,18},{18... | collective-permute-start | bytes 6291464 | tf_op jit(solution)/shard_map/ppermute | solution.py:1434
  208.6 69.8 %collective-permute-start.1 = (bf16[512,2048]{1,0:T(8,128)(2,1)}, bf16[512,2048]{1,0:T(8,128)(2,1)}, u32[]{:S(2)}, u32[]{:S(2)}) collective-permute-start(bf16[512,2048]{1,0:T(8,128)(2,1)} %get-tuple-element.70.refs_4_), channel_id=1, source_target_pairs={{1,0},{2,1},{5,4},{6,5},{9,8},{10,9},{13,12},{14,13},{17,16},{18,1... | collective-permute-start | bytes 6291464 | tf_op jit(solution)/shard_map/ppermute | solution.py:1435
  210.3 9.3 copy-start.19
  240.1 66.4 %all-to-all-start.1 = ((bf16[32,64,256]{2,1,0:T(8,128)(2,1)}), bf16[32,64,256]{2,1,0:T(8,128)(2,1)S(1)}, u32[]{:S(2)}, u32[]{:S(2)}) async-start(bf16[32,64,256]{2,1,0:T(8,128)(2,1)} %get-tuple-element.65), calls=%async_computation.1 | async-start | bytes 2097152 | tf_op jit(solution)/shard_map/all_to_all | solution.py:1427
  264.6 58.9 %collective-permute-start.2 = (bf16[512,2048]{1,0:T(8,128)(2,1)}, bf16[512,2048]{1,0:T(8,128)(2,1)}, u32[]{:S(2)}, u32[]{:S(2)}) collective-permute-start(bf16[512,2048]{1,0:T(8,128)(2,1)} %collective-permute-done.refs_2_), channel_id=1, source_target_pairs={{2,3},{6,7},{10,11},{14,15},{18,19},{22,23},{26,27},{30,31}} | collective-permute-start | bytes 6291464 | tf_op jit(solution)/shard_map/ppermute | solution.py:1434
  278.5 72.4 %collective-permute-start.3 = (bf16[512,2048]{1,0:T(8,128)(2,1)}, bf16[512,2048]{1,0:T(8,128)(2,1)}, u32[]{:S(2)}, u32[]{:S(2)}) collective-permute-start(bf16[512,2048]{1,0:T(8,128)(2,1)} %collective-permute-done.1.refs_5_), channel_id=1, source_target_pairs={{1,0},{5,4},{9,8},{13,12},{17,16},{21,20},{25,24},{29,28}} | collective-permute-start | bytes 6291464 | tf_op jit(solution)/shard_map/ppermute | solution.py:1435
  286.5 34.5 %copy-start.3 = (bf16[8,64,2048]{2,1,0:T(8,128)(2,1)S(1)}, bf16[8,64,2048]{2,1,0:T(8,128)(2,1)}, u32[]{:S(2)}) copy-start(bf16[8,64,2048]{2,1,0:T(8,128)(2,1)} %copy-done.2) | copy-start | bytes 6291460
  306.4 17.1 %copy-start.9 = (bf16[32,64,256]{2,1,0:T(8,128)(2,1)}, bf16[32,64,256]{2,1,0:T(8,128)(2,1)S(1)}, u32[]{:S(2)}) copy-start(bf16[32,64,256]{2,1,0:T(8,128)(2,1)S(1)} %all-to-all-done.1) | copy-start | bytes 3145732
  306.5 53.0 %all-to-all-start = ((bf16[32,64,256]{2,1,0:T(8,128)(2,1)}), bf16[32,64,256]{2,1,0:T(8,128)(2,1)}, u32[]{:S(2)}, u32[]{:S(2)}) async-start(bf16[32,64,256]{2,1,0:T(8,128)(2,1)} %get-tuple-element.76), calls=%async_computation | async-start | bytes 2097152 | tf_op jit(solution)/shard_map/all_to_all | solution.py:1427
  320.9 494.3 %reduce-scatter.3.cloned.1.call-start = ((), (), s32[]{:S(2)}) async-start(), calls=%async_computation.9 | async-start | bytes 9437184 | tf_op jit(solution)/shard_map/reduce_scatter | solution.py:1487
  368.0 3.4 copy-start
  648.1 4.2 copy-start.1
  648.1 4.7 copy-start.6
  648.1 4.7 copy-start.16
  648.1 4.7 copy-start.21
  648.1 4.7 copy-start.23
  675.5 370.2 %reduce-scatter.5.cloned.1.call-start = ((), (), s32[]{:S(2)}) async-start(), calls=%async_computation.10 | async-start | bytes 28311552 | tf_op jit(solution)/shard_map/reduce_scatter | solution.py:1487
  753.5 3.0 copy-start.10
  753.5 47.9 %collective-permute-start.4 = (bf16[512,2048]{1,0:T(8,128)(2,1)}, bf16[512,2048]{1,0:T(8,128)(2,1)}, u32[]{:S(2)}, u32[]{:S(2)}) collective-permute-start(bf16[512,2048]{1,0:T(8,128)(2,1)} %get-tuple-element.88), channel_id=1, source_target_pairs={{0,1},{4,5},{8,9},{12,13},{16,17},{20,21},{24,25},{28,29}} | collective-permute-start | bytes 6291464 | tf_op jit(solution)/shard_map/ppermute | solution.py:1434
  756.5 45.0 %collective-permute-start.6 = (bf16[512,2048]{1,0:T(8,128)(2,1)S(1)}, bf16[512,2048]{1,0:T(8,128)(2,1)}, u32[]{:S(2)}, u32[]{:S(2)}) collective-permute-start(bf16[512,2048]{1,0:T(8,128)(2,1)S(1)} %copy-done.10), channel_id=1, source_target_pairs={{3,2},{7,6},{11,10},{15,14},{19,18},{23,22},{27,26},{31,30}} | collective-permute-start | bytes 6291464 | tf_op jit(solution)/shard_map/ppermute | solution.py:1435
  787.6 56.8 %all-to-all-start.2 = ((bf16[32,64,384]{2,1,0:T(8,128)(2,1)}), bf16[32,64,384]{2,1,0:T(8,128)(2,1)}, u32[]{:S(2)}, u32[]{:S(2)}) async-start(bf16[32,64,384]{2,1,0:T(8,128)(2,1)} %attend_backward.2), calls=%async_computation.3 | async-start | bytes 3145728 | tf_op jit(solution)/shard_map/all_to_all | solution.py:1427
  808.3 36.2 %collective-permute-start.7 = (bf16[512,2048]{1,0:T(8,128)(2,1)}, bf16[512,2048]{1,0:T(8,128)(2,1)}, u32[]{:S(2)}, u32[]{:S(2)}) collective-permute-start(bf16[512,2048]{1,0:T(8,128)(2,1)} %get-tuple-element.163), channel_id=1, source_target_pairs={{2,1},{3,2},{6,5},{7,6},{10,9},{11,10},{14,13},{15,14},{18,17},{19... | collective-permute-start | bytes 6291464 | tf_op jit(solution)/shard_map/ppermute | solution.py:1435
  810.2 60.5 %collective-permute-start.5 = (bf16[512,2048]{1,0:T(8,128)(2,1)}, bf16[512,2048]{1,0:T(8,128)(2,1)}, u32[]{:S(2)}, u32[]{:S(2)}) collective-permute-start(bf16[512,2048]{1,0:T(8,128)(2,1)} %get-tuple-element.164), channel_id=1, source_target_pairs={{0,1},{1,2},{4,5},{5,6},{8,9},{9,10},{12,13},{13,14},{16,17},{17,1... | collective-permute-start | bytes 6291464 | tf_op jit(solution)/shard_map/ppermute | solution.py:1434
  815.1 68.6 %copy-start.28 = (s32[8]{0:T(128)S(1)}, s32[8]{0:T(128)}, u32[]{:S(2)}) copy-start(s32[8]{0:T(128)} %get-tuple-element.158) | copy-start | bytes 100
  870.8 50.4 %all-to-all-start.3 = ((bf16[32,64,384]{2,1,0:T(8,128)(2,1)}), bf16[32,64,384]{2,1,0:T(8,128)(2,1)}, u32[]{:S(2)}, u32[]{:S(2)}) async-start(bf16[32,64,384]{2,1,0:T(8,128)(2,1)} %attend_backward.3), calls=%async_computation.4 | async-start | bytes 3145728 | tf_op jit(solution)/shard_map/all_to_all | solution.py:1427
  921.2 92.8 %copy-start.18 = (f32[1,8,256]{2,0,1:T(1,128)S(1)}, f32[1,8,256]{2,0,1:T(1,128)}, u32[]{:S(2)}) copy-start(f32[1,8,256]{2,0,1:T(1,128)} %copy-done.17) | copy-start | bytes 24580
  921.2 92.8 %copy-start.25 = (f32[512]{0:T(512)S(1)}, f32[512]{0:T(512)}, u32[]{:S(2)}) copy-start(f32[512]{0:T(512)} %copy-done.24) | copy-start | bytes 6148
  1006.1 18.6 %copy-start.11 = (f32[256,768]{1,0:T(8,128)S(1)}, f32[256,768]{1,0:T(8,128)}, u32[]{:S(2)}) copy-start(f32[256,768]{1,0:T(8,128)} %get-tuple-element.106) | copy-start | bytes 2359300
  1008.1 35.2 %collective-permute-start.10 = (bf16[256,512]{1,0:T(8,128)(2,1)}, bf16[256,512]{1,0:T(8,128)(2,1)}, u32[]{:S(2)}, u32[]{:S(2)}) collective-permute-start(bf16[256,512]{1,0:T(8,128)(2,1)} %get-tuple-element.166), channel_id=1, source_target_pairs={{0,3},{1,0},{2,1},{3,2},{4,7},{5,4},{6,5},{7,6},{8,11},{9,8},{10,9... | collective-permute-start | bytes 786440 | tf_op jit(solution)/shard_map/ppermute | solution.py:1496
  1013.3 30.0 %collective-permute-start.8 = (bf16[256,512]{1,0:T(8,128)(2,1)S(1)}, bf16[256,512]{1,0:T(8,128)(2,1)}, u32[]{:S(2)}, u32[]{:S(2)}) collective-permute-start(bf16[256,512]{1,0:T(8,128)(2,1)S(1)} %get-tuple-element.165), channel_id=1, source_target_pairs={{0,1},{1,2},{2,3},{3,0},{4,5},{5,6},{6,7},{7,4},{8,9},{9,10},{10,1... | collective-permute-start | bytes 786440 | tf_op jit(solution)/shard_map/ppermute | solution.py:1496
  1013.3 12.5 %copy-start.4 = (bf16[8,64,2048]{2,1,0:T(8,128)(2,1)S(1)}, bf16[8,64,2048]{2,1,0:T(8,128)(2,1)}, u32[]{:S(2)}) copy-start(bf16[8,64,2048]{2,1,0:T(8,128)(2,1)} %copy-done.2) | copy-start | bytes 6291460
  1013.3 30.0 %collective-permute-start.9 = (bf16[256,512]{1,0:T(8,128)(2,1)S(1)}, bf16[256,512]{1,0:T(8,128)(2,1)}, u32[]{:S(2)}, u32[]{:S(2)}) collective-permute-start(bf16[256,512]{1,0:T(8,128)(2,1)S(1)} %get-tuple-element.167), channel_id=1, source_target_pairs={{0,2},{1,3},{2,0},{3,1},{4,6},{5,7},{6,4},{7,5},{8,10},{9,11},{10,... | collective-permute-start | bytes 786440 | tf_op jit(solution)/shard_map/ppermute | solution.py:1496
  1018.6 24.1 %all-to-all-start.4 = ((f32[32,2,256]{2,1,0:T(2,128)}), f32[32,2,256]{2,1,0:T(2,128)S(1)}, u32[]{:S(2)}, u32[]{:S(2)}) async-start(f32[32,2,256]{2,1,0:T(2,128)} %bitcast.26), calls=%async_computation.5 | async-start | bytes 131072 | tf_op jit(solution)/shard_map/all_to_all | solution.py:1546
  1035.6 5.1 copy-start.8
  (4 other events, 6.6 us)
Sparse Core Ops, SparseCore 0:
  128.9 87.7 all-gather.2
  218.6 142.7 all-gather.4
  675.6 88.1 reduce-scatter.2
  767.7 181.6 reduce-scatter.4

commit v12 on v11

--- a/solution.py
+++ b/solution.py
@@ -1464,7 +1464,7 @@
         saved.append((q_t, k_rows, k_t, v_rows, o_t, lse))
         mixed.append(trade_back(after(o_slots, chunks[1]) if g else o_slots))
     hidden_mid = hidden_in
-    mixed[0] = after(mixed[0], chunks[-1])
+    mixed[-1] = after(mixed[-1], chunks[-1])
     for g in groups:
         hidden_mid = gather_sum(mixed[g], w_out_t, g, hidden_mid)
 
@@ -1518,7 +1518,7 @@
             if tp_count > 3:
                 passing = pass_on(add_on(passing, 2), (0, 2), (tp_count - 2, tp_count))
                 steps = 3
-            back = after(back, (grad_qkv, passing))
+            grad_qkv = [after(value, passing) for value in grad_qkv]
         grad_qkv.append(trade_back(back))
     hidden = sum_mlp.shape[1] // 3
     for s in range(steps, tp_count - 1):

time: 1060 us -> 1060 us (level)
  transfers between devices with their start and end apart: 20 -> 20, of which waited for: 5 -> 6; matrix products, arithmetic and copies ran while one was open for 6% -> 6% of each run, Pallas kernels for 34% -> 34%
where the time goes in v12:
time: 1060 us; the launch traced here: 1050 us
  Pallas kernels  763 us (72%)
  waiting for transfers between devices  96.4 us (9%)
  starting transfers between devices  86 us (8%)
  other arithmetic  65.2 us (6%)
  local copies, waits for them, and re-layouts  27.6 us (3%)
  between operations  14.7 us (1%)
    pallas_call x1, Pallas kernels, feed(): pl.pallas_call(functools.partial(feed_kernel, ring, min(tile, hidden)), o...  277 us
    pallas_call x1, Pallas kernels, collect(): pl.pallas_call(functools.partial(collect_kernel, tp_count, dp_count), out...  106 us
    pallas_call x1, Pallas kernels, total_grads(): pl.pallas_call(functools.partial(total_kernel, tp_count, dp_count, len(pa...  90.6 us
    pallas_call x1, Pallas kernels, weigh(): pl.pallas_call(functools.partial(weigh_kernel, tp_count, dp_count, min(51...  69.1 us
    pallas_call x1, Pallas kernels, project(): pl.pallas_call(functools.partial(project_kernel, tp_count, dp_count), out...  68.5 us
    all_to_all x4, starting transfers between devices, trade(): lax.all_to_all(blocks, everyone, split_axis=0, concat_axis=0, tiled=True)  56.1 us
    pallas_call x2, Pallas kernels, attend_backward(): pl.pallas_call(functools.partial(backward_kernel, q_heads, kv_heads, page...  55.6 us
    pallas_call x2, Pallas kernels, attend_forward(): pl.pallas_call(functools.partial(forward_kernel, q_heads, kv_heads, page_...  37.9 us
  transfers between devices with their start and end apart: 20, of which 6 were waited for; matrix products, arithmetic and copies ran while one was open for 6% of the time, Pallas kernels for 34%

profile of v12, /device:TPU:0, one launch (start us, length us, event | category | flops | bytes accessed | tf_op | source)
XLA Modules:
  0.0 1052.8 jit_solution(11370219367240069698)
XLA Ops:
  13.5 2.3 gather_fusion.1
  22.6 106.1 %collect.1 = (bf16[4,2048,768]{2,1,0:T(8,128)(2,1)}, bf16[4,256,512]{2,1,0:T(8,128)(2,1)}, bf16[8,2,256]{2,1,0:T(2,128)(2,1)}, bf16[512,2048]{1,0:T(8,128)(2,1)}, bf16[512,2048]{1,0:T(8,128)(2,1)}) custom-call(bf16[256,768]{1,0:T(8,128)(2,1)} %concatenate.16.shard, bf16[256,512]{1,0:T(8,128)(2,1)} %bitcast.64, bf16[2,256]{1,0:T(2,128)(2,1)} %pad_maximum_fusion.4.gains, ...), custom_call_target="tpu_custom_call" | custom-call | bytes 100663296 | tf_op jit(solution)/shard_map/collect/pallas_call | solution.py:1004
  129.5 3.1 pad_maximum_fusion
  132.6 2.3 gather_fusion
  138.1 68.5 %project.1.refs_0_.refs_1_.refs_2_.refs_3_ = bf16[32,64,768]{2,1,0:T(8,128)(2,1)} custom-call(bf16[512,2048]{1,0:T(8,128)(2,1)} %multiply_convert_fusion.1.rows, bf16[4,2048,768]{2,1,0:T(8,128)(2,1)} %get-tuple-element.61.weights.refs_4_), custom_call_target="tpu_custom_call" | custom-call | flops 6442450944 | bytes 100663296 | tf_op jit(solution)/shard_map/project/pallas_call | solution.py:449
  206.6 2.0 collective-permute-start
  213.4 6.7 prepare.2
  220.1 18.9 %attend_forward.2 = (bf16[256,2048]{1,0:T(8,128)(2,1)}, f32[4,2048]{1,0:T(4,128)}, bf16[32,64,256]{2,1,0:T(8,128)(2,1)}) custom-call(s32[4]{0:T(128)} %and_select_fusion.4.first_block, s32[32]{0:T(128)} %fusion.14.perm, bf16[256,2048]{1,0:T(8,128)(2,1)} %get-tuple-element.62.q_t.refs_8_, bf16[1,2048,64]{2,1,0:T(8,128)(2,1)} %get-tuple-element.63.k_rows.refs_9_, ...), custom_call_target="tpu_custom_call" | custom-call | flops 1073741824 | bytes 4194304 | tf_op jit(solution)/shard_map/attend_forward/pallas_call | solution.py:174
  239.0 23.7 %all-to-all-start.1 = ((bf16[32,64,256]{2,1,0:T(8,128)(2,1)}), bf16[32,64,256]{2,1,0:T(8,128)(2,1)S(1)}, u32[]{:S(2)}, u32[]{:S(2)}) async-start(bf16[32,64,256]{2,1,0:T(8,128)(2,1)} %get-tuple-element.65), calls=%async_computation.1 | async-start | bytes 2097152 | tf_op jit(solution)/shard_map/all_to_all | solution.py:1427
  262.7 2.0 collective-permute-start.2
  264.8 14.7 %collective-permute-done.1.refs_5_ = bf16[512,2048]{1,0:T(8,128)(2,1)} collective-permute-done((bf16[512,2048]{1,0:T(8,128)(2,1)}, bf16[512,2048]{1,0:T(8,128)(2,1)}, u32[]{:S(2)}, u32[]{:S(2)}) %collective-permute-start.1) | collective-permute-done | bytes 2097184 | tf_op jit(solution)/shard_map/ppermute | solution.py:1435
  280.8 6.7 prepare.3
  287.5 19.0 %attend_forward.3 = (bf16[256,2048]{1,0:T(8,128)(2,1)}, f32[4,2048]{1,0:T(4,128)}, bf16[32,64,256]{2,1,0:T(8,128)(2,1)}) custom-call(s32[4]{0:T(128)} %and_select_fusion.4.first_block, s32[32]{0:T(128)} %fusion.14.perm, bf16[256,2048]{1,0:T(8,128)(2,1)} %get-tuple-element.72.q_t.refs_8_, bf16[1,2048,64]{2,1,0:T(8,128)(2,1)} %get-tuple-element.73.k_rows.refs_9_, ...), custom_call_target="tpu_custom_call" | custom-call | flops 1073741824 | bytes 4194304 | tf_op jit(solution)/shard_map/attend_forward/pallas_call | solution.py:174
  306.5 12.5 %all-to-all-start = ((bf16[32,64,256]{2,1,0:T(8,128)(2,1)}), bf16[32,64,256]{2,1,0:T(8,128)(2,1)}, u32[]{:S(2)}, u32[]{:S(2)}) async-start(bf16[32,64,256]{2,1,0:T(8,128)(2,1)} %get-tuple-element.76), calls=%async_computation | async-start | bytes 2097152 | tf_op jit(solution)/shard_map/all_to_all | solution.py:1427
  319.1 2.6 bitcast_convert_fusion.refs_0_
  321.8 8.7 gather_sum.2.refs_0_
  330.5 21.0 %collective-permute-done.3.refs_6_ = bf16[512,2048]{1,0:T(8,128)(2,1)} collective-permute-done((bf16[512,2048]{1,0:T(8,128)(2,1)}, bf16[512,2048]{1,0:T(8,128)(2,1)}, u32[]{:S(2)}, u32[]{:S(2)}) %collective-permute-start.3) | collective-permute-done | bytes 2097184 | tf_op jit(solution)/shard_map/ppermute | solution.py:1435
  351.6 5.8 all-to-all-done
  357.4 8.9 gather_sum.3
  366.3 2.7 multiply_reduce_fusion.2
  371.5 276.8 %feed_forward.1 = (bf16[2048,2048]{1,0:T(8,128)(2,1)}, bf16[2048,2048]{1,0:T(8,128)(2,1)}, bf16[4,512,2048]{2,1,0:T(8,128)(2,1)}, bf16[4,512,4096]{2,1,0:T(8,128...) custom-call(bf16[512,2048]{1,0:T(8,128)(2,1)} %multiply_convert_fusi, ...), custom_call_target="tpu_custom_call" | custom-call | flops 103079215104 | bytes 33554432 | tf_op jit(solution)/shard_map/feed_forward/pallas_call | solution.py:680
  648.3 4.2 fusion.5
  653.0 3.9 fusion.21.rows
  656.9 18.7 %outer.1 = bf16[2048,2048]{1,0:T(8,128)(2,1)} custom-call(bf16[512,2048]{1,0:T(8,128)(2,1)} %fusion.21.rows, bf16[4,512,256]{2,1,0:T(8,128)(2,1)} %bitcast.58, bf16[4,512,256]{2,1,0:T(8,128)(2,1)} %bitcast.12.part.refs_1_), custom_call_target="tpu_custom_call" | custom-call | flops 4294967296 | bytes 8388608 | tf_op jit(solution)/shard_map/outer/pallas_call | solution.py:1113
  675.7 8.7 spread.1.grads
  684.4 69.1 %weigh.1 = (bf16[32,64,512]{2,1,0:T(8,128)(2,1)}, bf16[2048,6144]{1,0:T(8,128)(2,1)}) custom-call(bf16[4,512,512]{2,1,0:T(8,128)(2,1)} %spread.1.grads, bf16[2048,2048]{1,0:T(8,128)(2,1)} %get-tuple-element.81.rows_t, bf16[2048,2048]{1,0:T(8,128)(2,1)} %get-tuple-element.82.grads_t, bf16[4,512,4096]{2,1,0:T(8,128)(2,1)} %get-tuple-element.83.gate_up, ...), custom_call_target="tpu_custom_call" | custom-call | flops 51539607552 | bytes 41943040 | tf_op jit(solution)/shard_map/weigh/pallas_call | solution.py:818
  753.5 5.0 collective-permute-start.4
  760.4 27.8 %attend_backward.2 = bf16[32,64,384]{2,1,0:T(8,128)(2,1)} custom-call(s32[4]{0:T(128)} %and_select_fusion.4.first_block, s32[32]{0:T(128)} %fusion.14.perm, bf16[32,64,512]{2,1,0:T(8,128)(2,1)} %get-tuple-element.95.refs_0_.refs_1_.refs_2_.refs_3_.refs_4_.refs_5_.refs_6_.refs_7_, ...), custom_call_target="tpu_custom_call" | custom-call | flops 3221225472 | bytes 6291456 | tf_op jit(solution)/shard_map/attend_backward/pallas_call | solution.py:335
  788.2 8.2 all-to-all-start.2
  796.4 6.6 collective-permute-done.4
  803.0 6.7 fusion.7
  809.7 1.9 collective-permute-start.7
  811.7 5.1 collective-permute-start.5
  816.7 27.8 %attend_backward.3 = bf16[32,64,384]{2,1,0:T(8,128)(2,1)} custom-call(s32[4]{0:T(128)} %and_select_fusion.4.first_block, s32[32]{0:T(128)} %fusion.14.perm, bf16[32,64,512]{2,1,0:T(8,128)(2,1)} %get-tuple-element.95.refs_0_.refs_1_.refs_2_.refs_3_.refs_4_.refs_5_.refs_6_.refs_7_, ...), custom_call_target="tpu_custom_call" | custom-call | flops 3221225472 | bytes 6291456 | tf_op jit(solution)/shard_map/attend_backward/pallas_call | solution.py:335
  844.6 11.7 %all-to-all-start.3 = ((bf16[32,64,384]{2,1,0:T(8,128)(2,1)}), bf16[32,64,384]{2,1,0:T(8,128)(2,1)}, u32[]{:S(2)}, u32[]{:S(2)}) async-start(bf16[32,64,384]{2,1,0:T(8,128)(2,1)} %attend_backward.3), calls=%async_computation.4 | async-start | bytes 3145728 | tf_op jit(solution)/shard_map/all_to_all | solution.py:1427
  856.4 17.1 %collective-permute-done.5 = bf16[512,2048]{1,0:T(8,128)(2,1)} collective-permute-done((bf16[512,2048]{1,0:T(8,128)(2,1)}, bf16[512,2048]{1,0:T(8,128)(2,1)}, u32[]{:S(2)}, u32[]{:S(2)}) %collective-permute-start.5) | collective-permute-done | bytes 2097184 | tf_op jit(solution)/shard_map/ppermute | solution.py:1434
  873.5 4.4 add_convert_fusion.1.refs_3_
  877.9 3.7 add_convert_fusion.2.refs_2_
  881.6 30.9 %all-to-all-done.3 = bf16[32,64,384]{2,1,0:T(8,128)(2,1)} async-done(((bf16[32,64,384]{2,1,0:T(8,128)(2,1)}), bf16[32,64,384]{2,1,0:T(8,128)(2,1)}, u32[]{:S(2)}, u32[]{:S(2)}) %all-to-all-start.3) | async-done | bytes 1572896 | tf_op jit(solution)/shard_map/all_to_all | solution.py:1427
  912.5 90.6 %total_grads.1 = (f32[256,768]{1,0:T(8,128)}, f32[512,2048]{1,0:T(8,128)}, bf16[2,512,2048]{2,1,0:T(8,128)(2,1)}) custom-call(bf16[512,2048]{1,0:T(8,128)(2,1)} %multiply_convert_fusion.1.rows, bf16[4,512,384]{2,1,0:T(8,128)(2,1)} %bitcast.16.refs_0_, bf16[4,512,384]{2,1,0:T(8,128)(2,1)} %bitcast.17.refs_1_, bf16[512,2048]{1,0:T(8,128)(2,1)} %add_convert_fusion.2.refs_2_, ...), custom_call_target="tpu_custom_call" | custom-call | flops 12884901888 | bytes 100663296 | tf_op jit(solution)/shard_map/total_grads/pallas_call | solution.py:1292
  1003.1 2.0 constant_dynamic-slice_fusion.2
  1005.1 3.1 collective-permute-start.10
  1009.2 4.0 multiply_reduce_fusion
  1013.8 4.8 all-to-all-start.4
  1020.4 9.1 add_convert_fusion
  1031.0 3.6 gather_fusion.4
  1034.6 2.0 gather_fusion.3
  1039.6 4.7 convert_bitcast_fusion
  (143 shorter events, 37.8 us)
Async XLA Ops:
  7.2 8.6 copy-start.13
  7.2 8.6 copy-start.14
  7.2 9.6 copy-start.30
  7.2 9.6 copy-start.31
  7.2 273.6 %all-gather.3.cloned.1.call-start = ((), (), s32[]{:S(2)}) async-start(), calls=%async_computation.7 | async-start | bytes 9437184 | tf_op jit(solution)/shard_map/all_gather | solution.py:1444
  13.5 3.4 copy-start.22
  15.8 113.0 %copy-start.5 = (bf16[8,64,2048]{2,1,0:T(8,128)(2,1)}, bf16[8,64,2048]{2,1,0:T(8,128)(2,1)S(1)}, u32[]{:S(2)}) copy-start(bf16[8,64,2048]{2,1,0:T(8,128)(2,1)S(1)} %gather_fusion.1) | copy-start | bytes 6291460
  16.9 112.0 %copy-start.12 = (bf16[2048,256]{1,0:T(8,128)(2,1)S(1)}, bf16[2048,256]{1,0:T(8,128)(2,1)}, u32[]{:S(2)}) copy-start(bf16[2048,256]{1,0:T(8,128)(2,1)} %param.27) | copy-start | bytes 3145732
  128.8 242.7 %all-gather.5.cloned.1.call-start = ((), (), s32[]{:S(2)}) async-start(), calls=%async_computation.8 | async-start | bytes 28311552 | tf_op jit(solution)/shard_map/all_gather | solution.py:1445
  135.5 71.2 %copy-start.24 = (f32[512]{0:T(512)}, f32[512]{0:T(512)S(1)}, u32[]{:S(2)}) copy-start(f32[512]{0:T(512)S(1)} %rsqrt.20) | copy-start | bytes 6148
  135.5 71.1 %copy-start.17 = (f32[1,8,256]{2,0,1:T(1,128)}, f32[1,8,256]{2,0,1:T(1,128)S(1)}, u32[]{:S(2)}) copy-start(f32[1,8,256]{2,0,1:T(1,128)S(1)} %get-tuple-element.181) | copy-start | bytes 24580
  135.5 233.5 %copy-start.15 = (f32[1,8,256]{2,0,1:T(1,128)}, f32[1,8,256]{2,0,1:T(1,128)S(1)}, u32[]{:S(2)}) copy-start(f32[1,8,256]{2,0,1:T(1,128)S(1)} %get-tuple-element.180) | copy-start | bytes 24580
  138.0 72.2 %copy-start.27 = (s32[1,2048]{1,0:T(1,128)S(1)}, s32[1,2048]{1,0:T(1,128)}, u32[]{:S(2)}) copy-start(s32[1,2048]{1,0:T(1,128)} %param.17) | copy-start | bytes 24580
  138.1 74.7 %copy-start.29 = (s32[256]{0:T(256)S(1)}, s32[256]{0:T(256)}, u32[]{:S(2)}) copy-start(s32[256]{0:T(256)} %param.18) | copy-start | bytes 3076
  206.6 56.1 %collective-permute-start = (bf16[512,2048]{1,0:T(8,128)(2,1)}, bf16[512,2048]{1,0:T(8,128)(2,1)}, u32[]{:S(2)}, u32[]{:S(2)}) collective-permute-start(bf16[512,2048]{1,0:T(8,128)(2,1)} %get-tuple-element.69.refs_1_), channel_id=1, source_target_pairs={{1,2},{2,3},{5,6},{6,7},{9,10},{10,11},{13,14},{14,15},{17,18},{18... | collective-permute-start | bytes 6291464 | tf_op jit(solution)/shard_map/ppermute | solution.py:1434
  208.6 70.9 %collective-permute-start.1 = (bf16[512,2048]{1,0:T(8,128)(2,1)}, bf16[512,2048]{1,0:T(8,128)(2,1)}, u32[]{:S(2)}, u32[]{:S(2)}) collective-permute-start(bf16[512,2048]{1,0:T(8,128)(2,1)} %get-tuple-element.70.refs_4_), channel_id=1, source_target_pairs={{1,0},{2,1},{5,4},{6,5},{9,8},{10,9},{13,12},{14,13},{17,16},{18,1... | collective-permute-start | bytes 6291464 | tf_op jit(solution)/shard_map/ppermute | solution.py:1435
  210.3 9.8 copy-start.19
  239.0 67.5 %all-to-all-start.1 = ((bf16[32,64,256]{2,1,0:T(8,128)(2,1)}), bf16[32,64,256]{2,1,0:T(8,128)(2,1)S(1)}, u32[]{:S(2)}, u32[]{:S(2)}) async-start(bf16[32,64,256]{2,1,0:T(8,128)(2,1)} %get-tuple-element.65), calls=%async_computation.1 | async-start | bytes 2097152 | tf_op jit(solution)/shard_map/all_to_all | solution.py:1427
  262.7 67.8 %collective-permute-start.2 = (bf16[512,2048]{1,0:T(8,128)(2,1)}, bf16[512,2048]{1,0:T(8,128)(2,1)}, u32[]{:S(2)}, u32[]{:S(2)}) collective-permute-start(bf16[512,2048]{1,0:T(8,128)(2,1)} %collective-permute-done.refs_2_), channel_id=1, source_target_pairs={{2,3},{6,7},{10,11},{14,15},{18,19},{22,23},{26,27},{30,31}} | collective-permute-start | bytes 6291464 | tf_op jit(solution)/shard_map/ppermute | solution.py:1434
  279.5 72.0 %collective-permute-start.3 = (bf16[512,2048]{1,0:T(8,128)(2,1)}, bf16[512,2048]{1,0:T(8,128)(2,1)}, u32[]{:S(2)}, u32[]{:S(2)}) collective-permute-start(bf16[512,2048]{1,0:T(8,128)(2,1)} %collective-permute-done.1.refs_5_), channel_id=1, source_target_pairs={{1,0},{5,4},{9,8},{13,12},{17,16},{21,20},{25,24},{29,28}} | collective-permute-start | bytes 6291464 | tf_op jit(solution)/shard_map/ppermute | solution.py:1435
  287.5 31.6 %copy-start.3 = (bf16[8,64,2048]{2,1,0:T(8,128)(2,1)S(1)}, bf16[8,64,2048]{2,1,0:T(8,128)(2,1)}, u32[]{:S(2)}) copy-start(bf16[8,64,2048]{2,1,0:T(8,128)(2,1)} %copy-done.2) | copy-start | bytes 6291460
  306.5 15.3 %copy-start.9 = (bf16[32,64,256]{2,1,0:T(8,128)(2,1)}, bf16[32,64,256]{2,1,0:T(8,128)(2,1)S(1)}, u32[]{:S(2)}) copy-start(bf16[32,64,256]{2,1,0:T(8,128)(2,1)S(1)} %all-to-all-done.1) | copy-start | bytes 3145732
  306.5 50.8 %all-to-all-start = ((bf16[32,64,256]{2,1,0:T(8,128)(2,1)}), bf16[32,64,256]{2,1,0:T(8,128)(2,1)}, u32[]{:S(2)}, u32[]{:S(2)}) async-start(bf16[32,64,256]{2,1,0:T(8,128)(2,1)} %get-tuple-element.76), calls=%async_computation | async-start | bytes 2097152 | tf_op jit(solution)/shard_map/all_to_all | solution.py:1427
  319.1 497.7 %reduce-scatter.3.cloned.1.call-start = ((), (), s32[]{:S(2)}) async-start(), calls=%async_computation.9 | async-start | bytes 9437184 | tf_op jit(solution)/shard_map/reduce_scatter | solution.py:1487
  366.3 3.4 copy-start
  648.2 4.2 copy-start.1
  648.2 4.7 copy-start.6
  648.2 4.7 copy-start.16
  648.2 4.7 copy-start.21
  648.3 4.7 copy-start.23
  675.6 364.0 %reduce-scatter.5.cloned.1.call-start = ((), (), s32[]{:S(2)}) async-start(), calls=%async_computation.10 | async-start | bytes 28311552 | tf_op jit(solution)/shard_map/reduce_scatter | solution.py:1487
  753.5 5.0 copy-start.10
  753.5 49.5 %collective-permute-start.4 = (bf16[512,2048]{1,0:T(8,128)(2,1)}, bf16[512,2048]{1,0:T(8,128)(2,1)}, u32[]{:S(2)}, u32[]{:S(2)}) collective-permute-start(bf16[512,2048]{1,0:T(8,128)(2,1)} %get-tuple-element.88), channel_id=1, source_target_pairs={{0,1},{4,5},{8,9},{12,13},{16,17},{20,21},{24,25},{28,29}} | collective-permute-start | bytes 6291464 | tf_op jit(solution)/shard_map/ppermute | solution.py:1434
  758.5 44.6 %collective-permute-start.6 = (bf16[512,2048]{1,0:T(8,128)(2,1)S(1)}, bf16[512,2048]{1,0:T(8,128)(2,1)}, u32[]{:S(2)}, u32[]{:S(2)}) collective-permute-start(bf16[512,2048]{1,0:T(8,128)(2,1)S(1)} %copy-done.10), channel_id=1, source_target_pairs={{3,2},{7,6},{11,10},{15,14},{19,18},{23,22},{27,26},{31,30}} | collective-permute-start | bytes 6291464 | tf_op jit(solution)/shard_map/ppermute | solution.py:1435
  788.2 56.4 %all-to-all-start.2 = ((bf16[32,64,384]{2,1,0:T(8,128)(2,1)}), bf16[32,64,384]{2,1,0:T(8,128)(2,1)}, u32[]{:S(2)}, u32[]{:S(2)}) async-start(bf16[32,64,384]{2,1,0:T(8,128)(2,1)} %attend_backward.2), calls=%async_computation.3 | async-start | bytes 3145728 | tf_op jit(solution)/shard_map/all_to_all | solution.py:1427
  809.7 46.6 %collective-permute-start.7 = (bf16[512,2048]{1,0:T(8,128)(2,1)}, bf16[512,2048]{1,0:T(8,128)(2,1)}, u32[]{:S(2)}, u32[]{:S(2)}) collective-permute-start(bf16[512,2048]{1,0:T(8,128)(2,1)} %get-tuple-element.163), channel_id=1, source_target_pairs={{2,1},{3,2},{6,5},{7,6},{10,9},{11,10},{14,13},{15,14},{18,17},{19... | collective-permute-start | bytes 6291464 | tf_op jit(solution)/shard_map/ppermute | solution.py:1435
  811.7 61.8 %collective-permute-start.5 = (bf16[512,2048]{1,0:T(8,128)(2,1)}, bf16[512,2048]{1,0:T(8,128)(2,1)}, u32[]{:S(2)}, u32[]{:S(2)}) collective-permute-start(bf16[512,2048]{1,0:T(8,128)(2,1)} %get-tuple-element.164), channel_id=1, source_target_pairs={{0,1},{1,2},{4,5},{5,6},{8,9},{9,10},{12,13},{13,14},{16,17},{17,1... | collective-permute-start | bytes 6291464 | tf_op jit(solution)/shard_map/ppermute | solution.py:1434
  816.7 39.6 %copy-start.28 = (s32[8]{0:T(128)S(1)}, s32[8]{0:T(128)}, u32[]{:S(2)}) copy-start(s32[8]{0:T(128)} %get-tuple-element.158) | copy-start | bytes 100
  844.6 67.9 %all-to-all-start.3 = ((bf16[32,64,384]{2,1,0:T(8,128)(2,1)}), bf16[32,64,384]{2,1,0:T(8,128)(2,1)}, u32[]{:S(2)}, u32[]{:S(2)}) async-start(bf16[32,64,384]{2,1,0:T(8,128)(2,1)} %attend_backward.3), calls=%async_computation.4 | async-start | bytes 3145728 | tf_op jit(solution)/shard_map/all_to_all | solution.py:1427
  912.5 96.6 %copy-start.18 = (f32[1,8,256]{2,0,1:T(1,128)S(1)}, f32[1,8,256]{2,0,1:T(1,128)}, u32[]{:S(2)}) copy-start(f32[1,8,256]{2,0,1:T(1,128)} %copy-done.17) | copy-start | bytes 24580
  912.5 96.6 %copy-start.25 = (f32[512]{0:T(512)S(1)}, f32[512]{0:T(512)}, u32[]{:S(2)}) copy-start(f32[512]{0:T(512)} %copy-done.24) | copy-start | bytes 6148
  1003.1 15.6 %copy-start.11 = (f32[256,768]{1,0:T(8,128)S(1)}, f32[256,768]{1,0:T(8,128)}, u32[]{:S(2)}) copy-start(f32[256,768]{1,0:T(8,128)} %get-tuple-element.106) | copy-start | bytes 2359300
  1005.1 32.2 %collective-permute-start.10 = (bf16[256,512]{1,0:T(8,128)(2,1)}, bf16[256,512]{1,0:T(8,128)(2,1)}, u32[]{:S(2)}, u32[]{:S(2)}) collective-permute-start(bf16[256,512]{1,0:T(8,128)(2,1)} %get-tuple-element.166), channel_id=1, source_target_pairs={{0,3},{1,0},{2,1},{3,2},{4,7},{5,4},{6,5},{7,6},{8,11},{9,8},{10,9... | collective-permute-start | bytes 786440 | tf_op jit(solution)/shard_map/ppermute | solution.py:1496
  1008.2 29.1 %collective-permute-start.8 = (bf16[256,512]{1,0:T(8,128)(2,1)S(1)}, bf16[256,512]{1,0:T(8,128)(2,1)}, u32[]{:S(2)}, u32[]{:S(2)}) collective-permute-start(bf16[256,512]{1,0:T(8,128)(2,1)S(1)} %get-tuple-element.165), channel_id=1, source_target_pairs={{0,1},{1,2},{2,3},{3,0},{4,5},{5,6},{6,7},{7,4},{8,9},{9,10},{10,1... | collective-permute-start | bytes 786440 | tf_op jit(solution)/shard_map/ppermute | solution.py:1496
  1008.2 11.5 %copy-start.4 = (bf16[8,64,2048]{2,1,0:T(8,128)(2,1)S(1)}, bf16[8,64,2048]{2,1,0:T(8,128)(2,1)}, u32[]{:S(2)}) copy-start(bf16[8,64,2048]{2,1,0:T(8,128)(2,1)} %copy-done.2) | copy-start | bytes 6291460
  1008.2 29.1 %collective-permute-start.9 = (bf16[256,512]{1,0:T(8,128)(2,1)S(1)}, bf16[256,512]{1,0:T(8,128)(2,1)}, u32[]{:S(2)}, u32[]{:S(2)}) collective-permute-start(bf16[256,512]{1,0:T(8,128)(2,1)S(1)} %get-tuple-element.167), channel_id=1, source_target_pairs={{0,2},{1,3},{2,0},{3,1},{4,6},{5,7},{6,4},{7,5},{8,10},{9,11},{10,... | collective-permute-start | bytes 786440 | tf_op jit(solution)/shard_map/ppermute | solution.py:1496
  1013.8 22.8 %all-to-all-start.4 = ((f32[32,2,256]{2,1,0:T(2,128)}), f32[32,2,256]{2,1,0:T(2,128)S(1)}, u32[]{:S(2)}, u32[]{:S(2)}) async-start(f32[32,2,256]{2,1,0:T(2,128)} %bitcast.26), calls=%async_computation.5 | async-start | bytes 131072 | tf_op jit(solution)/shard_map/all_to_all | solution.py:1546
  1029.5 5.1 copy-start.8
  (4 other events, 6.6 us)
Sparse Core Ops, SparseCore 0:
  128.9 87.7 all-gather.2
  218.6 142.6 all-gather.4
  675.7 87.6 reduce-scatter.2
  767.4 192.7 reduce-scatter.4

commit v13 on v12

--- a/solution.py
+++ b/solution.py
@@ -887,15 +887,35 @@
             device_id_type=MESH,
         )
 
-    def across(j):
+    def hand_on(way, far):
+        owner = lax.rem(my_tp + (tp_count - far, far)[way], tp_count)
+        spot = out.at[owner, pl.ds(my_dp * rows, rows), :]
         return pltpu.make_async_remote_copy(
-            src_ref=shard,
-            dst_ref=home,
-            send_sem=ring_send.at[j],
-            recv_sem=ring_recv.at[j],
-            device_id={"tensor": lax.rem(my_tp + j, tp_count)},
+            src_ref=shard if far == 0 else spot,
+            dst_ref=spot,
+            send_sem=ring_send.at[way, far],
+            recv_sem=ring_recv.at[way, far],
+            device_id={"tensor": lax.rem(my_tp + (1, tp_count - 1)[way], tp_count)},
             device_id_type=MESH,
         )
+
+    def hands_on(way, far):
+        if way == 0:
+            return (my_tp >= far) & (my_tp < tp_count - 1)
+        return (my_tp < tp_count - far) & (my_tp > 0)
+
+    def relay(far):
+        for way, here in ((0, my_tp >= far), (1, my_tp < tp_count - far)):
+
+            @pl.when(here)
+            def _(way=way):
+                hand_on(way, far - 1).wait_recv()
+
+                if far < tp_count - 1:
+
+                    @pl.when(hands_on(way, far))
+                    def _():
+                        hand_on(way, far).start()
 
     def gain_copy(j):
         return pltpu.make_async_remote_copy(
@@ -938,42 +958,51 @@
             device_id_type=MESH,
         )
 
-    for j in range(1, tp_count):
-        across(j).start()
+    for way in range(2):
+
+        @pl.when(hands_on(way, 0))
+        def _(way=way):
+            hand_on(way, 0).start()
+
     for j in range(1, dp_count):
         gain_copy(j).start()
 
-    @pl.when(has_right)
-    def _():
-        step(0).start()
-
-    @pl.when(has_left)
-    def _():
-        step(1).start()
-
     own.wait()
-    for phase in range(tp_count + steps):
+    for phase in range(2 * tp_count - 2 + steps):
+        if 1 <= phase < tp_count:
+            relay(phase)
         for k in reversed(range(steps + 1)):
-            j = phase - k
-            if not 0 <= j < tp_count:
-                continue
-            if k == 0:
-                if j > 0:
-                    across(j).wait_recv()
-            else:
+            for j in range(tp_count):
+                if (0 if j == 0 else tp_count - 2 + j) + k != phase:
+                    continue
                 for s in range(2):
-                    for m in range(1 << (k - 1)):
-                        within(j, s, k - 1, m).wait_recv()
-            if k < steps:
+                    if k > 0:
+                        for m in range(1 << (k - 1)):
+                            within(j, s, k - 1, m).wait_recv()
                 for s in range(2):
-                    for m in range(1 << k):
-                        within(j, s, k, m).start()
-        if phase == tp_count:
+                    if k < steps:
+                        for m in range(1 << k):
+                            within(j, s, k, m).start()
+        if phase == tp_count - 1:
+
+            @pl.when(has_right)
+            def _():
+                step(0).start()
+
+            @pl.when(has_left)
+            def _():
+                step(1).start()
+
             for j in range(1, tp_count):
                 second_copy(j).start()
     for j in range(tp_count):
-        if j > 0:
-            across(j).wait_send()
+        if j < tp_count - 1:
+            for way in range(2):
+
+                @pl.when(hands_on(way, j))
+                def _(way=way, j=j):
+                    hand_on(way, j).wait_send()
+
         for s in range(2):
             for k in range(steps):
                 for m in range(1 << k):
@@ -1016,8 +1045,8 @@
             dma((tp_count,)),
             dma((tp_count,)),
             dma((3,)),
-            dma((tp_count,)),
-            dma((tp_count,)),
+            dma((2, tp_count)),
+            dma((2, tp_count)),
             dma((tp_count, 2, dp_count - 1)),
             dma((tp_count, 2, dp_count - 1)),
             dma((dp_count,)),

time: 1060 us -> 1050 us (level)
  transfers between devices with their start and end apart: 20 -> 20, of which waited for: 6 -> 6; matrix products, arithmetic and copies ran while one was open for 6% -> 6% of each run, Pallas kernels for 34% -> 35%
where the time goes in v13:
time: 1050 us; the launch traced here: 1040 us
  Pallas kernels  758 us (72%)
  waiting for transfers between devices  91.3 us (9%)
  starting transfers between devices  86.7 us (8%)
  other arithmetic  65.2 us (6%)
  local copies, waits for them, and re-layouts  27.6 us (3%)
  between operations  14.7 us (1%)
    pallas_call x1, Pallas kernels, feed(): pl.pallas_call(functools.partial(feed_kernel, ring, min(tile, hidden)), o...  277 us
    pallas_call x1, Pallas kernels, collect(): pl.pallas_call(functools.partial(collect_kernel, tp_count, dp_count), out...  100 us
    pallas_call x1, Pallas kernels, total_grads(): pl.pallas_call(functools.partial(total_kernel, tp_count, dp_count, len(pa...  89.8 us
    pallas_call x1, Pallas kernels, weigh(): pl.pallas_call(functools.partial(weigh_kernel, tp_count, dp_count, min(51...  69.1 us
    pallas_call x1, Pallas kernels, project(): pl.pallas_call(functools.partial(project_kernel, tp_count, dp_count), out...  64.9 us
    pallas_call x2, Pallas kernels, attend_backward(): pl.pallas_call(functools.partial(backward_kernel, q_heads, kv_heads, page...  58.5 us
    all_to_all x4, starting transfers between devices, trade(): lax.all_to_all(blocks, everyone, split_axis=0, concat_axis=0, tiled=True)  57.2 us
    pallas_call x2, Pallas kernels, attend_forward(): pl.pallas_call(functools.partial(forward_kernel, q_heads, kv_heads, page_...  39.8 us
  transfers between devices with their start and end apart: 20, of which 6 were waited for; matrix products, arithmetic and copies ran while one was open for 6% of the time, Pallas kernels for 35%

profile of v13, /device:TPU:0, one launch (start us, length us, event | category | flops | bytes accessed | tf_op | source)
XLA Modules:
  0.0 1043.1 jit_solution(10781136408059121103)
XLA Ops:
  13.5 2.3 gather_fusion.1
  22.6 100.3 %collect.1 = (bf16[4,2048,768]{2,1,0:T(8,128)(2,1)}, bf16[4,256,512]{2,1,0:T(8,128)(2,1)}, bf16[8,2,256]{2,1,0:T(2,128)(2,1)}, bf16[512,2048]{1,0:T(8,128)(2,1)}, bf16[512,2048]{1,0:T(8,128)(2,1)}) custom-call(bf16[256,768]{1,0:T(8,128)(2,1)} %concatenate.16.shard, bf16[256,512]{1,0:T(8,128)(2,1)} %bitcast.64, bf16[2,256]{1,0:T(2,128)(2,1)} %pad_maximum_fusion.4.gains, ...), custom_call_target="tpu_custom_call" | custom-call | bytes 100663296 | tf_op jit(solution)/shard_map/collect/pallas_call | solution.py:1033
  123.7 3.1 pad_maximum_fusion
  126.8 2.3 gather_fusion
  132.3 64.9 %project.1.refs_0_.refs_1_.refs_2_.refs_3_ = bf16[32,64,768]{2,1,0:T(8,128)(2,1)} custom-call(bf16[512,2048]{1,0:T(8,128)(2,1)} %multiply_convert_fusion.1.rows, bf16[4,2048,768]{2,1,0:T(8,128)(2,1)} %get-tuple-element.61.weights.refs_4_), custom_call_target="tpu_custom_call" | custom-call | flops 6442450944 | bytes 100663296 | tf_op jit(solution)/shard_map/project/pallas_call | solution.py:449
  197.2 2.0 collective-permute-start
  204.1 6.7 prepare.2
  210.7 19.9 %attend_forward.2 = (bf16[256,2048]{1,0:T(8,128)(2,1)}, f32[4,2048]{1,0:T(4,128)}, bf16[32,64,256]{2,1,0:T(8,128)(2,1)}) custom-call(s32[4]{0:T(128)} %and_select_fusion.4.first_block, s32[32]{0:T(128)} %fusion.14.perm, bf16[256,2048]{1,0:T(8,128)(2,1)} %get-tuple-element.62.q_t.refs_8_, bf16[1,2048,64]{2,1,0:T(8,128)(2,1)} %get-tuple-element.63.k_rows.refs_9_, ...), custom_call_target="tpu_custom_call" | custom-call | flops 1073741824 | bytes 4194304 | tf_op jit(solution)/shard_map/attend_forward/pallas_call | solution.py:174
  230.6 23.2 %all-to-all-start.1 = ((bf16[32,64,256]{2,1,0:T(8,128)(2,1)}), bf16[32,64,256]{2,1,0:T(8,128)(2,1)S(1)}, u32[]{:S(2)}, u32[]{:S(2)}) async-start(bf16[32,64,256]{2,1,0:T(8,128)(2,1)} %get-tuple-element.65), calls=%async_computation.1 | async-start | bytes 2097152 | tf_op jit(solution)/shard_map/all_to_all | solution.py:1456
  253.9 2.0 collective-permute-start.2
  255.9 12.8 %collective-permute-done.1.refs_5_ = bf16[512,2048]{1,0:T(8,128)(2,1)} collective-permute-done((bf16[512,2048]{1,0:T(8,128)(2,1)}, bf16[512,2048]{1,0:T(8,128)(2,1)}, u32[]{:S(2)}, u32[]{:S(2)}) %collective-permute-start.1) | collective-permute-done | bytes 2097184 | tf_op jit(solution)/shard_map/ppermute | solution.py:1464
  270.1 6.7 prepare.3
  276.7 19.9 %attend_forward.3 = (bf16[256,2048]{1,0:T(8,128)(2,1)}, f32[4,2048]{1,0:T(4,128)}, bf16[32,64,256]{2,1,0:T(8,128)(2,1)}) custom-call(s32[4]{0:T(128)} %and_select_fusion.4.first_block, s32[32]{0:T(128)} %fusion.14.perm, bf16[256,2048]{1,0:T(8,128)(2,1)} %get-tuple-element.72.q_t.refs_8_, bf16[1,2048,64]{2,1,0:T(8,128)(2,1)} %get-tuple-element.73.k_rows.refs_9_, ...), custom_call_target="tpu_custom_call" | custom-call | flops 1073741824 | bytes 4194304 | tf_op jit(solution)/shard_map/attend_forward/pallas_call | solution.py:174
  296.7 13.5 %all-to-all-start = ((bf16[32,64,256]{2,1,0:T(8,128)(2,1)}), bf16[32,64,256]{2,1,0:T(8,128)(2,1)}, u32[]{:S(2)}, u32[]{:S(2)}) async-start(bf16[32,64,256]{2,1,0:T(8,128)(2,1)} %get-tuple-element.76), calls=%async_computation | async-start | bytes 2097152 | tf_op jit(solution)/shard_map/all_to_all | solution.py:1456
  310.3 2.6 bitcast_convert_fusion.refs_0_
  312.9 8.7 gather_sum.2.refs_0_
  321.7 20.0 %collective-permute-done.3.refs_6_ = bf16[512,2048]{1,0:T(8,128)(2,1)} collective-permute-done((bf16[512,2048]{1,0:T(8,128)(2,1)}, bf16[512,2048]{1,0:T(8,128)(2,1)}, u32[]{:S(2)}, u32[]{:S(2)}) %collective-permute-start.3) | collective-permute-done | bytes 2097184 | tf_op jit(solution)/shard_map/ppermute | solution.py:1464
  341.7 5.8 all-to-all-done
  347.5 8.5 gather_sum.3
  356.0 2.7 multiply_reduce_fusion.2
  361.2 277.1 %feed_forward.1 = (bf16[2048,2048]{1,0:T(8,128)(2,1)}, bf16[2048,2048]{1,0:T(8,128)(2,1)}, bf16[4,512,2048]{2,1,0:T(8,128)(2,1)}, bf16[4,512,4096]{2,1,0:T(8,128...) custom-call(bf16[512,2048]{1,0:T(8,128)(2,1)} %multiply_convert_fusi, ...), custom_call_target="tpu_custom_call" | custom-call | flops 103079215104 | bytes 33554432 | tf_op jit(solution)/shard_map/feed_forward/pallas_call | solution.py:680
  638.3 4.2 fusion.5
  643.0 3.9 fusion.21.rows
  646.9 18.7 %outer.1 = bf16[2048,2048]{1,0:T(8,128)(2,1)} custom-call(bf16[512,2048]{1,0:T(8,128)(2,1)} %fusion.21.rows, bf16[4,512,256]{2,1,0:T(8,128)(2,1)} %bitcast.58, bf16[4,512,256]{2,1,0:T(8,128)(2,1)} %bitcast.12.part.refs_1_), custom_call_target="tpu_custom_call" | custom-call | flops 4294967296 | bytes 8388608 | tf_op jit(solution)/shard_map/outer/pallas_call | solution.py:1142
  665.7 8.7 spread.1.grads
  674.4 69.1 %weigh.1 = (bf16[32,64,512]{2,1,0:T(8,128)(2,1)}, bf16[2048,6144]{1,0:T(8,128)(2,1)}) custom-call(bf16[4,512,512]{2,1,0:T(8,128)(2,1)} %spread.1.grads, bf16[2048,2048]{1,0:T(8,128)(2,1)} %get-tuple-element.81.rows_t, bf16[2048,2048]{1,0:T(8,128)(2,1)} %get-tuple-element.82.grads_t, bf16[4,512,4096]{2,1,0:T(8,128)(2,1)} %get-tuple-element.83.gate_up, ...), custom_call_target="tpu_custom_call" | custom-call | flops 51539607552 | bytes 41943040 | tf_op jit(solution)/shard_map/weigh/pallas_call | solution.py:818
  743.5 5.2 collective-permute-start.4
  750.6 29.2 %attend_backward.2 = bf16[32,64,384]{2,1,0:T(8,128)(2,1)} custom-call(s32[4]{0:T(128)} %and_select_fusion.4.first_block, s32[32]{0:T(128)} %fusion.14.perm, bf16[32,64,512]{2,1,0:T(8,128)(2,1)} %get-tuple-element.95.refs_0_.refs_1_.refs_2_.refs_3_.refs_4_.refs_5_.refs_6_.refs_7_, ...), custom_call_target="tpu_custom_call" | custom-call | flops 3221225472 | bytes 6291456 | tf_op jit(solution)/shard_map/attend_backward/pallas_call | solution.py:335
  779.9 8.0 all-to-all-start.2
  787.9 4.5 collective-permute-done.4
  792.5 6.7 fusion.7
  799.1 1.9 collective-permute-start.7
  801.1 5.0 collective-permute-start.5
  806.1 29.3 %attend_backward.3 = bf16[32,64,384]{2,1,0:T(8,128)(2,1)} custom-call(s32[4]{0:T(128)} %and_select_fusion.4.first_block, s32[32]{0:T(128)} %fusion.14.perm, bf16[32,64,512]{2,1,0:T(8,128)(2,1)} %get-tuple-element.95.refs_0_.refs_1_.refs_2_.refs_3_.refs_4_.refs_5_.refs_6_.refs_7_, ...), custom_call_target="tpu_custom_call" | custom-call | flops 3221225472 | bytes 6291456 | tf_op jit(solution)/shard_map/attend_backward/pallas_call | solution.py:335
  835.4 12.4 %all-to-all-start.3 = ((bf16[32,64,384]{2,1,0:T(8,128)(2,1)}), bf16[32,64,384]{2,1,0:T(8,128)(2,1)}, u32[]{:S(2)}, u32[]{:S(2)}) async-start(bf16[32,64,384]{2,1,0:T(8,128)(2,1)} %attend_backward.3), calls=%async_computation.4 | async-start | bytes 3145728 | tf_op jit(solution)/shard_map/all_to_all | solution.py:1456
  847.9 14.9 %collective-permute-done.5 = bf16[512,2048]{1,0:T(8,128)(2,1)} collective-permute-done((bf16[512,2048]{1,0:T(8,128)(2,1)}, bf16[512,2048]{1,0:T(8,128)(2,1)}, u32[]{:S(2)}, u32[]{:S(2)}) %collective-permute-start.5) | collective-permute-done | bytes 2097184 | tf_op jit(solution)/shard_map/ppermute | solution.py:1463
  862.8 4.4 add_convert_fusion.1.refs_3_
  867.2 3.7 add_convert_fusion.2.refs_2_
  870.9 33.1 %all-to-all-done.3 = bf16[32,64,384]{2,1,0:T(8,128)(2,1)} async-done(((bf16[32,64,384]{2,1,0:T(8,128)(2,1)}), bf16[32,64,384]{2,1,0:T(8,128)(2,1)}, u32[]{:S(2)}, u32[]{:S(2)}) %all-to-all-start.3) | async-done | bytes 1572896 | tf_op jit(solution)/shard_map/all_to_all | solution.py:1456
  904.1 89.8 %total_grads.1 = (f32[256,768]{1,0:T(8,128)}, f32[512,2048]{1,0:T(8,128)}, bf16[2,512,2048]{2,1,0:T(8,128)(2,1)}) custom-call(bf16[512,2048]{1,0:T(8,128)(2,1)} %multiply_convert_fusion.1.rows, bf16[4,512,384]{2,1,0:T(8,128)(2,1)} %bitcast.16.refs_0_, bf16[4,512,384]{2,1,0:T(8,128)(2,1)} %bitcast.17.refs_1_, bf16[512,2048]{1,0:T(8,128)(2,1)} %add_convert_fusion.2.refs_2_, ...), custom_call_target="tpu_custom_call" | custom-call | flops 12884901888 | bytes 100663296 | tf_op jit(solution)/shard_map/total_grads/pallas_call | solution.py:1321
  993.9 2.0 constant_dynamic-slice_fusion.2
  995.8 2.5 collective-permute-start.10
  1000.0 4.0 multiply_reduce_fusion
  1004.7 4.2 all-to-all-start.4
  1010.7 9.1 add_convert_fusion
  1021.3 3.6 gather_fusion.4
  1024.9 2.0 gather_fusion.3
  1029.8 4.7 convert_bitcast_fusion
  (143 shorter events, 38.4 us)
Async XLA Ops:
  7.2 8.6 copy-start.13
  7.2 8.6 copy-start.14
  7.2 9.6 copy-start.30
  7.2 9.6 copy-start.31
  7.2 262.8 %all-gather.3.cloned.1.call-start = ((), (), s32[]{:S(2)}) async-start(), calls=%async_computation.7 | async-start | bytes 9437184 | tf_op jit(solution)/shard_map/all_gather | solution.py:1473
  13.5 3.4 copy-start.22
  15.8 107.2 %copy-start.5 = (bf16[8,64,2048]{2,1,0:T(8,128)(2,1)}, bf16[8,64,2048]{2,1,0:T(8,128)(2,1)S(1)}, u32[]{:S(2)}) copy-start(bf16[8,64,2048]{2,1,0:T(8,128)(2,1)S(1)} %gather_fusion.1) | copy-start | bytes 6291460
  16.9 106.2 %copy-start.12 = (bf16[2048,256]{1,0:T(8,128)(2,1)S(1)}, bf16[2048,256]{1,0:T(8,128)(2,1)}, u32[]{:S(2)}) copy-start(bf16[2048,256]{1,0:T(8,128)(2,1)} %param.27) | copy-start | bytes 3145732
  123.0 238.2 %all-gather.5.cloned.1.call-start = ((), (), s32[]{:S(2)}) async-start(), calls=%async_computation.8 | async-start | bytes 28311552 | tf_op jit(solution)/shard_map/all_gather | solution.py:1474
  129.7 67.5 %copy-start.24 = (f32[512]{0:T(512)}, f32[512]{0:T(512)S(1)}, u32[]{:S(2)}) copy-start(f32[512]{0:T(512)S(1)} %rsqrt.20) | copy-start | bytes 6148
  129.7 67.5 %copy-start.17 = (f32[1,8,256]{2,0,1:T(1,128)}, f32[1,8,256]{2,0,1:T(1,128)S(1)}, u32[]{:S(2)}) copy-start(f32[1,8,256]{2,0,1:T(1,128)S(1)} %get-tuple-element.181) | copy-start | bytes 24580
  129.7 229.0 %copy-start.15 = (f32[1,8,256]{2,0,1:T(1,128)}, f32[1,8,256]{2,0,1:T(1,128)S(1)}, u32[]{:S(2)}) copy-start(f32[1,8,256]{2,0,1:T(1,128)S(1)} %get-tuple-element.180) | copy-start | bytes 24580
  132.3 68.5 %copy-start.27 = (s32[1,2048]{1,0:T(1,128)S(1)}, s32[1,2048]{1,0:T(1,128)}, u32[]{:S(2)}) copy-start(s32[1,2048]{1,0:T(1,128)} %param.17) | copy-start | bytes 24580
  132.3 71.1 %copy-start.29 = (s32[256]{0:T(256)S(1)}, s32[256]{0:T(256)}, u32[]{:S(2)}) copy-start(s32[256]{0:T(256)} %param.18) | copy-start | bytes 3076
  197.2 56.7 %collective-permute-start = (bf16[512,2048]{1,0:T(8,128)(2,1)}, bf16[512,2048]{1,0:T(8,128)(2,1)}, u32[]{:S(2)}, u32[]{:S(2)}) collective-permute-start(bf16[512,2048]{1,0:T(8,128)(2,1)} %get-tuple-element.69.refs_1_), channel_id=1, source_target_pairs={{1,2},{2,3},{5,6},{6,7},{9,10},{10,11},{13,14},{14,15},{17,18},{18... | collective-permute-start | bytes 6291464 | tf_op jit(solution)/shard_map/ppermute | solution.py:1463
  199.3 69.5 %collective-permute-start.1 = (bf16[512,2048]{1,0:T(8,128)(2,1)}, bf16[512,2048]{1,0:T(8,128)(2,1)}, u32[]{:S(2)}, u32[]{:S(2)}) collective-permute-start(bf16[512,2048]{1,0:T(8,128)(2,1)} %get-tuple-element.70.refs_4_), channel_id=1, source_target_pairs={{1,0},{2,1},{5,4},{6,5},{9,8},{10,9},{13,12},{14,13},{17,16},{18,1... | collective-permute-start | bytes 6291464 | tf_op jit(solution)/shard_map/ppermute | solution.py:1464
  200.9 9.8 copy-start.19
  230.6 66.1 %all-to-all-start.1 = ((bf16[32,64,256]{2,1,0:T(8,128)(2,1)}), bf16[32,64,256]{2,1,0:T(8,128)(2,1)S(1)}, u32[]{:S(2)}, u32[]{:S(2)}) async-start(bf16[32,64,256]{2,1,0:T(8,128)(2,1)} %get-tuple-element.65), calls=%async_computation.1 | async-start | bytes 2097152 | tf_op jit(solution)/shard_map/all_to_all | solution.py:1456
  253.9 67.8 %collective-permute-start.2 = (bf16[512,2048]{1,0:T(8,128)(2,1)}, bf16[512,2048]{1,0:T(8,128)(2,1)}, u32[]{:S(2)}, u32[]{:S(2)}) collective-permute-start(bf16[512,2048]{1,0:T(8,128)(2,1)} %collective-permute-done.refs_2_), channel_id=1, source_target_pairs={{2,3},{6,7},{10,11},{14,15},{18,19},{22,23},{26,27},{30,31}} | collective-permute-start | bytes 6291464 | tf_op jit(solution)/shard_map/ppermute | solution.py:1463
  268.7 73.0 %collective-permute-start.3 = (bf16[512,2048]{1,0:T(8,128)(2,1)}, bf16[512,2048]{1,0:T(8,128)(2,1)}, u32[]{:S(2)}, u32[]{:S(2)}) collective-permute-start(bf16[512,2048]{1,0:T(8,128)(2,1)} %collective-permute-done.1.refs_5_), channel_id=1, source_target_pairs={{1,0},{5,4},{9,8},{13,12},{17,16},{21,20},{25,24},{29,28}} | collective-permute-start | bytes 6291464 | tf_op jit(solution)/shard_map/ppermute | solution.py:1464
  276.7 33.5 %copy-start.3 = (bf16[8,64,2048]{2,1,0:T(8,128)(2,1)S(1)}, bf16[8,64,2048]{2,1,0:T(8,128)(2,1)}, u32[]{:S(2)}) copy-start(bf16[8,64,2048]{2,1,0:T(8,128)(2,1)} %copy-done.2) | copy-start | bytes 6291460
  296.7 16.2 %copy-start.9 = (bf16[32,64,256]{2,1,0:T(8,128)(2,1)}, bf16[32,64,256]{2,1,0:T(8,128)(2,1)S(1)}, u32[]{:S(2)}) copy-start(bf16[32,64,256]{2,1,0:T(8,128)(2,1)S(1)} %all-to-all-done.1) | copy-start | bytes 3145732
  296.7 50.8 %all-to-all-start = ((bf16[32,64,256]{2,1,0:T(8,128)(2,1)}), bf16[32,64,256]{2,1,0:T(8,128)(2,1)}, u32[]{:S(2)}, u32[]{:S(2)}) async-start(bf16[32,64,256]{2,1,0:T(8,128)(2,1)} %get-tuple-element.76), calls=%async_computation | async-start | bytes 2097152 | tf_op jit(solution)/shard_map/all_to_all | solution.py:1456
  310.2 495.9 %reduce-scatter.3.cloned.1.call-start = ((), (), s32[]{:S(2)}) async-start(), calls=%async_computation.9 | async-start | bytes 9437184 | tf_op jit(solution)/shard_map/reduce_scatter | solution.py:1516
  356.0 3.4 copy-start
  638.3 4.2 copy-start.1
  638.3 4.7 copy-start.6
  638.3 4.7 copy-start.16
  638.3 4.7 copy-start.21
  638.3 4.7 copy-start.23
  665.7 364.1 %reduce-scatter.5.cloned.1.call-start = ((), (), s32[]{:S(2)}) async-start(), calls=%async_computation.10 | async-start | bytes 28311552 | tf_op jit(solution)/shard_map/reduce_scatter | solution.py:1516
  743.5 5.2 copy-start.10
  743.5 48.9 %collective-permute-start.4 = (bf16[512,2048]{1,0:T(8,128)(2,1)}, bf16[512,2048]{1,0:T(8,128)(2,1)}, u32[]{:S(2)}, u32[]{:S(2)}) collective-permute-start(bf16[512,2048]{1,0:T(8,128)(2,1)} %get-tuple-element.88), channel_id=1, source_target_pairs={{0,1},{4,5},{8,9},{12,13},{16,17},{20,21},{24,25},{28,29}} | collective-permute-start | bytes 6291464 | tf_op jit(solution)/shard_map/ppermute | solution.py:1463
  748.7 43.8 %collective-permute-start.6 = (bf16[512,2048]{1,0:T(8,128)(2,1)S(1)}, bf16[512,2048]{1,0:T(8,128)(2,1)}, u32[]{:S(2)}, u32[]{:S(2)}) collective-permute-start(bf16[512,2048]{1,0:T(8,128)(2,1)S(1)} %copy-done.10), channel_id=1, source_target_pairs={{3,2},{7,6},{11,10},{15,14},{19,18},{23,22},{27,26},{31,30}} | collective-permute-start | bytes 6291464 | tf_op jit(solution)/shard_map/ppermute | solution.py:1464
  779.9 55.6 %all-to-all-start.2 = ((bf16[32,64,384]{2,1,0:T(8,128)(2,1)}), bf16[32,64,384]{2,1,0:T(8,128)(2,1)}, u32[]{:S(2)}, u32[]{:S(2)}) async-start(bf16[32,64,384]{2,1,0:T(8,128)(2,1)} %attend_backward.2), calls=%async_computation.3 | async-start | bytes 3145728 | tf_op jit(solution)/shard_map/all_to_all | solution.py:1456
  799.1 48.7 %collective-permute-start.7 = (bf16[512,2048]{1,0:T(8,128)(2,1)}, bf16[512,2048]{1,0:T(8,128)(2,1)}, u32[]{:S(2)}, u32[]{:S(2)}) collective-permute-start(bf16[512,2048]{1,0:T(8,128)(2,1)} %get-tuple-element.163), channel_id=1, source_target_pairs={{2,1},{3,2},{6,5},{7,6},{10,9},{11,10},{14,13},{15,14},{18,17},{19... | collective-permute-start | bytes 6291464 | tf_op jit(solution)/shard_map/ppermute | solution.py:1464
  801.1 61.7 %collective-permute-start.5 = (bf16[512,2048]{1,0:T(8,128)(2,1)}, bf16[512,2048]{1,0:T(8,128)(2,1)}, u32[]{:S(2)}, u32[]{:S(2)}) collective-permute-start(bf16[512,2048]{1,0:T(8,128)(2,1)} %get-tuple-element.164), channel_id=1, source_target_pairs={{0,1},{1,2},{4,5},{5,6},{8,9},{9,10},{12,13},{13,14},{16,17},{17,1... | collective-permute-start | bytes 6291464 | tf_op jit(solution)/shard_map/ppermute | solution.py:1463
  806.1 41.7 %copy-start.28 = (s32[8]{0:T(128)S(1)}, s32[8]{0:T(128)}, u32[]{:S(2)}) copy-start(s32[8]{0:T(128)} %get-tuple-element.158) | copy-start | bytes 100
  835.4 68.6 %all-to-all-start.3 = ((bf16[32,64,384]{2,1,0:T(8,128)(2,1)}), bf16[32,64,384]{2,1,0:T(8,128)(2,1)}, u32[]{:S(2)}, u32[]{:S(2)}) async-start(bf16[32,64,384]{2,1,0:T(8,128)(2,1)} %attend_backward.3), calls=%async_computation.4 | async-start | bytes 3145728 | tf_op jit(solution)/shard_map/all_to_all | solution.py:1456
  904.1 95.9 %copy-start.18 = (f32[1,8,256]{2,0,1:T(1,128)S(1)}, f32[1,8,256]{2,0,1:T(1,128)}, u32[]{:S(2)}) copy-start(f32[1,8,256]{2,0,1:T(1,128)} %copy-done.17) | copy-start | bytes 24580
  904.1 95.9 %copy-start.25 = (f32[512]{0:T(512)S(1)}, f32[512]{0:T(512)}, u32[]{:S(2)}) copy-start(f32[512]{0:T(512)} %copy-done.24) | copy-start | bytes 6148
  993.9 15.0 %copy-start.11 = (f32[256,768]{1,0:T(8,128)S(1)}, f32[256,768]{1,0:T(8,128)}, u32[]{:S(2)}) copy-start(f32[256,768]{1,0:T(8,128)} %get-tuple-element.106) | copy-start | bytes 2359300
  995.8 31.6 %collective-permute-start.10 = (bf16[256,512]{1,0:T(8,128)(2,1)}, bf16[256,512]{1,0:T(8,128)(2,1)}, u32[]{:S(2)}, u32[]{:S(2)}) collective-permute-start(bf16[256,512]{1,0:T(8,128)(2,1)} %get-tuple-element.166), channel_id=1, source_target_pairs={{0,3},{1,0},{2,1},{3,2},{4,7},{5,4},{6,5},{7,6},{8,11},{9,8},{10,9... | collective-permute-start | bytes 786440 | tf_op jit(solution)/shard_map/ppermute | solution.py:1525
  998.4 29.1 %collective-permute-start.8 = (bf16[256,512]{1,0:T(8,128)(2,1)S(1)}, bf16[256,512]{1,0:T(8,128)(2,1)}, u32[]{:S(2)}, u32[]{:S(2)}) collective-permute-start(bf16[256,512]{1,0:T(8,128)(2,1)S(1)} %get-tuple-element.165), channel_id=1, source_target_pairs={{0,1},{1,2},{2,3},{3,0},{4,5},{5,6},{6,7},{7,4},{8,9},{9,10},{10,1... | collective-permute-start | bytes 786440 | tf_op jit(solution)/shard_map/ppermute | solution.py:1525
  998.4 11.6 %copy-start.4 = (bf16[8,64,2048]{2,1,0:T(8,128)(2,1)S(1)}, bf16[8,64,2048]{2,1,0:T(8,128)(2,1)}, u32[]{:S(2)}) copy-start(bf16[8,64,2048]{2,1,0:T(8,128)(2,1)} %copy-done.2) | copy-start | bytes 6291460
  998.4 29.1 %collective-permute-start.9 = (bf16[256,512]{1,0:T(8,128)(2,1)S(1)}, bf16[256,512]{1,0:T(8,128)(2,1)}, u32[]{:S(2)}, u32[]{:S(2)}) collective-permute-start(bf16[256,512]{1,0:T(8,128)(2,1)S(1)} %get-tuple-element.167), channel_id=1, source_target_pairs={{0,2},{1,3},{2,0},{3,1},{4,6},{5,7},{6,4},{7,5},{8,10},{9,11},{10,... | collective-permute-start | bytes 786440 | tf_op jit(solution)/shard_map/ppermute | solution.py:1525
  1004.7 22.2 %all-to-all-start.4 = ((f32[32,2,256]{2,1,0:T(2,128)}), f32[32,2,256]{2,1,0:T(2,128)S(1)}, u32[]{:S(2)}, u32[]{:S(2)}) async-start(f32[32,2,256]{2,1,0:T(2,128)} %bitcast.26), calls=%async_computation.5 | async-start | bytes 131072 | tf_op jit(solution)/shard_map/all_to_all | solution.py:1575
  1019.7 5.1 copy-start.8
  (4 other events, 6.6 us)
Sparse Core Ops, SparseCore 0:
  123.1 84.1 all-gather.2
  209.3 142.9 all-gather.4
  665.8 87.6 reduce-scatter.2
  757.4 192.2 reduce-scatter.4

commit v14 on v13

--- a/solution.py
+++ b/solution.py
@@ -1398,12 +1398,13 @@
     everyone = ("tensor", "dp")
 
     local_ids = jnp.arange(dp_count, dtype=jnp.int32)
-    inverse = (
-        jnp.zeros((page_count,), jnp.int32).at[pages].set(jnp.arange(page_count, dtype=jnp.int32))
+    own_pages = device * dp_count + local_ids
+    page_ids = jnp.arange(page_count, dtype=jnp.int32)
+    dealt = jnp.sum(jnp.where(pages[None, :] == own_pages[:, None], page_ids[None, :], 0), axis=1)
+    dest_group = dealt // group_pages
+    send_order = jnp.sum(
+        jnp.where(dest_group[None, :] == local_ids[:, None], local_ids[None, :], 0), axis=1
     )
-    dealt = lax.dynamic_slice_in_dim(inverse, device * dp_count, dp_count)
-    dest_group = dealt // group_pages
-    send_order = jnp.zeros((dp_count,), jnp.int32).at[dest_group].set(local_ids)
     group_sources = lax.dynamic_slice_in_dim(pages, dp_index * group_pages, group_pages)
     perm = (
         (jnp.arange(group_pages, dtype=jnp.int32) // dp_count) * dp_count

time: 1050 us -> 1050 us (level)
  starting transfers between devices: 86.7 us -> 71.9 us
    all_to_all x4, starting transfers between devices: 57.2 us -> 42.3 us  [trade(): lax.all_to_all(blocks, everyone, split_axis=0, concat_axis=0, tiled=True)]
  transfers between devices with their start and end apart: 20 -> 20, of which waited for: 6 -> 6; matrix products, arithmetic and copies ran while one was open for 6% -> 6% of each run, Pallas kernels for 35% -> 36%
where the time goes in v14:
time: 1050 us; the launch traced here: 1040 us
  Pallas kernels  767 us (73%)
  waiting for transfers between devices  94 us (9%)
  starting transfers between devices  71.9 us (7%)
  other arithmetic  66 us (6%)
  local copies, waits for them, and re-layouts  25.6 us (2%)
  between operations  14.7 us (1%)
    pallas_call x1, Pallas kernels, feed(): pl.pallas_call(functools.partial(feed_kernel, ring, min(tile, hidden)), o...  277 us
    pallas_call x1, Pallas kernels, collect(): pl.pallas_call(functools.partial(collect_kernel, tp_count, dp_count), out...  100 us
    pallas_call x1, Pallas kernels, total_grads(): pl.pallas_call(functools.partial(total_kernel, tp_count, dp_count, len(pa...  89.9 us
    pallas_call x1, Pallas kernels, weigh(): pl.pallas_call(functools.partial(weigh_kernel, tp_count, dp_count, min(51...  68.9 us
    pallas_call x1, Pallas kernels, project(): pl.pallas_call(functools.partial(project_kernel, tp_count, dp_count), out...  64.9 us
    pallas_call x2, Pallas kernels, attend_backward(): pl.pallas_call(functools.partial(backward_kernel, q_heads, kv_heads, page...  64.5 us
    pallas_call x2, Pallas kernels, attend_forward(): pl.pallas_call(functools.partial(forward_kernel, q_heads, kv_heads, page_...  43.7 us
    all_to_all x4, starting transfers between devices, trade(): lax.all_to_all(blocks, everyone, split_axis=0, concat_axis=0, tiled=True)  42.3 us
  transfers between devices with their start and end apart: 20, of which 6 were waited for; matrix products, arithmetic and copies ran while one was open for 6% of the time, Pallas kernels for 36%

profile of v14, /device:TPU:0, one launch (start us, length us, event | category | flops | bytes accessed | tf_op | source)
XLA Modules:
  0.0 1039.7 jit_solution(2996131769693969205)
XLA Ops:
  11.2 2.3 gather_fusion.1
  20.4 100.3 %collect.1 = (bf16[4,2048,768]{2,1,0:T(8,128)(2,1)}, bf16[4,256,512]{2,1,0:T(8,128)(2,1)}, bf16[8,2,256]{2,1,0:T(2,128)(2,1)}, bf16[512,2048]{1,0:T(8,128)(2,1)}, bf16[512,2048]{1,0:T(8,128)(2,1)}) custom-call(bf16[256,768]{1,0:T(8,128)(2,1)} %concatenate.16.shard, bf16[256,512]{1,0:T(8,128)(2,1)} %bitcast.76, bf16[2,256]{1,0:T(2,128)(2,1)} %pad_maximum_fusion.4.gains, ...), custom_call_target="tpu_custom_call" | custom-call | bytes 100663296 | tf_op jit(solution)/shard_map/collect/pallas_call | solution.py:1033
  121.5 3.1 pad_maximum_fusion
  124.6 2.3 gather_fusion
  130.1 64.9 %project.1.refs_0_.refs_1_.refs_2_.refs_3_ = bf16[32,64,768]{2,1,0:T(8,128)(2,1)} custom-call(bf16[512,2048]{1,0:T(8,128)(2,1)} %multiply_convert_fusion.1.rows, bf16[4,2048,768]{2,1,0:T(8,128)(2,1)} %get-tuple-element.61.weights.refs_4_), custom_call_target="tpu_custom_call" | custom-call | flops 6442450944 | bytes 100663296 | tf_op jit(solution)/shard_map/project/pallas_call | solution.py:449
  195.0 2.0 collective-permute-start
  201.7 6.7 prepare.2
  208.4 21.8 %attend_forward.2 = (bf16[256,2048]{1,0:T(8,128)(2,1)}, f32[4,2048]{1,0:T(4,128)}, bf16[32,64,256]{2,1,0:T(8,128)(2,1)}) custom-call(s32[4]{0:T(128)} %and_select_fusion.5.first_block, s32[32]{0:T(128)} %fusion.14.perm, bf16[256,2048]{1,0:T(8,128)(2,1)} %get-tuple-element.62.q_t.refs_8_, bf16[1,2048,64]{2,1,0:T(8,128)(2,1)} %get-tuple-element.63.k_rows.refs_9_, ...), custom_call_target="tpu_custom_call" | custom-call | flops 1073741824 | bytes 4194304 | tf_op jit(solution)/shard_map/attend_forward/pallas_call | solution.py:174
  230.2 22.1 %all-to-all-start.1 = ((bf16[32,64,256]{2,1,0:T(8,128)(2,1)}), bf16[32,64,256]{2,1,0:T(8,128)(2,1)S(1)}, u32[]{:S(2)}, u32[]{:S(2)}) async-start(bf16[32,64,256]{2,1,0:T(8,128)(2,1)} %get-tuple-element.65), calls=%async_computation.1 | async-start | bytes 2097152 | tf_op jit(solution)/shard_map/all_to_all | solution.py:1457
  252.4 2.1 collective-permute-start.2
  254.4 11.9 %collective-permute-done.1.refs_5_ = bf16[512,2048]{1,0:T(8,128)(2,1)} collective-permute-done((bf16[512,2048]{1,0:T(8,128)(2,1)}, bf16[512,2048]{1,0:T(8,128)(2,1)}, u32[]{:S(2)}, u32[]{:S(2)}) %collective-permute-start.1) | collective-permute-done | bytes 2097184 | tf_op jit(solution)/shard_map/ppermute | solution.py:1465
  267.7 6.7 prepare.3
  274.4 21.9 %attend_forward.3 = (bf16[256,2048]{1,0:T(8,128)(2,1)}, f32[4,2048]{1,0:T(4,128)}, bf16[32,64,256]{2,1,0:T(8,128)(2,1)}) custom-call(s32[4]{0:T(128)} %and_select_fusion.5.first_block, s32[32]{0:T(128)} %fusion.14.perm, bf16[256,2048]{1,0:T(8,128)(2,1)} %get-tuple-element.72.q_t.refs_8_, bf16[1,2048,64]{2,1,0:T(8,128)(2,1)} %get-tuple-element.73.k_rows.refs_9_, ...), custom_call_target="tpu_custom_call" | custom-call | flops 1073741824 | bytes 4194304 | tf_op jit(solution)/shard_map/attend_forward/pallas_call | solution.py:174
  296.3 12.5 %all-to-all-start = ((bf16[32,64,256]{2,1,0:T(8,128)(2,1)}), bf16[32,64,256]{2,1,0:T(8,128)(2,1)}, u32[]{:S(2)}, u32[]{:S(2)}) async-start(bf16[32,64,256]{2,1,0:T(8,128)(2,1)} %get-tuple-element.76), calls=%async_computation | async-start | bytes 2097152 | tf_op jit(solution)/shard_map/all_to_all | solution.py:1457
  308.9 2.6 bitcast_convert_fusion.refs_0_
  311.5 8.6 gather_sum.2.refs_0_
  320.1 18.7 %collective-permute-done.3.refs_6_ = bf16[512,2048]{1,0:T(8,128)(2,1)} collective-permute-done((bf16[512,2048]{1,0:T(8,128)(2,1)}, bf16[512,2048]{1,0:T(8,128)(2,1)}, u32[]{:S(2)}, u32[]{:S(2)}) %collective-permute-start.3) | collective-permute-done | bytes 2097184 | tf_op jit(solution)/shard_map/ppermute | solution.py:1465
  338.9 6.4 all-to-all-done
  345.3 8.5 gather_sum.3
  353.8 2.7 multiply_reduce_fusion.2
  359.0 277.1 %feed_forward.1 = (bf16[2048,2048]{1,0:T(8,128)(2,1)}, bf16[2048,2048]{1,0:T(8,128)(2,1)}, bf16[4,512,2048]{2,1,0:T(8,128)(2,1)}, bf16[4,512,4096]{2,1,0:T(8,128...) custom-call(bf16[512,2048]{1,0:T(8,128)(2,1)} %multiply_convert_fusi, ...), custom_call_target="tpu_custom_call" | custom-call | flops 103079215104 | bytes 33554432 | tf_op jit(solution)/shard_map/feed_forward/pallas_call | solution.py:680
  636.1 4.2 fusion.5
  640.8 3.9 fusion.18.rows
  644.7 18.7 %outer.1 = bf16[2048,2048]{1,0:T(8,128)(2,1)} custom-call(bf16[512,2048]{1,0:T(8,128)(2,1)} %fusion.18.rows, bf16[4,512,256]{2,1,0:T(8,128)(2,1)} %bitcast.70, bf16[4,512,256]{2,1,0:T(8,128)(2,1)} %bitcast.12.part.refs_1_), custom_call_target="tpu_custom_call" | custom-call | flops 4294967296 | bytes 8388608 | tf_op jit(solution)/shard_map/outer/pallas_call | solution.py:1142
  663.5 8.9 spread.1.grads
  672.4 68.9 %weigh.1 = (bf16[32,64,512]{2,1,0:T(8,128)(2,1)}, bf16[2048,6144]{1,0:T(8,128)(2,1)}) custom-call(bf16[4,512,512]{2,1,0:T(8,128)(2,1)} %spread.1.grads, bf16[2048,2048]{1,0:T(8,128)(2,1)} %get-tuple-element.81.rows_t, bf16[2048,2048]{1,0:T(8,128)(2,1)} %get-tuple-element.82.grads_t, bf16[4,512,4096]{2,1,0:T(8,128)(2,1)} %get-tuple-element.83.gate_up, ...), custom_call_target="tpu_custom_call" | custom-call | flops 51539607552 | bytes 41943040 | tf_op jit(solution)/shard_map/weigh/pallas_call | solution.py:818
  741.3 5.3 collective-permute-start.4
  748.6 32.2 %attend_backward.2 = bf16[32,64,384]{2,1,0:T(8,128)(2,1)} custom-call(s32[4]{0:T(128)} %and_select_fusion.5.first_block, s32[32]{0:T(128)} %fusion.14.perm, bf16[32,64,512]{2,1,0:T(8,128)(2,1)} %get-tuple-element.95.refs_0_.refs_1_.refs_2_.refs_3_.refs_4_.refs_5_.refs_6_.refs_7_, ...), custom_call_target="tpu_custom_call" | custom-call | flops 3221225472 | bytes 6291456 | tf_op jit(solution)/shard_map/attend_backward/pallas_call | solution.py:335
  780.8 3.5 all-to-all-start.2
  784.3 7.4 collective-permute-done.4
  791.7 7.1 fusion.7
  798.8 2.0 collective-permute-start.7
  800.7 4.8 collective-permute-start.5
  805.6 32.3 %attend_backward.3 = bf16[32,64,384]{2,1,0:T(8,128)(2,1)} custom-call(s32[4]{0:T(128)} %and_select_fusion.5.first_block, s32[32]{0:T(128)} %fusion.14.perm, bf16[32,64,512]{2,1,0:T(8,128)(2,1)} %get-tuple-element.95.refs_0_.refs_1_.refs_2_.refs_3_.refs_4_.refs_5_.refs_6_.refs_7_, ...), custom_call_target="tpu_custom_call" | custom-call | flops 3221225472 | bytes 6291456 | tf_op jit(solution)/shard_map/attend_backward/pallas_call | solution.py:335
  837.9 4.1 all-to-all-start.3
  842.1 20.1 %collective-permute-done.5 = bf16[512,2048]{1,0:T(8,128)(2,1)} collective-permute-done((bf16[512,2048]{1,0:T(8,128)(2,1)}, bf16[512,2048]{1,0:T(8,128)(2,1)}, u32[]{:S(2)}, u32[]{:S(2)}) %collective-permute-start.5) | collective-permute-done | bytes 2097184 | tf_op jit(solution)/shard_map/ppermute | solution.py:1464
  862.3 4.8 add_convert_fusion.1.refs_3_
  867.1 4.0 add_convert_fusion.2.refs_2_
  871.1 29.3 %all-to-all-done.3 = bf16[32,64,384]{2,1,0:T(8,128)(2,1)} async-done(((bf16[32,64,384]{2,1,0:T(8,128)(2,1)}), bf16[32,64,384]{2,1,0:T(8,128)(2,1)}, u32[]{:S(2)}, u32[]{:S(2)}) %all-to-all-start.3) | async-done | bytes 1572896 | tf_op jit(solution)/shard_map/all_to_all | solution.py:1457
  900.4 89.9 %total_grads.1 = (f32[256,768]{1,0:T(8,128)}, f32[512,2048]{1,0:T(8,128)}, bf16[2,512,2048]{2,1,0:T(8,128)(2,1)}) custom-call(bf16[512,2048]{1,0:T(8,128)(2,1)} %multiply_convert_fusion.1.rows, bf16[4,512,384]{2,1,0:T(8,128)(2,1)} %bitcast.16.refs_0_, bf16[4,512,384]{2,1,0:T(8,128)(2,1)} %bitcast.17.refs_1_, bf16[512,2048]{1,0:T(8,128)(2,1)} %add_convert_fusion.2.refs_2_, ...), custom_call_target="tpu_custom_call" | custom-call | flops 12884901888 | bytes 100663296 | tf_op jit(solution)/shard_map/total_grads/pallas_call | solution.py:1321
  990.4 2.0 constant_dynamic-slice_fusion.1
  992.3 2.6 collective-permute-start.10
  996.5 4.0 multiply_reduce_fusion
  1001.2 4.3 all-to-all-start.4
  1007.3 9.1 add_convert_fusion
  1017.9 3.6 gather_fusion.4
  1021.5 2.0 gather_fusion.3
  1026.4 4.7 convert_bitcast_fusion
  (144 shorter events, 36.0 us)
Async XLA Ops:
  7.2 6.3 copy-start.15
  7.2 6.4 copy-start.16
  7.2 7.4 copy-start.31
  7.2 7.4 copy-start.32
  7.2 260.4 %all-gather.3.cloned.1.call-start = ((), (), s32[]{:S(2)}) async-start(), calls=%async_computation.7 | async-start | bytes 9437184 | tf_op jit(solution)/shard_map/all_gather | solution.py:1474
  8.2 8.2 copy-start
  13.5 107.3 %copy-start.7 = (bf16[8,64,2048]{2,1,0:T(8,128)(2,1)}, bf16[8,64,2048]{2,1,0:T(8,128)(2,1)S(1)}, u32[]{:S(2)}) copy-start(bf16[8,64,2048]{2,1,0:T(8,128)(2,1)S(1)} %gather_fusion.1) | copy-start | bytes 6291460
  14.6 106.2 %copy-start.14 = (bf16[2048,256]{1,0:T(8,128)(2,1)S(1)}, bf16[2048,256]{1,0:T(8,128)(2,1)}, u32[]{:S(2)}) copy-start(bf16[2048,256]{1,0:T(8,128)(2,1)} %param.27) | copy-start | bytes 3145732
  120.8 238.2 %all-gather.5.cloned.1.call-start = ((), (), s32[]{:S(2)}) async-start(), calls=%async_computation.8 | async-start | bytes 28311552 | tf_op jit(solution)/shard_map/all_gather | solution.py:1475
  127.5 67.5 %copy-start.26 = (f32[512]{0:T(512)}, f32[512]{0:T(512)S(1)}, u32[]{:S(2)}) copy-start(f32[512]{0:T(512)S(1)} %rsqrt.20) | copy-start | bytes 6148
  127.5 67.5 %copy-start.19 = (f32[1,8,256]{2,0,1:T(1,128)}, f32[1,8,256]{2,0,1:T(1,128)S(1)}, u32[]{:S(2)}) copy-start(f32[1,8,256]{2,0,1:T(1,128)S(1)} %get-tuple-element.178) | copy-start | bytes 24580
  127.5 229.0 %copy-start.17 = (f32[1,8,256]{2,0,1:T(1,128)}, f32[1,8,256]{2,0,1:T(1,128)S(1)}, u32[]{:S(2)}) copy-start(f32[1,8,256]{2,0,1:T(1,128)S(1)} %get-tuple-element.177) | copy-start | bytes 24580
  130.1 68.5 %copy-start.29 = (s32[1,2048]{1,0:T(1,128)S(1)}, s32[1,2048]{1,0:T(1,128)}, u32[]{:S(2)}) copy-start(s32[1,2048]{1,0:T(1,128)} %param.17) | copy-start | bytes 24580
  130.1 71.1 %copy-start.30 = (s32[256]{0:T(256)S(1)}, s32[256]{0:T(256)}, u32[]{:S(2)}) copy-start(s32[256]{0:T(256)} %param.18) | copy-start | bytes 3076
  195.0 57.4 %collective-permute-start = (bf16[512,2048]{1,0:T(8,128)(2,1)}, bf16[512,2048]{1,0:T(8,128)(2,1)}, u32[]{:S(2)}, u32[]{:S(2)}) collective-permute-start(bf16[512,2048]{1,0:T(8,128)(2,1)} %get-tuple-element.69.refs_1_), channel_id=1, source_target_pairs={{1,2},{2,3},{5,6},{6,7},{9,10},{10,11},{13,14},{14,15},{17,18},{18... | collective-permute-start | bytes 6291464 | tf_op jit(solution)/shard_map/ppermute | solution.py:1464
  197.1 69.3 %collective-permute-start.1 = (bf16[512,2048]{1,0:T(8,128)(2,1)}, bf16[512,2048]{1,0:T(8,128)(2,1)}, u32[]{:S(2)}, u32[]{:S(2)}) collective-permute-start(bf16[512,2048]{1,0:T(8,128)(2,1)} %get-tuple-element.70.refs_4_), channel_id=1, source_target_pairs={{1,0},{2,1},{5,4},{6,5},{9,8},{10,9},{13,12},{14,13},{17,16},{18,1... | collective-permute-start | bytes 6291464 | tf_op jit(solution)/shard_map/ppermute | solution.py:1465
  198.7 9.7 copy-start.21
  230.2 66.0 %all-to-all-start.1 = ((bf16[32,64,256]{2,1,0:T(8,128)(2,1)}), bf16[32,64,256]{2,1,0:T(8,128)(2,1)S(1)}, u32[]{:S(2)}, u32[]{:S(2)}) async-start(bf16[32,64,256]{2,1,0:T(8,128)(2,1)} %get-tuple-element.65), calls=%async_computation.1 | async-start | bytes 2097152 | tf_op jit(solution)/shard_map/all_to_all | solution.py:1457
  252.4 67.7 %collective-permute-start.2 = (bf16[512,2048]{1,0:T(8,128)(2,1)}, bf16[512,2048]{1,0:T(8,128)(2,1)}, u32[]{:S(2)}, u32[]{:S(2)}) collective-permute-start(bf16[512,2048]{1,0:T(8,128)(2,1)} %collective-permute-done.refs_2_), channel_id=1, source_target_pairs={{2,3},{6,7},{10,11},{14,15},{18,19},{22,23},{26,27},{30,31}} | collective-permute-start | bytes 6291464 | tf_op jit(solution)/shard_map/ppermute | solution.py:1464
  266.4 72.5 %collective-permute-start.3 = (bf16[512,2048]{1,0:T(8,128)(2,1)}, bf16[512,2048]{1,0:T(8,128)(2,1)}, u32[]{:S(2)}, u32[]{:S(2)}) collective-permute-start(bf16[512,2048]{1,0:T(8,128)(2,1)} %collective-permute-done.1.refs_5_), channel_id=1, source_target_pairs={{1,0},{5,4},{9,8},{13,12},{17,16},{21,20},{25,24},{29,28}} | collective-permute-start | bytes 6291464 | tf_op jit(solution)/shard_map/ppermute | solution.py:1465
  274.4 34.5 %copy-start.5 = (bf16[8,64,2048]{2,1,0:T(8,128)(2,1)S(1)}, bf16[8,64,2048]{2,1,0:T(8,128)(2,1)}, u32[]{:S(2)}) copy-start(bf16[8,64,2048]{2,1,0:T(8,128)(2,1)} %copy-done.4) | copy-start | bytes 6291460
  296.3 15.2 %copy-start.11 = (bf16[32,64,256]{2,1,0:T(8,128)(2,1)}, bf16[32,64,256]{2,1,0:T(8,128)(2,1)S(1)}, u32[]{:S(2)}) copy-start(bf16[32,64,256]{2,1,0:T(8,128)(2,1)S(1)} %all-to-all-done.1) | copy-start | bytes 3145732
  296.3 49.0 %all-to-all-start = ((bf16[32,64,256]{2,1,0:T(8,128)(2,1)}), bf16[32,64,256]{2,1,0:T(8,128)(2,1)}, u32[]{:S(2)}, u32[]{:S(2)}) async-start(bf16[32,64,256]{2,1,0:T(8,128)(2,1)} %get-tuple-element.76), calls=%async_computation | async-start | bytes 2097152 | tf_op jit(solution)/shard_map/all_to_all | solution.py:1457
  308.8 496.7 %reduce-scatter.3.cloned.1.call-start = ((), (), s32[]{:S(2)}) async-start(), calls=%async_computation.9 | async-start | bytes 9437184 | tf_op jit(solution)/shard_map/reduce_scatter | solution.py:1517
  353.8 3.4 copy-start.2
  636.1 4.2 copy-start.3
  636.1 4.7 copy-start.8
  636.1 4.7 copy-start.18
  636.1 4.7 copy-start.23
  636.1 4.7 copy-start.25
  663.5 362.9 %reduce-scatter.5.cloned.1.call-start = ((), (), s32[]{:S(2)}) async-start(), calls=%async_computation.10 | async-start | bytes 28311552 | tf_op jit(solution)/shard_map/reduce_scatter | solution.py:1517
  741.3 5.4 copy-start.12
  741.3 50.3 %collective-permute-start.4 = (bf16[512,2048]{1,0:T(8,128)(2,1)}, bf16[512,2048]{1,0:T(8,128)(2,1)}, u32[]{:S(2)}, u32[]{:S(2)}) collective-permute-start(bf16[512,2048]{1,0:T(8,128)(2,1)} %get-tuple-element.88), channel_id=1, source_target_pairs={{0,1},{4,5},{8,9},{12,13},{16,17},{20,21},{24,25},{28,29}} | collective-permute-start | bytes 6291464 | tf_op jit(solution)/shard_map/ppermute | solution.py:1464
  746.7 45.0 %collective-permute-start.6 = (bf16[512,2048]{1,0:T(8,128)(2,1)S(1)}, bf16[512,2048]{1,0:T(8,128)(2,1)}, u32[]{:S(2)}, u32[]{:S(2)}) collective-permute-start(bf16[512,2048]{1,0:T(8,128)(2,1)S(1)} %copy-done.12), channel_id=1, source_target_pairs={{3,2},{7,6},{11,10},{15,14},{19,18},{23,22},{27,26},{31,30}} | collective-permute-start | bytes 6291464 | tf_op jit(solution)/shard_map/ppermute | solution.py:1465
  780.8 57.1 %all-to-all-start.2 = ((bf16[32,64,384]{2,1,0:T(8,128)(2,1)}), bf16[32,64,384]{2,1,0:T(8,128)(2,1)}, u32[]{:S(2)}, u32[]{:S(2)}) async-start(bf16[32,64,384]{2,1,0:T(8,128)(2,1)} %attend_backward.2), calls=%async_computation.3 | async-start | bytes 3145728 | tf_op jit(solution)/shard_map/all_to_all | solution.py:1457
  798.8 43.3 %collective-permute-start.7 = (bf16[512,2048]{1,0:T(8,128)(2,1)}, bf16[512,2048]{1,0:T(8,128)(2,1)}, u32[]{:S(2)}, u32[]{:S(2)}) collective-permute-start(bf16[512,2048]{1,0:T(8,128)(2,1)} %get-tuple-element.160), channel_id=1, source_target_pairs={{2,1},{3,2},{6,5},{7,6},{10,9},{11,10},{14,13},{15,14},{18,17},{19... | collective-permute-start | bytes 6291464 | tf_op jit(solution)/shard_map/ppermute | solution.py:1465
  800.7 61.5 %collective-permute-start.5 = (bf16[512,2048]{1,0:T(8,128)(2,1)}, bf16[512,2048]{1,0:T(8,128)(2,1)}, u32[]{:S(2)}, u32[]{:S(2)}) collective-permute-start(bf16[512,2048]{1,0:T(8,128)(2,1)} %get-tuple-element.161), channel_id=1, source_target_pairs={{0,1},{1,2},{4,5},{5,6},{8,9},{9,10},{12,13},{13,14},{16,17},{17,1... | collective-permute-start | bytes 6291464 | tf_op jit(solution)/shard_map/ppermute | solution.py:1464
  805.6 36.5 %copy-start.1 = (s32[8]{0:T(128)S(1)}, s32[8]{0:T(128)}, u32[]{:S(2)}) copy-start(s32[8]{0:T(128)} %copy-done) | copy-start | bytes 100
  837.9 62.5 %all-to-all-start.3 = ((bf16[32,64,384]{2,1,0:T(8,128)(2,1)}), bf16[32,64,384]{2,1,0:T(8,128)(2,1)}, u32[]{:S(2)}, u32[]{:S(2)}) async-start(bf16[32,64,384]{2,1,0:T(8,128)(2,1)} %attend_backward.3), calls=%async_computation.4 | async-start | bytes 3145728 | tf_op jit(solution)/shard_map/all_to_all | solution.py:1457
  900.4 96.1 %copy-start.20 = (f32[1,8,256]{2,0,1:T(1,128)S(1)}, f32[1,8,256]{2,0,1:T(1,128)}, u32[]{:S(2)}) copy-start(f32[1,8,256]{2,0,1:T(1,128)} %copy-done.19) | copy-start | bytes 24580
  900.4 96.1 %copy-start.27 = (f32[512]{0:T(512)S(1)}, f32[512]{0:T(512)}, u32[]{:S(2)}) copy-start(f32[512]{0:T(512)} %copy-done.26) | copy-start | bytes 6148
  990.3 15.2 %copy-start.13 = (f32[256,768]{1,0:T(8,128)S(1)}, f32[256,768]{1,0:T(8,128)}, u32[]{:S(2)}) copy-start(f32[256,768]{1,0:T(8,128)} %get-tuple-element.106) | copy-start | bytes 2359300
  992.3 31.8 %collective-permute-start.10 = (bf16[256,512]{1,0:T(8,128)(2,1)}, bf16[256,512]{1,0:T(8,128)(2,1)}, u32[]{:S(2)}, u32[]{:S(2)}) collective-permute-start(bf16[256,512]{1,0:T(8,128)(2,1)} %get-tuple-element.163), channel_id=1, source_target_pairs={{0,3},{1,0},{2,1},{3,2},{4,7},{5,4},{6,5},{7,6},{8,11},{9,8},{10,9... | collective-permute-start | bytes 786440 | tf_op jit(solution)/shard_map/ppermute | solution.py:1526
  994.9 29.1 %collective-permute-start.8 = (bf16[256,512]{1,0:T(8,128)(2,1)S(1)}, bf16[256,512]{1,0:T(8,128)(2,1)}, u32[]{:S(2)}, u32[]{:S(2)}) collective-permute-start(bf16[256,512]{1,0:T(8,128)(2,1)S(1)} %get-tuple-element.162), channel_id=1, source_target_pairs={{0,1},{1,2},{2,3},{3,0},{4,5},{5,6},{6,7},{7,4},{8,9},{9,10},{10,1... | collective-permute-start | bytes 786440 | tf_op jit(solution)/shard_map/ppermute | solution.py:1526
  994.9 11.6 %copy-start.6 = (bf16[8,64,2048]{2,1,0:T(8,128)(2,1)S(1)}, bf16[8,64,2048]{2,1,0:T(8,128)(2,1)}, u32[]{:S(2)}) copy-start(bf16[8,64,2048]{2,1,0:T(8,128)(2,1)} %copy-done.4) | copy-start | bytes 6291460
  994.9 29.1 %collective-permute-start.9 = (bf16[256,512]{1,0:T(8,128)(2,1)S(1)}, bf16[256,512]{1,0:T(8,128)(2,1)}, u32[]{:S(2)}, u32[]{:S(2)}) collective-permute-start(bf16[256,512]{1,0:T(8,128)(2,1)S(1)} %get-tuple-element.164), channel_id=1, source_target_pairs={{0,2},{1,3},{2,0},{3,1},{4,6},{5,7},{6,4},{7,5},{8,10},{9,11},{10,... | collective-permute-start | bytes 786440 | tf_op jit(solution)/shard_map/ppermute | solution.py:1526
  1001.2 22.3 %all-to-all-start.4 = ((f32[32,2,256]{2,1,0:T(2,128)}), f32[32,2,256]{2,1,0:T(2,128)S(1)}, u32[]{:S(2)}, u32[]{:S(2)}) async-start(f32[32,2,256]{2,1,0:T(2,128)} %bitcast.28), calls=%async_computation.5 | async-start | bytes 131072 | tf_op jit(solution)/shard_map/all_to_all | solution.py:1576
  1016.3 5.1 copy-start.10
  (5 other events, 10.0 us)
Sparse Core Ops, SparseCore 0:
  120.9 84.2 all-gather.2
  207.1 142.8 all-gather.4
  663.6 87.3 reduce-scatter.2
  754.9 191.3 reduce-scatter.4
